TPU v7x, 32 devices: a whole 2x2x4 slice. The times are simulated.
32 devices in a mesh: dp: 8 (over z, x), mp: 4 (over y, core).
Axes of the slice: x: 2, y: 2, z: 4, core: 2. Of those that a mesh axis runs over, the one named last changes fastest.
Arguments:
- inputs: bfloat16 [16384, 768], P('dp'), may hold values from -6 to 6
- segments: int32 [256, 64], P('dp'), may hold values from 0 to 5, never falling along the last dimension, each value on 1 to 24 neighbouring positions
- cotangent: bfloat16 [16384, 768], P('dp'), may hold values from -12 to 12
- triple_weight: float32 [3, 768, 768], P(None, 'dp', 'mp'), may hold values from -0.21875 to 0.21875
- triple_first: float32 [3, 768, 768], P(None, 'dp', 'mp')
- triple_second: float32 [3, 768, 768], P(None, 'dp', 'mp'), as said below
- outward_weight: float32 [768, 768], P('mp', 'dp'), may hold values from -0.625 to 0.625
- outward_first: float32 [768, 768], P('mp', 'dp')
- outward_second: float32 [768, 768], P('mp', 'dp'), as said below
- expand_weight: float32 [768, 3072], P('dp', 'mp'), may hold values from -2 to 2
- expand_first: float32 [768, 3072], P('dp', 'mp')
- expand_second: float32 [768, 3072], P('dp', 'mp'), as said below
- reduce_weight: float32 [3072, 768], P('mp', 'dp'), may hold values from -0.109375 to 0.109375
- reduce_first: float32 [3072, 768], P('mp', 'dp')
- reduce_second: float32 [3072, 768], P('mp', 'dp'), as said below
- norm_params: float32 [6, 768], replicated, may hold values from -3 to 4
- norm_first: float32 [6, 768], replicated
- norm_second: float32 [6, 768], replicated, as said below
- paired_bias: float32 [2, 768], P(None, 'mp'), may hold values from -1.8 to 1.8
- paired_first: float32 [2, 768], P(None, 'mp')
- paired_second: float32 [2, 768], P(None, 'mp'), as said below
- hidden_bias: float32 [3072], P('mp'), may hold values from -1.8 to 1.8
- hidden_first: float32 [3072], P('mp')
- hidden_second: float32 [3072], P('mp'), as said below
Outputs:
- outputs: bfloat16 [16384, 768], P('dp')
- input_gradient: bfloat16 [16384, 768], P('dp')
- gradient_norm: float32 [], replicated
- triple_moment: float32 [3, 768, 768], P(None, 'dp', 'mp')
- triple_square: float32 [3, 768, 768], P(None, 'dp', 'mp')
- triple_updated: float32 [3, 768, 768], P(None, 'dp', 'mp')
- outward_moment: float32 [768, 768], P('mp', 'dp')
- outward_square: float32 [768, 768], P('mp', 'dp')
- outward_updated: float32 [768, 768], P('mp', 'dp')
- expand_moment: float32 [768, 3072], P('dp', 'mp')
- expand_square: float32 [768, 3072], P('dp', 'mp')
- expand_updated: float32 [768, 3072], P('dp', 'mp')
- reduce_moment: float32 [3072, 768], P('mp', 'dp')
- reduce_square: float32 [3072, 768], P('mp', 'dp')
- reduce_updated: float32 [3072, 768], P('mp', 'dp')
- norm_moment: float32 [6, 768], replicated
- norm_square: float32 [6, 768], replicated
- norm_updated: float32 [6, 768], replicated
- paired_moment: float32 [2, 768], P(None, 'mp')
- paired_square: float32 [2, 768], P(None, 'mp')
- paired_updated: float32 [2, 768], P(None, 'mp')
- hidden_moment: float32 [3072], P('mp')
- hidden_square: float32 [3072], P('mp')
- hidden_updated: float32 [3072], P('mp')
Inputs may be any that keep to these rules, and one draw needn't show every extreme that they name: `segments`: within each row of 64 tokens the numbers never fall; each of the 6 captions holds 1 to 24 tokens, one exactly 24. `triple_second`: positive. `outward_second`: positive. `expand_second`: positive. `reduce_second`: positive. `norm_second`: positive. `paired_second`: positive. `hidden_second`: positive.
All inputs are finite; a program needn't handle non-finite values.
Results may differ from a plain program's by a relative error of at most 0.02.
Values may be sent and summed in bfloat16 or wider, within the bound.
No kernel may reach another device: no remote copies, remote signals or barrier semaphores. Data moves between devices by JAX's collectives and lax.ppermute only.
A program may use at most 128 MiB of HBM per device.

v0:
```python
import jax
import jax.numpy as jnp
from jax import lax
from jax.sharding import PartitionSpec as P

HD = 64
STEP = 5


EPS_NORM = 1e-06
BETA = 0.5
LR_MATRIX = 0.03
LR_VECTOR = 0.2
DECAY = 0.1
ADAM_EPS = 1e-08
CLIP = 1.0
NEG = -1e30


def norm_forward(rows_in, gain_row, shift_row):
    row_mean = jnp.mean(rows_in, axis=-1, keepdims=True)
    centred = rows_in - row_mean
    variance = jnp.mean(centred * centred, axis=-1, keepdims=True)
    scaled = lax.rsqrt(variance + EPS_NORM)
    normal_rows = centred * scaled
    return (normal_rows * gain_row + shift_row, normal_rows, scaled)


def norm_backward(upstream, normal_rows, scaled, gain_row):
    gained = upstream * gain_row
    mean_one = jnp.mean(gained, axis=-1, keepdims=True)
    mean_two = jnp.mean(gained * normal_rows, axis=-1, keepdims=True)
    return scaled * (gained - mean_one - normal_rows * mean_two)


def smooth_gate(values_in):
    return jax.nn.gelu(values_in, approximate=True)


def adam_step(weight, first, second, grad, factor, rate, decay):
    clipped = grad * factor
    first_new = BETA * first + (1.0 - BETA) * clipped
    second_new = BETA * second + (1.0 - BETA) * clipped * clipped
    correction = 1.0 - BETA**STEP
    direction = first_new / correction / (jnp.sqrt(second_new / correction) + ADAM_EPS)
    return (first_new, second_new, weight - rate * (direction + decay * weight))


def per_device(
    inputs,
    segments,
    cotangent,
    triple_weight,
    triple_first,
    triple_second,
    outward_weight,
    outward_first,
    outward_second,
    expand_weight,
    expand_first,
    expand_second,
    reduce_weight,
    reduce_first,
    reduce_second,
    norm_params,
    norm_first,
    norm_second,
    paired_bias,
    paired_first,
    paired_second,
    hidden_bias,
    hidden_first,
    hidden_second,
):
    f32 = jnp.float32
    bf16 = jnp.bfloat16
    dp_count = lax.axis_size("dp")
    mp_count = lax.axis_size("mp")
    triple_full, outward_full, expand_full, reduce_full = (
        lax.all_gather(triple_weight.astype(bf16), "dp", axis=1, tiled=True),
        lax.all_gather(outward_weight.astype(bf16), "dp", axis=1, tiled=True),
        lax.all_gather(expand_weight.astype(bf16), "dp", axis=0, tiled=True),
        lax.all_gather(reduce_weight.astype(bf16), "dp", axis=1, tiled=True),
    )
    row_count, row_length = segments.shape
    token_count = inputs.shape[0]
    head_width = triple_full.shape[2]
    head_count = head_width // HD
    scale_factor = HD ** (-0.5)
    grid = (row_count, row_length, head_count, HD)
    x_full = inputs.astype(f32)
    normed_one, normal_one, scaled_one = norm_forward(x_full, norm_params[0], norm_params[1])
    first_low = normed_one.astype(bf16)
    projected = jnp.einsum("td,cdw->ctw", first_low, triple_full, preferred_element_type=f32)
    queries = (projected[0] + paired_bias[0]).astype(bf16).reshape(grid)
    key_rows = projected[1].astype(bf16).reshape(grid)
    value_rows = (projected[2] + paired_bias[1]).astype(bf16).reshape(grid)
    same_caption = (segments[:, :, None] == segments[:, None, :])[:, None, :, :]

    def scores_of(query_in, key_in):
        raw_scores = jnp.einsum("rqhd,rkhd->rhqk", query_in, key_in, preferred_element_type=f32)
        return jnp.where(same_caption, raw_scores * scale_factor, NEG)

    scores = scores_of(queries, key_rows)
    row_top = jnp.max(scores, axis=-1, keepdims=True)
    lifted = jnp.exp(scores - row_top)
    row_total = jnp.sum(lifted, axis=-1, keepdims=True)
    probs = lifted / row_total
    log_total = row_top + jnp.log(row_total)
    context = jnp.einsum(
        "rhqk,rkhd->rqhd", probs.astype(bf16), value_rows, preferred_element_type=f32
    )
    context_low = context.astype(bf16).reshape(token_count, head_width)
    attn_part = jnp.dot(context_low, outward_full, preferred_element_type=f32)
    attended = lax.psum(attn_part.astype(jnp.bfloat16), "mp").astype(jnp.float32)
    middle = x_full + attended + norm_params[4]
    normed_two, normal_two, scaled_two = norm_forward(middle, norm_params[2], norm_params[3])
    second_low = normed_two.astype(bf16)
    hidden_pre = jnp.dot(second_low, expand_full, preferred_element_type=f32) + hidden_bias
    gate_out, gelu_pull = jax.vjp(smooth_gate, hidden_pre)
    activated = gate_out.astype(bf16)
    fed_part = jnp.dot(activated, reduce_full, preferred_element_type=f32)
    fed = lax.psum(fed_part.astype(jnp.bfloat16), "mp").astype(jnp.float32)
    outputs = (middle + fed + norm_params[5]).astype(bf16)
    cot_full = cotangent.astype(f32)
    grad_reduce = jnp.einsum("tf,td->fd", activated, cotangent, preferred_element_type=f32)
    act_grad = jnp.einsum("td,fd->tf", cotangent, reduce_full, preferred_element_type=f32)
    hidden_grad = gelu_pull(act_grad)[0].astype(bf16)
    grad_expand = jnp.einsum("td,tf->df", second_low, hidden_grad, preferred_element_type=f32)
    grad_hidden = jnp.sum(hidden_grad, axis=0, dtype=f32)
    second_part = jnp.einsum("tf,df->td", hidden_grad, expand_full, preferred_element_type=f32)
    second_grad = lax.psum(second_part.astype(jnp.bfloat16), "mp").astype(jnp.float32)
    middle_grad = cot_full + norm_backward(second_grad, normal_two, scaled_two, norm_params[2])
    middle_low = middle_grad.astype(bf16)
    grad_outward = jnp.einsum("tw,td->wd", context_low, middle_low, preferred_element_type=f32)
    context_grad = (
        jnp.einsum("td,wd->tw", middle_low, outward_full, preferred_element_type=f32)
        .astype(bf16)
        .reshape(grid)
    )
    probs_again = jnp.exp(scores_of(queries, key_rows) - log_total)
    probs_low = probs_again.astype(bf16)
    value_grad = jnp.einsum(
        "rhqk,rqhd->rkhd", probs_low, context_grad, preferred_element_type=f32
    ).astype(bf16)
    prob_grad = jnp.einsum("rqhd,rkhd->rhqk", context_grad, value_rows, preferred_element_type=f32)
    inner = jnp.sum(prob_grad * probs_again, axis=-1, keepdims=True)
    score_grad = (probs_again * (prob_grad - inner) * scale_factor).astype(bf16)
    query_grad = jnp.einsum(
        "rhqk,rkhd->rqhd", score_grad, key_rows, preferred_element_type=f32
    ).astype(bf16)
    key_grad = jnp.einsum(
        "rhqk,rqhd->rkhd", score_grad, queries, preferred_element_type=f32
    ).astype(bf16)
    stacked = jnp.stack([query_grad, key_grad, value_grad]).reshape(3, token_count, head_width)
    grad_triple = jnp.einsum("td,ctw->cdw", first_low, stacked, preferred_element_type=f32)
    grad_paired = jnp.stack(
        [jnp.sum(stacked[0], axis=0, dtype=f32), jnp.sum(stacked[2], axis=0, dtype=f32)]
    )
    first_part = jnp.einsum("ctw,cdw->td", stacked, triple_full, preferred_element_type=f32)
    first_grad = lax.psum(first_part.astype(jnp.bfloat16), "mp").astype(jnp.float32)
    input_gradient = (
        middle_grad + norm_backward(first_grad, normal_one, scaled_one, norm_params[0])
    ).astype(bf16)
    grad_norms = jnp.stack(
        [
            jnp.sum(first_grad * normal_one, axis=0),
            jnp.sum(first_grad, axis=0),
            jnp.sum(second_grad * normal_two, axis=0),
            jnp.sum(second_grad, axis=0),
            jnp.sum(middle_grad, axis=0),
            jnp.sum(cot_full, axis=0),
        ]
    )
    owned = (
        lax.psum_scatter(grad_triple, "dp", scatter_dimension=1, tiled=True),
        lax.psum_scatter(grad_outward, "dp", scatter_dimension=1, tiled=True),
        lax.psum_scatter(grad_expand, "dp", scatter_dimension=0, tiled=True),
        lax.psum_scatter(grad_reduce, "dp", scatter_dimension=1, tiled=True),
    )
    vectors = lax.psum((grad_norms, grad_paired, grad_hidden), "dp")
    local_square = jnp.zeros((), f32)
    for grad_item in owned:
        local_square = local_square + jnp.sum(grad_item * grad_item)
    local_square = local_square + jnp.sum(vectors[0] * vectors[0]) / (dp_count * mp_count)
    local_square = (
        local_square
        + (jnp.sum(vectors[1] * vectors[1]) + jnp.sum(vectors[2] * vectors[2])) / dp_count
    )
    total_square = lax.psum(local_square, ("dp", "mp"))
    gradient_norm = jnp.sqrt(total_square)
    factor = jnp.minimum(1.0, CLIP / gradient_norm)
    triple_new = adam_step(
        triple_weight, triple_first, triple_second, owned[0], factor, LR_MATRIX, DECAY
    )
    outward_new = adam_step(
        outward_weight, outward_first, outward_second, owned[1], factor, LR_MATRIX, DECAY
    )
    expand_new = adam_step(
        expand_weight, expand_first, expand_second, owned[2], factor, LR_MATRIX, DECAY
    )
    reduce_new = adam_step(
        reduce_weight, reduce_first, reduce_second, owned[3], factor, LR_MATRIX, DECAY
    )
    norm_new = adam_step(norm_params, norm_first, norm_second, vectors[0], factor, LR_VECTOR, 0.0)
    paired_new = adam_step(
        paired_bias, paired_first, paired_second, vectors[1], factor, LR_VECTOR, 0.0
    )
    hidden_new = adam_step(
        hidden_bias, hidden_first, hidden_second, vectors[2], factor, LR_VECTOR, 0.0
    )
    return (
        outputs,
        input_gradient,
        gradient_norm,
        triple_new[0],
        triple_new[1],
        triple_new[2],
        outward_new[0],
        outward_new[1],
        outward_new[2],
        expand_new[0],
        expand_new[1],
        expand_new[2],
        reduce_new[0],
        reduce_new[1],
        reduce_new[2],
        norm_new[0],
        norm_new[1],
        norm_new[2],
        paired_new[0],
        paired_new[1],
        paired_new[2],
        hidden_new[0],
        hidden_new[1],
        hidden_new[2],
    )


def solution(mesh):
    placed = (
        P("dp", None),
        P("dp", None),
        P("dp", None),
        P(None, "dp", "mp"),
        P(None, "dp", "mp"),
        P(None, "dp", "mp"),
        P("mp", "dp"),
        P("mp", "dp"),
        P("mp", "dp"),
        P("dp", "mp"),
        P("dp", "mp"),
        P("dp", "mp"),
        P("mp", "dp"),
        P("mp", "dp"),
        P("mp", "dp"),
        P(),
        P(),
        P(),
        P(None, "mp"),
        P(None, "mp"),
        P(None, "mp"),
        P("mp"),
        P("mp"),
        P("mp"),
    )
    return jax.shard_map(
        per_device,
        mesh=mesh,
        in_specs=placed,
        out_specs=(
            P("dp", None),
            P("dp", None),
            P(),
            P(None, "dp", "mp"),
            P(None, "dp", "mp"),
            P(None, "dp", "mp"),
            P("mp", "dp"),
            P("mp", "dp"),
            P("mp", "dp"),
            P("dp", "mp"),
            P("dp", "mp"),
            P("dp", "mp"),
            P("mp", "dp"),
            P("mp", "dp"),
            P("mp", "dp"),
            P(),
            P(),
            P(),
            P(None, "mp"),
            P(None, "mp"),
            P(None, "mp"),
            P("mp"),
            P("mp"),
            P("mp"),
        ),
        check_vma=False,
    )
```

profile of v0, /device:TPU:0, one launch (start us, length us, event | category | flops | bytes accessed | tf_op | source)
XLA Modules:
  0.0 715.4 jit_solution(5087993690982692376)
XLA Ops:
  12.8 40.5 %all_gather.12 = bf16[3,768,192]{2,0,1:T(4,128)(2,1)} all-gather(bf16[3,96,192]{2,0,1:T(4,128)(2,1)S(1)} %copy.118), channel_id=1, replica_groups=mesh['dp'=8,'mp'=4] {'dp'}, dimensions={1}, use_global_device_ids=true | all-gather | bytes 995328 | tf_op jit(solution)/shard_map/all_gather | solution.py:80
  65.1 31.9 %all_gather.13 = bf16[192,768]{0,1:T(8,128)(2,1)S(1)} all-gather(bf16[192,96]{0,1:T(8,128)(2,1)} %copy.127), channel_id=1, replica_groups=mesh['dp'=8,'mp'=4] {'dp'}, dimensions={1}, use_global_device_ids=true | all-gather | bytes 331776 | tf_op jit(solution)/shard_map/all_gather | solution.py:81
  107.4 3.9 copy.120
  114.9 5.7 fusion.108
  130.4 3.9 convolution_convert_fusion.2
  138.0 63.8 %all-reduce.6.cloned.1.call-done = bf16[2048,768]{1,0:T(8,128)(2,1)} async-done(((bf16[2048,768]{1,0:T(8,128)(2,1)}), bf16[2048,768]{1,0:T(8,128)(2,1)}) %all-reduce.6.cloned.1.call-update) | async-done | bytes 3145744 | tf_op jit(solution)/shard_map/psum | solution.py:115
  210.4 7.5 %fusion.111 = f32[2048,768]{1,0:T(8,128)} fusion(bf16[2048,768]{1,0:T(8,128)(2,1)} %add_convert_fusion.1, bf16[768,768]{1,0:T(8,128)(2,1)} %all-gather.3.cloned.1.call-done), kind=kOutput, calls=%fused_computation.161 | convolution fusion | flops 2415919104 | bytes 10616832 | tf_op jit(solution)/shard_map/dot_general | solution.py:119
  220.3 10.8 %convert_reduce_fusion.4 = (f32[768]{0:T(1024)}, bf16[2048,768]{1,0:T(8,128)(2,1)S(1)}, bf16[2048,768]{1,0:T(8,128)(2,1)}) fusion(f32[2048,768]{1,0:T(8,128)} %fusion.111, f32[768]{0:T(1024)} %param.45, bf16[2048,768]{1,0:T(8,128)(2,1)} %param.26, bf16[768,768]{0,1:T(8,128)(2,1)} %all-gather.5.cloned.1.call-done), kind=kOutput, calls=%fused_computation.46 | convolution fusion | flops 2455239936 | bytes 16914432 | tf_op jit(solution)/shard_map/td,fd->tf/dot_general | solution.py:127
  232.8 4.0 convolution_convert_fusion
  238.7 6.6 convolution_convert_fusion.1
  245.2 58.7 %all-reduce.8.cloned.1.call-done = bf16[2048,768]{1,0:T(8,128)(2,1)} async-done(((bf16[2048,768]{1,0:T(8,128)(2,1)}), bf16[2048,768]{1,0:T(8,128)(2,1)}) %all-reduce.8.cloned.1.call-update) | async-done | bytes 3145744 | tf_op jit(solution)/shard_map/psum | solution.py:132
  303.9 7.1 fusion.30
  311.1 4.7 fusion.106
  320.7 4.9 convolution_convert_fusion.3
  332.7 5.1 fusion.81
  337.8 10.3 %fusion.71 = bf16[32,64,3,64]{1,3,2,0:T(8,128)(2,1)} fusion(f32[32,3,64,64]{2,3,1,0:T(8,128)} %fusion.81, f32[32,3,64,64]{2,3,1,0:T(8,128)} %copy-done.4, f32[32,3,64]{2,1,0:T(4,128)S(1)} %copy-done.23, f32[32,64,3,64]{1,0,3,2:T(8,128)} %squeeze.10, f32[3,64]{1,0:T(4,128)S(1)} %copy-done.47), kind=kOutput, calls=%fused_computation.91 | convolution fusion | flops 54270016 | bytes 5530368 | tf_op jit(solution)/shard_map/rhqk,rqhd->rkhd/dot_general | solution.py:152
  348.1 8.1 %convert_reduce_fusion.6 = (f32[3,64]{1,0:T(4,128)S(1)}, bf16[32,64,3,64]{3,1,2,0:T(8,128)(2,1)}) fusion(bf16[32,64,3,64]{3,1,2,0:T(8,128)(2,1)} %copy.123, f32[32,3,64,64]{2,3,1,0:T(8,128)} %fusion.81, f32[32,3,64,64]{2,3,1,0:T(8,128)} %copy-done.4, f32[32,3,64]{2,1,0:T(4,128)S(1)} %copy-done.23), kind=kOutput, calls=%fused_computation.60 | convolution fusion | flops 54269824 | bytes 4743936 | tf_op jit(solution)/shard_map/rhqk,rkhd->rqhd/dot_general | solution.py:149
  356.2 4.4 convert_reduce_fusion.5
  360.6 3.6 copy.131
  387.9 6.0 bitcast_convert_fusion
  394.0 7.1 fusion.112
  401.4 6.9 fusion.113
  408.4 5.2 fusion.65
  413.6 4.2 copy.149
  417.8 4.7 reshape.151
  429.0 85.0 %all-reduce.10.cloned.1.call-done = (bf16[2048,768]{1,0:T(8,128)(2,1)}, bf16[2048,768]{1,0:T(8,128)(2,1)}) async-done(((bf16[2048,768]{1,0:T(8,128)(2,1)}, bf16[2048,768]{1,0:T(8,128)(2,1)}), (bf16[2048,768]{1,0:T(8,128)(2,1)}, bf16[2048,768]{1,0:T(8,128)(2,1)})) %all-reduce.10.cloned.1.call-update) | async-done | bytes 6291472 | tf_op jit(solution)/shard_map/psum | solution.py:123
  514.0 4.6 fusion.31
  518.7 37.3 %all-reduce = (f32[6,768]{1,0:T(8,128)S(1)}, f32[2,192]{1,0:T(2,128)S(1)}, f32[768]{0:T(1024)S(1)}) all-reduce(f32[6,768]{1,0:T(8,128)S(1)} %stack.52, f32[2,192]{1,0:T(2,128)S(1)} %pad_maximum_fusion, f32[768]{0:T(1024)S(1)} %copy-done.53), channel_id=1, replica_groups=mesh['dp'=8,'mp'=4] {'dp'}, use_global_device_ids=true, to_apply=%region_29.30 | all-reduce | flops 5760 | bytes 46080 | tf_op jit(solution)/shard_map/psum | solution.py:181
  561.4 6.3 reduce-scatter.11.cloned.1.call-done
  570.5 67.2 %reduce-scatter.13.cloned.1.call-done = f32[96,576]{1,0:T(8,128)} async-done(((f32[768,576]{1,0:T(8,128)}), f32[96,576]{1,0:T(8,128)}) %reduce-scatter.13.cloned.1.call-update) | async-done | bytes 221200
  644.0 10.6 %fusion.16 = (bf16[2048,768]{1,0:T(8,128)(2,1)}, bf16[2048,768]{1,0:T(8,128)(2,1)}) fusion(f32[2048,768]{1,0:T(8,128)} %copy-done.3, bf16[2048,768]{1,0:T(8,128)(2,1)S(1)} %copy-done, bf16[2048,768]{1,0:T(8,128)(2,1)} %get-tuple-element.140, f32[2048]{0:T(1024)} %broadcast_multiply_fusion, f32[2048]{0:T(1024)} %broadcast_multiply_fusion.1, ...), kind=kLoop, calls=%fused_computation.29 | loop fusion | flops 28311552 | bytes 25207808 | tf_op jit(solution)/shard_map/convert_element_type | solution.py:164
  654.7 39.5 %psum.63 = f32[]{:T(128)} all-reduce(f32[]{:T(128)S(6)} %add.294), channel_id=1, replica_groups=mesh['dp'=8,'mp'=4] {'dp','mp'}, use_global_device_ids=true, to_apply=%region_38.39 | all-reduce | flops 1 | bytes 8 | tf_op jit(solution)/shard_map/psum | solution.py:190
  (217 shorter events, 122.9 us)
Async XLA Ops:
  8.1 193.7 %all-reduce.6.cloned.1.call-start = ((), (), s32[]{:S(2)}) async-start(), calls=%async_computation.4 | async-start | bytes 6291456 | tf_op jit(solution)/shard_map/psum | solution.py:115
  10.9 45.8 %copy-start.25 = (f32[2048]{0:T(1024)}, f32[2048]{0:T(1024)S(1)}, u32[]{:S(2)}) copy-start(f32[2048]{0:T(1024)S(1)} %broadcast_multiply_fusion.5) | copy-start | bytes 24580
  12.0 48.1 %copy-start.32 = (f32[2048]{0:T(1024)}, f32[2048]{0:T(1024)S(1)}, u32[]{:S(2)}) copy-start(f32[2048]{0:T(1024)S(1)} %add_rsqrt_fusion.1) | copy-start | bytes 24580
  12.6 47.5 %copy-start.35 = (f32[768]{0:T(1024)}, f32[768]{0:T(1024)S(1)}, u32[]{:S(2)}) copy-start(f32[768]{0:T(1024)S(1)} %get-tuple-element.133) | copy-start | bytes 9220
  12.6 47.5 %copy-start.54 = (f32[768]{0:T(1024)}, f32[768]{0:T(1024)S(1)}, u32[]{:S(2)}) copy-start(f32[768]{0:T(1024)S(1)} %get-tuple-element.132) | copy-start | bytes 9220
  63.2 58.3 %copy-start.44 = (f32[3,64]{1,0:T(4,128)}, f32[3,64]{1,0:T(4,128)S(1)}, u32[]{:S(2)}) copy-start(f32[3,64]{1,0:T(4,128)S(1)} %add.264) | copy-start | bytes 2308
  63.3 51.6 %copy-start.46 = (f32[3,64]{1,0:T(4,128)}, f32[3,64]{1,0:T(4,128)S(1)}, u32[]{:S(2)}) copy-start(f32[3,64]{1,0:T(4,128)S(1)} %add.267) | copy-start | bytes 2308
  134.3 76.0 %all-gather.3.cloned.1.call-start = ((), (), s32[]{:S(2)}) async-start(), calls=%async_computation.5 | async-start | bytes 1327104 | tf_op jit(solution)/shard_map/all_gather | solution.py:82
  136.0 84.2 %all-gather.5.cloned.1.call-start = ((), (), s32[]{:S(2)}) async-start(), calls=%async_computation.6 | async-start | bytes 1327104 | tf_op jit(solution)/shard_map/all_gather | solution.py:83
  137.8 166.2 %all-reduce.8.cloned.1.call-start = ((), (), s32[]{:S(2)}) async-start(), calls=%async_computation.7 | async-start | bytes 6291456 | tf_op jit(solution)/shard_map/psum | solution.py:132
  220.3 12.5 %copy-start.56 = (bf16[768,768]{1,0:T(8,128)(2,1)S(1)}, bf16[768,768]{1,0:T(8,128)(2,1)}, u32[]{:S(2)}) copy-start(bf16[768,768]{1,0:T(8,128)(2,1)} %all-gather.3.cloned.1.call-done) | copy-start | bytes 3538948
  236.9 190.5 %reduce-scatter.15.cloned.1.call-start = ((), (), s32[]{:S(2)}) async-start(), calls=%async_computation.11 | async-start | bytes 884736
  360.5 153.4 %all-reduce.10.cloned.1.call-start = ((), (), s32[]{:S(2)}) async-start(), calls=%async_computation.12 | async-start | bytes 12582912 | tf_op jit(solution)/shard_map/psum | solution.py:123
  394.0 165.8 %reduce-scatter.9.cloned.1.call-start = ((), (), s32[]{:S(2)}) async-start(), calls=%async_computation.8 | async-start | bytes 2654208 | tf_op jit(solution)/shard_map/reduce_scatter | solution.py:178
  401.1 166.6 %reduce-scatter.11.cloned.1.call-start = ((), (), s32[]{:S(2)}) async-start(), calls=%async_computation.9 | async-start | bytes 2654208 | tf_op jit(solution)/shard_map/reduce_scatter | solution.py:179
  408.3 229.4 %reduce-scatter.13.cloned.1.call-start = ((), (), s32[]{:S(2)}) async-start(), calls=%async_computation.10 | async-start | bytes 2211840
  556.0 83.6 %copy-start.30 = (f32[6,768]{1,0:T(8,128)}, f32[6,768]{1,0:T(8,128)S(1)}, u32[]{:S(2)}) copy-start(f32[6,768]{1,0:T(8,128)S(1)} %get-tuple-element.136) | copy-start | bytes 55300
  556.0 83.6 %copy-start.40 = (f32[768]{0:T(1024)}, f32[768]{0:T(1024)S(1)}, u32[]{:S(2)}) copy-start(f32[768]{0:T(1024)S(1)} %get-tuple-element.138) | copy-start | bytes 9220
  556.0 83.6 %copy-start.48 = (f32[2,192]{1,0:T(2,128)}, f32[2,192]{1,0:T(2,128)S(1)}, u32[]{:S(2)}) copy-start(f32[2,192]{1,0:T(2,128)S(1)} %get-tuple-element.137) | copy-start | bytes 4612
  654.6 44.5 %copy-start.49 = (f32[2,192]{1,0:T(2,128)S(1)}, f32[2,192]{1,0:T(2,128)}, u32[]{:S(2)}) copy-start(f32[2,192]{1,0:T(2,128)} %copy-done.48) | copy-start | bytes 4612
  654.6 44.5 %copy-start.51 = (f32[2,192]{1,0:T(2,128)S(1)}, f32[2,192]{1,0:T(2,128)}, u32[]{:S(2)}) copy-start(f32[2,192]{1,0:T(2,128)} %param.42) | copy-start | bytes 4612
  654.6 45.8 %copy-start.41 = (f32[768]{0:T(1024)S(1)}, f32[768]{0:T(1024)}, u32[]{:S(2)}) copy-start(f32[768]{0:T(1024)} %copy-done.40) | copy-start | bytes 9220
  654.6 45.8 %copy-start.52 = (f32[768]{0:T(1024)S(1)}, f32[768]{0:T(1024)}, u32[]{:S(2)}) copy-start(f32[768]{0:T(1024)} %param.45) | copy-start | bytes 9220
  654.7 48.5 %copy-start.18 = (f32[192,96]{1,0:T(8,128)S(1)}, f32[192,96]{1,0:T(8,128)}, u32[]{:S(2)}) copy-start(f32[192,96]{1,0:T(8,128)} %param.30) | copy-start | bytes 221188
  654.7 48.5 %copy-start.29 = (f32[192,96]{1,0:T(8,128)S(1)}, f32[192,96]{1,0:T(8,128)}, u32[]{:S(2)}) copy-start(f32[192,96]{1,0:T(8,128)} %param.32) | copy-start | bytes 221188
  654.7 50.1 %copy-start.9 = (f32[96,768]{1,0:T(8,128)S(1)}, f32[96,768]{1,0:T(8,128)}, u32[]{:S(2)}) copy-start(f32[96,768]{1,0:T(8,128)} %param.33) | copy-start | bytes 884740
  654.7 50.1 %copy-start.11 = (f32[96,768]{1,0:T(8,128)S(1)}, f32[96,768]{1,0:T(8,128)}, u32[]{:S(2)}) copy-start(f32[96,768]{1,0:T(8,128)} %reduce-scatter.9.cloned.1.call-done) | copy-start | bytes 884740
  654.7 50.1 %copy-start.19 = (f32[96,768]{1,0:T(8,128)S(1)}, f32[96,768]{1,0:T(8,128)}, u32[]{:S(2)}) copy-start(f32[96,768]{1,0:T(8,128)} %param.35) | copy-start | bytes 884740
  654.7 50.1 %copy-start.20 = (f32[96,768]{1,0:T(8,128)S(1)}, f32[96,768]{1,0:T(8,128)}, u32[]{:S(2)}) copy-start(f32[96,768]{1,0:T(8,128)} %param.34) | copy-start | bytes 884740
  695.0 10.9 %copy-start.10 = (f32[768,96]{0,1:T(8,128)S(1)}, f32[768,96]{0,1:T(8,128)}, u32[]{:S(2)}) copy-start(f32[768,96]{0,1:T(8,128)} %param.36) | copy-start | bytes 884740
  695.0 10.9 %copy-start.12 = (f32[768,96]{0,1:T(8,128)S(1)}, f32[768,96]{0,1:T(8,128)}, u32[]{:S(2)}) copy-start(f32[768,96]{0,1:T(8,128)} %reduce-scatter.11.cloned.1.call-done) | copy-start | bytes 884740
  695.0 10.9 %copy-start.21 = (f32[768,96]{0,1:T(8,128)S(1)}, f32[768,96]{0,1:T(8,128)}, u32[]{:S(2)}) copy-start(f32[768,96]{0,1:T(8,128)} %param.38) | copy-start | bytes 884740
  (35 other events, 164.8 us)
Sparse Core Ops, SparseCore 0:
  134.4 67.2 all-reduce.5
  237.0 66.9 all-reduce.7
  394.1 119.8 all-reduce.9
Sparse Core Ops, SparseCore 1:
  137.6 40.2 all-gather.2
  180.5 39.8 all-gather.4
  360.6 62.6 reduce-scatter.14
  427.2 68.3 reduce-scatter.8
  499.5 68.2 reduce-scatter.10
  571.6 66.1 reduce-scatter.12
where the time goes:
time: 722 us; the launch traced here: 715 us
  waiting for transfers between devices  284 us (39%)
  blocking collectives  149 us (21%)
  matrix products  103 us (14%)
  local copies, waits for them, and re-layouts  94 us (13%)
  other arithmetic  62.2 us (9%)
  between operations  22.6 us (3%)
    psum x1, waiting for transfers between devices, per_device(): fed = lax.psum(fed_part.astype(jnp.bfloat16), 'mp').astype(jnp.float32)  85 us
    unnamed x11, waiting for transfers between devices  67.4 us
    psum x1, waiting for transfers between devices, per_device(): lax.psum(attn_part.astype(jnp.bfloat16), 'mp').astype(jnp.float32)  63.8 us
    psum x1, waiting for transfers between devices, per_device(): lax.psum(second_part.astype(jnp.bfloat16), 'mp').astype(jnp.float32)  58.7 us
    all_gather x1, blocking collectives, per_device(): lax.all_gather(triple_weight.astype(bf16), 'dp', axis=1, tiled=True)  40.5 us
    psum x1, blocking collectives, per_device(): total_square = lax.psum(local_square, ('dp', 'mp'))  39.5 us
    psum x1, blocking collectives, per_device(): vectors = lax.psum((grad_norms, grad_paired, grad_hidden), 'dp')  37.3 us
    unnamed x130, local copies, waits for them, and re-layouts  32.6 us
  transfers between devices with their start and end apart: 9, of which 6 were waited for; matrix products, arithmetic and copies ran while one was open for 15% of the time, Pallas kernels for 0%

commit v1 on v0

v1 whole, which is shorter than its diff:
```python
import functools

import jax
import jax.numpy as jnp
from jax import lax
from jax.experimental import pallas as pl
from jax.experimental.pallas import tpu as pltpu
from jax.sharding import PartitionSpec as P

HD = 64
STEP = 5
EPS_NORM = 1e-06
BETA = 0.5
LR_MATRIX = 0.03
LR_VECTOR = 0.2
DECAY = 0.1
ADAM_EPS = 1e-08
CLIP = 1.0
NEG = -1e30
GELU_C = 0.7978845608028654
GELU_K = 0.044715

f32 = jnp.float32
bf16 = jnp.bfloat16
AXES = ("dp", "mp")
LANES = 128
CHUNK = 256
MIB = 1 << 20


def mm(left, right):
    return lax.dot_general(left, right, (((1,), (0,)), ((), ())), preferred_element_type=f32)


def mm_nt(left, right):
    return lax.dot_general(left, right, (((1,), (1,)), ((), ())), preferred_element_type=f32)


def mm_tn(left, right):
    return lax.dot_general(left, right, (((0,), (0,)), ((), ())), preferred_element_type=f32)


def norm_stats(rows_in):
    centred = rows_in - jnp.mean(rows_in, axis=-1, keepdims=True)
    scaled = lax.rsqrt(jnp.mean(centred * centred, axis=-1, keepdims=True) + EPS_NORM)
    return centred * scaled, scaled


def norm_backward(upstream, normal_rows, scaled, gain_row):
    gained = upstream * gain_row
    mean_one = jnp.mean(gained, axis=-1, keepdims=True)
    mean_two = jnp.mean(gained * normal_rows, axis=-1, keepdims=True)
    return scaled * (gained - mean_one - normal_rows * mean_two)


def lane_low(shape):
    return lax.broadcasted_iota(jnp.int32, shape, 1) % LANES < HD


def split_heads(block):
    low = lane_low(block.shape)
    zero = jnp.zeros_like(block)
    return jnp.concatenate([jnp.where(low, block, zero), jnp.where(low, zero, block)], axis=0)


def join_heads(stacked):
    half = stacked.shape[0] // 2
    low = lane_low((half, stacked.shape[1]))
    return jnp.where(low, stacked[:half], stacked[half:])


class Plan:
    def __init__(self, ndp, nmp, width, hidden):
        assert ndp % 2 == 0 and nmp == 4
        self.ndev = ndp * nmp
        self.nz = ndp // 2
        self.rows = width // ndp
        self.half = self.rows // 2
        self.width = width
        self.cols = width // 2
        self.part = hidden // nmp
        self.direct = self.half % 16 == 0

    def perm(self, move):
        pairs = []
        for z in range(self.nz):
            for x in range(2):
                for y in range(2):
                    for c in range(2):
                        there = move(z, x, y, c)
                        pairs.append((self.index(z, x, y, c), self.index(*there)))
        return pairs

    def index(self, z, x, y, c):
        return (2 * z + x) * 4 + 2 * y + c

    def core(self, value):
        return lax.ppermute(value, AXES, self.perm(lambda z, x, y, c: (z, x, y, 1 - c)))

    def along_x(self, value):
        return lax.ppermute(value, AXES, self.perm(lambda z, x, y, c: (z, 1 - x, y, c)))

    def along_y(self, value):
        return lax.ppermute(value, AXES, self.perm(lambda z, x, y, c: (z, x, 1 - y, c)))

    def along_z(self, value, step):
        return lax.ppermute(
            value, AXES, self.perm(lambda z, x, y, c: ((z + step) % self.nz, x, y, c))
        )

    def first(self, value):
        return lax.ppermute(
            value,
            AXES,
            self.perm(lambda z, x, y, c: (z, x, 1 - y, c) if c else (z, 1 - x, y, c)),
        )

    def second(self, value):
        return lax.ppermute(
            value,
            AXES,
            self.perm(lambda z, x, y, c: (z, 1 - x, y, c) if c else (z, x, 1 - y, c)),
        )


def piece_spot(plan, meta, r, fy, fx, k, sign):
    z, x, y, c = meta[1], meta[2], meta[3], meta[4]
    cc = jnp.bitwise_xor(c, r)
    zz = lax.rem(z + sign * k + plan.nz, plan.nz)
    xx = jnp.bitwise_xor(x, fx)
    yy = jnp.bitwise_xor(y, fy)
    return cc, zz, xx, yy


def attn_weight_copies(plan, meta, own, other, w, sem, lanes):
    if not plan.direct:
        src = own.at[:, :, lanes]
        return [pltpu.make_async_copy(src, w, sem.at[0])]
    copies = []
    for r, src in enumerate((own, other)):
        for s2 in range(2):
            for s1 in range(2):
                for k in range(plan.nz):
                    cc = jnp.bitwise_xor(meta[4], r)
                    fx = jnp.where(cc == 0, s1, s2)
                    fy = jnp.where(cc == 0, s2, s1)
                    _, zz, xx, yy = piece_spot(plan, meta, r, fy, fx, k, -1)
                    row = pl.multiple_of((zz * 2 + xx) * plan.rows + cc * plan.half, 16)
                    copies.append(
                        pltpu.make_async_copy(
                            src.at[s2, s1, k, :, lanes],
                            w.at[yy, pl.ds(row, plan.half), :],
                            sem.at[len(copies)],
                        )
                    )
    return copies


def attn_fwd_kernel(
    plan,
    meta,
    x_ref,
    segc_ref,
    segr_ref,
    np_ref,
    pb_ref,
    own,
    other,
    sl_ref,
    mid_ref,
    fl_ref,
    qkv_ref,
    p_ref,
    ctx_ref,
    w,
    sem,
):
    cols = plan.cols
    first = pl.program_id(0) == 0

    @pl.when(first)
    def _():
        for copy in attn_weight_copies(plan, meta, own, other, w, sem, slice(None)):
            copy.start()

    x = x_ref[...].astype(f32)
    normal, _ = norm_stats(x)
    fl = (normal * np_ref[0:1, :] + np_ref[1:2, :]).astype(bf16)
    fl_ref[...] = fl

    @pl.when(first)
    def _():
        for copy in attn_weight_copies(plan, meta, own, other, w, sem, slice(None)):
            copy.wait()

    for y in range(2):
        for part in range(3):
            got = mm(fl, w[y, :, part * cols : (part + 1) * cols])
            if part != 1:
                got = got + pb_ref[part // 2 : part // 2 + 1, y * cols : (y + 1) * cols]
            qkv_ref[y, :, part * cols : (part + 1) * cols] = got.astype(bf16)
    tiles = x.shape[0] // LANES
    pairs = cols // LANES
    for t in range(tiles):
        tok = slice(t * LANES, (t + 1) * LANES)
        same = segc_ref[tok, :] == segr_ref[0, t : t + 1, :]
        same = jnp.concatenate([same, same], axis=0)
        for y in range(2):
            for p in range(pairs):
                at = [slice(b * cols + p * LANES, b * cols + (p + 1) * LANES) for b in range(3)]
                qs = split_heads(qkv_ref[y, tok, at[0]])
                s = mm_nt(qs, qkv_ref[y, tok, at[1]]) * HD**-0.5
                s = jnp.where(same, s, NEG)
                e = jnp.exp(s - jnp.max(s, axis=-1, keepdims=True))
                probs = (e / jnp.sum(e, axis=-1, keepdims=True)).astype(bf16)
                p_ref[(t * 2 + y) * pairs + p] = probs
                ctx = join_heads(mm(probs, qkv_ref[y, tok, at[2]]))
                ctx_ref[tok, y * cols + p * LANES : y * cols + (p + 1) * LANES] = ctx.astype(bf16)
    attended = mm_nt(ctx_ref[:, 0:cols], w[0, :, 3 * cols :])
    attended = attended + mm_nt(ctx_ref[:, cols:], w[1, :, 3 * cols :])
    middle = x + attended + np_ref[4:5, :]
    mid_ref[...] = middle
    normal, _ = norm_stats(middle)
    sl_ref[...] = (normal * np_ref[2:3, :] + np_ref[3:4, :]).astype(bf16)


def ff_weight_copies(plan, meta, own, other, w, sem, r, e):
    if not plan.direct:
        return [pltpu.make_async_copy((own, other)[r].at[e], w.at[e, r], sem.at[r, e, 0])]
    copies = []
    src = (own, other)[r]
    for fx in range(2):
        for k in range(plan.nz):
            _, zz, xx, _ = piece_spot(plan, meta, r, 0, fx, k, -1)
            row = pl.multiple_of((zz * 2 + xx) * plan.rows, 16)
            copies.append(
                pltpu.make_async_copy(
                    src.at[fx, k, e],
                    w.at[e, r, pl.ds(row, plan.rows), :],
                    sem.at[r, e, len(copies)],
                )
            )
    return copies


def ff_kernel(
    plan, meta, sl_ref, cot_ref, hb_ref, own, other, sg_ref, fed_ref, act_ref, hg_ref, gh_ref, w, sem
):
    step = pl.program_id(0)
    first = step == 0

    def when_first(action, r, e):
        @pl.when(first)
        def _():
            for copy in ff_weight_copies(plan, meta, own, other, w, sem, r, e):
                getattr(copy, action)()

    for r in range(2):
        for e in range(2):
            when_first("start", r, e)

    @pl.when(first)
    def _():
        gh_ref[...] = jnp.zeros_like(gh_ref)

    sl = sl_ref[...]
    cot = cot_ref[...]
    sg = None
    fed = None
    for r in range(2):
        when_first("wait", r, 0)
        h = mm(sl, w[0, r]) + hb_ref[r : r + 1, :]
        square = h * h
        t = jnp.tanh(GELU_C * (h + GELU_K * h * square))
        act = (0.5 * h * (1.0 + t)).astype(bf16)
        slope = 0.5 * (1.0 + t) + (0.5 * GELU_C) * h * (1.0 - t * t) * (
            1.0 + (3.0 * GELU_K) * square
        )
        act_ref[r] = act
        when_first("wait", r, 1)
        hg = (mm(cot, w[1, r]) * slope).astype(bf16)
        hg_ref[r] = hg
        gh_ref[r : r + 1, :] += jnp.sum(hg.astype(f32), axis=0, keepdims=True)
        part = mm_nt(hg, w[0, r])
        sg = part if sg is None else sg + part
        part = mm_nt(act, w[1, r])
        fed = part if fed is None else fed + part
    sg_ref[...] = sg.astype(sg_ref.dtype)
    fed_ref[...] = fed.astype(fed_ref.dtype)


def ff_grad_copies(plan, meta, buf, outs, sem, r):
    if not plan.direct:
        return [pltpu.make_async_copy(buf.at[r], outs[r], sem.at[r, 0])]
    copies = []
    for e in range(2):
        for fx in range(2):
            for k in range(plan.nz):
                _, zz, xx, _ = piece_spot(plan, meta, r, 0, fx, k, 1)
                row = pl.multiple_of((zz * 2 + xx) * plan.rows, 16)
                copies.append(
                    pltpu.make_async_copy(
                        buf.at[r, e, pl.ds(row, plan.rows), :],
                        outs[r].at[fx, k, e],
                        sem.at[r, len(copies)],
                    )
                )
    return copies


def ff_grad_kernel(
    plan,
    meta,
    sl_a,
    sl_b,
    cot_a,
    cot_b,
    act_a,
    act_b,
    hg_a,
    hg_b,
    mine,
    theirs,
    left,
    buf,
    sem,
):
    step = pl.program_id(0)
    count = sl_a.shape[0]

    @pl.when(step == 0)
    def _():
        left[0, :, :count] = sl_a[...].T
        left[0, :, count:] = sl_b[...].T
        left[1, :, :count] = cot_a[...].T
        left[1, :, count:] = cot_b[...].T

    wide = plan.part // 2
    for r in range(2):

        @pl.when(step == r)
        def _():
            for e, (one, two) in enumerate(((hg_a, hg_b), (act_a, act_b))):
                for n in range(2):
                    at = slice(n * wide, (n + 1) * wide)
                    got = mm(left[e, :, :count], one[0, :, at])
                    got = got + mm(left[e, :, count:], two[0, :, at])
                    buf[r, e, :, at] = got.astype(bf16)
            for copy in ff_grad_copies(plan, meta, buf, (mine, theirs), sem, r):
                copy.start()

    @pl.when(step == 1)
    def _():
        for r in range(2):
            for copy in ff_grad_copies(plan, meta, buf, (mine, theirs), sem, r):
                copy.wait()


def attn_bwd_kernel(
    plan,
    meta,
    sga_ref,
    sgb_ref,
    mid_ref,
    cot_ref,
    np_ref,
    qkv_ref,
    p_ref,
    own,
    other,
    dqkv_ref,
    ml_ref,
    mg_ref,
    vec_ref,
    pair_ref,
    w,
    sem,
):
    cols = plan.cols
    first = pl.program_id(0) == 0
    lanes = slice(3 * cols, 4 * cols)

    @pl.when(first)
    def _():
        for copy in attn_weight_copies(plan, meta, own, other, w, sem, lanes):
            copy.start()
        vec_ref[...] = jnp.zeros_like(vec_ref)
        pair_ref[...] = jnp.zeros_like(pair_ref)

    sg = sga_ref[...].astype(f32) + sgb_ref[...].astype(f32)
    cot = cot_ref[...].astype(f32)
    normal, scaled = norm_stats(mid_ref[...])
    mg = cot + norm_backward(sg, normal, scaled, np_ref[2:3, :])
    mg_ref[...] = mg
    ml = mg.astype(bf16)
    ml_ref[...] = ml
    vec_ref[0:1, :] += jnp.sum(sg * normal, axis=0, keepdims=True)
    vec_ref[1:2, :] += jnp.sum(sg, axis=0, keepdims=True)
    vec_ref[2:3, :] += jnp.sum(mg, axis=0, keepdims=True)
    vec_ref[3:4, :] += jnp.sum(cot, axis=0, keepdims=True)

    @pl.when(first)
    def _():
        for copy in attn_weight_copies(plan, meta, own, other, w, sem, lanes):
            copy.wait()

    tiles = ml.shape[0] // LANES
    pairs = cols // LANES
    for y in range(2):
        dctx = mm(ml, w[y]).astype(bf16)
        for t in range(tiles):
            tok = slice(t * LANES, (t + 1) * LANES)
            for p in range(pairs):
                at = [slice(b * cols + p * LANES, b * cols + (p + 1) * LANES) for b in range(3)]
                dcs = split_heads(dctx[tok, p * LANES : (p + 1) * LANES])
                qs = split_heads(qkv_ref[y, tok, at[0]])
                low = p_ref[(t * 2 + y) * pairs + p]
                probs = low.astype(f32)
                dp = mm_nt(dcs, qkv_ref[y, tok, at[2]])
                inner = jnp.sum(dp * probs, axis=-1, keepdims=True)
                ds = (probs * (dp - inner) * HD**-0.5).astype(bf16)
                dq = join_heads(mm(ds, qkv_ref[y, tok, at[1]])).astype(bf16)
                dk = mm_tn(ds, qs).astype(bf16)
                dv = mm_tn(low, dcs).astype(bf16)
                dqkv_ref[y, tok, at[0]] = dq
                dqkv_ref[y, tok, at[1]] = dk
                dqkv_ref[y, tok, at[2]] = dv
        for b in (0, 2):
            at = slice(b * cols, (b + 1) * cols)
            pair_ref[b // 2 : b // 2 + 1, y * cols : (y + 1) * cols] += jnp.sum(
                dqkv_ref[y, :, at].astype(f32), axis=0, keepdims=True
            )


def attn_grad_copies(plan, meta, buf, outs, sem, fy):
    if not plan.direct:
        yy = jnp.bitwise_xor(meta[3], fy)
        return [pltpu.make_async_copy(buf.at[fy], outs[0].at[yy], sem.at[fy, 0])]
    copies = []
    for r in range(2):
        for fx in range(2):
            for k in range(plan.nz):
                cc, zz, xx, _ = piece_spot(plan, meta, r, fy, fx, k, 1)
                s1 = jnp.where(cc == 0, fx, fy)
                s2 = jnp.where(cc == 0, fy, fx)
                row = pl.multiple_of((zz * 2 + xx) * plan.rows + cc * plan.half, 16)
                copies.append(
                    pltpu.make_async_copy(
                        buf.at[fy, pl.ds(row, plan.half), :],
                        outs[r].at[s2, s1, k],
                        sem.at[fy, len(copies)],
                    )
                )
    return copies


def attn_grad_kernel(plan, meta, fl_ref, ml_ref, dqkv_ref, ctx_ref, *rest):
    *outs, left, buf, sem = rest
    step = pl.program_id(0)
    cols = plan.cols

    @pl.when(step == 0)
    def _():
        left[0] = fl_ref[...].T
        left[1] = ml_ref[...].T

    for fy in range(2):

        @pl.when(step == fy)
        def _():
            for b in range(3):
                at = slice(b * cols, (b + 1) * cols)
                buf[fy, :, at] = mm(left[0], dqkv_ref[0, :, at]).astype(bf16)
            buf[fy, :, 3 * cols :] = mm(left[1], ctx_ref[...]).astype(bf16)
            for copy in attn_grad_copies(plan, meta, buf, outs, sem, fy):
                copy.start()

    @pl.when(step == 1)
    def _():
        for fy in range(2):
            for copy in attn_grad_copies(plan, meta, buf, outs, sem, fy):
                copy.wait()


def input_grad_kernel(
    plan, meta, x_ref, mg_ref, np_ref, dqkv_ref, own, other, ig_ref, vec_ref, w, sem
):
    cols = plan.cols
    first = pl.program_id(0) == 0
    lanes = slice(0, 3 * cols)

    @pl.when(first)
    def _():
        for copy in attn_weight_copies(plan, meta, own, other, w, sem, lanes):
            copy.start()
        vec_ref[...] = jnp.zeros_like(vec_ref)

    normal, scaled = norm_stats(x_ref[...].astype(f32))

    @pl.when(first)
    def _():
        for copy in attn_weight_copies(plan, meta, own, other, w, sem, lanes):
            copy.wait()

    fg = mm_nt(dqkv_ref[0], w[0]) + mm_nt(dqkv_ref[1], w[1])
    vec_ref[0:1, :] += jnp.sum(fg * normal, axis=0, keepdims=True)
    vec_ref[1:2, :] += jnp.sum(fg, axis=0, keepdims=True)
    ig = mg_ref[...] + norm_backward(fg, normal, scaled, np_ref[0:1, :])
    ig_ref[...] = ig.astype(bf16)


def place_kernel(meta, own, by_y, by_c, by_yc, out, sem):
    count = own.shape[0]
    copies = []
    for fy, fc, src in ((0, 0, own), (1, 0, by_y), (0, 1, by_c), (1, 1, by_yc)):
        at = jnp.bitwise_xor(meta[3], fy) * 2 + jnp.bitwise_xor(meta[4], fc)
        dst = out.at[pl.ds(pl.multiple_of(at * count, 16), count), :]
        copies.append(pltpu.make_async_copy(src, dst, sem.at[len(copies)]))
    for copy in copies:
        copy.start()
    for copy in copies:
        copy.wait()


def adam_kernel(rates, factor_ref, *refs):
    count = len(rates)
    factor = factor_ref[0, 0]
    correction = 1.0 - BETA**STEP
    for i, (rate, decay) in enumerate(rates):
        w_ref, m_ref, s_ref, g_ref = refs[4 * i : 4 * i + 4]
        m_out, s_out, w_out = refs[4 * count + 3 * i : 4 * count + 3 * i + 3]
        clipped = g_ref[...] * factor
        first = BETA * m_ref[...] + (1.0 - BETA) * clipped
        second = BETA * s_ref[...] + (1.0 - BETA) * clipped * clipped
        weight = w_ref[...]
        direction = first / correction / (jnp.sqrt(second / correction) + ADAM_EPS)
        m_out[...] = first
        s_out[...] = second
        w_out[...] = weight - rate * (direction + decay * weight)


def any_spec():
    return pl.BlockSpec(memory_space=pl.ANY)


def call(kernel, name, grid, ins, outs, scratch, flops, moved, vmem=56):
    def spec(item):
        if item[1] is None:
            return any_spec()
        return pl.BlockSpec(item[1], item[2])

    return pl.pallas_call(
        kernel,
        name=name,
        out_shape=[o[0] for o in outs],
        grid_spec=pltpu.PrefetchScalarGridSpec(
            num_scalar_prefetch=1,
            grid=grid,
            in_specs=[spec(i) for i in ins],
            out_specs=[spec(o) for o in outs],
            scratch_shapes=scratch,
        ),
        compiler_params=pltpu.CompilerParams(vmem_limit_bytes=vmem * MIB),
        cost_estimate=pl.CostEstimate(flops=flops, bytes_accessed=moved, transcendentals=0),
    )


def per_device(
    inputs,
    segments,
    cotangent,
    triple_weight,
    triple_first,
    triple_second,
    outward_weight,
    outward_first,
    outward_second,
    expand_weight,
    expand_first,
    expand_second,
    reduce_weight,
    reduce_first,
    reduce_second,
    norm_params,
    norm_first,
    norm_second,
    paired_bias,
    paired_first,
    paired_second,
    hidden_bias,
    hidden_first,
    hidden_second,
):
    ndp, nmp = lax.axis_size("dp"), lax.axis_size("mp")
    width = inputs.shape[1]
    hidden = hidden_bias.shape[0] * nmp
    plan = Plan(ndp, nmp, width, hidden)
    nz, rows, half, cols, part = plan.nz, plan.rows, plan.half, plan.cols, plan.part
    count = inputs.shape[0] // nmp
    row_count, row_length = segments.shape
    own_rows = row_count // nmp
    steps = count // CHUNK
    tiles = CHUNK // LANES
    units = tiles * 2 * (cols // LANES)
    quarter = cols // 2

    dp, mp = lax.axis_index("dp"), lax.axis_index("mp")
    z, x, y, c = dp // 2, dp % 2, mp // 2, mp % 2
    meta = jnp.stack([mp, z, x, y, c, jnp.bitwise_xor(mp, 2)]).astype(jnp.int32)
    core_zero = c == 0
    SDS = jax.ShapeDtypeStruct

    shard = jnp.concatenate(
        [triple_weight.astype(bf16), outward_weight.T.astype(bf16)[None]], axis=0
    ).transpose(1, 0, 2)
    keep = lax.dynamic_slice_in_dim(shard, c * half, half, 0)
    send = lax.dynamic_slice_in_dim(shard, (1 - c) * half, half, 0)
    got = plan.core(send)
    low = jnp.where(core_zero, keep, got)
    high = jnp.where(core_zero, got, keep)
    unit = jnp.concatenate([low, high], axis=2).reshape(half, 4 * cols)
    spread = jnp.stack([unit] + [plan.along_z(unit, k) for k in range(1, nz)])
    spread = jnp.stack([spread, plan.first(spread)])
    attn_own = jnp.stack([spread, plan.second(spread)])
    attn_other = plan.core(attn_own)

    unit = jnp.stack([expand_weight.astype(bf16), reduce_weight.T.astype(bf16)])
    spread = jnp.stack([unit] + [plan.along_z(unit, k) for k in range(1, nz)])
    ff_own = jnp.stack([spread, plan.along_x(spread)])
    ff_other = plan.core(ff_own)

    if not plan.direct:
        attn_own = absolute_attn(plan, attn_own, attn_other, z, x, y, c)
        attn_other = meta
        ff_own = absolute_ff(plan, ff_own, z, x)
        ff_other = absolute_ff(plan, ff_other, z, x)

    by_core = plan.core(jnp.concatenate([paired_bias.reshape(-1), hidden_bias]))
    other_pair = by_core[: 2 * quarter].reshape(2, quarter)
    near = jnp.where(
        core_zero,
        jnp.concatenate([paired_bias, other_pair], axis=1),
        jnp.concatenate([other_pair, paired_bias], axis=1),
    )
    far = plan.along_y(near)
    pair_full = jnp.where(
        y == 0, jnp.concatenate([near, far], axis=1), jnp.concatenate([far, near], axis=1)
    )
    hidden_rows = jnp.stack([hidden_bias, by_core[2 * quarter :]])

    marks = lax.dynamic_slice_in_dim(segments, mp * own_rows, own_rows, 0)
    marks = marks + row_length * lax.broadcasted_iota(jnp.int32, marks.shape, 0)
    mark_col = marks.reshape(count, 1)
    mark_row = marks.reshape(steps, tiles, LANES)

    whole = lambda shape: (shape, lambda i, m: (0,) * len(shape))
    chunk = lambda n: ((CHUNK, n), lambda i, m: (i, 0))
    mine_rows = ((CHUNK, width), lambda i, m: (m[0] * steps + i, 0))
    pair_rows = ((CHUNK, width), lambda i, m: (m[5] * steps + i, 0))
    pieces = 2 * 2 * 2 * nz if plan.direct else 1
    dma = pltpu.SemaphoreType.DMA
    qkv_block = ((2, CHUNK, 3 * cols), lambda i, m: (0, i, 0))
    p_block = ((units, 2 * LANES, LANES), lambda i, m: (i, 0, 0))

    sl, middle, fl, qkv, probs, ctx = call(
        functools.partial(attn_fwd_kernel, plan),
        "attn_fwd",
        (steps,),
        [
            (inputs, *mine_rows),
            (mark_col, *chunk(1)),
            (mark_row, (1, tiles, LANES), lambda i, m: (i, 0, 0)),
            (norm_params, *whole(norm_params.shape)),
            (pair_full, *whole(pair_full.shape)),
            (attn_own, None, None),
            (attn_other, None, None),
        ],
        [
            (SDS((count, width), bf16), *chunk(width)),
            (SDS((count, width), f32), *chunk(width)),
            (SDS((count, width), bf16), *chunk(width)),
            (SDS((2, count, 3 * cols), bf16), *qkv_block),
            (SDS((steps * units, 2 * LANES, LANES), bf16), *p_block),
            (SDS((count, width), bf16), *chunk(width)),
        ],
        [pltpu.VMEM((2, width, 4 * cols), bf16), dma((pieces,))],
        flops=8 * count * width * width,
        moved=16 * MIB,
    )(meta, inputs, mark_col, mark_row, norm_params, pair_full, attn_own, attn_other)

    sl_far = plan.along_y(sl)

    def feed_forward(sl_in, cot_rows, out_type):
        return call(
            functools.partial(ff_kernel, plan),
            "feed_forward",
            (steps,),
            [
                (sl_in, *chunk(width)),
                (cotangent, *cot_rows),
                (hidden_rows, *whole(hidden_rows.shape)),
                (ff_own, None, None),
                (ff_other, None, None),
            ],
            [
                (SDS((count, width), out_type), *chunk(width)),
                (SDS((count, width), out_type), *chunk(width)),
                (SDS((2, count, part), bf16), (2, CHUNK, part), lambda i, m: (0, i, 0)),
                (SDS((2, count, part), bf16), (2, CHUNK, part), lambda i, m: (0, i, 0)),
                (SDS((2, part), f32), *whole((2, part))),
            ],
            [
                pltpu.VMEM((2, 2, width, part), bf16),
                dma((2, 2, 2 * nz if plan.direct else 1)),
            ],
            flops=16 * count * width * part,
            moved=14 * MIB,
        )(meta, sl_in, cotangent, hidden_rows, ff_own, ff_other)

    sg_near, fed_near, act_near, hg_near, gh_near = feed_forward(sl, mine_rows, f32)
    sg_send, fed_send, act_far, hg_far, gh_far = feed_forward(sl_far, pair_rows, bf16)
    sg_far = plan.along_y(sg_send)
    fed_far = plan.along_y(fed_send)

    half_block = ((1, count, part), lambda i, m: (i, 0, 0))
    all_mine = ((count, width), lambda i, m: (m[0], 0))
    all_pair = ((count, width), lambda i, m: (m[5], 0))
    if plan.direct:
        grad_shape = SDS((2, nz, 2, rows, part), bf16)
    else:
        grad_shape = SDS((2, width, part), bf16)
    ff_mine, ff_theirs = call(
        functools.partial(ff_grad_kernel, plan),
        "ff_grad",
        (2,),
        [
            (sl, *whole((count, width))),
            (sl_far, *whole((count, width))),
            (cotangent, *all_mine),
            (cotangent, *all_pair),
            (act_near, *half_block),
            (act_far, *half_block),
            (hg_near, *half_block),
            (hg_far, *half_block),
        ],
        [(grad_shape, None, None), (grad_shape, None, None)],
        [
            pltpu.VMEM((2, width, 2 * count), bf16),
            pltpu.VMEM((2, 2, width, part), bf16),
            dma((2, 4 * nz if plan.direct else 1)),
        ],
        flops=16 * count * width * part,
        moved=16 * MIB,
    )(meta, sl, sl_far, cotangent, cotangent, act_near, act_far, hg_near, hg_far)

    dqkv, ml, mg, vec_two, pair_sum = call(
        functools.partial(attn_bwd_kernel, plan),
        "attn_bwd",
        (steps,),
        [
            (sg_near, *chunk(width)),
            (sg_far, *chunk(width)),
            (middle, *chunk(width)),
            (cotangent, *mine_rows),
            (norm_params, *whole(norm_params.shape)),
            (qkv, *qkv_block),
            (probs, *p_block),
            (attn_own, None, None),
            (attn_other, None, None),
        ],
        [
            (SDS((2, count, 3 * cols), bf16), *qkv_block),
            (SDS((count, width), bf16), *chunk(width)),
            (SDS((count, width), f32), *chunk(width)),
            (SDS((8, width), f32), *whole((8, width))),
            (SDS((2, width), f32), *whole((2, width))),
        ],
        [pltpu.VMEM((2, width, cols), bf16), dma((pieces,))],
        flops=6 * count * width * width,
        moved=12 * MIB,
    )(meta, sg_near, sg_far, middle, cotangent, norm_params, qkv, probs, attn_own, attn_other)

    if plan.direct:
        grad_shapes = [SDS((2, 2, nz, half, 4 * cols), bf16)] * 2
    else:
        grad_shapes = [SDS((2, width, 4 * cols), bf16)]
    attn_grads = call(
        functools.partial(attn_grad_kernel, plan),
        "attn_grad",
        (2,),
        [
            (fl, *whole((count, width))),
            (ml, *whole((count, width))),
            (dqkv, (1, count, 3 * cols), lambda i, m: (jnp.bitwise_xor(m[3], i), 0, 0)),
            (ctx, (count, cols), lambda i, m: (0, jnp.bitwise_xor(m[3], i))),
        ],
        [(s, None, None) for s in grad_shapes],
        [
            pltpu.VMEM((2, width, count), bf16),
            pltpu.VMEM((2, width, 4 * cols), bf16),
            dma((2, 4 * nz if plan.direct else 1)),
        ],
        flops=8 * count * width * width,
        moved=10 * MIB,
    )(meta, fl, ml, dqkv, ctx)
    if plan.direct:
        attn_mine, attn_theirs = attn_grads
    else:
        attn_mine, attn_theirs = relative_attn(plan, attn_grads[0], z, x, y, c)
        ff_mine = relative_ff(plan, ff_mine, z, x)
        ff_theirs = relative_ff(plan, ff_theirs, z, x)

    ig, vec_one = call(
        functools.partial(input_grad_kernel, plan),
        "input_grad",
        (steps,),
        [
            (inputs, *mine_rows),
            (mg, *chunk(width)),
            (norm_params, *whole(norm_params.shape)),
            (dqkv, *qkv_block),
            (attn_own, None, None),
            (attn_other, None, None),
        ],
        [
            (SDS((count, width), bf16), *chunk(width)),
            (SDS((8, width), f32), *whole((8, width))),
        ],
        [pltpu.VMEM((2, width, 3 * cols), bf16), dma((pieces,))],
        flops=6 * count * width * width,
        moved=10 * MIB,
    )(meta, inputs, mg, norm_params, dqkv, attn_own, attn_other)

    out = (middle + fed_near + fed_far.astype(f32) + norm_params[5]).astype(bf16)

    def everywhere(block):
        by_y = plan.along_y(block)
        by_c = plan.core(block)
        by_yc = plan.core(by_y)
        return call(
            place_kernel,
            "place",
            (1,),
            [(b, None, None) for b in (block, by_y, by_c, by_yc)],
            [(SDS((count * nmp, width), bf16), None, None)],
            [dma((4,))],
            flops=0,
            moved=6 * MIB,
            vmem=8,
        )(meta, block, by_y, by_c, by_yc)[0]

    outputs = everywhere(out)
    input_gradient = everywhere(ig)

    def plus(one, two):
        return (one.astype(f32) + two.astype(f32)).astype(bf16)

    def sum_z(parts):
        total = parts[0].astype(f32)
        for k in range(1, nz):
            total = total + plan.along_z(parts[k], k).astype(f32)
        return total

    got = plan.core(ff_theirs)
    keep, send = plus(ff_mine[0], got[0]), plus(ff_mine[1], got[1])
    ff_grads = sum_z(plus(keep, plan.along_x(send)))
    grad_expand = ff_grads[0]
    grad_reduce = ff_grads[1].T

    got = plan.core(attn_theirs)
    keep, send = plus(attn_mine[0], got[0]), plus(attn_mine[1], got[1])
    got = plan.second(send)
    keep, send = plus(keep[0], got[0]), plus(keep[1], got[1])
    unit = sum_z(plus(keep, plan.first(send))).reshape(half, 4, 2, quarter)
    keep = jnp.where(core_zero, unit[:, :, 0], unit[:, :, 1])
    got = plan.core(jnp.where(core_zero, unit[:, :, 1], unit[:, :, 0]))
    shard = jnp.concatenate(
        [jnp.where(core_zero, keep, got), jnp.where(core_zero, got, keep)], axis=0
    )
    grad_triple = shard[:, :3].transpose(1, 0, 2)
    grad_outward = shard[:, 3].T

    gh = gh_near + gh_far
    gh = jnp.where(core_zero, gh, gh[::-1]).reshape(-1)
    zero = jnp.zeros_like(gh)
    gh = jnp.where(y == 0, jnp.concatenate([gh, zero]), jnp.concatenate([zero, gh]))
    vectors = jnp.concatenate(
        [vec_one[:2].reshape(-1), vec_two[:4].reshape(-1), pair_sum.reshape(-1), gh]
    )
    size = vectors.shape[0] // plan.ndev
    got = lax.all_to_all(vectors.reshape(plan.ndev, size), AXES, 0, 0, tiled=True)
    local = jnp.sum(got, axis=0)
    square = jnp.sum(ff_grads * ff_grads) + jnp.sum(unit * unit)
    square = square + jnp.sum(local * local)
    payload = jnp.concatenate([local, square[None]])
    payload = jnp.broadcast_to(payload[None], (plan.ndev, size + 1))
    got = lax.all_to_all(payload, AXES, 0, 0, tiled=True)
    gradient_norm = jnp.sqrt(jnp.sum(got[:, size]))
    factor = jnp.minimum(1.0, CLIP / gradient_norm)
    vectors = got[:, :size].reshape(-1)
    grad_norms = vectors[: 6 * width].reshape(6, width)
    grad_paired = vectors[6 * width : 8 * width].reshape(2, width)
    grad_paired = lax.dynamic_slice_in_dim(grad_paired, mp * quarter, quarter, 1)
    grad_hidden = lax.dynamic_slice_in_dim(vectors[8 * width :], mp * part, part, 0)

    matrix, vector = (LR_MATRIX, DECAY), (LR_VECTOR, 0.0)
    groups = [
        (triple_weight, triple_first, triple_second, grad_triple),
        (outward_weight, outward_first, outward_second, grad_outward),
        (expand_weight, expand_first, expand_second, grad_expand),
        (reduce_weight, reduce_first, reduce_second, grad_reduce),
        (norm_params, norm_first, norm_second, grad_norms),
        (paired_bias, paired_first, paired_second, grad_paired),
        tuple(
            v.reshape(1, -1) for v in (hidden_bias, hidden_first, hidden_second, grad_hidden)
        ),
    ]
    flat = [v for group in groups for v in group]
    vmem = pl.BlockSpec(memory_space=pltpu.VMEM)
    new = pl.pallas_call(
        functools.partial(adam_kernel, (matrix,) * 4 + (vector,) * 3),
        name="adam",
        out_shape=[SDS(group[0].shape, f32) for group in groups for _ in range(3)],
        in_specs=[pl.BlockSpec(memory_space=pltpu.SMEM)] + [vmem] * len(flat),
        out_specs=[vmem] * (3 * len(groups)),
        compiler_params=pltpu.CompilerParams(vmem_limit_bytes=32 * MIB),
    )(factor.reshape(1, 1), *flat)
    new = list(new)
    new[18:] = [v.reshape(-1) for v in new[18:]]
    return (outputs, input_gradient, gradient_norm, *new)


def turn(plan, value, z, axis):
    value = jnp.flip(value, axis)
    return jnp.roll(value, z + 1, axis)


def unturn(plan, value, z, axis):
    return jnp.roll(value, -z, axis)


def swap(value, flag, axis):
    return jnp.where(flag == 1, jnp.flip(value, axis), value)


def absolute_ff(plan, value, z, x):
    value = swap(turn(plan, value, z, 1), x, 0)
    value = value.transpose(2, 1, 0, 3, 4)
    return value.reshape(2, plan.width, plan.part)


def relative_ff(plan, value, z, x):
    value = value.reshape(2, plan.nz, 2, plan.rows, plan.part).transpose(2, 1, 0, 3, 4)
    return unturn(plan, swap(value, x, 0), z, 1)


def absolute_attn(plan, own, other, z, x, y, c):
    zero = jnp.where(c == 0, own, other)
    one = jnp.where(c == 0, other, own).transpose(1, 0, 2, 3, 4)
    value = jnp.stack([zero, one])
    value = turn(plan, swap(swap(value, y, 1), x, 2), z, 3)
    value = value.transpose(1, 3, 2, 0, 4, 5)
    return value.reshape(2, plan.width, 4 * plan.cols)


def relative_attn(plan, value, z, x, y, c):
    value = value.reshape(2, plan.nz, 2, 2, plan.half, 4 * plan.cols)
    value = value.transpose(3, 0, 2, 1, 4, 5)
    value = unturn(plan, swap(swap(value, y, 1), x, 2), z, 3)
    zero, one = value[0], value[1].transpose(1, 0, 2, 3, 4)
    return jnp.where(c == 0, zero, one), jnp.where(c == 0, one, zero)


def solution(mesh):
    tokens = P("dp", None)
    triple = P(None, "dp", "mp")
    tall = P("mp", "dp")
    wide = P("dp", "mp")
    pair = P(None, "mp")
    states = ((triple,) * 3, (tall,) * 3, (wide,) * 3, (tall,) * 3, (P(),) * 3, (pair,) * 3)
    states = sum(states, ()) + (P("mp"),) * 3
    return jax.shard_map(
        per_device,
        mesh=mesh,
        in_specs=(tokens,) * 3 + states,
        out_specs=(tokens, tokens, P()) + states,
        check_vma=False,
    )
```

time: 722 us -> 493 us (0.68)
  Pallas kernels: 0 us -> 209 us
  blocking collectives: 149 us -> 0 us
  waiting for transfers between devices: 284 us -> 146 us
  matrix products: 103 us -> 0 us
  starting transfers between devices: 0.94 us -> 51.2 us
  local copies, waits for them, and re-layouts: 94 us -> 49.2 us
  other arithmetic: 62.2 us -> 26.4 us
  between operations: 22.6 us -> 5.66 us
    pallas_call x0 -> x10, Pallas kernels: none -> 209 us  [the longest x2 122 us: everywhere(): call(place_kernel, 'place', (1,), [(b, None, None) for b in (block, by_y,...]
    psum x3 -> x0, waiting for transfers between devices: 208 us -> none  [the longest x1 85 us: per_device(): fed = lax.psum(fed_part.astype(jnp.bfloat16), 'mp').astype(jnp.float32)]
    ppermute x0 -> x35, waiting for transfers between devices: none -> 121 us  [the longest x6 40.6 us: along_y(): lax.ppermute(value, AXES, self.perm(lambda z, x, y, c: (z, x, 1 - y, c)))]
    dot_general x16 -> x0, matrix products: 97.3 us -> none  [the longest x1 10.8 us: per_device(): jnp.einsum('td,fd->tf', cotangent, reduce_full, preferred_element_type=f32)]
    psum x2 -> x0, blocking collectives: 76.8 us -> none  [the longest x1 39.5 us: per_device(): total_square = lax.psum(local_square, ('dp', 'mp'))]
    all_gather x2 -> x0, blocking collectives: 72.4 us -> none  [the longest x1 40.5 us: per_device(): lax.all_gather(triple_weight.astype(bf16), 'dp', axis=1, tiled=True)]
    unnamed x11 -> x0, waiting for transfers between devices: 67.4 us -> none
    ppermute x0 -> x35, starting transfers between devices: none -> 42.9 us  [the longest x12 26.4 us: along_z(): lax.ppermute(value, AXES, self.perm(lambda z, x, y, c: ((z + step) % self...]
  transfers between devices with their start and end apart: 9 -> 37, of which waited for: 6 -> 17; matrix products, arithmetic and copies ran while one was open for 15% -> 8% of each run, Pallas kernels for 0% -> 40%
where the time goes in v1:
time: 493 us; the launch traced here: 488 us
  Pallas kernels  209 us (42%)
  waiting for transfers between devices  146 us (30%)
  starting transfers between devices  51.2 us (10%)
  local copies, waits for them, and re-layouts  49.2 us (10%)
  other arithmetic  26.4 us (5%)
  between operations  5.66 us (1%)
    pallas_call x2, Pallas kernels, everywhere(): call(place_kernel, 'place', (1,), [(b, None, None) for b in (block, by_y,...  122 us
    ppermute x6, waiting for transfers between devices, along_y(): lax.ppermute(value, AXES, self.perm(lambda z, x, y, c: (z, x, 1 - y, c)))  40.6 us
    ppermute x12, waiting for transfers between devices, along_z(): lax.ppermute(value, AXES, self.perm(lambda z, x, y, c: ((z + step) % self...  35.1 us
    unnamed x111, local copies, waits for them, and re-layouts  29.2 us
    ppermute x2, waiting for transfers between devices, along_x(): lax.ppermute(value, AXES, self.perm(lambda z, x, y, c: (z, 1 - x, y, c)))  26.4 us
    ppermute x12, starting transfers between devices, along_z(): lax.ppermute(value, AXES, self.perm(lambda z, x, y, c: ((z + step) % self...  26.4 us
    pallas_call x2, Pallas kernels, feed_forward(): call(functools.partial(ff_kernel, plan), 'feed_forward', (steps,), [(sl_i...  26.4 us
    all_to_all x1, waiting for transfers between devices, per_device(): lax.all_to_all(vectors.reshape(plan.ndev, size), AXES, 0, 0, tiled=True)  19.3 us
  transfers between devices with their start and end apart: 37, of which 17 were waited for; matrix products, arithmetic and copies ran while one was open for 8% of the time, Pallas kernels for 40%

profile of v1, /device:TPU:0, one launch (start us, length us, event | category | flops | bytes accessed | tf_op | source)
XLA Modules:
  0.0 487.8 jit_solution(15653642935889426865)
XLA Ops:
  4.9 3.0 collective-permute-start.3
  7.9 2.6 collective-permute-start.4
  12.0 2.7 collective-permute-done.3
  14.6 5.8 %collective-permute-done.4 = bf16[48,1536]{1,0:T(8,128)(2,1)S(1)} collective-permute-done((bf16[48,1536]{1,0:T(8,128)(2,1)S(1)}, bf16[48,1536]{1,0:T(8,128)(2,1)S(1)}, u32[]{:S(2)}, u32[]{:S(2)}) %collective-permute-start.4) | collective-permute-done | bytes 147488 | tf_op jit(solution)/shard_map/ppermute | solution.py:107
  22.1 8.4 %collective-permute-done.6 = bf16[4,48,1536]{2,1,0:T(8,128)(2,1)S(1)} collective-permute-done((bf16[4,48,1536]{2,1,0:T(8,128)(2,1)S(1)}, bf16[4,48,1536]{2,1,0:T(8,128)(2,1)S(1)}, u32[]{:S(2)}, u32[]{:S(2)}) %collective-permute-start.6) | collective-permute-done | bytes 589856 | tf_op jit(solution)/shard_map/ppermute | solution.py:112
  32.4 3.7 collective-permute-start.9
  38.5 6.7 %collective-permute-done.9 = bf16[2,96,768]{2,1,0:T(8,128)(2,1)S(1)} collective-permute-done((bf16[2,96,768]{2,1,0:T(8,128)(2,1)S(1)}, bf16[2,96,768]{2,1,0:T(8,128)(2,1)S(1)}, u32[]{:S(2)}, u32[]{:S(2)}) %collective-permute-start.9) | collective-permute-done | bytes 294944 | tf_op jit(solution)/shard_map/ppermute | solution.py:107
  45.2 10.0 %collective-permute-done.10 = bf16[2,96,768]{2,1,0:T(8,128)(2,1)S(1)} collective-permute-done((bf16[2,96,768]{2,1,0:T(8,128)(2,1)S(1)}, bf16[2,96,768]{2,1,0:T(8,128)(2,1)S(1)}, u32[]{:S(2)}, u32[]{:S(2)}) %collective-permute-start.10) | collective-permute-done | bytes 294944 | tf_op jit(solution)/shard_map/ppermute | solution.py:107
  56.8 26.4 %collective-permute-done.12 = bf16[4,2,96,768]{3,2,1,0:T(8,128)(2,1)S(1)} collective-permute-done((bf16[4,2,96,768]{3,2,1,0:T(8,128)(2,1)S(1)}, bf16[4,2,96,768]{3,2,1,0:T(8,128)(2,1)S(1)}, u32[]{:S(2)}, u32[]{:S(2)}) %collective-permute-start.12) | collective-permute-done | bytes 1179680 | tf_op jit(solution)/shard_map/ppermute | solution.py:101
  85.6 3.5 collective-permute-done
  94.3 13.1 %attn_fwd.1 = (bf16[512,768]{1,0:T(8,128)(2,1)}, f32[512,768]{1,0:T(8,128)}, bf16[512,768]{1,0:T(8,128)(2,1)}, bf16[2,512,1152]{2,1,0:T(8,128)(2,1)}, bf16[24,25...) custom-call(s32[6]{0:T(128)} %stack.99.meta, bf16[2048,768]{1,0:T(8,128)(2,1)} %x_ref.3, s32[512,1]{1,0:T(8,128)} %reshape.196.segc_ref, ...), custom_call_target="tpu_custom_call" | custom-call | flops 2415919104 | bytes 16777216 | tf_op jit(solution)/shard_map/attn_fwd/pallas_call | solution.py:665
  108.7 18.4 %collective-permute-done.14.sl_ref.sl_b = bf16[512,768]{1,0:T(8,128)(2,1)S(1)} collective-permute-done((bf16[512,768]{1,0:T(8,128)(2,1)}, bf16[512,768]{1,0:T(8,128)(2,1)S(1)}, u32[]{:S(2)}, u32[]{:S(2)}) %collective-permute-start.14) | collective-permute-done | bytes 786464 | tf_op jit(solution)/shard_map/ppermute | solution.py:104
  128.1 13.1 %feed_forward.3 = (bf16[512,768]{1,0:T(8,128)(2,1)}, bf16[512,768]{1,0:T(8,128)(2,1)}, bf16[2,512,768]{2,1,0:T(8,128)(2,1)}, bf16[2,512,768]{2,1,0:T(8,128)(2,1)}, f32[2,768]{1,0:T(2,128)}) custom-call(s32[6]{0:T(128)} %stack.99.meta, bf16[512,768]{1,0:T(8,128)(2,1)} %copy-done.49, bf16[2048,768]{1,0:T(8,128)(2,1)} %cot_b.1, ...), custom_call_target="tpu_custom_call" | custom-call | flops 4831838208 | bytes 14680064 | tf_op jit(solution)/shard_map/feed_forward/pallas_call | solution.py:694
  141.8 13.3 %feed_forward.2 = (f32[512,768]{1,0:T(8,128)}, f32[512,768]{1,0:T(8,128)}, bf16[2,512,768]{2,1,0:T(8,128)(2,1)}, bf16[2,512,768]{2,1,0:T(8,128)(2,1)}, f32[2,768]{1,0:T(2,128)}) custom-call(s32[6]{0:T(128)} %stack.99.meta, bf16[512,768]{1,0:T(8,128)(2,1)} %get-tuple-element.73.sl_ref.sl_a, bf16[2048,768]{1,0:T(8,128)(2,1)} %cot_b.1, ...), custom_call_target="tpu_custom_call" | custom-call | flops 4831838208 | bytes 14680064 | tf_op jit(solution)/shard_map/feed_forward/pallas_call | solution.py:694
  155.1 12.6 %ff_grad.1 = (bf16[2,4,2,96,768]{4,3,2,1,0:T(8,128)(2,1)}, bf16[2,4,2,96,768]{4,3,2,1,0:T(8,128)(2,1)}) custom-call(s32[6]{0:T(128)} %stack.99.meta, bf16[512,768]{1,0:T(8,128)(2,1)} %get-tuple-element.73.sl_ref.sl_a, bf16[512,768]{1,0:T(8,128)(2,1)} %copy-done.49, bf16[2048,768]{1,0:T(8,128)(2,1)} %cot_b.1, bf16[2048,768]{1,0:T(8,128)(2,1)} %cot_b.1, ...), custom_call_target="tpu_custom_call" | custom-call | flops 4831838208 | bytes 16777216 | tf_op jit(solution)/shard_map/ff_grad/pallas_call | solution.py:732
  168.6 16.0 %attn_bwd.1 = (bf16[2,512,1152]{2,1,0:T(8,128)(2,1)}, bf16[512,768]{1,0:T(8,128)(2,1)}, f32[512,768]{1,0:T(8,128)}, f32[8,768]{1,0:T(8,128)}, f32[2,768]{1,0:T(2,128)}) custom-call(s32[6]{0:T(128)} %stack.99.meta, f32[512,768]{1,0:T(8,128)} %get-tuple-element.76.sga_ref, bf16[512,768]{1,0:T(8,128)(2,1)} %copy-done.41, f32[512,768]{1,0:T(8,128)} %get-tuple-element.72.mid_ref, ...), custom_call_target="tpu_custom_call" | custom-call | flops 1811939328 | bytes 12582912 | tf_op jit(solution)/shard_map/attn_bwd/pallas_call | solution.py:756
  184.6 8.1 %attn_grad.1 = (bf16[2,2,4,48,1536]{4,3,2,1,0:T(8,128)(2,1)}, bf16[2,2,4,48,1536]{4,3,2,1,0:T(8,128)(2,1)}) custom-call(s32[6]{0:T(128)} %stack.99.meta, bf16[512,768]{1,0:T(8,128)(2,1)} %get-tuple-element.94.fl_ref, bf16[512,768]{1,0:T(8,128)(2,1)} %get-tuple-element.95.ml_ref, bf16[2,512,1152]{2,1,0:T(8,128)(2,1)} %get-tuple-element.81.dqkv_ref, ...), custom_call_target="tpu_custom_call" | custom-call | flops 2415919104 | bytes 10485760 | tf_op jit(solution)/shard_map/attn_grad/pallas_call | solution.py:787
  195.7 8.8 %input_grad.1 = (bf16[512,768]{1,0:T(8,128)(2,1)}, f32[8,768]{1,0:T(8,128)}) custom-call(s32[6]{0:T(128)} %stack.99.meta, bf16[2048,768]{1,0:T(8,128)(2,1)} %x_ref.3, f32[512,768]{1,0:T(8,128)} %get-tuple-element.80.mg_ref, f32[6,768]{1,0:T(8,128)} %refs_16_.1, bf16[2,512,1152]{2,1,0:T(8,128)(2,1)} %get-tuple-element.81.dqkv_ref, ...), custom_call_target="tpu_custom_call" | custom-call | flops 1811939328 | bytes 10485760 | tf_op jit(solution)/shard_map/input_grad/pallas_call | solution.py:813
  207.9 6.2 %collective-permute-done.15 = bf16[512,768]{1,0:T(8,128)(2,1)} collective-permute-done((bf16[512,768]{1,0:T(8,128)(2,1)}, bf16[512,768]{1,0:T(8,128)(2,1)}, u32[]{:S(2)}, u32[]{:S(2)}) %collective-permute-start.15) | collective-permute-done | bytes 786464 | tf_op jit(solution)/shard_map/ppermute | solution.py:104
  220.1 4.5 copy.128
  231.2 15.8 %collective-permute-done.16.by_y = bf16[512,768]{1,0:T(8,128)(2,1)} collective-permute-done((bf16[512,768]{1,0:T(8,128)(2,1)S(1)}, bf16[512,768]{1,0:T(8,128)(2,1)}, u32[]{:S(2)}, u32[]{:S(2)}) %collective-permute-start.16) | collective-permute-done | bytes 786464 | tf_op jit(solution)/shard_map/ppermute | solution.py:104
  250.0 3.0 fusion
  254.0 5.6 %collective-permute-done.29 = bf16[2,4,48,1536]{3,2,1,0:T(8,128)(2,1)} collective-permute-done((bf16[2,4,48,1536]{3,2,1,0:T(8,128)(2,1)}, bf16[2,4,48,1536]{3,2,1,0:T(8,128)(2,1)}, u32[]{:S(2)}, u32[]{:S(2)}) %collective-permute-start.29) | collective-permute-done | bytes 1179680 | tf_op jit(solution)/shard_map/ppermute | solution.py:119
  259.6 6.9 %collective-permute-start.25 = (bf16[2,96,768]{1,2,0:T(8,128)(2,1)}, bf16[2,96,768]{1,2,0:T(8,128)(2,1)}, u32[]{:S(2)}, u32[]{:S(2)}) collective-permute-start(bf16[2,96,768]{1,2,0:T(8,128)(2,1)} %get-tuple-element.246), channel_id=1, source_target_pairs={{0,8},{1,9},{2,10},{3,11},{4,12},{5,13},{6,14},{7,15},{8,16},{9,17... | collective-permute-start | bytes 884744 | tf_op jit(solution)/shard_map/ppermute | solution.py:107
  272.8 3.7 all-to-all-start
  279.0 19.3 %all-to-all-done = f32[32,1,288]{2,1,0:T(1,128)S(1)} async-done(((f32[32,1,288]{2,1,0:T(1,128)}), f32[32,1,288]{2,1,0:T(1,128)S(1)}, u32[]{:S(2)}, u32[]{:S(2)}) %all-to-all-start) | async-done | bytes 36896 | tf_op jit(solution)/shard_map/all_to_all | solution.py:891
  300.1 49.3 %place.3 = bf16[2048,768]{1,0:T(8,128)(2,1)} custom-call(s32[6]{0:T(128)S(1)} %copy-done.19, bf16[512,768]{1,0:T(8,128)(2,1)S(1)} %copy-done.2, bf16[512,768]{1,0:T(8,128)(2,1)S(1)} %copy-done.4, bf16[512,768]{1,0:T(8,128)(2,1)} %collective-permute-done.21.by_c, bf16[512,768]{1,0:T(8,128)(2,1)} %collective-permute-done.22.by_yc), custom_call_target="tpu_custom_call" | custom-call | bytes 6291456 | tf_op jit(solution)/shard_map/place/pallas_call | solution.py:840
  349.5 73.2 %place.2 = bf16[2048,768]{1,0:T(8,128)(2,1)} custom-call(s32[6]{0:T(128)S(1)} %copy-done.19, bf16[512,768]{1,0:T(8,128)(2,1)S(1)} %add_convert_fusion.4.own, bf16[512,768]{1,0:T(8,128)(2,1)} %collective-permute-done.16.by_y, bf16[512,768]{1,0:T(8,128)(2,1)} %collective-permute-done.17.by_c, bf16[512,768]{1,0:T(8,128)(2,1)} %collective-permute-done.18.by_yc), custom_call_target="tpu_custom_call" | custom-call | bytes 6291456 | tf_op jit(solution)/shard_map/place/pallas_call | solution.py:840
  431.4 4.7 collective-permute-done.31
  436.1 5.2 %collective-permute-done.32 = bf16[48,1536]{1,0:T(8,128)(2,1)} collective-permute-done((bf16[48,1536]{1,0:T(8,128)(2,1)S(1)}, bf16[48,1536]{1,0:T(8,128)(2,1)}, u32[]{:S(2)}, u32[]{:S(2)}) %collective-permute-start.32) | collective-permute-done | bytes 147488 | tf_op jit(solution)/shard_map/ppermute | solution.py:107
  446.8 4.6 all-to-all-start.1
  452.6 6.1 %all-to-all-done.1 = f32[32,1,289]{2,1,0:T(1,128)S(1)} async-done(((f32[32,1,289]{2,1,0:T(1,128)}), f32[32,1,289]{2,1,0:T(1,128)S(1)}, u32[]{:S(2)}, u32[]{:S(2)}) %all-to-all-start.1) | async-done | bytes 37024 | tf_op jit(solution)/shard_map/all_to_all | solution.py:897
  (246 shorter events, 97.9 us)
Async XLA Ops:
  7.9 12.6 %collective-permute-start.4 = (bf16[48,1536]{1,0:T(8,128)(2,1)S(1)}, bf16[48,1536]{1,0:T(8,128)(2,1)S(1)}, u32[]{:S(2)}, u32[]{:S(2)}) collective-permute-start(bf16[48,1536]{1,0:T(8,128)(2,1)S(1)} %copy.122), channel_id=1, source_target_pairs={{0,16},{1,17},{2,18},{3,19},{4,20},{5,21},{6,22},{7,23},{8,24},{9,... | collective-permute-start | bytes 442376 | tf_op jit(solution)/shard_map/ppermute | solution.py:107
  10.4 10.0 %collective-permute-start.5 = (bf16[48,1536]{1,0:T(8,128)(2,1)S(1)}, bf16[48,1536]{1,0:T(8,128)(2,1)S(1)}, u32[]{:S(2)}, u32[]{:S(2)}) collective-permute-start(bf16[48,1536]{1,0:T(8,128)(2,1)S(1)} %copy.122), channel_id=1, source_target_pairs={{0,24},{1,25},{2,26},{3,27},{4,28},{5,29},{6,30},{7,31},{8,0},{9,1... | collective-permute-start | bytes 442376 | tf_op jit(solution)/shard_map/ppermute | solution.py:107
  20.5 9.9 %collective-permute-start.6 = (bf16[4,48,1536]{2,1,0:T(8,128)(2,1)S(1)}, bf16[4,48,1536]{2,1,0:T(8,128)(2,1)S(1)}, u32[]{:S(2)}, u32[]{:S(2)}) collective-permute-start(bf16[4,48,1536]{2,1,0:T(8,128)(2,1)S(1)} %get-tuple-element.261), channel_id=1, source_target_pairs={{0,4},{1,3},{2,6},{3,1},{4,0},{5,7},{6,2},{7,5},{8,12},{9,11},{10,... | collective-permute-start | bytes 1769480 | tf_op jit(solution)/shard_map/ppermute | solution.py:112
  30.7 25.8 %collective-permute-start.7 = (bf16[2,4,48,1536]{3,2,1,0:T(8,128)(2,1)S(1)}, bf16[2,4,48,1536]{3,2,1,0:T(8,128)(2,1)S(1)}, u32[]{:S(2)}, u32[]{:S(2)}) collective-permute-start(bf16[2,4,48,1536]{3,2,1,0:T(8,128)(2,1)S(1)} %get-tuple-element.254), channel_id=1, source_target_pairs={{0,2},{1,5},{2,0},{3,7},{4,6},{5,1},{6,4},{7,3},{8,10},{9,13},{10,... | collective-permute-start | bytes 3538952 | tf_op jit(solution)/shard_map/ppermute | solution.py:119
  32.4 12.8 %collective-permute-start.9 = (bf16[2,96,768]{2,1,0:T(8,128)(2,1)S(1)}, bf16[2,96,768]{2,1,0:T(8,128)(2,1)S(1)}, u32[]{:S(2)}, u32[]{:S(2)}) collective-permute-start(bf16[2,96,768]{2,1,0:T(8,128)(2,1)S(1)} %get-tuple-element.267), channel_id=1, source_target_pairs={{0,8},{1,9},{2,10},{3,11},{4,12},{5,13},{6,14},{7,15},{8,16},{9,17... | collective-permute-start | bytes 884744 | tf_op jit(solution)/shard_map/ppermute | solution.py:107
  36.0 19.2 %collective-permute-start.10 = (bf16[2,96,768]{2,1,0:T(8,128)(2,1)S(1)}, bf16[2,96,768]{2,1,0:T(8,128)(2,1)S(1)}, u32[]{:S(2)}, u32[]{:S(2)}) collective-permute-start(bf16[2,96,768]{2,1,0:T(8,128)(2,1)S(1)} %get-tuple-element.267), channel_id=1, source_target_pairs={{0,16},{1,17},{2,18},{3,19},{4,20},{5,21},{6,22},{7,23},{8,24},{9,... | collective-permute-start | bytes 884744 | tf_op jit(solution)/shard_map/ppermute | solution.py:107
  37.7 17.5 %collective-permute-start.11 = (bf16[2,96,768]{2,1,0:T(8,128)(2,1)S(1)}, bf16[2,96,768]{2,1,0:T(8,128)(2,1)S(1)}, u32[]{:S(2)}, u32[]{:S(2)}) collective-permute-start(bf16[2,96,768]{2,1,0:T(8,128)(2,1)S(1)} %get-tuple-element.267), channel_id=1, source_target_pairs={{0,24},{1,25},{2,26},{3,27},{4,28},{5,29},{6,30},{7,31},{8,0},{9,1... | collective-permute-start | bytes 884744 | tf_op jit(solution)/shard_map/ppermute | solution.py:107
  55.4 27.9 %collective-permute-start.12 = (bf16[4,2,96,768]{3,2,1,0:T(8,128)(2,1)S(1)}, bf16[4,2,96,768]{3,2,1,0:T(8,128)(2,1)S(1)}, u32[]{:S(2)}, u32[]{:S(2)}) collective-permute-start(bf16[4,2,96,768]{3,2,1,0:T(8,128)(2,1)S(1)} %get-tuple-element.252), channel_id=1, source_target_pairs={{0,4},{1,5},{2,6},{3,7},{4,0},{5,1},{6,2},{7,3},{8,12},{9,13},{10,... | collective-permute-start | bytes 3538952 | tf_op jit(solution)/shard_map/ppermute | solution.py:101
  56.7 37.6 %collective-permute-start.8 = (bf16[2,2,4,48,1536]{4,3,2,1,0:T(8,128)(2,1)S(1)}, bf16[2,2,4,48,1536]{4,3,2,1,0:T(8,128)(2,1)}, u32[]{:S(2)}, u32[]{:S(2)}) collective-permute-start(bf16[2,2,4,48,1536]{4,3,2,1,0:T(8,128)(2,1)S(1)} %pad_maximum_fusion.own), channel_id=1, source_target_pairs={{0,1},{1,0},{2,3},{3,2},{4,5},{5,4},{6,7},{7,6},{8,9},{9,8},{10,11... | collective-permute-start | bytes 7077896 | tf_op jit(solution)/shard_map/ppermute | solution.py:98
  84.9 23.8 %collective-permute-start.13 = (bf16[2,4,2,96,768]{4,3,2,1,0:T(8,128)(2,1)}, bf16[2,4,2,96,768]{4,3,2,1,0:T(8,128)(2,1)}, u32[]{:S(2)}, u32[]{:S(2)}) collective-permute-start(bf16[2,4,2,96,768]{4,3,2,1,0:T(8,128)(2,1)} %pad_maximum_fusion.1.own), channel_id=1, source_target_pairs={{0,1},{1,0},{2,3},{3,2},{4,5},{5,4},{6,7},{7,6},{8,9},{9,8},{10,11... | collective-permute-start | bytes 7077896 | tf_op jit(solution)/shard_map/ppermute | solution.py:98
  107.4 19.8 %collective-permute-start.14 = (bf16[512,768]{1,0:T(8,128)(2,1)}, bf16[512,768]{1,0:T(8,128)(2,1)S(1)}, u32[]{:S(2)}, u32[]{:S(2)}) collective-permute-start(bf16[512,768]{1,0:T(8,128)(2,1)} %get-tuple-element.73.sl_ref.sl_a), channel_id=1, source_target_pairs={{0,2},{1,3},{2,0},{3,1},{4,6},{5,7},{6,4},{7,5},{8,10},{9,11},{10,... | collective-permute-start | bytes 2359304 | tf_op jit(solution)/shard_map/ppermute | solution.py:104
  141.2 26.5 %collective-permute-start.19 = (bf16[512,768]{1,0:T(8,128)(2,1)}, bf16[512,768]{1,0:T(8,128)(2,1)S(1)}, u32[]{:S(2)}, u32[]{:S(2)}) collective-permute-start(bf16[512,768]{1,0:T(8,128)(2,1)} %get-tuple-element.77), channel_id=1, source_target_pairs={{0,2},{1,3},{2,0},{3,1},{4,6},{5,7},{6,4},{7,5},{8,10},{9,11},{10,... | collective-permute-start | bytes 2359304 | tf_op jit(solution)/shard_map/ppermute | solution.py:104
  167.6 37.4 %collective-permute-start.23 = (bf16[2,4,2,96,768]{4,3,2,1,0:T(8,128)(2,1)}, bf16[2,4,2,96,768]{4,3,2,1,0:T(8,128)(2,1)S(1)}, u32[]{:S(2)}, u32[]{:S(2)}) collective-permute-start(bf16[2,4,2,96,768]{4,3,2,1,0:T(8,128)(2,1)} %get-tuple-element.93), channel_id=1, source_target_pairs={{0,1},{1,0},{2,3},{3,2},{4,5},{5,4},{6,7},{7,6},{8,9},{9,8},{10,11... | collective-permute-start | bytes 7077896 | tf_op jit(solution)/shard_map/ppermute | solution.py:98
  192.8 24.6 %collective-permute-start.28 = (bf16[2,2,4,48,1536]{4,3,2,1,0:T(8,128)(2,1)}, bf16[2,2,4,48,1536]{4,3,2,1,0:T(8,128)(2,1)S(1)}, u32[]{:S(2)}, u32[]{:S(2)}) collective-permute-start(bf16[2,2,4,48,1536]{4,3,2,1,0:T(8,128)(2,1)} %get-tuple-element.98), channel_id=1, source_target_pairs={{0,1},{1,0},{2,3},{3,2},{4,5},{5,4},{6,7},{7,6},{8,9},{9,8},{10,11... | collective-permute-start | bytes 7077896 | tf_op jit(solution)/shard_map/ppermute | solution.py:98
  193.4 20.7 %collective-permute-start.15 = (bf16[512,768]{1,0:T(8,128)(2,1)}, bf16[512,768]{1,0:T(8,128)(2,1)}, u32[]{:S(2)}, u32[]{:S(2)}) collective-permute-start(bf16[512,768]{1,0:T(8,128)(2,1)} %get-tuple-element.75), channel_id=1, source_target_pairs={{0,2},{1,3},{2,0},{3,1},{4,6},{5,7},{6,4},{7,5},{8,10},{9,11},{10,... | collective-permute-start | bytes 2359304 | tf_op jit(solution)/shard_map/ppermute | solution.py:104
  204.5 26.4 %collective-permute-start.20 = (bf16[512,768]{1,0:T(8,128)(2,1)}, bf16[512,768]{1,0:T(8,128)(2,1)S(1)}, u32[]{:S(2)}, u32[]{:S(2)}) collective-permute-start(bf16[512,768]{1,0:T(8,128)(2,1)} %get-tuple-element.82.own), channel_id=1, source_target_pairs={{0,2},{1,3},{2,0},{3,1},{4,6},{5,7},{6,4},{7,5},{8,10},{9,11},{10,... | collective-permute-start | bytes 2359304 | tf_op jit(solution)/shard_map/ppermute | solution.py:104
  206.9 40.1 %collective-permute-start.24 = (bf16[4,2,96,768]{3,2,1,0:T(8,128)(2,1)}, bf16[4,2,96,768]{3,2,1,0:T(8,128)(2,1)}, u32[]{:S(2)}, u32[]{:S(2)}) collective-permute-start(bf16[4,2,96,768]{3,2,1,0:T(8,128)(2,1)} %fusion.2), channel_id=1, source_target_pairs={{0,4},{1,5},{2,6},{3,7},{4,0},{5,1},{6,2},{7,3},{8,12},{9,13},{10,... | collective-permute-start | bytes 3538952 | tf_op jit(solution)/shard_map/ppermute | solution.py:101
  215.8 31.2 %collective-permute-start.16 = (bf16[512,768]{1,0:T(8,128)(2,1)S(1)}, bf16[512,768]{1,0:T(8,128)(2,1)}, u32[]{:S(2)}, u32[]{:S(2)}) collective-permute-start(bf16[512,768]{1,0:T(8,128)(2,1)S(1)} %add_convert_fusion.4.own), channel_id=1, source_target_pairs={{0,2},{1,3},{2,0},{3,1},{4,6},{5,7},{6,4},{7,5},{8,10},{9,11},{10,... | collective-permute-start | bytes 2359304 | tf_op jit(solution)/shard_map/ppermute | solution.py:104
  219.6 40.0 %collective-permute-start.29 = (bf16[2,4,48,1536]{3,2,1,0:T(8,128)(2,1)}, bf16[2,4,48,1536]{3,2,1,0:T(8,128)(2,1)}, u32[]{:S(2)}, u32[]{:S(2)}) collective-permute-start(bf16[2,4,48,1536]{3,2,1,0:T(8,128)(2,1)} %get-tuple-element.245), channel_id=1, source_target_pairs={{0,2},{1,5},{2,0},{3,7},{4,6},{5,1},{6,4},{7,3},{8,10},{9,13},{10,... | collective-permute-start | bytes 3538952 | tf_op jit(solution)/shard_map/ppermute | solution.py:119
  224.9 43.7 %collective-permute-start.21 = (bf16[512,768]{1,0:T(8,128)(2,1)S(1)}, bf16[512,768]{1,0:T(8,128)(2,1)}, u32[]{:S(2)}, u32[]{:S(2)}) collective-permute-start(bf16[512,768]{1,0:T(8,128)(2,1)S(1)} %copy-done.2), channel_id=1, source_target_pairs={{0,1},{1,0},{2,3},{3,2},{4,5},{5,4},{6,7},{7,6},{8,9},{9,8},{10,11... | collective-permute-start | bytes 2359304 | tf_op jit(solution)/shard_map/ppermute | solution.py:98
  230.9 38.5 %collective-permute-start.17 = (bf16[512,768]{1,0:T(8,128)(2,1)S(1)}, bf16[512,768]{1,0:T(8,128)(2,1)}, u32[]{:S(2)}, u32[]{:S(2)}) collective-permute-start(bf16[512,768]{1,0:T(8,128)(2,1)S(1)} %add_convert_fusion.4.own), channel_id=1, source_target_pairs={{0,1},{1,0},{2,3},{3,2},{4,5},{5,4},{6,7},{7,6},{8,9},{9,8},{10,11... | collective-permute-start | bytes 2359304 | tf_op jit(solution)/shard_map/ppermute | solution.py:98
  247.0 24.1 %collective-permute-start.22 = (bf16[512,768]{1,0:T(8,128)(2,1)S(1)}, bf16[512,768]{1,0:T(8,128)(2,1)}, u32[]{:S(2)}, u32[]{:S(2)}) collective-permute-start(bf16[512,768]{1,0:T(8,128)(2,1)S(1)} %collective-permute-done.20.by_y), channel_id=1, source_target_pairs={{0,1},{1,0},{2,3},{3,2},{4,5},{5,4},{6,7},{7,6},{8,9},{9,8},{10,11... | collective-permute-start | bytes 2359304 | tf_op jit(solution)/shard_map/ppermute | solution.py:98
  247.0 102.5 %collective-permute-start.18 = (bf16[512,768]{1,0:T(8,128)(2,1)}, bf16[512,768]{1,0:T(8,128)(2,1)}, u32[]{:S(2)}, u32[]{:S(2)}) collective-permute-start(bf16[512,768]{1,0:T(8,128)(2,1)} %collective-permute-done.16.by_y), channel_id=1, source_target_pairs={{0,1},{1,0},{2,3},{3,2},{4,5},{5,4},{6,7},{7,6},{8,9},{9,8},{10,11... | collective-permute-start | bytes 2359304 | tf_op jit(solution)/shard_map/ppermute | solution.py:98
  259.6 163.1 %collective-permute-start.25 = (bf16[2,96,768]{1,2,0:T(8,128)(2,1)}, bf16[2,96,768]{1,2,0:T(8,128)(2,1)}, u32[]{:S(2)}, u32[]{:S(2)}) collective-permute-start(bf16[2,96,768]{1,2,0:T(8,128)(2,1)} %get-tuple-element.246), channel_id=1, source_target_pairs={{0,8},{1,9},{2,10},{3,11},{4,12},{5,13},{6,14},{7,15},{8,16},{9,17... | collective-permute-start | bytes 884744 | tf_op jit(solution)/shard_map/ppermute | solution.py:107
  268.6 154.1 %collective-permute-start.26 = (bf16[2,96,768]{1,2,0:T(8,128)(2,1)}, bf16[2,96,768]{1,2,0:T(8,128)(2,1)}, u32[]{:S(2)}, u32[]{:S(2)}) collective-permute-start(bf16[2,96,768]{1,2,0:T(8,128)(2,1)} %get-tuple-element.248), channel_id=1, source_target_pairs={{0,16},{1,17},{2,18},{3,19},{4,20},{5,21},{6,22},{7,23},{8,24},{9,... | collective-permute-start | bytes 884744 | tf_op jit(solution)/shard_map/ppermute | solution.py:107
  269.4 153.3 %collective-permute-start.27 = (bf16[2,96,768]{1,2,0:T(8,128)(2,1)S(1)}, bf16[2,96,768]{1,2,0:T(8,128)(2,1)}, u32[]{:S(2)}, u32[]{:S(2)}) collective-permute-start(bf16[2,96,768]{1,2,0:T(8,128)(2,1)S(1)} %get-tuple-element.247), channel_id=1, source_target_pairs={{0,24},{1,25},{2,26},{3,27},{4,28},{5,29},{6,30},{7,31},{8,0},{9,1... | collective-permute-start | bytes 884744 | tf_op jit(solution)/shard_map/ppermute | solution.py:107
  271.0 154.0 %collective-permute-start.30 = (bf16[4,48,1536]{2,1,0:T(8,128)(2,1)}, bf16[4,48,1536]{2,1,0:T(8,128)(2,1)}, u32[]{:S(2)}, u32[]{:S(2)}) collective-permute-start(bf16[4,48,1536]{2,1,0:T(8,128)(2,1)} %fusion.10), channel_id=1, source_target_pairs={{0,4},{1,3},{2,6},{3,1},{4,0},{5,7},{6,2},{7,5},{8,12},{9,11},{10,... | collective-permute-start | bytes 1769480 | tf_op jit(solution)/shard_map/ppermute | solution.py:112
  272.8 25.5 %all-to-all-start = ((f32[32,1,288]{2,1,0:T(1,128)}), f32[32,1,288]{2,1,0:T(1,128)S(1)}, u32[]{:S(2)}, u32[]{:S(2)}) async-start(f32[32,1,288]{2,1,0:T(1,128)} %all_to_all.12), calls=%async_computation | async-start | bytes 98304 | tf_op jit(solution)/shard_map/all_to_all | solution.py:891
  427.8 13.5 %collective-permute-start.32 = (bf16[48,1536]{1,0:T(8,128)(2,1)S(1)}, bf16[48,1536]{1,0:T(8,128)(2,1)}, u32[]{:S(2)}, u32[]{:S(2)}) collective-permute-start(bf16[48,1536]{1,0:T(8,128)(2,1)S(1)} %get-tuple-element.259), channel_id=1, source_target_pairs={{0,16},{1,17},{2,18},{3,19},{4,20},{5,21},{6,22},{7,23},{8,24},{9,... | collective-permute-start | bytes 442376 | tf_op jit(solution)/shard_map/ppermute | solution.py:107
  429.8 11.5 %collective-permute-start.33 = (bf16[48,1536]{1,0:T(8,128)(2,1)S(1)}, bf16[48,1536]{1,0:T(8,128)(2,1)}, u32[]{:S(2)}, u32[]{:S(2)}) collective-permute-start(bf16[48,1536]{1,0:T(8,128)(2,1)S(1)} %get-tuple-element.258), channel_id=1, source_target_pairs={{0,24},{1,25},{2,26},{3,27},{4,28},{5,29},{6,30},{7,31},{8,0},{9,1... | collective-permute-start | bytes 442376 | tf_op jit(solution)/shard_map/ppermute | solution.py:107
  446.8 11.9 %all-to-all-start.1 = ((f32[32,1,289]{2,1,0:T(1,128)}), f32[32,1,289]{2,1,0:T(1,128)S(1)}, u32[]{:S(2)}, u32[]{:S(2)}) async-start(f32[32,1,289]{2,1,0:T(1,128)} %broadcast_in_dim.15), calls=%async_computation.1 | async-start | bytes 98304 | tf_op jit(solution)/shard_map/all_to_all | solution.py:897
  452.2 10.2 %collective-permute-start.34 = (f32[48,4,192]{0,2,1:T(8,128)}, f32[48,4,192]{0,2,1:T(8,128)S(1)}, u32[]{:S(2)}, u32[]{:S(2)}) collective-permute-start(f32[48,4,192]{0,2,1:T(8,128)} %select_bitcast_fusion), channel_id=1, source_target_pairs={{0,1},{1,0},{2,3},{3,2},{4,5},{5,4},{6,7},{7,6},{8,9},{9,8},{10,11... | collective-permute-start | bytes 442376 | tf_op jit(solution)/shard_map/ppermute | solution.py:98
  (55 other events, 284.2 us)

commit v2 on v1

--- a/solution.py
+++ b/solution.py
@@ -132,13 +132,12 @@
     return cc, zz, xx, yy
 
 
-def attn_weight_copies(plan, meta, own, other, w, sem, lanes):
+def attn_weight_copies(plan, meta, srcs, w, sem, lanes):
     if not plan.direct:
-        src = own.at[:, :, lanes]
-        return [pltpu.make_async_copy(src, w, sem.at[0])]
+        return [pltpu.make_async_copy(srcs[0].at[:, :, lanes], w, sem.at[0])]
     copies = []
-    for r, src in enumerate((own, other)):
-        for s2 in range(2):
+    for s2 in range(2):
+        for r in range(2):
             for s1 in range(2):
                 for k in range(plan.nz):
                     cc = jnp.bitwise_xor(meta[4], r)
@@ -148,7 +147,7 @@
                     row = pl.multiple_of((zz * 2 + xx) * plan.rows + cc * plan.half, 16)
                     copies.append(
                         pltpu.make_async_copy(
-                            src.at[s2, s1, k, :, lanes],
+                            srcs[2 * r + s2].at[s1, k, :, lanes],
                             w.at[yy, pl.ds(row, plan.half), :],
                             sem.at[len(copies)],
                         )
@@ -164,8 +163,10 @@
     segr_ref,
     np_ref,
     pb_ref,
-    own,
-    other,
+    w_a,
+    w_b,
+    w_c,
+    w_d,
     sl_ref,
     mid_ref,
     fl_ref,
@@ -177,10 +178,11 @@
 ):
     cols = plan.cols
     first = pl.program_id(0) == 0
+    srcs = (w_a, w_b, w_c, w_d)
 
     @pl.when(first)
     def _():
-        for copy in attn_weight_copies(plan, meta, own, other, w, sem, slice(None)):
+        for copy in attn_weight_copies(plan, meta, srcs, w, sem, slice(None)):
             copy.start()
 
     x = x_ref[...].astype(f32)
@@ -190,7 +192,7 @@
 
     @pl.when(first)
     def _():
-        for copy in attn_weight_copies(plan, meta, own, other, w, sem, slice(None)):
+        for copy in attn_weight_copies(plan, meta, srcs, w, sem, slice(None)):
             copy.wait()
 
     for y in range(2):
@@ -224,18 +226,18 @@
     sl_ref[...] = (normal * np_ref[2:3, :] + np_ref[3:4, :]).astype(bf16)
 
 
-def ff_weight_copies(plan, meta, own, other, w, sem, r, e):
+def ff_weight_copies(plan, meta, srcs, w, sem, r, e):
+    src = srcs[4 * e + 2 * r : 4 * e + 2 * r + 2]
     if not plan.direct:
-        return [pltpu.make_async_copy((own, other)[r].at[e], w.at[e, r], sem.at[r, e, 0])]
+        return [pltpu.make_async_copy(src[0], w.at[e, r], sem.at[r, e, 0])]
     copies = []
-    src = (own, other)[r]
     for fx in range(2):
         for k in range(plan.nz):
             _, zz, xx, _ = piece_spot(plan, meta, r, 0, fx, k, -1)
             row = pl.multiple_of((zz * 2 + xx) * plan.rows, 16)
             copies.append(
                 pltpu.make_async_copy(
-                    src.at[fx, k, e],
+                    src[fx].at[k],
                     w.at[e, r, pl.ds(row, plan.rows), :],
                     sem.at[r, e, len(copies)],
                 )
@@ -243,16 +245,18 @@
     return copies
 
 
-def ff_kernel(
-    plan, meta, sl_ref, cot_ref, hb_ref, own, other, sg_ref, fed_ref, act_ref, hg_ref, gh_ref, w, sem
-):
+def ff_kernel(plan, own, meta, sl_ref, cot_ref, hb_ref, *refs):
+    srcs, refs = refs[:8], refs[8:]
+    if own:
+        mid_ref, *refs = refs
+    sg_ref, fed_ref, act_ref, hg_ref, gh_ref, w, sem = refs
     step = pl.program_id(0)
     first = step == 0
 
     def when_first(action, r, e):
         @pl.when(first)
         def _():
-            for copy in ff_weight_copies(plan, meta, own, other, w, sem, r, e):
+            for copy in ff_weight_copies(plan, meta, srcs, w, sem, r, e):
                 getattr(copy, action)()
 
     for r in range(2):
@@ -286,12 +290,16 @@
         part = mm_nt(act, w[1, r])
         fed = part if fed is None else fed + part
     sg_ref[...] = sg.astype(sg_ref.dtype)
+    if own:
+        fed = fed + mid_ref[...]
     fed_ref[...] = fed.astype(fed_ref.dtype)
 
 
 def ff_grad_copies(plan, meta, buf, outs, sem, r):
     if not plan.direct:
-        return [pltpu.make_async_copy(buf.at[r], outs[r], sem.at[r, 0])]
+        return [
+            pltpu.make_async_copy(buf.at[r, e], outs[2 * r + e], sem.at[r, e]) for e in range(2)
+        ]
     copies = []
     for e in range(2):
         for fx in range(2):
@@ -301,7 +309,7 @@
                 copies.append(
                     pltpu.make_async_copy(
                         buf.at[r, e, pl.ds(row, plan.rows), :],
-                        outs[r].at[fx, k, e],
+                        outs[4 * r + 2 * e + fx].at[k],
                         sem.at[r, len(copies)],
                     )
                 )
@@ -319,12 +327,9 @@
     act_b,
     hg_a,
     hg_b,
-    mine,
-    theirs,
-    left,
-    buf,
-    sem,
+    *rest,
 ):
+    *outs, left, buf, sem = rest
     step = pl.program_id(0)
     count = sl_a.shape[0]
 
@@ -346,13 +351,13 @@
                     got = mm(left[e, :, :count], one[0, :, at])
                     got = got + mm(left[e, :, count:], two[0, :, at])
                     buf[r, e, :, at] = got.astype(bf16)
-            for copy in ff_grad_copies(plan, meta, buf, (mine, theirs), sem, r):
+            for copy in ff_grad_copies(plan, meta, buf, outs, sem, r):
                 copy.start()
 
     @pl.when(step == 1)
     def _():
         for r in range(2):
-            for copy in ff_grad_copies(plan, meta, buf, (mine, theirs), sem, r):
+            for copy in ff_grad_copies(plan, meta, buf, outs, sem, r):
                 copy.wait()
 
 
@@ -366,8 +371,10 @@
     np_ref,
     qkv_ref,
     p_ref,
-    own,
-    other,
+    w_a,
+    w_b,
+    w_c,
+    w_d,
     dqkv_ref,
     ml_ref,
     mg_ref,
@@ -379,10 +386,11 @@
     cols = plan.cols
     first = pl.program_id(0) == 0
     lanes = slice(3 * cols, 4 * cols)
+    srcs = (w_a, w_b, w_c, w_d)
 
     @pl.when(first)
     def _():
-        for copy in attn_weight_copies(plan, meta, own, other, w, sem, lanes):
+        for copy in attn_weight_copies(plan, meta, srcs, w, sem, lanes):
             copy.start()
         vec_ref[...] = jnp.zeros_like(vec_ref)
         pair_ref[...] = jnp.zeros_like(pair_ref)
@@ -401,7 +409,7 @@
 
     @pl.when(first)
     def _():
-        for copy in attn_weight_copies(plan, meta, own, other, w, sem, lanes):
+        for copy in attn_weight_copies(plan, meta, srcs, w, sem, lanes):
             copy.wait()
 
     tiles = ml.shape[0] // LANES
@@ -447,7 +455,7 @@
                 copies.append(
                     pltpu.make_async_copy(
                         buf.at[fy, pl.ds(row, plan.half), :],
-                        outs[r].at[s2, s1, k],
+                        outs[r * plan.nz + k].at[s2, s1],
                         sem.at[fy, len(copies)],
                     )
                 )
@@ -483,15 +491,16 @@
 
 
 def input_grad_kernel(
-    plan, meta, x_ref, mg_ref, np_ref, dqkv_ref, own, other, ig_ref, vec_ref, w, sem
+    plan, meta, x_ref, mg_ref, np_ref, dqkv_ref, w_a, w_b, w_c, w_d, ig_ref, vec_ref, w, sem
 ):
     cols = plan.cols
     first = pl.program_id(0) == 0
     lanes = slice(0, 3 * cols)
+    srcs = (w_a, w_b, w_c, w_d)
 
     @pl.when(first)
     def _():
-        for copy in attn_weight_copies(plan, meta, own, other, w, sem, lanes):
+        for copy in attn_weight_copies(plan, meta, srcs, w, sem, lanes):
             copy.start()
         vec_ref[...] = jnp.zeros_like(vec_ref)
 
@@ -499,7 +508,7 @@
 
     @pl.when(first)
     def _():
-        for copy in attn_weight_copies(plan, meta, own, other, w, sem, lanes):
+        for copy in attn_weight_copies(plan, meta, srcs, w, sem, lanes):
             copy.wait()
 
     fg = mm_nt(dqkv_ref[0], w[0]) + mm_nt(dqkv_ref[1], w[1])
@@ -507,6 +516,125 @@
     vec_ref[1:2, :] += jnp.sum(fg, axis=0, keepdims=True)
     ig = mg_ref[...] + norm_backward(fg, normal, scaled, np_ref[0:1, :])
     ig_ref[...] = ig.astype(bf16)
+
+
+def add_kernel(meta, left, right, *outs):
+    for i, out in enumerate(outs):
+        out[...] = (left[i].astype(f32) + right[i].astype(f32)).astype(out.dtype)
+
+
+def add_parts(meta, left, right):
+    n, size = left.shape[0], left.shape[-1]
+    shape = left.shape[1:]
+    left, right = left.reshape(n, -1, size), right.reshape(n, -1, size)
+    length = left.shape[1]
+    blocks = 4 if length % 64 == 0 and length >= 384 else 1
+    step = length // blocks
+    outs = call(
+        add_kernel,
+        "add_parts",
+        (blocks,),
+        [(v, (n, step, size), lambda i, m: (0, i, 0)) for v in (left, right)],
+        [(jax.ShapeDtypeStruct((length, size), bf16), (step, size), lambda i, m: (i, 0))] * n,
+        [],
+        vmem=24,
+    )(meta, left, right)
+    return [v.reshape(shape) for v in outs]
+
+
+def sums_kernel(meta, *refs):
+    n = len(refs) // 3
+    for left, right, out in zip(refs[:n], refs[n : 2 * n], refs[2 * n :]):
+        out[...] = (left[...].astype(f32) + right[...].astype(f32)).astype(out.dtype)
+
+
+def add_lists(meta, left, right):
+    n, shape = len(left), left[0].shape
+    flat = [v.reshape(-1, shape[-1]) for v in (*left, *right)]
+    length, size = flat[0].shape
+    blocks = 2 if length % 32 == 0 and length >= 384 else 1
+    block = ((length // blocks, size), lambda i, m: (i, 0))
+    outs = call(
+        sums_kernel,
+        "add_lists",
+        (blocks,),
+        [(v, *block) for v in flat],
+        [(jax.ShapeDtypeStruct((length, size), bf16), *block)] * n,
+        [],
+    )(meta, *flat)
+    return [v.reshape(shape) for v in outs]
+
+
+def first_kernel(meta, *refs):
+    n = (len(refs) - 2) // 2
+    for k in range(n):
+        for s in range(2):
+            total = refs[k][s].astype(f32) + refs[n + k][s].astype(f32)
+            refs[2 * n + s][:, k] = total.astype(bf16)
+
+
+def add_first(meta, left, right):
+    shape = left[0].shape[1:]
+    row = 16 if shape[1] % 16 == 0 else shape[1]
+    grid = (shape[0], shape[1] // row)
+    block = (2, 1, row, shape[2])
+    out = (shape[0], len(left), *shape[1:])
+    out_block = (1, len(left), row, shape[2])
+    return call(
+        first_kernel,
+        "add_first",
+        grid,
+        [(v, block, lambda i, j, m: (0, i, j, 0)) for v in (*left, *right)],
+        [(jax.ShapeDtypeStruct(out, bf16), out_block, lambda i, j, m: (i, 0, j, 0))] * 2,
+        [],
+    )(meta, *left, *right)
+
+
+def by_z_kernel(meta, a, b, c, d, *outs):
+    for k, out in enumerate(outs):
+        out[0] = (a[k].astype(f32) + b[k].astype(f32)).astype(out.dtype)
+        out[1] = (c[k].astype(f32) + d[k].astype(f32)).astype(out.dtype)
+
+
+def add_by_z(meta, a, b, c, d):
+    shape = (2, *a.shape[1:])
+    full = (a.shape, lambda i, m: (0, 0, 0))
+    return call(
+        by_z_kernel,
+        "add_by_z",
+        (1,),
+        [(v, *full) for v in (a, b, c, d)],
+        [(jax.ShapeDtypeStruct(shape, bf16), shape, lambda i, m: (0, 0, 0))] * a.shape[0],
+        [],
+    )(meta, a, b, c, d)
+
+
+def total_kernel(meta, *refs):
+    *parts, ff_square, local, keep, send, payload = refs
+    total = parts[0][...].astype(f32)
+    for part in parts[1:]:
+        total = total + part[...].astype(f32)
+    quarter = total.shape[1] // 8
+    for core in range(2):
+        for out, c in ((keep, core), (send, 1 - core)):
+
+            @pl.when(meta[4] == core)
+            def _():
+                for b in range(4):
+                    at = (2 * b + c) * quarter
+                    out[:, b * quarter : (b + 1) * quarter] = total[:, at : at + quarter]
+
+    square = jnp.sum(total * total) + jnp.sum(ff_square[...]) + jnp.sum(local[...] * local[...])
+    size = local.shape[1]
+    count = payload.shape[0]
+    payload[:, :, :size] = jnp.broadcast_to(local[...][None], (count, 1, size))
+    payload[:, :, size:] = jnp.full((count, 1, LANES), square, f32)
+
+
+def out_kernel(meta, pre_a, fed_a, pre_b, fed_b, np_ref, out_a, out_b):
+    for pre, fed, out in ((pre_a, fed_a, out_a), (pre_b, fed_b, out_b)):
+        total = pre[...].astype(f32) + fed[...].astype(f32) + np_ref[5:6, :]
+        out[...] = total.astype(bf16)
 
 
 def place_kernel(meta, own, by_y, by_c, by_yc, out, sem):
@@ -522,28 +650,68 @@
         copy.wait()
 
 
-def adam_kernel(rates, factor_ref, *refs):
-    count = len(rates)
-    factor = factor_ref[0, 0]
+def adam_kernel(plan, rates, meta, got, *refs):
+    per = got.shape[2] // LANES - 1
+    total = jnp.sum(got[:, 0, per * LANES :], axis=0, keepdims=True)[:, 0:1]
+    norm = jnp.sqrt(total)
+    refs[-1][...] = norm
+    factor = jnp.minimum(1.0, CLIP / norm)
     correction = 1.0 - BETA**STEP
+    width, quarter, part = plan.width, plan.width // 4, plan.part
+
+    def line(start, length):
+        spots = range(start // LANES, (start + length) // LANES)
+        return jnp.concatenate(
+            [got[b // per, :, b % per * LANES : (b % per + 1) * LANES] for b in spots],
+            axis=1,
+        )
+
+    def owned(pick):
+        value = pick(0)
+        for m in range(1, 4):
+            value = jnp.where(meta[0] == m, pick(m), value)
+        return value
+
+    pairs = [line((6 + i) * width, width) for i in range(2)]
+    small = (
+        jnp.concatenate([line(i * width, width) for i in range(6)], axis=0),
+        jnp.concatenate(
+            [owned(lambda m: v[:, m * quarter : (m + 1) * quarter]) for v in pairs], axis=0
+        ),
+        owned(lambda m: line(8 * width + m * part, part)),
+    )
+    ins, outs = refs[: 4 * 4 + 3 * 3], refs[4 * 4 + 3 * 3 : -1]
     for i, (rate, decay) in enumerate(rates):
-        w_ref, m_ref, s_ref, g_ref = refs[4 * i : 4 * i + 4]
-        m_out, s_out, w_out = refs[4 * count + 3 * i : 4 * count + 3 * i + 3]
-        clipped = g_ref[...] * factor
-        first = BETA * m_ref[...] + (1.0 - BETA) * clipped
-        second = BETA * s_ref[...] + (1.0 - BETA) * clipped * clipped
-        weight = w_ref[...]
-        direction = first / correction / (jnp.sqrt(second / correction) + ADAM_EPS)
-        m_out[...] = first
-        s_out[...] = second
-        w_out[...] = weight - rate * (direction + decay * weight)
+        if i < 4:
+            w_ref, m_ref, s_ref, g_ref = ins[4 * i : 4 * i + 4]
+        else:
+            w_ref, m_ref, s_ref = ins[3 * i + 4 : 3 * i + 7]
+            g_ref = {Ellipsis: small[i - 4]}
+        m_out, s_out, w_out = outs[3 * i : 3 * i + 3]
+        planes = range(w_ref.shape[0]) if len(w_ref.shape) == 3 else (Ellipsis,)
+        for p in planes:
+            clipped = g_ref[p] * factor
+            shape = w_ref[p].shape
+            weight, first, second = (
+                v[p].reshape(clipped.shape) for v in (w_ref, m_ref, s_ref)
+            )
+            first = BETA * first + (1.0 - BETA) * clipped
+            second = BETA * second + (1.0 - BETA) * clipped * clipped
+            direction = first / correction / (jnp.sqrt(second / correction) + ADAM_EPS)
+            m_out[p] = first.reshape(shape)
+            s_out[p] = second.reshape(shape)
+            w_out[p] = (weight - rate * (direction + decay * weight)).reshape(shape)
+
+
+def after(value, *others):
+    return lax.optimization_barrier((value, *others))[0]
 
 
 def any_spec():
     return pl.BlockSpec(memory_space=pl.ANY)
 
 
-def call(kernel, name, grid, ins, outs, scratch, flops, moved, vmem=56):
+def call(kernel, name, grid, ins, outs, scratch, vmem=60):
     def spec(item):
         if item[1] is None:
             return any_spec()
@@ -561,7 +729,7 @@
             scratch_shapes=scratch,
         ),
         compiler_params=pltpu.CompilerParams(vmem_limit_bytes=vmem * MIB),
-        cost_estimate=pl.CostEstimate(flops=flops, bytes_accessed=moved, transcendentals=0),
+        cost_estimate=pl.CostEstimate(flops=1, bytes_accessed=1, transcendentals=0),
     )
 
 
@@ -619,23 +787,15 @@
     low = jnp.where(core_zero, keep, got)
     high = jnp.where(core_zero, got, keep)
     unit = jnp.concatenate([low, high], axis=2).reshape(half, 4 * cols)
-    spread = jnp.stack([unit] + [plan.along_z(unit, k) for k in range(1, nz)])
-    spread = jnp.stack([spread, plan.first(spread)])
-    attn_own = jnp.stack([spread, plan.second(spread)])
-    attn_other = plan.core(attn_own)
-
-    unit = jnp.stack([expand_weight.astype(bf16), reduce_weight.T.astype(bf16)])
-    spread = jnp.stack([unit] + [plan.along_z(unit, k) for k in range(1, nz)])
-    ff_own = jnp.stack([spread, plan.along_x(spread)])
-    ff_other = plan.core(ff_own)
-
-    if not plan.direct:
-        attn_own = absolute_attn(plan, attn_own, attn_other, z, x, y, c)
-        attn_other = meta
-        ff_own = absolute_ff(plan, ff_own, z, x)
-        ff_other = absolute_ff(plan, ff_other, z, x)
-
-    by_core = plan.core(jnp.concatenate([paired_bias.reshape(-1), hidden_bias]))
+    attn_z = [plan.along_z(unit, k) for k in range(1, nz)]
+
+    e_unit = after(expand_weight.astype(bf16), unit)
+    e_z = [plan.along_z(e_unit, k) for k in range(1, nz)]
+    r_unit = after(reduce_weight.T.astype(bf16), e_z[0])
+    r_z = [plan.along_z(r_unit, k) for k in range(1, nz)]
+
+    biases = jnp.concatenate([paired_bias.reshape(-1), hidden_bias])
+    by_core = plan.core(after(biases, attn_z[0]))
     other_pair = by_core[: 2 * quarter].reshape(2, quarter)
     near = jnp.where(
         core_zero,
@@ -653,6 +813,23 @@
     mark_col = marks.reshape(count, 1)
     mark_row = marks.reshape(steps, tiles, LANES)
 
+    spread = after(jnp.stack([unit] + attn_z), e_z[0])
+    spread = jnp.stack([spread, plan.first(spread)])
+    spread, *_, meta, mark_col, mark_row, pair_full, hidden_rows = lax.optimization_barrier(
+        (spread, *e_z[1:], meta, mark_col, mark_row, pair_full, hidden_rows)
+    )
+    e_spread = jnp.stack([e_unit] + e_z)
+    e_x = plan.along_x(e_spread)
+    attn_w = [spread, after(plan.second(spread), *r_z, e_x)]
+    r_spread = jnp.stack([r_unit] + r_z)
+    r_x = plan.along_x(r_spread)
+    attn_w = attn_w + [plan.core(v) for v in attn_w]
+    attn_w[1] = after(attn_w[1], e_spread, r_spread)
+
+    if not plan.direct:
+        attn_w = [absolute_attn(plan, jnp.stack(attn_w[:2]), jnp.stack(attn_w[2:]), z, x, y, c)]
+        attn_w = attn_w + [meta] * 3
+
     whole = lambda shape: (shape, lambda i, m: (0,) * len(shape))
     chunk = lambda n: ((CHUNK, n), lambda i, m: (i, 0))
     mine_rows = ((CHUNK, width), lambda i, m: (m[0] * steps + i, 0))
@@ -672,8 +849,7 @@
             (mark_row, (1, tiles, LANES), lambda i, m: (i, 0, 0)),
             (norm_params, *whole(norm_params.shape)),
             (pair_full, *whole(pair_full.shape)),
-            (attn_own, None, None),
-            (attn_other, None, None),
+            *[(v, None, None) for v in attn_w],
         ],
         [
             (SDS((count, width), bf16), *chunk(width)),
@@ -684,27 +860,33 @@
             (SDS((count, width), bf16), *chunk(width)),
         ],
         [pltpu.VMEM((2, width, 4 * cols), bf16), dma((pieces,))],
-        flops=8 * count * width * width,
-        moved=16 * MIB,
-    )(meta, inputs, mark_col, mark_row, norm_params, pair_full, attn_own, attn_other)
+    )(meta, inputs, mark_col, mark_row, norm_params, pair_full, *attn_w)
 
     sl_far = plan.along_y(sl)
-
-    def feed_forward(sl_in, cot_rows, out_type):
+    e_x, r_x = after(e_x, sl), after(r_x, sl)
+    ff_w = []
+    for near, far in ((e_spread, e_x), (r_spread, r_x)):
+        pieces_of = [near, far, plan.core(near), plan.core(far)]
+        if not plan.direct:
+            pairs = (pieces_of[:2], pieces_of[2:])
+            pieces_of = [v for p in pairs for v in (absolute_ff(plan, jnp.stack(p), z, x), meta)]
+        ff_w = ff_w + pieces_of
+
+    def feed_forward(sl_in, cot_rows, sg_type, base):
         return call(
-            functools.partial(ff_kernel, plan),
+            functools.partial(ff_kernel, plan, len(base) > 0),
             "feed_forward",
             (steps,),
             [
                 (sl_in, *chunk(width)),
                 (cotangent, *cot_rows),
                 (hidden_rows, *whole(hidden_rows.shape)),
-                (ff_own, None, None),
-                (ff_other, None, None),
+                *[(v, None, None) for v in ff_w],
+                *[(v, *chunk(width)) for v in base],
             ],
             [
-                (SDS((count, width), out_type), *chunk(width)),
-                (SDS((count, width), out_type), *chunk(width)),
+                (SDS((count, width), sg_type), *chunk(width)),
+                (SDS((count, width), bf16), *chunk(width)),
                 (SDS((2, count, part), bf16), (2, CHUNK, part), lambda i, m: (0, i, 0)),
                 (SDS((2, count, part), bf16), (2, CHUNK, part), lambda i, m: (0, i, 0)),
                 (SDS((2, part), f32), *whole((2, part))),
@@ -713,23 +895,22 @@
                 pltpu.VMEM((2, 2, width, part), bf16),
                 dma((2, 2, 2 * nz if plan.direct else 1)),
             ],
-            flops=16 * count * width * part,
-            moved=14 * MIB,
-        )(meta, sl_in, cotangent, hidden_rows, ff_own, ff_other)
-
-    sg_near, fed_near, act_near, hg_near, gh_near = feed_forward(sl, mine_rows, f32)
-    sg_send, fed_send, act_far, hg_far, gh_far = feed_forward(sl_far, pair_rows, bf16)
-    sg_far = plan.along_y(sg_send)
-    fed_far = plan.along_y(fed_send)
+        )(meta, sl_in, cotangent, hidden_rows, *ff_w, *base)
+
+    sg_near, pre_near, act_near, hg_near, gh_near = feed_forward(sl, mine_rows, f32, [middle])
+    sl_far = after(sl_far, sg_near)
+    sg_send, fed_send, act_far, hg_far, gh_far = feed_forward(sl_far, pair_rows, bf16, [])
+    pre_far = plan.along_y(pre_near)
+    sg_far = plan.along_y(after(sg_send, pre_far))
 
     half_block = ((1, count, part), lambda i, m: (i, 0, 0))
     all_mine = ((count, width), lambda i, m: (m[0], 0))
     all_pair = ((count, width), lambda i, m: (m[5], 0))
     if plan.direct:
-        grad_shape = SDS((2, nz, 2, rows, part), bf16)
+        grad_shapes = [SDS((nz, rows, part), bf16)] * 8
     else:
-        grad_shape = SDS((2, width, part), bf16)
-    ff_mine, ff_theirs = call(
+        grad_shapes = [SDS((width, part), bf16)] * 4
+    ff_grads = call(
         functools.partial(ff_grad_kernel, plan),
         "ff_grad",
         (2,),
@@ -743,15 +924,23 @@
             (hg_near, *half_block),
             (hg_far, *half_block),
         ],
-        [(grad_shape, None, None), (grad_shape, None, None)],
+        [(v, None, None) for v in grad_shapes],
         [
             pltpu.VMEM((2, width, 2 * count), bf16),
             pltpu.VMEM((2, 2, width, part), bf16),
-            dma((2, 4 * nz if plan.direct else 1)),
+            dma((2, 4 * nz if plan.direct else 2)),
         ],
-        flops=16 * count * width * part,
-        moved=16 * MIB,
     )(meta, sl, sl_far, cotangent, cotangent, act_near, act_far, hg_near, hg_far)
+    if not plan.direct:
+        ff_grads = [v for g in ff_grads for v in relative_ff(plan, g, z, x)]
+
+    e_keep, e_send, r_keep, r_send = add_lists(
+        meta, ff_grads[:4], [plan.core(v) for v in ff_grads[4:]]
+    )
+    sg_far = after(sg_far, e_send, r_send)
+    e_send, r_send, fed_send = lax.optimization_barrier((e_send, r_send, fed_send, sg_far))[:3]
+    e_got, r_got = plan.along_x(e_send), plan.along_x(r_send)
+    fed_far = plan.along_y(fed_send)
 
     dqkv, ml, mg, vec_two, pair_sum = call(
         functools.partial(attn_bwd_kernel, plan),
@@ -765,8 +954,7 @@
             (norm_params, *whole(norm_params.shape)),
             (qkv, *qkv_block),
             (probs, *p_block),
-            (attn_own, None, None),
-            (attn_other, None, None),
+            *[(v, None, None) for v in attn_w],
         ],
         [
             (SDS((2, count, 3 * cols), bf16), *qkv_block),
@@ -776,14 +964,13 @@
             (SDS((2, width), f32), *whole((2, width))),
         ],
         [pltpu.VMEM((2, width, cols), bf16), dma((pieces,))],
-        flops=6 * count * width * width,
-        moved=12 * MIB,
-    )(meta, sg_near, sg_far, middle, cotangent, norm_params, qkv, probs, attn_own, attn_other)
+    )(meta, sg_near, sg_far, middle, cotangent, norm_params, qkv, probs, *attn_w)
 
     if plan.direct:
-        grad_shapes = [SDS((2, 2, nz, half, 4 * cols), bf16)] * 2
+        grad_shapes = [SDS((2, 2, half, 4 * cols), bf16)] * (2 * nz)
     else:
         grad_shapes = [SDS((2, width, 4 * cols), bf16)]
+    ml = after(ml, e_got)
     attn_grads = call(
         functools.partial(attn_grad_kernel, plan),
         "attn_grad",
@@ -800,16 +987,22 @@
             pltpu.VMEM((2, width, 4 * cols), bf16),
             dma((2, 4 * nz if plan.direct else 1)),
         ],
-        flops=8 * count * width * width,
-        moved=10 * MIB,
     )(meta, fl, ml, dqkv, ctx)
-    if plan.direct:
-        attn_mine, attn_theirs = attn_grads
-    else:
-        attn_mine, attn_theirs = relative_attn(plan, attn_grads[0], z, x, y, c)
-        ff_mine = relative_ff(plan, ff_mine, z, x)
-        ff_theirs = relative_ff(plan, ff_theirs, z, x)
-
+    if not plan.direct:
+        both = relative_attn(plan, attn_grads[0], z, x, y, c)
+        attn_grads = [v[:, :, k] for v in both for k in range(nz)]
+    attn_mine, attn_theirs = list(attn_grads[:nz]), list(attn_grads[nz:])
+    attn_theirs[0] = after(attn_theirs[0], r_got, fed_far)
+    attn_got = [plan.core(v) for v in attn_theirs]
+
+    ff_parts = add_by_z(meta, e_keep, e_got, r_keep, after(r_got, attn_theirs[0]))
+
+    attn_got[0] = after(attn_got[0], *ff_parts)
+    attn_keep, attn_send = add_first(meta, attn_mine, attn_got)
+    attn_got = plan.second(attn_send)
+    ff_parts = [after(v, attn_send) for v in ff_parts]
+    ff_z = [plan.along_z(ff_parts[k], k) for k in range(1, nz)]
+    dqkv_late = after(dqkv, attn_send)
     ig, vec_one = call(
         functools.partial(input_grad_kernel, plan),
         "input_grad",
@@ -819,66 +1012,17 @@
             (mg, *chunk(width)),
             (norm_params, *whole(norm_params.shape)),
             (dqkv, *qkv_block),
-            (attn_own, None, None),
-            (attn_other, None, None),
+            *[(v, None, None) for v in attn_w],
         ],
         [
             (SDS((count, width), bf16), *chunk(width)),
             (SDS((8, width), f32), *whole((8, width))),
         ],
         [pltpu.VMEM((2, width, 3 * cols), bf16), dma((pieces,))],
-        flops=6 * count * width * width,
-        moved=10 * MIB,
-    )(meta, inputs, mg, norm_params, dqkv, attn_own, attn_other)
-
-    out = (middle + fed_near + fed_far.astype(f32) + norm_params[5]).astype(bf16)
-
-    def everywhere(block):
-        by_y = plan.along_y(block)
-        by_c = plan.core(block)
-        by_yc = plan.core(by_y)
-        return call(
-            place_kernel,
-            "place",
-            (1,),
-            [(b, None, None) for b in (block, by_y, by_c, by_yc)],
-            [(SDS((count * nmp, width), bf16), None, None)],
-            [dma((4,))],
-            flops=0,
-            moved=6 * MIB,
-            vmem=8,
-        )(meta, block, by_y, by_c, by_yc)[0]
-
-    outputs = everywhere(out)
-    input_gradient = everywhere(ig)
-
-    def plus(one, two):
-        return (one.astype(f32) + two.astype(f32)).astype(bf16)
-
-    def sum_z(parts):
-        total = parts[0].astype(f32)
-        for k in range(1, nz):
-            total = total + plan.along_z(parts[k], k).astype(f32)
-        return total
-
-    got = plan.core(ff_theirs)
-    keep, send = plus(ff_mine[0], got[0]), plus(ff_mine[1], got[1])
-    ff_grads = sum_z(plus(keep, plan.along_x(send)))
-    grad_expand = ff_grads[0]
-    grad_reduce = ff_grads[1].T
-
-    got = plan.core(attn_theirs)
-    keep, send = plus(attn_mine[0], got[0]), plus(attn_mine[1], got[1])
-    got = plan.second(send)
-    keep, send = plus(keep[0], got[0]), plus(keep[1], got[1])
-    unit = sum_z(plus(keep, plan.first(send))).reshape(half, 4, 2, quarter)
-    keep = jnp.where(core_zero, unit[:, :, 0], unit[:, :, 1])
-    got = plan.core(jnp.where(core_zero, unit[:, :, 1], unit[:, :, 0]))
-    shard = jnp.concatenate(
-        [jnp.where(core_zero, keep, got), jnp.where(core_zero, got, keep)], axis=0
-    )
-    grad_triple = shard[:, :3].transpose(1, 0, 2)
-    grad_outward = shard[:, 3].T
+    )(meta, inputs, mg, norm_params, dqkv_late, *attn_w)
+    attn_got = after(attn_got, ig, *(ff_z[:1] + ff_z[2:]))
+    attn_keep, attn_send = add_parts(meta, attn_keep, attn_got)
+    attn_got = plan.first(attn_send)
 
     gh = gh_near + gh_far
     gh = jnp.where(core_zero, gh, gh[::-1]).reshape(-1)
@@ -887,46 +1031,99 @@
     vectors = jnp.concatenate(
         [vec_one[:2].reshape(-1), vec_two[:4].reshape(-1), pair_sum.reshape(-1), gh]
     )
-    size = vectors.shape[0] // plan.ndev
+    size = -(-vectors.shape[0] // (LANES * plan.ndev)) * LANES
+    vectors = jnp.pad(vectors, (0, size * plan.ndev - vectors.shape[0]))
     got = lax.all_to_all(vectors.reshape(plan.ndev, size), AXES, 0, 0, tiled=True)
-    local = jnp.sum(got, axis=0)
-    square = jnp.sum(ff_grads * ff_grads) + jnp.sum(unit * unit)
-    square = square + jnp.sum(local * local)
-    payload = jnp.concatenate([local, square[None]])
-    payload = jnp.broadcast_to(payload[None], (plan.ndev, size + 1))
-    got = lax.all_to_all(payload, AXES, 0, 0, tiled=True)
-    gradient_norm = jnp.sqrt(jnp.sum(got[:, size]))
-    factor = jnp.minimum(1.0, CLIP / gradient_norm)
-    vectors = got[:, :size].reshape(-1)
-    grad_norms = vectors[: 6 * width].reshape(6, width)
-    grad_paired = vectors[6 * width : 8 * width].reshape(2, width)
-    grad_paired = lax.dynamic_slice_in_dim(grad_paired, mp * quarter, quarter, 1)
-    grad_hidden = lax.dynamic_slice_in_dim(vectors[8 * width :], mp * part, part, 0)
+    local = jnp.sum(got, axis=0, keepdims=True)
+
+    ff_grads = ff_parts[0].astype(f32)
+    for part_z in ff_z:
+        ff_grads = ff_grads + part_z.astype(f32)
+    ff_square = jnp.sum(ff_grads * ff_grads).reshape(1, 1)
+
+    attn_parts = add_parts(meta, attn_keep, after(attn_got, local, ff_square))
+
+    pre_in = after(pre_near, attn_parts[0])
+    out, out_pair = call(
+        out_kernel,
+        "out_sum",
+        (steps,),
+        [
+            (pre_in, *chunk(width)),
+            (fed_far, *chunk(width)),
+            (pre_far, *chunk(width)),
+            (fed_send, *chunk(width)),
+            (norm_params, *whole(norm_params.shape)),
+        ],
+        [(SDS((count, width), bf16), *chunk(width))] * 2,
+        [],
+    )(meta, pre_in, fed_far, pre_far, fed_send, norm_params)
+    ig = after(ig, attn_parts[0])
+    ig_pair = plan.along_y(ig)
+    attn_z = [attn_parts[0]] + [plan.along_z(attn_parts[k], k) for k in range(1, nz)]
+    total_in = attn_z + [ff_square, local]
+    def everywhere(block, by_y):
+        blocks = [block, by_y, plan.core(block), plan.core(by_y)]
+        return call(
+            place_kernel,
+            "place",
+            (1,),
+            [(b, *whole((count, width))) for b in blocks],
+            [(SDS((count * nmp, width), bf16), None, None)],
+            [dma((4,))],
+        )(meta, *blocks)[0]
+
+    outputs = everywhere(out, out_pair)
+    total_in[-1] = after(total_in[-1], outputs)
+    keep, send, payload = call(
+        total_kernel,
+        "total",
+        (1,),
+        [(v, *whole(v.shape)) for v in total_in],
+        [
+            (SDS((half, 2 * cols), f32), *whole((half, 2 * cols))),
+            (SDS((half, 2 * cols), f32), *whole((half, 2 * cols))),
+            (
+                SDS((plan.ndev, 1, size + LANES), f32),
+                *whole((plan.ndev, 1, size + LANES)),
+            ),
+        ],
+        [],
+    )(meta, *total_in)
+    by_core = plan.core(send)
+    ig_pair = after(ig_pair, keep)
+    input_gradient = everywhere(ig, ig_pair)
+    got = after(lax.all_to_all(payload, AXES, 0, 0, tiled=True), input_gradient)
+
+    low, high = jnp.where(core_zero, keep, by_core), jnp.where(core_zero, by_core, keep)
+    shard = jnp.concatenate([low, high], axis=0).reshape(rows, 4, quarter)
+    grad_triple = shard[:, :3].transpose(1, 0, 2)
+    grad_outward = shard[:, 3].T
 
     matrix, vector = (LR_MATRIX, DECAY), (LR_VECTOR, 0.0)
     groups = [
-        (triple_weight, triple_first, triple_second, grad_triple),
-        (outward_weight, outward_first, outward_second, grad_outward),
-        (expand_weight, expand_first, expand_second, grad_expand),
-        (reduce_weight, reduce_first, reduce_second, grad_reduce),
-        (norm_params, norm_first, norm_second, grad_norms),
-        (paired_bias, paired_first, paired_second, grad_paired),
-        tuple(
-            v.reshape(1, -1) for v in (hidden_bias, hidden_first, hidden_second, grad_hidden)
-        ),
+        [triple_weight, triple_first, triple_second, grad_triple],
+        [outward_weight, outward_first, outward_second, grad_outward],
+        [expand_weight, expand_first, expand_second, ff_grads[0]],
+        [reduce_weight.T, reduce_first.T, reduce_second.T, ff_grads[1]],
+        [norm_params, norm_first, norm_second],
+        [paired_bias, paired_first, paired_second],
+        [hidden_bias, hidden_first, hidden_second],
     ]
-    flat = [v for group in groups for v in group]
-    vmem = pl.BlockSpec(memory_space=pltpu.VMEM)
-    new = pl.pallas_call(
-        functools.partial(adam_kernel, (matrix,) * 4 + (vector,) * 3),
-        name="adam",
-        out_shape=[SDS(group[0].shape, f32) for group in groups for _ in range(3)],
-        in_specs=[pl.BlockSpec(memory_space=pltpu.SMEM)] + [vmem] * len(flat),
-        out_specs=[vmem] * (3 * len(groups)),
-        compiler_params=pltpu.CompilerParams(vmem_limit_bytes=32 * MIB),
-    )(factor.reshape(1, 1), *flat)
+    flat = [got] + [v for group in groups for v in group]
+    new_shapes = [SDS(group[0].shape, f32) for group in groups for _ in range(3)]
+    new_shapes.append(SDS((1, 1), f32))
+    new = call(
+        functools.partial(adam_kernel, plan, (matrix,) * 4 + (vector,) * 3),
+        "adam",
+        (1,),
+        [(v, *whole(v.shape)) for v in flat],
+        [(s, *whole(s.shape)) for s in new_shapes],
+        [],
+    )(meta, *flat)
     new = list(new)
-    new[18:] = [v.reshape(-1) for v in new[18:]]
+    gradient_norm = new.pop().reshape(())
+    new[9:12] = [v.T for v in new[9:12]]
     return (outputs, input_gradient, gradient_norm, *new)
 
 
@@ -945,13 +1142,13 @@
 
 def absolute_ff(plan, value, z, x):
     value = swap(turn(plan, value, z, 1), x, 0)
-    value = value.transpose(2, 1, 0, 3, 4)
-    return value.reshape(2, plan.width, plan.part)
+    return value.transpose(1, 0, 2, 3).reshape(plan.width, plan.part)
 
 
 def relative_ff(plan, value, z, x):
-    value = value.reshape(2, plan.nz, 2, plan.rows, plan.part).transpose(2, 1, 0, 3, 4)
-    return unturn(plan, swap(value, x, 0), z, 1)
+    value = value.reshape(plan.nz, 2, plan.rows, plan.part).transpose(1, 0, 2, 3)
+    value = unturn(plan, swap(value, x, 0), z, 1)
+    return value[0], value[1]
 
 
 def absolute_attn(plan, own, other, z, x, y, c):

time: 493 us -> 272 us (0.55)
  waiting for transfers between devices: 146 us -> 58.8 us
  Pallas kernels: 209 us -> 122 us
  local copies, waits for them, and re-layouts: 49.2 us -> 18 us
  other arithmetic: 26.4 us -> 11.3 us
  starting transfers between devices: 51.2 us -> 59.9 us
    pallas_call x5 -> x12, Pallas kernels: 150 us -> 62.8 us  [the longest x2 26.5 us: feed_forward(): call(functools.partial(ff_kernel, plan, len(base) > 0), 'feed_forward', (...]
    ppermute x6, waiting for transfers between devices: 40.6 us -> 5.81 us  [along_y(): lax.ppermute(value, AXES, self.perm(lambda z, x, y, c: (z, x, 1 - y, c)))]
    ppermute x2 -> x4, waiting for transfers between devices: 26.4 us -> 4.27 us  [along_x(): lax.ppermute(value, AXES, self.perm(lambda z, x, y, c: (z, 1 - x, y, c)))]
    unnamed x111 -> x82, local copies, waits for them, and re-layouts: 29.2 us -> 9.37 us
    all_to_all x1, waiting for transfers between devices: 19.3 us -> 8.03 us  [per_device(): lax.all_to_all(vectors.reshape(plan.ndev, size), AXES, 0, 0, tiled=True)]
    ppermute x11 -> x21, starting transfers between devices: 3.12 us -> 13.8 us  [core(): lax.ppermute(value, AXES, self.perm(lambda z, x, y, c: (z, x, y, 1 - c)))]
    convert_element_type x6 -> x3, other arithmetic: 11.7 us -> 1.01 us  [the longest x1 0.98 us: per_device(): triple_weight.astype(bf16)]
    ppermute x2, waiting for transfers between devices: 8.39 us -> 0.01 us  [first(): lax.ppermute(value, AXES, self.perm(lambda z, x, y, c: (z, x, 1 - y, c) i...]
  transfers between devices with their start and end apart: 37 -> 52, of which waited for: 17 -> 21; matrix products, arithmetic and copies ran while one was open for 8% -> 7% of each run, Pallas kernels for 40% -> 39%
where the time goes in v2:
time: 272 us; the launch traced here: 271 us
  Pallas kernels  122 us (45%)
  starting transfers between devices  59.9 us (22%)
  waiting for transfers between devices  58.8 us (22%)
  local copies, waits for them, and re-layouts  18 us (7%)
  other arithmetic  11.3 us (4%)
    ppermute x15, waiting for transfers between devices, along_z(): lax.ppermute(value, AXES, self.perm(lambda z, x, y, c: ((z + step) % self...  35.6 us
    pallas_call x2, Pallas kernels, feed_forward(): call(functools.partial(ff_kernel, plan, len(base) > 0), 'feed_forward', (...  26.5 us
    ppermute x15, starting transfers between devices, along_z(): lax.ppermute(value, AXES, self.perm(lambda z, x, y, c: ((z + step) % self...  21 us
    pallas_call x1, Pallas kernels, per_device(): call(functools.partial(attn_bwd_kernel, plan), 'attn_bwd', (steps,), [(sg...  16 us
    ppermute x21, starting transfers between devices, core(): lax.ppermute(value, AXES, self.perm(lambda z, x, y, c: (z, x, y, 1 - c)))  13.8 us
    pallas_call x1, Pallas kernels, per_device(): call(functools.partial(attn_fwd_kernel, plan), 'attn_fwd', (steps,), [(in...  13.1 us
    pallas_call x1, Pallas kernels, per_device(): call(functools.partial(ff_grad_kernel, plan), 'ff_grad', (2,), [(sl, *who...  12.7 us
    unnamed x82, local copies, waits for them, and re-layouts  9.37 us
  transfers between devices with their start and end apart: 52, of which 21 were waited for; matrix products, arithmetic and copies ran while one was open for 7% of the time, Pallas kernels for 39%

profile of v2, /device:TPU:0, one launch (start us, length us, event | category | flops | bytes accessed | tf_op | source)
XLA Modules:
  0.0 271.0 jit_solution(17278593594177091637)
XLA Ops:
  4.4 5.0 %collective-permute-start.3 = (bf16[48,1536]{1,0:T(8,128)(2,1)S(1)}, bf16[48,1536]{1,0:T(8,128)(2,1)S(1)}, u32[]{:S(2)}, u32[]{:S(2)}) collective-permute-start(bf16[48,1536]{1,0:T(8,128)(2,1)S(1)} %bitcast.103), channel_id=1, source_target_pairs={{0,24},{1,25},{2,26},{3,27},{4,28},{5,29},{6,30},{7,31},{8,0},{9,1... | collective-permute-start | bytes 442376 | tf_op jit(solution)/shard_map/ppermute | solution.py:107
  10.7 2.5 collective-permute-start.4
  13.7 11.7 %collective-permute-done.2 = bf16[48,1536]{1,0:T(8,128)(2,1)S(1)} collective-permute-done((bf16[48,1536]{1,0:T(8,128)(2,1)S(1)}, bf16[48,1536]{1,0:T(8,128)(2,1)S(1)}, u32[]{:S(2)}, u32[]{:S(2)}) %collective-permute-start.2) | collective-permute-done | bytes 147488 | tf_op jit(solution)/shard_map/ppermute | solution.py:107
  29.6 2.3 collective-permute-start.6
  36.4 6.3 %collective-permute-done.6 = bf16[96,768]{1,0:T(8,128)(2,1)S(1)} collective-permute-done((bf16[96,768]{1,0:T(8,128)(2,1)S(1)}, bf16[96,768]{1,0:T(8,128)(2,1)S(1)}, u32[]{:S(2)}, u32[]{:S(2)}) %collective-permute-start.6) | collective-permute-done | bytes 147488 | tf_op jit(solution)/shard_map/ppermute | solution.py:107
  47.8 4.0 %collective-permute-done.13 = bf16[96,768]{1,0:T(8,128)(2,1)S(1)} collective-permute-done((bf16[96,768]{1,0:T(8,128)(2,1)S(1)}, bf16[96,768]{1,0:T(8,128)(2,1)S(1)}, u32[]{:S(2)}, u32[]{:S(2)}) %collective-permute-start.13) | collective-permute-done | bytes 147488 | tf_op jit(solution)/shard_map/ppermute | solution.py:107
  51.8 7.3 %collective-permute-done.12 = bf16[96,768]{1,0:T(8,128)(2,1)S(1)} collective-permute-done((bf16[96,768]{1,0:T(8,128)(2,1)S(1)}, bf16[96,768]{1,0:T(8,128)(2,1)S(1)}, u32[]{:S(2)}, u32[]{:S(2)}) %collective-permute-start.12) | collective-permute-done | bytes 147488 | tf_op jit(solution)/shard_map/ppermute | solution.py:107
  59.1 2.6 collective-permute-done.14.refs_1_
  61.7 8.7 %collective-permute-start.16 = (bf16[2,4,48,1536]{3,2,1,0:T(8,128)(2,1)S(1)}, bf16[2,4,48,1536]{3,2,1,0:T(8,128)(2,1)}, u32[]{:S(2)}, u32[]{:S(2)}) collective-permute-start(bf16[2,4,48,1536]{3,2,1,0:T(8,128)(2,1)S(1)} %collective-permute-done.10.w_b), channel_id=1, source_target_pairs={{0,1},{1,0},{2,3},{3,2},{4,5},{5,4},{6,7},{7,6},{8,9},{9,8},{10,11... | collective-permute-start | bytes 3538952 | tf_op jit(solution)/shard_map/ppermute | solution.py:98
  74.3 13.1 %attn_fwd.1 = (bf16[512,768]{1,0:T(8,128)(2,1)}, f32[512,768]{1,0:T(8,128)}, bf16[512,768]{1,0:T(8,128)(2,1)}, bf16[2,512,1152]{2,1,0:T(8,128)(2,1)}, bf16[24,25...) custom-call(s32[6]{0:T(128)} %stack.94.meta, bf16[2048,768]{1,0:T(8,128)(2,1)} %x_ref.3, s32[512,1]{1,0:T(8,128)} %copy.68.segc_ref, ...), custom_call_target="tpu_custom_call" | custom-call | flops 1 | bytes 1 | tf_op jit(solution)/shard_map/attn_fwd/pallas_call | solution.py:842
  91.4 13.4 %feed_forward.2 = (f32[512,768]{1,0:T(8,128)}, bf16[512,768]{1,0:T(8,128)(2,1)}, bf16[2,512,768]{2,1,0:T(8,128)(2,1)}, bf16[2,512,768]{2,1,0:T(8,128)(2,1)}, f32[2,768]{1,0:T(2,128)}) custom-call(s32[6]{0:T(128)} %stack.94.meta, bf16[512,768]{1,0:T(8,128)(2,1)} %get-tuple-element.153.sl_ref.sl_a, bf16[2048,768]{1,0:T(8,128)(2,1)} %cot_ref.5, ...), custom_call_target="tpu_custom_call" | custom-call | flops 1 | bytes 1 | tf_op jit(solution)/shard_map/feed_forward/pallas_call | solution.py:876
  108.6 13.1 %feed_forward.3 = (bf16[512,768]{1,0:T(8,128)(2,1)}, bf16[512,768]{1,0:T(8,128)(2,1)}, bf16[2,512,768]{2,1,0:T(8,128)(2,1)}, bf16[2,512,768]{2,1,0:T(8,128)(2,1)}, f32[2,768]{1,0:T(2,128)}) custom-call(s32[6]{0:T(128)} %stack.94.meta, bf16[512,768]{1,0:T(8,128)(2,1)} %copy-done.6, bf16[2048,768]{1,0:T(8,128)(2,1)} %cot_ref.5, ...), custom_call_target="tpu_custom_call" | custom-call | flops 1 | bytes 1 | tf_op jit(solution)/shard_map/feed_forward/pallas_call | solution.py:876
  121.6 3.0 %collective-permute-done.23.pre_b = bf16[512,768]{1,0:T(8,128)(2,1)S(1)} collective-permute-done((bf16[512,768]{1,0:T(8,128)(2,1)}, bf16[512,768]{1,0:T(8,128)(2,1)S(1)}, u32[]{:S(2)}, u32[]{:S(2)}) %collective-permute-start.23) | collective-permute-done | bytes 786464 | tf_op jit(solution)/shard_map/ppermute | solution.py:104
  126.2 12.7 %ff_grad.1 = (bf16[4,96,768]{2,1,0:T(8,128)(2,1)}, bf16[4,96,768]{2,1,0:T(8,128)(2,1)}, bf16[4,96,768]{2,1,0:T(8,128)(2,1)}, bf16[4,96,768]{2,1,0:T(8,128)(2,1)}...) custom-call(s32[6]{0:T(128)} %stack.94.meta, ...), custom_call_target="tpu_custom_call" | custom-call | flops 1 | bytes 1 | tf_op jit(solution)/shard_map/ff_grad/pallas_call | solution.py:913
  144.5 4.3 %add_lists.1 = (bf16[384,768]{1,0:T(8,128)(2,1)}, bf16[384,768]{1,0:T(8,128)(2,1)}, bf16[384,768]{1,0:T(8,128)(2,1)}, bf16[384,768]{1,0:T(8,128)(2,1)}) custom-call(s32[6]{0:T(128)} %stack.94.meta, bf16[384,768]{1,0:T(8,128)(2,1)} %bitcast.79, bf16[384,768]{1,0:T(8,128)(2,1)} %bitcast.80, bf16[384,768]{1,0:T(8,128)(2,1)} %bitcast.81, ...), custom_call_target="tpu_custom_call" | custom-call | flops 1 | bytes 1 | tf_op jit(solution)/shard_map/add_lists/pallas_call | solution.py:557
  151.5 16.0 %attn_bwd.1 = (bf16[2,512,1152]{2,1,0:T(8,128)(2,1)}, bf16[512,768]{1,0:T(8,128)(2,1)}, f32[512,768]{1,0:T(8,128)}, f32[8,768]{1,0:T(8,128)}, f32[2,768]{1,0:T(2,128)}) custom-call(s32[6]{0:T(128)} %stack.94.meta, f32[512,768]{1,0:T(8,128)} %get-tuple-element.160.sga_ref, bf16[512,768]{1,0:T(8,128)(2,1)} %copy-done.11, ...), custom_call_target="tpu_custom_call" | custom-call | flops 1 | bytes 1 | tf_op jit(solution)/shard_map/attn_bwd/pallas_call | solution.py:945
  167.5 8.2 %attn_grad.1 = (bf16[2,2,48,1536]{3,2,1,0:T(8,128)(2,1)}, bf16[2,2,48,1536]{3,2,1,0:T(8,128)(2,1)}, bf16[2,2,48,1536]{3,2,1,0:T(8,128)(2,1)}, bf16[2,2,48,1536]{...) custom-call(s32[6]{0:T(128)} %stack.94.meta, ...), custom_call_target="tpu_custom_call" | custom-call | flops 1 | bytes 1 | tf_op jit(solution)/shard_map/attn_grad/pallas_call | solution.py:974
  178.7 3.3 %add_by_z.1 = (bf16[2,96,768]{2,1,0:T(8,128)(2,1)}, bf16[2,96,768]{2,1,0:T(8,128)(2,1)}, bf16[2,96,768]{2,1,0:T(8,128)(2,1)}, bf16[2,96,768]{2,1,0:T(8,128)(2,1)}) custom-call(s32[6]{0:T(128)} %stack.94.meta, bf16[4,96,768]{2,1,0:T(8,128)(2,1)} %bitcast.89, bf16[4,96,768]{2,1,0:T(8,128)(2,1)} %copy-done.27, bf16[4,96,768]{2,1,0:T(8,128)(2,1)} %bitcast.90, ...), custom_call_target="tpu_custom_call" | custom-call | flops 1 | bytes 1 | tf_op jit(solution)/shard_map/add_by_z/pallas_call | solution.py:602
  183.5 6.5 %add_first.1 = (bf16[2,4,48,1536]{3,2,1,0:T(8,128)(2,1)}, bf16[2,4,48,1536]{3,2,1,0:T(8,128)(2,1)}) custom-call(s32[6]{0:T(128)} %stack.94.meta, bf16[2,2,48,1536]{3,2,1,0:T(8,128)(2,1)} %get-tuple-element.187.refs_0_, bf16[2,2,48,1536]{3,2,1,0:T(8,128)(2,1)} %get-tuple-element.188.refs_1_, bf16[2,2,48,1536]{3,2,1,0:T(8,128)(2,1)} %get-tuple-element.189.refs_2_, ...), custom_call_target="tpu_custom_call" | custom-call | flops 1 | bytes 1 | tf_op jit(solution)/shard_map/add_first/pallas_call | solution.py:583
  191.8 3.8 %collective-permute-start.38 = (bf16[2,96,768]{2,1,0:T(8,128)(2,1)}, bf16[2,96,768]{2,1,0:T(8,128)(2,1)S(1)}, u32[]{:S(2)}, u32[]{:S(2)}) collective-permute-start(bf16[2,96,768]{2,1,0:T(8,128)(2,1)} %get-tuple-element.212), channel_id=1, source_target_pairs={{0,24},{1,25},{2,26},{3,27},{4,28},{5,29},{6,30},{7,31},{8,0},{9,1... | collective-permute-start | bytes 884744 | tf_op jit(solution)/shard_map/ppermute | solution.py:107
  196.9 8.8 %input_grad.1 = (bf16[512,768]{1,0:T(8,128)(2,1)}, f32[8,768]{1,0:T(8,128)}) custom-call(s32[6]{0:T(128)} %stack.94.meta, bf16[2048,768]{1,0:T(8,128)(2,1)} %x_ref.3, f32[512,768]{1,0:T(8,128)} %get-tuple-element.208.mg_ref, f32[6,768]{1,0:T(8,128)} %refs_16_.1, bf16[2,512,1152]{2,1,0:T(8,128)(2,1)} %get-tuple-element.209.dqkv_ref, ...), custom_call_target="tpu_custom_call" | custom-call | flops 1 | bytes 1 | tf_op jit(solution)/shard_map/input_grad/pallas_call | solution.py:1006
  211.6 3.8 %all-to-all-start = ((f32[32,1,384]{2,1,0:T(1,128)}), f32[32,1,384]{2,1,0:T(1,128)S(1)}, u32[]{:S(2)}, u32[]{:S(2)}) async-start(f32[32,1,384]{2,1,0:T(1,128)} %bitcast.40), calls=%async_computation | async-start | bytes 98304 | tf_op jit(solution)/shard_map/all_to_all | solution.py:1036
  215.4 8.0 %all-to-all-done = f32[32,1,384]{2,1,0:T(1,128)S(1)} async-done(((f32[32,1,384]{2,1,0:T(1,128)}), f32[32,1,384]{2,1,0:T(1,128)S(1)}, u32[]{:S(2)}, u32[]{:S(2)}) %all-to-all-start) | async-done | bytes 49184 | tf_op jit(solution)/shard_map/all_to_all | solution.py:1036
  224.0 2.0 multiply_reduce_fusion
  227.4 3.7 %out_sum.1 = (bf16[512,768]{1,0:T(8,128)(2,1)}, bf16[512,768]{1,0:T(8,128)(2,1)}) custom-call(s32[6]{0:T(128)} %stack.94.meta, bf16[512,768]{1,0:T(8,128)(2,1)} %get-tuple-element.225.pre_a, bf16[512,768]{1,0:T(8,128)(2,1)} %copy-done.18, bf16[512,768]{1,0:T(8,128)(2,1)} %copy-done.16, bf16[512,768]{1,0:T(8,128)(2,1)} %get-tuple-element.193.fed_b, ...), custom_call_target="tpu_custom_call" | custom-call | flops 1 | bytes 1 | tf_op jit(solution)/shard_map/out_sum/pallas_call | solution.py:1047
  234.2 1.9 collective-permute-start.46
  236.1 4.2 %place.2 = bf16[2048,768]{1,0:T(8,128)(2,1)} custom-call(s32[6]{0:T(128)} %stack.94.meta, bf16[512,768]{1,0:T(8,128)(2,1)} %get-tuple-element.226.own, bf16[512,768]{1,0:T(8,128)(2,1)} %get-tuple-element.227.by_y, bf16[512,768]{1,0:T(8,128)(2,1)} %copy-done.15, bf16[512,768]{1,0:T(8,128)(2,1)} %collective-permute-done.42.by_yc), custom_call_target="tpu_custom_call" | custom-call | flops 1 | bytes 1 | tf_op jit(solution)/shard_map/place/pallas_call | solution.py:1067
  240.9 5.2 %collective-permute-done.45.refs_2_ = bf16[48,1536]{1,0:T(8,128)(2,1)S(1)} collective-permute-done((bf16[48,1536]{1,0:T(8,128)(2,1)S(1)}, bf16[48,1536]{1,0:T(8,128)(2,1)S(1)}, u32[]{:S(2)}, u32[]{:S(2)}) %collective-permute-start.45) | collective-permute-done | bytes 147488 | tf_op jit(solution)/shard_map/ppermute | solution.py:107
  247.4 3.5 %total.1 = (f32[48,768]{1,0:T(8,128)}, f32[48,768]{1,0:T(8,128)}, f32[32,1,512]{2,1,0:T(1,128)}) custom-call(s32[6]{0:T(128)} %stack.94.meta, bf16[48,1536]{1,0:T(8,128)(2,1)} %copy-done.2, bf16[48,1536]{1,0:T(8,128)(2,1)} %copy-done.31, bf16[48,1536]{1,0:T(8,128)(2,1)} %copy-done.32, bf16[48,1536]{1,0:T(8,128)(2,1)} %copy-done.33, f32[1,1]{1,0:T(1,128)} %bitcast.41.refs_4_, ...), custom_call_target="tpu_custom_call" | custom-call | flops 1 | bytes 1 | tf_op jit(solution)/shard_map/total/pallas_call | solution.py:1078
  252.3 4.7 %all-to-all-start.1 = ((f32[32,1,512]{2,1,0:T(1,128)}), f32[32,1,512]{2,1,0:T(1,128)S(1)}, u32[]{:S(2)}, u32[]{:S(2)}) async-start(f32[32,1,512]{2,1,0:T(1,128)} %get-tuple-element.235), calls=%async_computation.1 | async-start | bytes 131072 | tf_op jit(solution)/shard_map/all_to_all | solution.py:1096
  260.9 4.2 %place.3 = bf16[2048,768]{1,0:T(8,128)(2,1)} custom-call(s32[6]{0:T(128)} %stack.94.meta, bf16[512,768]{1,0:T(8,128)(2,1)} %get-tuple-element.228.own, bf16[512,768]{1,0:T(8,128)(2,1)} %copy-done.13, bf16[512,768]{1,0:T(8,128)(2,1)} %copy-done.14, bf16[512,768]{1,0:T(8,128)(2,1)} %collective-permute-done.48.by_yc), custom_call_target="tpu_custom_call" | custom-call | flops 1 | bytes 1 | tf_op jit(solution)/shard_map/place/pallas_call | solution.py:1067
  265.7 5.0 %adam.1 = (f32[3,96,192]{2,1,0:T(8,128)}, f32[3,96,192]{2,1,0:T(8,128)}, f32[3,96,192]{2,1,0:T(8,128)}, f32[192,96]{1,0:T(8,128)}, f32[192,96]{1,0:T(8,128)}, /*...) custom-call(s32[6]{0:T(128)} %stack.94.meta, ...), custom_call_target="tpu_custom_call" | custom-call | flops 1 | bytes 1 | tf_op jit(solution)/shard_map/adam/pallas_call | solution.py:1116
  (224 shorter events, 66.5 us)
Async XLA Ops:
  4.4 9.3 %collective-permute-start.3 = (bf16[48,1536]{1,0:T(8,128)(2,1)S(1)}, bf16[48,1536]{1,0:T(8,128)(2,1)S(1)}, u32[]{:S(2)}, u32[]{:S(2)}) collective-permute-start(bf16[48,1536]{1,0:T(8,128)(2,1)S(1)} %bitcast.103), channel_id=1, source_target_pairs={{0,24},{1,25},{2,26},{3,27},{4,28},{5,29},{6,30},{7,31},{8,0},{9,1... | collective-permute-start | bytes 442376 | tf_op jit(solution)/shard_map/ppermute | solution.py:107
  9.4 16.0 %collective-permute-start.2 = (bf16[48,1536]{1,0:T(8,128)(2,1)S(1)}, bf16[48,1536]{1,0:T(8,128)(2,1)S(1)}, u32[]{:S(2)}, u32[]{:S(2)}) collective-permute-start(bf16[48,1536]{1,0:T(8,128)(2,1)S(1)} %bitcast.104), channel_id=1, source_target_pairs={{0,16},{1,17},{2,18},{3,19},{4,20},{5,21},{6,22},{7,23},{8,24},{9,... | collective-permute-start | bytes 442376 | tf_op jit(solution)/shard_map/ppermute | solution.py:107
  9.4 16.0 %collective-permute-start.1 = (bf16[48,1536]{1,0:T(8,128)(2,1)S(1)}, bf16[48,1536]{1,0:T(8,128)(2,1)S(1)}, u32[]{:S(2)}, u32[]{:S(2)}) collective-permute-start(bf16[48,1536]{1,0:T(8,128)(2,1)S(1)} %bitcast.105), channel_id=1, source_target_pairs={{0,8},{1,9},{2,10},{3,11},{4,12},{5,13},{6,14},{7,15},{8,16},{9,17... | collective-permute-start | bytes 442376 | tf_op jit(solution)/shard_map/ppermute | solution.py:107
  10.7 14.8 %collective-permute-start.4 = (bf16[96,768]{1,0:T(8,128)(2,1)S(1)}, bf16[96,768]{1,0:T(8,128)(2,1)S(1)}, u32[]{:S(2)}, u32[]{:S(2)}) collective-permute-start(bf16[96,768]{1,0:T(8,128)(2,1)S(1)} %convert_element_type.32), channel_id=1, source_target_pairs={{0,8},{1,9},{2,10},{3,11},{4,12},{5,13},{6,14},{7,15},{8,16},{9,17... | collective-permute-start | bytes 442376 | tf_op jit(solution)/shard_map/ppermute | solution.py:107
  25.5 10.7 %collective-permute-start.5 = (bf16[4,48,1536]{2,1,0:T(8,128)(2,1)S(1)}, bf16[4,48,1536]{2,1,0:T(8,128)(2,1)S(1)}, u32[]{:S(2)}, u32[]{:S(2)}) collective-permute-start(bf16[4,48,1536]{2,1,0:T(8,128)(2,1)S(1)} %pad_maximum_fusion.1), channel_id=1, source_target_pairs={{0,4},{1,3},{2,6},{3,1},{4,0},{5,7},{6,2},{7,5},{8,12},{9,11},{10,... | collective-permute-start | bytes 1769480 | tf_op jit(solution)/shard_map/ppermute | solution.py:112
  29.6 13.1 %collective-permute-start.6 = (bf16[96,768]{1,0:T(8,128)(2,1)S(1)}, bf16[96,768]{1,0:T(8,128)(2,1)S(1)}, u32[]{:S(2)}, u32[]{:S(2)}) collective-permute-start(bf16[96,768]{1,0:T(8,128)(2,1)S(1)} %convert_element_type.32), channel_id=1, source_target_pairs={{0,16},{1,17},{2,18},{3,19},{4,20},{5,21},{6,22},{7,23},{8,24},{9,... | collective-permute-start | bytes 442376 | tf_op jit(solution)/shard_map/ppermute | solution.py:107
  42.7 19.0 %collective-permute-start.10 = (bf16[2,4,48,1536]{3,2,1,0:T(8,128)(2,1)S(1)}, bf16[2,4,48,1536]{3,2,1,0:T(8,128)(2,1)S(1)}, u32[]{:S(2)}, u32[]{:S(2)}) collective-permute-start(bf16[2,4,48,1536]{3,2,1,0:T(8,128)(2,1)S(1)} %pad_maximum_fusion.w_a), channel_id=1, source_target_pairs={{0,2},{1,5},{2,0},{3,7},{4,6},{5,1},{6,4},{7,3},{8,10},{9,13},{10,... | collective-permute-start | bytes 3538952 | tf_op jit(solution)/shard_map/ppermute | solution.py:119
  45.1 16.6 %collective-permute-start.14 = (bf16[4,96,768]{2,1,0:T(8,128)(2,1)}, bf16[4,96,768]{2,1,0:T(8,128)(2,1)}, u32[]{:S(2)}, u32[]{:S(2)}) collective-permute-start(bf16[4,96,768]{2,1,0:T(8,128)(2,1)} %pad_maximum_fusion.2.refs_0_), channel_id=1, source_target_pairs={{0,4},{1,5},{2,6},{3,7},{4,0},{5,1},{6,2},{7,3},{8,12},{9,13},{10,... | collective-permute-start | bytes 1769480 | tf_op jit(solution)/shard_map/ppermute | solution.py:101
  47.0 12.1 %collective-permute-start.12 = (bf16[96,768]{1,0:T(8,128)(2,1)S(1)}, bf16[96,768]{1,0:T(8,128)(2,1)S(1)}, u32[]{:S(2)}, u32[]{:S(2)}) collective-permute-start(bf16[96,768]{1,0:T(8,128)(2,1)S(1)} %bitcast_convert_fusion), channel_id=1, source_target_pairs={{0,16},{1,17},{2,18},{3,19},{4,20},{5,21},{6,22},{7,23},{8,24},{9,... | collective-permute-start | bytes 442376 | tf_op jit(solution)/shard_map/ppermute | solution.py:107
  47.0 12.1 %collective-permute-start.11 = (bf16[96,768]{1,0:T(8,128)(2,1)S(1)}, bf16[96,768]{1,0:T(8,128)(2,1)S(1)}, u32[]{:S(2)}, u32[]{:S(2)}) collective-permute-start(bf16[96,768]{1,0:T(8,128)(2,1)S(1)} %bitcast_convert_fusion), channel_id=1, source_target_pairs={{0,8},{1,9},{2,10},{3,11},{4,12},{5,13},{6,14},{7,15},{8,16},{9,17... | collective-permute-start | bytes 442376 | tf_op jit(solution)/shard_map/ppermute | solution.py:107
  51.8 21.5 %collective-permute-start.15 = (bf16[2,4,48,1536]{3,2,1,0:T(8,128)(2,1)S(1)}, bf16[2,4,48,1536]{3,2,1,0:T(8,128)(2,1)S(1)}, u32[]{:S(2)}, u32[]{:S(2)}) collective-permute-start(bf16[2,4,48,1536]{3,2,1,0:T(8,128)(2,1)S(1)} %pad_maximum_fusion.w_a), channel_id=1, source_target_pairs={{0,1},{1,0},{2,3},{3,2},{4,5},{5,4},{6,7},{7,6},{8,9},{9,8},{10,11... | collective-permute-start | bytes 3538952 | tf_op jit(solution)/shard_map/ppermute | solution.py:98
  61.7 11.6 %collective-permute-start.16 = (bf16[2,4,48,1536]{3,2,1,0:T(8,128)(2,1)S(1)}, bf16[2,4,48,1536]{3,2,1,0:T(8,128)(2,1)}, u32[]{:S(2)}, u32[]{:S(2)}) collective-permute-start(bf16[2,4,48,1536]{3,2,1,0:T(8,128)(2,1)S(1)} %collective-permute-done.10.w_b), channel_id=1, source_target_pairs={{0,1},{1,0},{2,3},{3,2},{4,5},{5,4},{6,7},{7,6},{8,9},{9,8},{10,11... | collective-permute-start | bytes 3538952 | tf_op jit(solution)/shard_map/ppermute | solution.py:98
  71.3 16.0 %collective-permute-start.19 = (bf16[4,96,768]{2,1,0:T(8,128)(2,1)}, bf16[4,96,768]{2,1,0:T(8,128)(2,1)}, u32[]{:S(2)}, u32[]{:S(2)}) collective-permute-start(bf16[4,96,768]{2,1,0:T(8,128)(2,1)} %pad_maximum_fusion.3.refs_4_), channel_id=1, source_target_pairs={{0,4},{1,5},{2,6},{3,7},{4,0},{5,1},{6,2},{7,3},{8,12},{9,13},{10,... | collective-permute-start | bytes 1769480 | tf_op jit(solution)/shard_map/ppermute | solution.py:101
  71.9 17.6 %collective-permute-start.17 = (bf16[4,96,768]{2,1,0:T(8,128)(2,1)}, bf16[4,96,768]{2,1,0:T(8,128)(2,1)}, u32[]{:S(2)}, u32[]{:S(2)}) collective-permute-start(bf16[4,96,768]{2,1,0:T(8,128)(2,1)} %pad_maximum_fusion.2.refs_0_), channel_id=1, source_target_pairs={{0,1},{1,0},{2,3},{3,2},{4,5},{5,4},{6,7},{7,6},{8,9},{9,8},{10,11... | collective-permute-start | bytes 1769480 | tf_op jit(solution)/shard_map/ppermute | solution.py:98
  71.9 17.6 %collective-permute-start.20 = (bf16[4,96,768]{2,1,0:T(8,128)(2,1)}, bf16[4,96,768]{2,1,0:T(8,128)(2,1)}, u32[]{:S(2)}, u32[]{:S(2)}) collective-permute-start(bf16[4,96,768]{2,1,0:T(8,128)(2,1)} %pad_maximum_fusion.3.refs_4_), channel_id=1, source_target_pairs={{0,1},{1,0},{2,3},{3,2},{4,5},{5,4},{6,7},{7,6},{8,9},{9,8},{10,11... | collective-permute-start | bytes 1769480 | tf_op jit(solution)/shard_map/ppermute | solution.py:98
  88.0 19.7 %collective-permute-start.22 = (bf16[512,768]{1,0:T(8,128)(2,1)}, bf16[512,768]{1,0:T(8,128)(2,1)S(1)}, u32[]{:S(2)}, u32[]{:S(2)}) collective-permute-start(bf16[512,768]{1,0:T(8,128)(2,1)} %get-tuple-element.153.sl_ref.sl_a), channel_id=1, source_target_pairs={{0,2},{1,3},{2,0},{3,1},{4,6},{5,7},{6,4},{7,5},{8,10},{9,11},{10,... | collective-permute-start | bytes 2359304 | tf_op jit(solution)/shard_map/ppermute | solution.py:104
  104.8 19.9 %collective-permute-start.23 = (bf16[512,768]{1,0:T(8,128)(2,1)}, bf16[512,768]{1,0:T(8,128)(2,1)S(1)}, u32[]{:S(2)}, u32[]{:S(2)}) collective-permute-start(bf16[512,768]{1,0:T(8,128)(2,1)} %get-tuple-element.225.pre_a), channel_id=1, source_target_pairs={{0,2},{1,3},{2,0},{3,1},{4,6},{5,7},{6,4},{7,5},{8,10},{9,11},{10,... | collective-permute-start | bytes 2359304 | tf_op jit(solution)/shard_map/ppermute | solution.py:104
  124.7 24.2 %collective-permute-start.24 = (bf16[512,768]{1,0:T(8,128)(2,1)}, bf16[512,768]{1,0:T(8,128)(2,1)S(1)}, u32[]{:S(2)}, u32[]{:S(2)}) collective-permute-start(bf16[512,768]{1,0:T(8,128)(2,1)} %get-tuple-element.163), channel_id=1, source_target_pairs={{0,2},{1,3},{2,0},{3,1},{4,6},{5,7},{6,4},{7,5},{8,10},{9,11},{10,... | collective-permute-start | bytes 2359304 | tf_op jit(solution)/shard_map/ppermute | solution.py:104
  148.8 28.5 %collective-permute-start.31 = (bf16[512,768]{1,0:T(8,128)(2,1)S(1)}, bf16[512,768]{1,0:T(8,128)(2,1)S(1)}, u32[]{:S(2)}, u32[]{:S(2)}) collective-permute-start(bf16[512,768]{1,0:T(8,128)(2,1)S(1)} %copy-done.17), channel_id=1, source_target_pairs={{0,2},{1,3},{2,0},{3,1},{4,6},{5,7},{6,4},{7,5},{8,10},{9,11},{10,... | collective-permute-start | bytes 2359304 | tf_op jit(solution)/shard_map/ppermute | solution.py:104
  149.4 18.1 %collective-permute-start.29 = (bf16[4,96,768]{2,1,0:T(8,128)(2,1)}, bf16[4,96,768]{2,1,0:T(8,128)(2,1)S(1)}, u32[]{:S(2)}, u32[]{:S(2)}) collective-permute-start(bf16[4,96,768]{2,1,0:T(8,128)(2,1)} %bitcast.107), channel_id=1, source_target_pairs={{0,4},{1,5},{2,6},{3,7},{4,0},{5,1},{6,2},{7,3},{8,12},{9,13},{10,... | collective-permute-start | bytes 1769480 | tf_op jit(solution)/shard_map/ppermute | solution.py:101
  150.9 26.4 %collective-permute-start.30 = (bf16[4,96,768]{2,1,0:T(8,128)(2,1)}, bf16[4,96,768]{2,1,0:T(8,128)(2,1)S(1)}, u32[]{:S(2)}, u32[]{:S(2)}) collective-permute-start(bf16[4,96,768]{2,1,0:T(8,128)(2,1)} %bitcast.106), channel_id=1, source_target_pairs={{0,4},{1,5},{2,6},{3,7},{4,0},{5,1},{6,2},{7,3},{8,12},{9,13},{10,... | collective-permute-start | bytes 1769480 | tf_op jit(solution)/shard_map/ppermute | solution.py:101
  190.0 17.2 %collective-permute-start.36 = (bf16[2,4,48,1536]{3,2,1,0:T(8,128)(2,1)}, bf16[2,4,48,1536]{3,2,1,0:T(8,128)(2,1)S(1)}, u32[]{:S(2)}, u32[]{:S(2)}) collective-permute-start(bf16[2,4,48,1536]{3,2,1,0:T(8,128)(2,1)} %get-tuple-element.207), channel_id=1, source_target_pairs={{0,2},{1,5},{2,0},{3,7},{4,6},{5,1},{6,4},{7,3},{8,10},{9,13},{10,... | collective-permute-start | bytes 3538952 | tf_op jit(solution)/shard_map/ppermute | solution.py:119
  191.8 15.4 %collective-permute-start.37 = (bf16[2,96,768]{2,1,0:T(8,128)(2,1)}, bf16[2,96,768]{2,1,0:T(8,128)(2,1)}, u32[]{:S(2)}, u32[]{:S(2)}) collective-permute-start(bf16[2,96,768]{2,1,0:T(8,128)(2,1)} %get-tuple-element.211), channel_id=1, source_target_pairs={{0,8},{1,9},{2,10},{3,11},{4,12},{5,13},{6,14},{7,15},{8,16},{9,17... | collective-permute-start | bytes 884744 | tf_op jit(solution)/shard_map/ppermute | solution.py:107
  191.8 15.3 %collective-permute-start.38 = (bf16[2,96,768]{2,1,0:T(8,128)(2,1)}, bf16[2,96,768]{2,1,0:T(8,128)(2,1)S(1)}, u32[]{:S(2)}, u32[]{:S(2)}) collective-permute-start(bf16[2,96,768]{2,1,0:T(8,128)(2,1)} %get-tuple-element.212), channel_id=1, source_target_pairs={{0,24},{1,25},{2,26},{3,27},{4,28},{5,29},{6,30},{7,31},{8,0},{9,1... | collective-permute-start | bytes 884744 | tf_op jit(solution)/shard_map/ppermute | solution.py:107
  207.1 16.9 %collective-permute-start.40 = (bf16[2,96,768]{2,1,0:T(8,128)(2,1)}, bf16[2,96,768]{2,1,0:T(8,128)(2,1)}, u32[]{:S(2)}, u32[]{:S(2)}) collective-permute-start(bf16[2,96,768]{2,1,0:T(8,128)(2,1)} %get-tuple-element.222), channel_id=1, source_target_pairs={{0,16},{1,17},{2,18},{3,19},{4,20},{5,21},{6,22},{7,23},{8,24},{9,... | collective-permute-start | bytes 884744 | tf_op jit(solution)/shard_map/ppermute | solution.py:107
  208.7 17.4 %collective-permute-start.39 = (bf16[4,48,1536]{2,1,0:T(8,128)(2,1)S(1)}, bf16[4,48,1536]{2,1,0:T(8,128)(2,1)S(1)}, u32[]{:S(2)}, u32[]{:S(2)}) collective-permute-start(bf16[4,48,1536]{2,1,0:T(8,128)(2,1)S(1)} %bitcast.74), channel_id=1, source_target_pairs={{0,4},{1,3},{2,6},{3,1},{4,0},{5,7},{6,2},{7,5},{8,12},{9,11},{10,... | collective-permute-start | bytes 1769480 | tf_op jit(solution)/shard_map/ppermute | solution.py:112
  211.6 11.8 %all-to-all-start = ((f32[32,1,384]{2,1,0:T(1,128)}), f32[32,1,384]{2,1,0:T(1,128)S(1)}, u32[]{:S(2)}, u32[]{:S(2)}) async-start(f32[32,1,384]{2,1,0:T(1,128)} %bitcast.40), calls=%async_computation | async-start | bytes 98304 | tf_op jit(solution)/shard_map/all_to_all | solution.py:1036
  231.6 25.4 %collective-permute-start.43 = (bf16[512,768]{1,0:T(8,128)(2,1)S(1)}, bf16[512,768]{1,0:T(8,128)(2,1)S(1)}, u32[]{:S(2)}, u32[]{:S(2)}) collective-permute-start(bf16[512,768]{1,0:T(8,128)(2,1)S(1)} %copy-done.12), channel_id=1, source_target_pairs={{0,2},{1,3},{2,0},{3,1},{4,6},{5,7},{6,4},{7,5},{8,10},{9,11},{10,... | collective-permute-start | bytes 2359304 | tf_op jit(solution)/shard_map/ppermute | solution.py:104
  232.2 8.6 %collective-permute-start.44 = (bf16[48,1536]{1,0:T(8,128)(2,1)S(1)}, bf16[48,1536]{1,0:T(8,128)(2,1)S(1)}, u32[]{:S(2)}, u32[]{:S(2)}) collective-permute-start(bf16[48,1536]{1,0:T(8,128)(2,1)S(1)} %get-tuple-element.229), channel_id=1, source_target_pairs={{0,8},{1,9},{2,10},{3,11},{4,12},{5,13},{6,14},{7,15},{8,16},{9,17... | collective-permute-start | bytes 442376 | tf_op jit(solution)/shard_map/ppermute | solution.py:107
  232.7 13.4 %collective-permute-start.45 = (bf16[48,1536]{1,0:T(8,128)(2,1)S(1)}, bf16[48,1536]{1,0:T(8,128)(2,1)S(1)}, u32[]{:S(2)}, u32[]{:S(2)}) collective-permute-start(bf16[48,1536]{1,0:T(8,128)(2,1)S(1)} %get-tuple-element.230), channel_id=1, source_target_pairs={{0,16},{1,17},{2,18},{3,19},{4,20},{5,21},{6,22},{7,23},{8,24},{9,... | collective-permute-start | bytes 442376 | tf_op jit(solution)/shard_map/ppermute | solution.py:107
  234.2 11.9 %collective-permute-start.46 = (bf16[48,1536]{1,0:T(8,128)(2,1)S(1)}, bf16[48,1536]{1,0:T(8,128)(2,1)S(1)}, u32[]{:S(2)}, u32[]{:S(2)}) collective-permute-start(bf16[48,1536]{1,0:T(8,128)(2,1)S(1)} %get-tuple-element.231), channel_id=1, source_target_pairs={{0,24},{1,25},{2,26},{3,27},{4,28},{5,29},{6,30},{7,31},{8,0},{9,1... | collective-permute-start | bytes 442376 | tf_op jit(solution)/shard_map/ppermute | solution.py:107
  252.3 12.8 %all-to-all-start.1 = ((f32[32,1,512]{2,1,0:T(1,128)}), f32[32,1,512]{2,1,0:T(1,128)S(1)}, u32[]{:S(2)}, u32[]{:S(2)}) async-start(f32[32,1,512]{2,1,0:T(1,128)} %get-tuple-element.235), calls=%async_computation.1 | async-start | bytes 131072 | tf_op jit(solution)/shard_map/all_to_all | solution.py:1096
  (61 other events, 331.8 us)

commit v3 on v2

v3 whole, which is shorter than its diff:
```python
import functools

import jax
import jax.numpy as jnp
from jax import lax
from jax.experimental import pallas as pl
from jax.experimental.pallas import tpu as pltpu
from jax.sharding import PartitionSpec as P

HD = 64
STEP = 5
EPS_NORM = 1e-06
BETA = 0.5
LR_MATRIX = 0.03
LR_VECTOR = 0.2
DECAY = 0.1
ADAM_EPS = 1e-08
CLIP = 1.0
NEG = -1e30
GELU_C = 0.7978845608028654
GELU_K = 0.044715

f32 = jnp.float32
bf16 = jnp.bfloat16
AXES = ("dp", "mp")
LANES = 128
CHUNK = 256
MIB = 1 << 20


def mm(left, right):
    return lax.dot_general(left, right, (((1,), (0,)), ((), ())), preferred_element_type=f32)


def mm_nt(left, right):
    return lax.dot_general(left, right, (((1,), (1,)), ((), ())), preferred_element_type=f32)


def mm_tn(left, right):
    return lax.dot_general(left, right, (((0,), (0,)), ((), ())), preferred_element_type=f32)


def norm_stats(rows_in):
    centred = rows_in - jnp.mean(rows_in, axis=-1, keepdims=True)
    scaled = lax.rsqrt(jnp.mean(centred * centred, axis=-1, keepdims=True) + EPS_NORM)
    return centred * scaled, scaled


def norm_backward(upstream, normal_rows, scaled, gain_row):
    gained = upstream * gain_row
    mean_one = jnp.mean(gained, axis=-1, keepdims=True)
    mean_two = jnp.mean(gained * normal_rows, axis=-1, keepdims=True)
    return scaled * (gained - mean_one - normal_rows * mean_two)


def lane_low(shape):
    return lax.broadcasted_iota(jnp.int32, shape, 1) % LANES < HD


def split_heads(block):
    low = lane_low(block.shape)
    zero = jnp.zeros_like(block)
    return jnp.concatenate([jnp.where(low, block, zero), jnp.where(low, zero, block)], axis=0)


def join_heads(stacked):
    half = stacked.shape[0] // 2
    low = lane_low((half, stacked.shape[1]))
    return jnp.where(low, stacked[:half], stacked[half:])


class Plan:
    def __init__(self, ndp, nmp, width, hidden):
        assert ndp % 2 == 0 and nmp == 4
        self.ndev = ndp * nmp
        self.nz = ndp // 2
        self.rows = width // ndp
        self.half = self.rows // 2
        self.width = width
        self.cols = width // 2
        self.part = hidden // nmp
        self.direct = self.half % 16 == 0

    def perm(self, move):
        pairs = []
        for z in range(self.nz):
            for x in range(2):
                for y in range(2):
                    for c in range(2):
                        there = move(z, x, y, c)
                        pairs.append((self.index(z, x, y, c), self.index(*there)))
        return pairs

    def index(self, z, x, y, c):
        return (2 * z + x) * 4 + 2 * y + c

    def core(self, value):
        return lax.ppermute(value, AXES, self.perm(lambda z, x, y, c: (z, x, y, 1 - c)))

    def along_x(self, value):
        return lax.ppermute(value, AXES, self.perm(lambda z, x, y, c: (z, 1 - x, y, c)))

    def along_y(self, value):
        return lax.ppermute(value, AXES, self.perm(lambda z, x, y, c: (z, x, 1 - y, c)))

    def along_z(self, value, step):
        return lax.ppermute(
            value, AXES, self.perm(lambda z, x, y, c: ((z + step) % self.nz, x, y, c))
        )

    def first(self, value):
        return lax.ppermute(
            value,
            AXES,
            self.perm(lambda z, x, y, c: (z, x, 1 - y, c) if c else (z, 1 - x, y, c)),
        )

    def second(self, value):
        return lax.ppermute(
            value,
            AXES,
            self.perm(lambda z, x, y, c: (z, 1 - x, y, c) if c else (z, x, 1 - y, c)),
        )


def piece_spot(plan, meta, r, fy, fx, k, sign):
    z, x, y, c = meta[1], meta[2], meta[3], meta[4]
    cc = jnp.bitwise_xor(c, r)
    zz = lax.rem(z + sign * k + plan.nz, plan.nz)
    xx = jnp.bitwise_xor(x, fx)
    yy = jnp.bitwise_xor(y, fy)
    return cc, zz, xx, yy


def attn_weight_copies(plan, meta, srcs, w, sem, lanes):
    if not plan.direct:
        return [pltpu.make_async_copy(srcs[0].at[:, :, lanes], w, sem.at[0])]
    copies = []
    for s2 in range(2):
        for r in range(2):
            for s1 in range(2):
                for k in range(plan.nz):
                    cc = jnp.bitwise_xor(meta[4], r)
                    fx = jnp.where(cc == 0, s1, s2)
                    fy = jnp.where(cc == 0, s2, s1)
                    _, zz, xx, yy = piece_spot(plan, meta, r, fy, fx, k, -1)
                    row = pl.multiple_of((zz * 2 + xx) * plan.rows + cc * plan.half, 16)
                    copies.append(
                        pltpu.make_async_copy(
                            srcs[2 * r + s2].at[s1, k, :, lanes],
                            w.at[yy, pl.ds(row, plan.half), :],
                            sem.at[len(copies)],
                        )
                    )
    return copies


def token_copy(src, block, dst, sem):
    count = dst.shape[0]
    return pltpu.make_async_copy(
        src.at[pl.ds(pl.multiple_of(block * count, 16), count), :], dst, sem
    )


def chunks(count, body):
    def step(i, carry):
        body(i, pl.ds(pl.multiple_of(i * CHUNK, CHUNK), CHUNK))
        return carry

    lax.fori_loop(0, count // CHUNK, step, 0)


def lanes_of(base, b, cols, p):
    return slice(base + b * cols + p * LANES, base + b * cols + (p + 1) * LANES)


def attn_fwd_kernel(plan, meta, x_all, segc_ref, segr_ref, np_ref, pb_ref, *refs):
    srcs, refs = refs[:4], refs[4:]
    sl_ref, mid_ref, fl_ref, qkv_ref, p_ref, ctx_ref, w, sl_buf, x_ref, sem, sem_x = refs
    cols = plan.cols
    count = x_ref.shape[0]
    copies = attn_weight_copies(plan, meta, srcs, w, sem, slice(None))
    load = token_copy(x_all, meta[0], x_ref, sem_x.at[0])
    load.start()
    for copy in copies:
        copy.start()
    load.wait()

    def first(i, at):
        normal, _ = norm_stats(x_ref[at, :].astype(f32))
        fl_ref[at, :] = (normal * np_ref[0:1, :] + np_ref[1:2, :]).astype(bf16)

    chunks(count, first)
    for copy in copies:
        copy.wait()
    tiles = CHUNK // LANES
    pairs = cols // LANES

    def second(i, at):
        for y in range(2):
            for part in range(3):
                lanes = slice(part * cols, (part + 1) * cols)
                got = mm(fl_ref[at, :], w[y, :, lanes])
                if part != 1:
                    got = got + pb_ref[part // 2 : part // 2 + 1, y * cols : (y + 1) * cols]
                qkv_ref[y, at, lanes] = got.astype(bf16)
        for t in range(tiles):
            tile = i * tiles + t
            tok = pl.ds(pl.multiple_of(tile * LANES, LANES), LANES)
            same = segc_ref[tok, :] == segr_ref[pl.ds(tile, 1), :]
            same = jnp.concatenate([same] * (2 * pairs), axis=0)
            for y in range(2):
                s = jnp.concatenate(
                    [
                        mm_nt(
                            split_heads(qkv_ref[y, tok, lanes_of(0, 0, cols, p)]),
                            qkv_ref[y, tok, lanes_of(0, 1, cols, p)],
                        )
                        for p in range(pairs)
                    ],
                    axis=0,
                )
                s = jnp.where(same, s * HD**-0.5, NEG)
                e = jnp.exp(s - jnp.max(s, axis=-1, keepdims=True))
                probs = (e * (1.0 / jnp.sum(e, axis=-1, keepdims=True))).astype(bf16)
                p_ref[tile * 2 + y] = probs
                for p in range(pairs):
                    own = probs[p * 2 * LANES : (p + 1) * 2 * LANES]
                    ctx = join_heads(mm(own, qkv_ref[y, tok, lanes_of(0, 2, cols, p)]))
                    ctx_ref[tok, lanes_of(y * cols, 0, cols, p)] = ctx.astype(bf16)
        attended = mm_nt(ctx_ref[at, 0:cols], w[0, :, 3 * cols :])
        attended = attended + mm_nt(ctx_ref[at, cols:], w[1, :, 3 * cols :])
        middle = x_ref[at, :].astype(f32) + attended + np_ref[4:5, :]
        mid_ref[at, :] = middle
        normal, _ = norm_stats(middle)
        sl = (normal * np_ref[2:3, :] + np_ref[3:4, :]).astype(bf16)
        sl_buf[at, :] = sl
        pltpu.make_async_copy(sl_buf.at[at, :], sl_ref.at[at, :], sem_x.at[i]).start()

    chunks(count, second)
    for i in range(count // CHUNK):
        at = pl.ds(i * CHUNK, CHUNK)
        pltpu.make_async_copy(sl_buf.at[at, :], sl_ref.at[at, :], sem_x.at[i]).wait()


def ff_weight_copies(plan, meta, srcs, w, sem, r, e):
    src = srcs[4 * e + 2 * r : 4 * e + 2 * r + 2]
    if not plan.direct:
        return [pltpu.make_async_copy(src[0], w.at[e, r], sem.at[r, e, 0])]
    copies = []
    for fx in range(2):
        for k in range(plan.nz):
            _, zz, xx, _ = piece_spot(plan, meta, r, 0, fx, k, -1)
            row = pl.multiple_of((zz * 2 + xx) * plan.rows, 16)
            copies.append(
                pltpu.make_async_copy(
                    src[fx].at[k],
                    w.at[e, r, pl.ds(row, plan.rows), :],
                    sem.at[r, e, len(copies)],
                )
            )
    return copies


def ff_kernel(plan, own, meta, sl_ref, cot_all, hb_ref, *refs):
    copies = []
    if own:
        w, mid_ref, sg_ref, fed_ref, act_ref, hg_ref, gh_ref, cot_ref, buf, sem_x = refs
    else:
        *srcs, sg_ref, fed_ref, act_ref, hg_ref, gh_ref, cot_ref, w, sg_buf, buf, sem, sem_x = refs
        for r in range(2):
            for e in range(2):
                copies = copies + ff_weight_copies(plan, meta, srcs, w, sem, r, e)
    for copy in copies:
        copy.start()
    count = cot_ref.shape[0]
    load = token_copy(cot_all, meta[0 if own else 5], cot_ref, sem_x.at[0])
    load.start()
    gh_ref[...] = jnp.zeros_like(gh_ref)
    load.wait()
    for copy in copies:
        copy.wait()

    def body(i, at):
        sl = sl_ref[at, :]
        cot = cot_ref[at, :]
        total = [None, None]
        for r in range(2):
            h = mm(sl, w[0, r]) + hb_ref[r : r + 1, :]
            grown = mm(cot, w[1, r])
            square = h * h
            half = 0.5 * jnp.tanh(h * (GELU_C + (GELU_C * GELU_K) * square)) + 0.5
            act = h * half
            slope = half + (act - act * half) * (2.0 * GELU_C + (6.0 * GELU_C * GELU_K) * square)
            grown = grown * slope
            gh_ref[r : r + 1, :] += jnp.sum(grown, axis=0, keepdims=True)
            act = act.astype(bf16)
            grown = grown.astype(bf16)
            act_ref[r, at, :] = act
            hg_ref[r, at, :] = grown
            for e, left in enumerate((grown, act)):
                got = mm_nt(left, w[e, r])
                total[e] = got if total[e] is None else total[e] + got
        fed = total[1] + mid_ref[at, :] if own else total[1]
        buf[at, :] = fed.astype(bf16)
        pltpu.make_async_copy(buf.at[at, :], fed_ref.at[at, :], sem_x.at[i]).start()
        if own:
            sg_ref[at, :] = total[0].astype(bf16)
        else:
            sg_buf[at, :] = total[0].astype(bf16)
            pltpu.make_async_copy(
                sg_buf.at[at, :], sg_ref.at[at, :], sem_x.at[count // CHUNK + i]
            ).start()

    chunks(count, body)
    for i in range(count // CHUNK):
        at = pl.ds(i * CHUNK, CHUNK)
        pltpu.make_async_copy(buf.at[at, :], fed_ref.at[at, :], sem_x.at[i]).wait()
        if not own:
            pltpu.make_async_copy(
                sg_buf.at[at, :], sg_ref.at[at, :], sem_x.at[count // CHUNK + i]
            ).wait()


def ff_grad_copies(plan, meta, buf, outs, sem, r):
    if not plan.direct:
        return [
            pltpu.make_async_copy(buf.at[r, e], outs[2 * r + e], sem.at[r, e]) for e in range(2)
        ]
    copies = []
    for e in range(2):
        for fx in range(2):
            for k in range(plan.nz):
                _, zz, xx, _ = piece_spot(plan, meta, r, 0, fx, k, 1)
                row = pl.multiple_of((zz * 2 + xx) * plan.rows, 16)
                copies.append(
                    pltpu.make_async_copy(
                        buf.at[r, e, pl.ds(row, plan.rows), :],
                        outs[4 * r + 2 * e + fx].at[k],
                        sem.at[r, len(copies)],
                    )
                )
    return copies


def ff_grad_kernel(plan, meta, sl_a, sl_b, cot_a, cot_b, act_a, act_b, hg_a, hg_b, *rest):
    *outs, buf, sem = rest
    for r in (1, 0):
        for e, (a, b, one, two) in enumerate(
            ((sl_a, sl_b, hg_a, hg_b), (cot_a, cot_b, act_a, act_b))
        ):
            buf[r, e] = (mm_tn(a[...], one[r]) + mm_tn(b[...], two[r])).astype(bf16)
        for copy in ff_grad_copies(plan, meta, buf, outs, sem, r):
            copy.start()
    for r in range(2):
        for copy in ff_grad_copies(plan, meta, buf, outs, sem, r):
            copy.wait()


def attn_bwd_kernel(
    plan,
    meta,
    sga_ref,
    sgb_ref,
    mid_ref,
    cot_ref,
    np_ref,
    qkv_ref,
    p_ref,
    w,
    dqkv_ref,
    ml_ref,
    mg_ref,
    vec_ref,
    pair_ref,
):
    cols = plan.cols
    tiles = CHUNK // LANES
    pairs = cols // LANES
    vec_ref[...] = jnp.zeros_like(vec_ref)
    pair_ref[...] = jnp.zeros_like(pair_ref)

    def body(i, at):
        sg = sga_ref[at, :].astype(f32) + sgb_ref[at, :].astype(f32)
        cot = cot_ref[at, :].astype(f32)
        normal, scaled = norm_stats(mid_ref[at, :])
        mg = cot + norm_backward(sg, normal, scaled, np_ref[2:3, :])
        mg_ref[at, :] = mg
        ml = mg.astype(bf16)
        ml_ref[at, :] = ml
        vec_ref[0:1, :] += jnp.sum(sg * normal, axis=0, keepdims=True)
        vec_ref[1:2, :] += jnp.sum(sg, axis=0, keepdims=True)
        vec_ref[2:3, :] += jnp.sum(mg, axis=0, keepdims=True)
        vec_ref[3:4, :] += jnp.sum(cot, axis=0, keepdims=True)
        for y in range(2):
            dctx = mm(ml, w[y, :, 3 * cols :]).astype(bf16)
            for t in range(tiles):
                tile = i * tiles + t
                tok = pl.ds(pl.multiple_of(tile * LANES, LANES), LANES)
                dcs = [
                    split_heads(dctx[t * LANES : (t + 1) * LANES, lanes_of(0, 0, cols, p)])
                    for p in range(pairs)
                ]
                low = p_ref[tile * 2 + y]
                probs = low.astype(f32)
                dp = jnp.concatenate(
                    [
                        mm_nt(dcs[p], qkv_ref[y, tok, lanes_of(0, 2, cols, p)])
                        for p in range(pairs)
                    ],
                    axis=0,
                )
                inner = jnp.sum(dp * probs, axis=-1, keepdims=True)
                ds = (probs * (dp - inner) * HD**-0.5).astype(bf16)
                for p in range(pairs):
                    at_q, at_k, at_v = (lanes_of(0, b, cols, p) for b in range(3))
                    rows = slice(p * 2 * LANES, (p + 1) * 2 * LANES)
                    qs = split_heads(qkv_ref[y, tok, at_q])
                    dq = join_heads(mm(ds[rows], qkv_ref[y, tok, at_k])).astype(bf16)
                    dqkv_ref[y, tok, at_q] = dq
                    dqkv_ref[y, tok, at_k] = mm_tn(ds[rows], qs).astype(bf16)
                    dqkv_ref[y, tok, at_v] = mm_tn(low[rows], dcs[p]).astype(bf16)
            for b in (0, 2):
                lanes = slice(b * cols, (b + 1) * cols)
                pair_ref[b // 2 : b // 2 + 1, y * cols : (y + 1) * cols] += jnp.sum(
                    dqkv_ref[y, at, lanes].astype(f32), axis=0, keepdims=True
                )

    chunks(sga_ref.shape[0], body)


def attn_grad_pieces(plan, meta, buf, outs, sem, fy):
    if not plan.direct:
        yy = jnp.bitwise_xor(meta[3], fy)
        return [pltpu.make_async_copy(buf.at[fy], outs[0].at[yy], sem.at[fy, 0])]
    copies = []
    for r in range(2):
        for fx in range(2):
            for k in range(plan.nz):
                cc, zz, xx, _ = piece_spot(plan, meta, r, fy, fx, k, 1)
                s1 = jnp.where(cc == 0, fx, fy)
                s2 = jnp.where(cc == 0, fy, fx)
                row = pl.multiple_of((zz * 2 + xx) * plan.rows + cc * plan.half, 16)
                out = outs[r * plan.nz + k]
                if r == 0:
                    out[s2, s1] = buf[fy, pl.ds(row, plan.half), :]
                else:
                    copies.append(
                        pltpu.make_async_copy(
                            buf.at[fy, pl.ds(row, plan.half), :],
                            out.at[s2, s1],
                            sem.at[fy, len(copies)],
                        )
                    )
    return copies


def attn_grad_kernel(plan, meta, fl_ref, ml_ref, dqkv_ref, ctx_ref, *rest):
    *outs, buf, sem = rest
    cols = plan.cols
    copies = []
    for fy in range(2):
        y = jnp.bitwise_xor(meta[3], fy)
        lanes = pl.ds(pl.multiple_of(y * cols, LANES), cols)
        buf[fy, :, : 3 * cols] = mm_tn(fl_ref[...], dqkv_ref[y]).astype(bf16)
        buf[fy, :, 3 * cols :] = mm_tn(ml_ref[...], ctx_ref[:, lanes]).astype(bf16)
        some = attn_grad_pieces(plan, meta, buf, outs, sem, fy)
        for copy in some:
            copy.start()
        copies = copies + some
    for copy in copies:
        copy.wait()


def input_grad_kernel(
    plan, meta, x_all, mg_ref, np_ref, dqkv_ref, w, ig_ref, vec_ref, x_ref, buf, sem
):
    cols = plan.cols
    count = x_ref.shape[0]
    load = token_copy(x_all, meta[0], x_ref, sem.at[0])
    load.start()
    vec_ref[...] = jnp.zeros_like(vec_ref)
    load.wait()

    def body(i, at):
        normal, scaled = norm_stats(x_ref[at, :].astype(f32))
        fg = mm_nt(dqkv_ref[0, at, :], w[0, :, : 3 * cols])
        fg = fg + mm_nt(dqkv_ref[1, at, :], w[1, :, : 3 * cols])
        vec_ref[0:1, :] += jnp.sum(fg * normal, axis=0, keepdims=True)
        vec_ref[1:2, :] += jnp.sum(fg, axis=0, keepdims=True)
        ig = mg_ref[at, :] + norm_backward(fg, normal, scaled, np_ref[0:1, :])
        buf[at, :] = ig.astype(bf16)
        pltpu.make_async_copy(buf.at[at, :], ig_ref.at[at, :], sem.at[i]).start()

    chunks(count, body)
    for i in range(count // CHUNK):
        at = pl.ds(i * CHUNK, CHUNK)
        pltpu.make_async_copy(buf.at[at, :], ig_ref.at[at, :], sem.at[i]).wait()


def add_kernel(meta, left, right, *outs):
    for i, out in enumerate(outs):
        out[...] = (left[i].astype(f32) + right[i].astype(f32)).astype(out.dtype)


def add_parts(meta, left, right):
    n, size = left.shape[0], left.shape[-1]
    shape = left.shape[1:]
    left, right = left.reshape(n, -1, size), right.reshape(n, -1, size)
    length = left.shape[1]
    blocks = 4 if length % 64 == 0 and length >= 384 else 1
    step = length // blocks
    outs = call(
        add_kernel,
        "add_parts",
        (blocks,),
        [(v, (n, step, size), lambda i, m: (0, i, 0)) for v in (left, right)],
        [(jax.ShapeDtypeStruct((length, size), bf16), (step, size), lambda i, m: (i, 0))] * n,
        [],
    )(meta, left, right)
    return [v.reshape(shape) for v in outs]


def sums_kernel(meta, *refs):
    n = len(refs) // 3
    for left, right, out in zip(refs[:n], refs[n : 2 * n], refs[2 * n :]):
        out[...] = (left[...].astype(f32) + right[...].astype(f32)).astype(out.dtype)


def add_lists(meta, left, right):
    n, shape = len(left), left[0].shape
    flat = [v.reshape(-1, shape[-1]) for v in (*left, *right)]
    length, size = flat[0].shape
    blocks = 2 if length % 32 == 0 and length >= 384 else 1
    block = ((length // blocks, size), lambda i, m: (i, 0))
    outs = call(
        sums_kernel,
        "add_lists",
        (blocks,),
        [(v, *block) for v in flat],
        [(jax.ShapeDtypeStruct((length, size), bf16), *block)] * n,
        [],
    )(meta, *flat)
    return [v.reshape(shape) for v in outs]


def first_kernel(n, meta, *refs):
    left, right, (keep, send, got, buf, sem) = refs[:n], refs[n : 2 * n], refs[2 * n :]
    loads = [pltpu.make_async_copy(right[k], got.at[k], sem.at[k]) for k in range(n)]
    for load in loads:
        load.start()
    for k in range(n):
        loads[k].wait()
        for s, out in enumerate((keep, buf)):
            for i in range(out.shape[0]):
                out[i, k] = (left[k][s, i].astype(f32) + got[k, s, i].astype(f32)).astype(bf16)
    store = pltpu.make_async_copy(buf, send, sem.at[n])
    store.start()
    store.wait()


def add_first(meta, left, right):
    n, shape = len(left), left[0].shape[1:]
    out = jax.ShapeDtypeStruct((shape[0], n, *shape[1:]), bf16)
    return local_call(
        meta,
        functools.partial(first_kernel, n),
        "add_first",
        [(v, True) for v in left] + [(v, False) for v in right],
        [(out, True), (out, False)],
        [
            pltpu.VMEM((n, 2, *shape), bf16),
            pltpu.VMEM(out.shape, bf16),
            pltpu.SemaphoreType.DMA((n + 1,)),
        ],
    )


def vectors_kernel(plan, meta, one, two, pair, near, far, out, buf, sem):
    buf[...] = jnp.zeros_like(buf)
    per = buf.shape[2] // LANES
    lines = plan.width // LANES

    def put(start, row):
        for q in range(row.shape[1] // LANES):
            b = start + q
            at = slice(b % per * LANES, (b % per + 1) * LANES)
            buf[b // per, :, at] = row[:, q * LANES : (q + 1) * LANES]

    for i in range(2):
        put(i * lines, one[i : i + 1, :])
        put((6 + i) * lines, pair[i : i + 1, :])
    for i in range(4):
        put((2 + i) * lines, two[i : i + 1, :])
    total = near[...] + far[...]
    for y in range(2):
        for c in range(2):

            @pl.when((meta[3] == y) & (meta[4] == c))
            def _():
                for r in range(2):
                    m = 2 * y + (c + r) % 2
                    put(8 * lines + m * plan.part // LANES, total[r : r + 1, :])

    copy = pltpu.make_async_copy(buf, out, sem.at[0])
    copy.start()
    copy.wait()


def ff_total_kernel(meta, *refs):
    *parts, expand, reduce, square = refs
    half = len(parts) // 2
    sums = None
    for out, some in ((expand, parts[:half]), (reduce, parts[half:])):
        total = some[0][...].astype(f32)
        for part in some[1:]:
            total = total + part[...].astype(f32)
        out[...] = total
        line = jnp.sum(total * total, axis=0, keepdims=True)
        sums = line if sums is None else sums + line
    square[...] = jnp.sum(sums, axis=1, keepdims=True)


def total_kernel(meta, *refs):
    *parts, ff_square, local, keep, send, payload = refs
    total = parts[0][...].astype(f32)
    for part in parts[1:]:
        total = total + part[...].astype(f32)
    quarter = total.shape[1] // 8
    for core in range(2):
        for out, c in ((keep, core), (send, 1 - core)):

            @pl.when(meta[4] == core)
            def _():
                for b in range(4):
                    at = (2 * b + c) * quarter
                    out[:, b * quarter : (b + 1) * quarter] = total[:, at : at + quarter]

    square = jnp.sum(total * total) + jnp.sum(ff_square[...]) + jnp.sum(local[...] * local[...])
    size = local.shape[1]
    count = payload.shape[0]
    payload[:, :, :size] = jnp.broadcast_to(local[...][None], (count, 1, size))
    payload[:, :, size:] = jnp.full((count, 1, LANES), square, f32)


def out_kernel(meta, pre_a, fed_a, pre_b, fed_b, np_ref, out_a, out_b):
    for pre, fed, out in ((pre_a, fed_a, out_a), (pre_b, fed_b, out_b)):
        total = pre[...].astype(f32) + fed[...].astype(f32) + np_ref[5:6, :]
        out[...] = total.astype(bf16)


def place_kernel(meta, own, by_y, by_c, by_yc, out, sem):
    count = own.shape[0]
    copies = []
    for fy, fc, src in ((0, 0, own), (1, 0, by_y), (0, 1, by_c), (1, 1, by_yc)):
        at = jnp.bitwise_xor(meta[3], fy) * 2 + jnp.bitwise_xor(meta[4], fc)
        dst = out.at[pl.ds(pl.multiple_of(at * count, 16), count), :]
        copies.append(pltpu.make_async_copy(src, dst, sem.at[len(copies)]))
    for copy in copies:
        copy.start()
    for copy in copies:
        copy.wait()


def adam_kernel(plan, rates, meta, got, *refs):
    per = got.shape[2] // LANES - 1
    total = jnp.sum(got[:, 0, per * LANES :], axis=0, keepdims=True)[:, 0:1]
    norm = jnp.sqrt(total)
    refs[-1][...] = norm
    factor = jnp.minimum(1.0, CLIP / norm)
    correction = 1.0 - BETA**STEP
    width, quarter, part = plan.width, plan.width // 4, plan.part

    def line(start, length):
        spots = range(start // LANES, (start + length) // LANES)
        return jnp.concatenate(
            [got[b // per, :, b % per * LANES : (b % per + 1) * LANES] for b in spots],
            axis=1,
        )

    def owned(pick):
        value = pick(0)
        for m in range(1, 4):
            value = jnp.where(meta[0] == m, pick(m), value)
        return value

    pairs = [line((6 + i) * width, width) for i in range(2)]
    small = (
        jnp.concatenate([line(i * width, width) for i in range(6)], axis=0),
        jnp.concatenate(
            [owned(lambda m: v[:, m * quarter : (m + 1) * quarter]) for v in pairs], axis=0
        ),
        owned(lambda m: line(8 * width + m * part, part)),
    )
    ins, outs = refs[: 4 * 4 + 3 * 3], refs[4 * 4 + 3 * 3 : -1]
    for i, (rate, decay) in enumerate(rates):
        if i < 4:
            w_ref, m_ref, s_ref, g_ref = ins[4 * i : 4 * i + 4]
        else:
            w_ref, m_ref, s_ref = ins[3 * i + 4 : 3 * i + 7]
            g_ref = {Ellipsis: small[i - 4]}
        m_out, s_out, w_out = outs[3 * i : 3 * i + 3]
        planes = range(w_ref.shape[0]) if len(w_ref.shape) == 3 else (Ellipsis,)
        for p in planes:
            clipped = g_ref[p] * factor
            shape = w_ref[p].shape
            weight, first, second = (
                v[p].reshape(clipped.shape) for v in (w_ref, m_ref, s_ref)
            )
            first = BETA * first + (1.0 - BETA) * clipped
            second = BETA * second + (1.0 - BETA) * clipped * clipped
            direction = first / correction / (jnp.sqrt(second / correction) + ADAM_EPS)
            m_out[p] = first.reshape(shape)
            s_out[p] = second.reshape(shape)
            w_out[p] = (weight - rate * (direction + decay * weight)).reshape(shape)


def after(value, *others):
    return lax.optimization_barrier((value, *others))[0]


def any_spec():
    return pl.BlockSpec(memory_space=pl.ANY)


def local_call(meta, kernel, name, ins, outs, scratch, vmem=16):
    def space(item):
        return pltpu.VMEM if item[1] else pltpu.HBM

    def place(item):
        return item[0] if item[1] else pltpu.with_memory_space_constraint(item[0], pltpu.HBM)

    kernel_call = pl.pallas_call(
        kernel,
        name=name,
        out_shape=[space(o)(o[0].shape, o[0].dtype) for o in outs],
        in_specs=[pl.BlockSpec(memory_space=s) for s in (pltpu.SMEM, *map(space, ins))],
        out_specs=[pl.BlockSpec(memory_space=space(o)) for o in outs],
        scratch_shapes=scratch,
        compiler_params=pltpu.CompilerParams(vmem_limit_bytes=vmem * MIB),
        cost_estimate=pl.CostEstimate(flops=1, bytes_accessed=1, transcendentals=0),
    )
    return kernel_call(meta, *map(place, ins))


def call(kernel, name, grid, ins, outs, scratch, vmem=16):
    def spec(item):
        if item[1] is None:
            return any_spec()
        return pl.BlockSpec(item[1], item[2])

    return pl.pallas_call(
        kernel,
        name=name,
        out_shape=[o[0] for o in outs],
        grid_spec=pltpu.PrefetchScalarGridSpec(
            num_scalar_prefetch=1,
            grid=grid,
            in_specs=[spec(i) for i in ins],
            out_specs=[spec(o) for o in outs],
            scratch_shapes=scratch,
        ),
        compiler_params=pltpu.CompilerParams(vmem_limit_bytes=vmem * MIB),
        cost_estimate=pl.CostEstimate(flops=1, bytes_accessed=1, transcendentals=0),
    )


def per_device(
    inputs,
    segments,
    cotangent,
    triple_weight,
    triple_first,
    triple_second,
    outward_weight,
    outward_first,
    outward_second,
    expand_weight,
    expand_first,
    expand_second,
    reduce_weight,
    reduce_first,
    reduce_second,
    norm_params,
    norm_first,
    norm_second,
    paired_bias,
    paired_first,
    paired_second,
    hidden_bias,
    hidden_first,
    hidden_second,
):
    ndp, nmp = lax.axis_size("dp"), lax.axis_size("mp")
    width = inputs.shape[1]
    hidden = hidden_bias.shape[0] * nmp
    plan = Plan(ndp, nmp, width, hidden)
    nz, rows, half, cols, part = plan.nz, plan.rows, plan.half, plan.cols, plan.part
    count = inputs.shape[0] // nmp
    row_count, row_length = segments.shape
    own_rows = row_count // nmp
    steps = count // CHUNK
    quarter = cols // 2

    dp, mp = lax.axis_index("dp"), lax.axis_index("mp")
    z, x, y, c = dp // 2, dp % 2, mp // 2, mp % 2
    meta = jnp.stack([mp, z, x, y, c, jnp.bitwise_xor(mp, 2)]).astype(jnp.int32)
    core_zero = c == 0
    SDS = jax.ShapeDtypeStruct

    shard = jnp.concatenate(
        [triple_weight.astype(bf16), outward_weight.T.astype(bf16)[None]], axis=0
    ).transpose(1, 0, 2)
    keep = lax.dynamic_slice_in_dim(shard, c * half, half, 0)
    send = lax.dynamic_slice_in_dim(shard, (1 - c) * half, half, 0)
    got = plan.core(send)
    low = jnp.where(core_zero, keep, got)
    high = jnp.where(core_zero, got, keep)
    unit = jnp.concatenate([low, high], axis=2).reshape(half, 4 * cols)
    attn_z = [plan.along_z(unit, k) for k in range(1, nz)]

    e_unit = after(expand_weight.astype(bf16), attn_z[0])
    e_z = [plan.along_z(e_unit, k) for k in range(1, nz)]
    r_unit = after(reduce_weight.T.astype(bf16), e_z[0])
    r_z = [plan.along_z(r_unit, k) for k in range(1, nz)]

    biases = jnp.concatenate([paired_bias.reshape(-1), hidden_bias])
    by_core = plan.core(after(biases, attn_z[0]))
    other_pair = by_core[: 2 * quarter].reshape(2, quarter)
    near = jnp.where(
        core_zero,
        jnp.concatenate([paired_bias, other_pair], axis=1),
        jnp.concatenate([other_pair, paired_bias], axis=1),
    )
    far = plan.along_y(near)
    pair_full = jnp.where(
        y == 0, jnp.concatenate([near, far], axis=1), jnp.concatenate([far, near], axis=1)
    )
    hidden_rows = jnp.stack([hidden_bias, by_core[2 * quarter :]])

    marks = lax.dynamic_slice_in_dim(segments, mp * own_rows, own_rows, 0)
    marks = marks + row_length * lax.broadcasted_iota(jnp.int32, marks.shape, 0)
    mark_col = marks.reshape(count, 1)
    mark_row = marks.reshape(count // LANES, LANES)

    spread = jnp.stack([unit] + attn_z)
    spread = jnp.stack([spread, plan.first(spread)])
    spread, *_, meta, mark_col, mark_row, pair_full, hidden_rows = lax.optimization_barrier(
        (spread, e_z[0], meta, mark_col, mark_row, pair_full, hidden_rows)
    )
    attn_w = [spread, after(plan.second(spread), *e_z)]
    e_spread = after(jnp.stack([e_unit] + e_z), attn_w[1])
    e_x = plan.along_x(e_spread)
    attn_w = attn_w + [plan.core(v) for v in attn_w]
    attn_w[1] = after(attn_w[1], e_spread, r_z[0])

    if not plan.direct:
        attn_w = [absolute_attn(plan, jnp.stack(attn_w[:2]), jnp.stack(attn_w[2:]), z, x, y, c)]
        attn_w = attn_w + [meta] * 3

    whole = lambda shape: (shape, lambda i, m: (0,) * len(shape))
    chunk = lambda n: ((CHUNK, n), lambda i, m: (i, 0))
    pieces = 2 * 2 * 2 * nz if plan.direct else 1
    dma = pltpu.SemaphoreType.DMA

    tokens_low, tokens_f32 = SDS((count, width), bf16), SDS((count, width), f32)
    sem_x = dma((2 * steps,))
    buf_low = pltpu.VMEM((count, width), bf16)
    sl, middle, fl, qkv, probs, ctx, attn_full = local_call(
        meta,
        functools.partial(attn_fwd_kernel, plan),
        "attn_fwd",
        [
            (inputs, False),
            (mark_col, True),
            (mark_row, True),
            (norm_params, True),
            (pair_full, True),
            *[(v, False) for v in attn_w],
        ],
        [
            (tokens_low, False),
            (tokens_f32, True),
            (tokens_low, True),
            (SDS((2, count, 3 * cols), bf16), True),
            (SDS((count // LANES * 2, 2 * cols, LANES), bf16), True),
            (tokens_low, True),
            (SDS((2, width, 4 * cols), bf16), True),
        ],
        [buf_low, buf_low, dma((pieces,)), sem_x],
    )

    sl_far = plan.along_y(sl)
    r_spread = jnp.stack([r_unit, r_z[0]] + [after(v, sl) for v in r_z[1:]])
    r_x = plan.along_x(r_spread)
    e_x = after(e_x, sl)
    ff_w = []
    for near, far in ((e_spread, e_x), (r_spread, r_x)):
        pieces_of = [near, far, plan.core(near), plan.core(far)]
        if not plan.direct:
            pairs = (pieces_of[:2], pieces_of[2:])
            pieces_of = [v for p in pairs for v in (absolute_ff(plan, jnp.stack(p), z, x), meta)]
        ff_w = ff_w + pieces_of

    act_shape = SDS((2, count, part), bf16)
    gh_shape = SDS((2, part), f32)
    sg_send, fed_send, act_far, hg_far, gh_far, cot_far, ff_full = local_call(
        meta,
        functools.partial(ff_kernel, plan, False),
        "ff_far",
        [
            (sl_far, True),
            (cotangent, False),
            (hidden_rows, True),
            *[(v, False) for v in ff_w],
        ],
        [
            (tokens_low, False),
            (tokens_low, False),
            (act_shape, True),
            (act_shape, True),
            (gh_shape, True),
            (tokens_low, True),
            (SDS((2, 2, width, part), bf16), True),
        ],
        [buf_low, buf_low, dma((2, 2, 2 * nz if plan.direct else 1)), sem_x],
    )
    sg_far = plan.along_y(sg_send)
    sg_near, pre_near, act_near, hg_near, gh_near, cot_near = local_call(
        meta,
        functools.partial(ff_kernel, plan, True),
        "ff_near",
        [
            (sl, True),
            (cotangent, False),
            (hidden_rows, True),
            (ff_full, True),
            (middle, True),
        ],
        [
            (tokens_low, True),
            (tokens_low, False),
            (act_shape, True),
            (act_shape, True),
            (gh_shape, True),
            (tokens_low, True),
        ],
        [buf_low, sem_x],
    )

    if plan.direct:
        grad_shapes = [SDS((nz, rows, part), bf16)] * 8
    else:
        grad_shapes = [SDS((width, part), bf16)] * 4
    ff_ins = (sl, sl_far, cot_near, cot_far, act_near, act_far, hg_near, hg_far)
    ff_grads = local_call(
        meta,
        functools.partial(ff_grad_kernel, plan),
        "ff_grad",
        [(v, True) for v in ff_ins],
        [(v, False) for v in grad_shapes],
        [pltpu.VMEM((2, 2, width, part), bf16), dma((2, 4 * nz if plan.direct else 2))],
    )
    if not plan.direct:
        ff_grads = [v for g in ff_grads for v in relative_ff(plan, g, z, x)]

    ff_got = [plan.core(v) for v in ff_grads[4:]]
    sg_far = after(sg_far, ff_grads[0])
    fed_far = plan.along_y(after(fed_send, sg_far))

    bwd_ins = (sg_near, sg_far, middle, cot_near, norm_params, qkv, probs, attn_full)
    dqkv, ml, mg, vec_two, pair_sum = local_call(
        meta,
        functools.partial(attn_bwd_kernel, plan),
        "attn_bwd",
        [(v, True) for v in bwd_ins],
        [
            (SDS((2, count, 3 * cols), bf16), True),
            (tokens_low, True),
            (tokens_f32, True),
            (SDS((8, width), f32), True),
            (SDS((2, width), f32), True),
        ],
        [],
    )

    ff_got[0] = after(ff_got[0], dqkv)
    e_keep, e_send, r_keep, r_send = add_lists(meta, ff_grads[:4], ff_got)
    e_got = plan.along_x(e_send)

    if plan.direct:
        grad_shapes = [SDS((2, 2, half, 4 * cols), bf16)] * (2 * nz)
    else:
        grad_shapes = [SDS((2, width, 4 * cols), bf16)]
    ml = after(ml, e_send, r_send)
    attn_grads = local_call(
        meta,
        functools.partial(attn_grad_kernel, plan),
        "attn_grad",
        [(v, True) for v in (fl, ml, dqkv, ctx)],
        [(v, plan.direct and i < nz) for i, v in enumerate(grad_shapes)],
        [pltpu.VMEM((2, width, 4 * cols), bf16), dma((2, 4 * nz if plan.direct else 1))],
    )
    if not plan.direct:
        both = relative_attn(plan, attn_grads[0], z, x, y, c)
        attn_grads = [v[:, :, k] for v in both for k in range(nz)]
    attn_mine, attn_theirs = list(attn_grads[:nz]), list(attn_grads[nz:])
    attn_theirs[0] = after(attn_theirs[0], fed_far)
    attn_got = [plan.core(v) for v in attn_theirs]

    dqkv_late = after(dqkv, attn_theirs[0])
    ig, vec_one = local_call(
        meta,
        functools.partial(input_grad_kernel, plan),
        "input_grad",
        [
            (inputs, False),
            (mg, True),
            (norm_params, True),
            (dqkv_late, True),
            (attn_full, True),
        ],
        [(tokens_low, False), (SDS((8, width), f32), True)],
        [buf_low, buf_low, sem_x],
    )
    attn_got[0] = after(attn_got[0], ig, e_got)
    attn_keep, attn_send = add_first(meta, attn_mine, attn_got)
    attn_got = plan.second(attn_send)
    pre_far = plan.along_y(after(pre_near, attn_send))
    r_got = plan.along_x(after(r_send, attn_send))
    e_parts = add_parts(meta, e_keep, after(e_got, attn_send))
    e_z = [e_parts[0]] + [plan.along_z(e_parts[k], k) for k in range(1, nz)]
    size = -(-(8 * width + hidden) // (LANES * plan.ndev)) * LANES
    parts_in = (vec_one, vec_two, pair_sum, gh_near, gh_far)
    (vectors,) = local_call(
        meta,
        functools.partial(vectors_kernel, plan),
        "vectors",
        [(v, True) for v in parts_in],
        [(SDS((plan.ndev, 1, size), f32), False)],
        [pltpu.VMEM((plan.ndev, 1, size), f32), dma((1,))],
    )
    got = lax.all_to_all(vectors, AXES, 0, 0, tiled=True)
    local = jnp.sum(got, axis=0)

    attn_got = after(attn_got, local, *e_z, r_got)
    attn_keep, attn_send = add_parts(meta, attn_keep, attn_got)
    r_parts = add_parts(meta, r_keep, after(r_got, attn_send))
    r_z = [r_parts[0]] + [plan.along_z(r_parts[k], k) for k in range(1, nz)]
    attn_got = plan.first(attn_send)

    attn_parts = add_parts(meta, attn_keep, after(attn_got, pre_far, *r_z))

    ff_in = [*e_z, *r_z]
    grad_expand, grad_reduce, ff_square = call(
        ff_total_kernel,
        "ff_total",
        (1,),
        [(v, *whole(v.shape)) for v in ff_in],
        [
            (SDS((rows, part), f32), *whole((rows, part))),
            (SDS((rows, part), f32), *whole((rows, part))),
            (SDS((1, 1), f32), *whole((1, 1))),
        ],
        [],
    )(meta, *ff_in)

    pre_in = after(pre_near, attn_parts[0])
    out, out_pair = call(
        out_kernel,
        "out_sum",
        (steps,),
        [
            (pre_in, *chunk(width)),
            (fed_far, *chunk(width)),
            (pre_far, *chunk(width)),
            (fed_send, *chunk(width)),
            (norm_params, *whole(norm_params.shape)),
        ],
        [(SDS((count, width), bf16), *chunk(width))] * 2,
        [],
    )(meta, pre_in, fed_far, pre_far, fed_send, norm_params)
    ig = after(ig, attn_parts[0])
    ig_pair = plan.along_y(ig)
    attn_z = [attn_parts[0]] + [plan.along_z(attn_parts[k], k) for k in range(1, nz)]
    total_in = attn_z + [ff_square, local]
    def everywhere(block, by_y):
        blocks = [block, by_y, plan.core(block), plan.core(by_y)]
        return call(
            place_kernel,
            "place",
            (1,),
            [(b, *whole((count, width))) for b in blocks],
            [(SDS((count * nmp, width), bf16), None, None)],
            [dma((4,))],
        )(meta, *blocks)[0]

    outputs = everywhere(out, out_pair)
    total_in[-1] = after(total_in[-1], outputs)
    keep, send, payload = call(
        total_kernel,
        "total",
        (1,),
        [(v, *whole(v.shape)) for v in total_in],
        [
            (SDS((half, 2 * cols), f32), *whole((half, 2 * cols))),
            (SDS((half, 2 * cols), f32), *whole((half, 2 * cols))),
            (
                SDS((plan.ndev, 1, size + LANES), f32),
                *whole((plan.ndev, 1, size + LANES)),
            ),
        ],
        [],
    )(meta, *total_in)
    by_core = plan.core(send)
    ig_pair = after(ig_pair, keep)
    input_gradient = everywhere(ig, ig_pair)
    got = after(lax.all_to_all(payload, AXES, 0, 0, tiled=True), input_gradient)

    low, high = jnp.where(core_zero, keep, by_core), jnp.where(core_zero, by_core, keep)
    shard = jnp.concatenate([low, high], axis=0).reshape(rows, 4, quarter)
    grad_triple = shard[:, :3].transpose(1, 0, 2)
    grad_outward = shard[:, 3].T

    matrix, vector = (LR_MATRIX, DECAY), (LR_VECTOR, 0.0)
    groups = [
        [triple_weight, triple_first, triple_second, grad_triple],
        [outward_weight, outward_first, outward_second, grad_outward],
        [expand_weight, expand_first, expand_second, grad_expand],
        [reduce_weight.T, reduce_first.T, reduce_second.T, grad_reduce],
        [norm_params, norm_first, norm_second],
        [paired_bias, paired_first, paired_second],
        [hidden_bias, hidden_first, hidden_second],
    ]
    flat = [got] + [v for group in groups for v in group]
    new_shapes = [SDS(group[0].shape, f32) for group in groups for _ in range(3)]
    new_shapes.append(SDS((1, 1), f32))
    new = call(
        functools.partial(adam_kernel, plan, (matrix,) * 4 + (vector,) * 3),
        "adam",
        (1,),
        [(v, *whole(v.shape)) for v in flat],
        [(s, *whole(s.shape)) for s in new_shapes],
        [],
        vmem=60,
    )(meta, *flat)
    new = list(new)
    gradient_norm = new.pop().reshape(())
    new[9:12] = [v.T for v in new[9:12]]
    return (outputs, input_gradient, gradient_norm, *new)


def turn(plan, value, z, axis):
    value = jnp.flip(value, axis)
    return jnp.roll(value, z + 1, axis)


def unturn(plan, value, z, axis):
    return jnp.roll(value, -z, axis)


def swap(value, flag, axis):
    return jnp.where(flag == 1, jnp.flip(value, axis), value)


def absolute_ff(plan, value, z, x):
    value = swap(turn(plan, value, z, 1), x, 0)
    return value.transpose(1, 0, 2, 3).reshape(plan.width, plan.part)


def relative_ff(plan, value, z, x):
    value = value.reshape(plan.nz, 2, plan.rows, plan.part).transpose(1, 0, 2, 3)
    value = unturn(plan, swap(value, x, 0), z, 1)
    return value[0], value[1]


def absolute_attn(plan, own, other, z, x, y, c):
    zero = jnp.where(c == 0, own, other)
    one = jnp.where(c == 0, other, own).transpose(1, 0, 2, 3, 4)
    value = jnp.stack([zero, one])
    value = turn(plan, swap(swap(value, y, 1), x, 2), z, 3)
    value = value.transpose(1, 3, 2, 0, 4, 5)
    return value.reshape(2, plan.width, 4 * plan.cols)


def relative_attn(plan, value, z, x, y, c):
    value = value.reshape(2, plan.nz, 2, 2, plan.half, 4 * plan.cols)
    value = value.transpose(3, 0, 2, 1, 4, 5)
    value = unturn(plan, swap(swap(value, y, 1), x, 2), z, 3)
    zero, one = value[0], value[1].transpose(1, 0, 2, 3, 4)
    return jnp.where(c == 0, zero, one), jnp.where(c == 0, one, zero)


def solution(mesh):
    tokens = P("dp", None)
    triple = P(None, "dp", "mp")
    tall = P("mp", "dp")
    wide = P("dp", "mp")
    pair = P(None, "mp")
    states = ((triple,) * 3, (tall,) * 3, (wide,) * 3, (tall,) * 3, (P(),) * 3, (pair,) * 3)
    states = sum(states, ()) + (P("mp"),) * 3
    return jax.shard_map(
        per_device,
        mesh=mesh,
        in_specs=(tokens,) * 3 + states,
        out_specs=(tokens, tokens, P()) + states,
        check_vma=False,
    )
```

time: 272 us -> 251 us (0.923)
  Pallas kernels: 122 us -> 83 us
  blocking collectives: 0 us -> 18.8 us
  local copies, waits for them, and re-layouts: 18 us -> 10.1 us
  starting transfers between devices: 59.9 us -> 65.5 us
  waiting for transfers between devices: 58.8 us -> 64.1 us
  other arithmetic: 11.3 us -> 7.03 us
    pallas_call x9 -> x10, Pallas kernels: 95.1 us -> 62.7 us  [the longest x9 60.3 us: local_call(): return kernel_call(meta, *map(place, ins))]
    all_to_all x0 -> x1, blocking collectives: none -> 18.8 us  [per_device(): got = lax.all_to_all(vectors, AXES, 0, 0, tiled=True)]
    ppermute x15 -> x18, starting transfers between devices: 21 us -> 39.7 us  [along_z(): lax.ppermute(value, AXES, self.perm(lambda z, x, y, c: ((z + step) % self...]
    ppermute x4, waiting for transfers between devices: 4.27 us -> 13.9 us  [along_x(): lax.ppermute(value, AXES, self.perm(lambda z, x, y, c: (z, 1 - x, y, c)))]
    ppermute x21, starting transfers between devices: 13.8 us -> 4.6 us  [core(): lax.ppermute(value, AXES, self.perm(lambda z, x, y, c: (z, x, y, 1 - c)))]
    all_to_all x1 -> x0, waiting for transfers between devices: 8.03 us -> none  [per_device(): lax.all_to_all(vectors.reshape(plan.ndev, size), AXES, 0, 0, tiled=True)]
    unnamed x82 -> x68, local copies, waits for them, and re-layouts: 9.37 us -> 2.99 us
    ppermute x21, waiting for transfers between devices: 5.06 us -> 0.23 us  [core(): lax.ppermute(value, AXES, self.perm(lambda z, x, y, c: (z, x, y, 1 - c)))]
  transfers between devices with their start and end apart: 52 -> 54, of which waited for: 21 -> 17; matrix products, arithmetic and copies ran while one was open for 7% -> 5% of each run, Pallas kernels for 39% -> 25%
where the time goes in v3:
time: 251 us; the launch traced here: 250 us
  Pallas kernels  83 us (33%)
  starting transfers between devices  65.5 us (26%)
  waiting for transfers between devices  64.1 us (26%)
  blocking collectives  18.8 us (7%)
  local copies, waits for them, and re-layouts  10.1 us (4%)
  other arithmetic  7.03 us (3%)
    pallas_call x9, Pallas kernels, local_call(): return kernel_call(meta, *map(place, ins))  60.3 us
    ppermute x18, starting transfers between devices, along_z(): lax.ppermute(value, AXES, self.perm(lambda z, x, y, c: ((z + step) % self...  39.7 us
    ppermute x18, waiting for transfers between devices, along_z(): lax.ppermute(value, AXES, self.perm(lambda z, x, y, c: ((z + step) % self...  35.3 us
    all_to_all x1, blocking collectives, per_device(): got = lax.all_to_all(vectors, AXES, 0, 0, tiled=True)  18.8 us
    ppermute x4, waiting for transfers between devices, along_x(): lax.ppermute(value, AXES, self.perm(lambda z, x, y, c: (z, 1 - x, y, c)))  13.9 us
    ppermute x6, starting transfers between devices, along_y(): lax.ppermute(value, AXES, self.perm(lambda z, x, y, c: (z, x, 1 - y, c)))  9.14 us
    ppermute x6, waiting for transfers between devices, along_y(): lax.ppermute(value, AXES, self.perm(lambda z, x, y, c: (z, x, 1 - y, c)))  8.42 us
    pallas_call x1, Pallas kernels, per_device(): call(functools.partial(adam_kernel, plan, (matrix,) * 4 + (vector,) * 3),...  5.04 us
  transfers between devices with their start and end apart: 54, of which 17 were waited for; matrix products, arithmetic and copies ran while one was open for 5% of the time, Pallas kernels for 25%

profile of v3, /device:TPU:0, one launch (start us, length us, event | category | flops | bytes accessed | tf_op | source)
XLA Modules:
  0.0 250.2 jit_solution(17936531589165670854)
XLA Ops:
  4.4 5.0 %collective-permute-start.3 = (bf16[48,1536]{1,0:T(8,128)(2,1)S(1)}, bf16[48,1536]{1,0:T(8,128)(2,1)S(1)}, u32[]{:S(2)}, u32[]{:S(2)}) collective-permute-start(bf16[48,1536]{1,0:T(8,128)(2,1)S(1)} %bitcast.95), channel_id=1, source_target_pairs={{0,24},{1,25},{2,26},{3,27},{4,28},{5,29},{6,30},{7,31},{8,0},{9,1... | collective-permute-start | bytes 442376 | tf_op jit(solution)/shard_map/ppermute | solution.py:107
  10.7 3.0 %collective-permute-done.3 = bf16[48,1536]{1,0:T(8,128)(2,1)S(1)} collective-permute-done((bf16[48,1536]{1,0:T(8,128)(2,1)S(1)}, bf16[48,1536]{1,0:T(8,128)(2,1)S(1)}, u32[]{:S(2)}, u32[]{:S(2)}) %collective-permute-start.3) | collective-permute-done | bytes 147488 | tf_op jit(solution)/shard_map/ppermute | solution.py:107
  13.7 8.5 %collective-permute-done.2 = bf16[48,1536]{1,0:T(8,128)(2,1)S(1)} collective-permute-done((bf16[48,1536]{1,0:T(8,128)(2,1)S(1)}, bf16[48,1536]{1,0:T(8,128)(2,1)S(1)}, u32[]{:S(2)}, u32[]{:S(2)}) %collective-permute-start.2) | collective-permute-done | bytes 147488 | tf_op jit(solution)/shard_map/ppermute | solution.py:107
  36.8 3.7 %collective-permute-done.10 = bf16[96,768]{1,0:T(8,128)(2,1)S(1)} collective-permute-done((bf16[96,768]{1,0:T(8,128)(2,1)S(1)}, bf16[96,768]{1,0:T(8,128)(2,1)S(1)}, u32[]{:S(2)}, u32[]{:S(2)}) %collective-permute-start.10) | collective-permute-done | bytes 147488 | tf_op jit(solution)/shard_map/ppermute | solution.py:107
  40.5 5.2 %collective-permute-done.9 = bf16[96,768]{1,0:T(8,128)(2,1)S(1)} collective-permute-done((bf16[96,768]{1,0:T(8,128)(2,1)S(1)}, bf16[96,768]{1,0:T(8,128)(2,1)S(1)}, u32[]{:S(2)}, u32[]{:S(2)}) %collective-permute-start.9) | collective-permute-done | bytes 147488 | tf_op jit(solution)/shard_map/ppermute | solution.py:107
  45.7 4.2 %collective-permute-done.8.refs_1_ = bf16[2,4,48,1536]{3,2,1,0:T(8,128)(2,1)S(1)} collective-permute-done((bf16[2,4,48,1536]{3,2,1,0:T(8,128)(2,1)S(1)}, bf16[2,4,48,1536]{3,2,1,0:T(8,128)(2,1)S(1)}, u32[]{:S(2)}, u32[]{:S(2)}) %collective-permute-start.8) | collective-permute-done | bytes 1179680 | tf_op jit(solution)/shard_map/ppermute | solution.py:119
  50.6 3.8 %collective-permute-start.19 = (bf16[96,768]{1,0:T(8,128)(2,1)}, bf16[96,768]{1,0:T(8,128)(2,1)S(1)}, u32[]{:S(2)}, u32[]{:S(2)}) collective-permute-start(bf16[96,768]{1,0:T(8,128)(2,1)} %bitcast_convert_fusion), channel_id=1, source_target_pairs={{0,24},{1,25},{2,26},{3,27},{4,28},{5,29},{6,30},{7,31},{8,0},{9,1... | collective-permute-start | bytes 442376 | tf_op jit(solution)/shard_map/ppermute | solution.py:107
  56.3 3.0 %collective-permute-done.11 = bf16[96,768]{1,0:T(8,128)(2,1)S(1)} collective-permute-done((bf16[96,768]{1,0:T(8,128)(2,1)}, bf16[96,768]{1,0:T(8,128)(2,1)S(1)}, u32[]{:S(2)}, u32[]{:S(2)}) %collective-permute-start.11) | collective-permute-done | bytes 147488 | tf_op jit(solution)/shard_map/ppermute | solution.py:107
  59.9 13.0 %attn_fwd.1 = (bf16[512,768]{1,0:T(8,128)(2,1)}, f32[512,768]{1,0:T(8,128)S(1)}, bf16[512,768]{1,0:T(8,128)(2,1)S(1)}, bf16[2,512,1152]{2,1,0:T(8,128)(2,1)S(1)}...) custom-call(s32[6]{0:T(128)S(1)} %stack.94.meta, ...), custom_call_target="tpu_custom_call" | custom-call | flops 1 | bytes 1 | tf_op jit(solution)/shard_map/attn_fwd/pallas_call | solution.py:743
  77.7 10.6 %collective-permute-done.20.refs_5_ = bf16[4,96,768]{2,1,0:T(8,128)(2,1)S(1)} collective-permute-done((bf16[4,96,768]{2,1,0:T(8,128)(2,1)S(1)}, bf16[4,96,768]{2,1,0:T(8,128)(2,1)S(1)}, u32[]{:S(2)}, u32[]{:S(2)}) %collective-permute-start.20) | collective-permute-done | bytes 589856 | tf_op jit(solution)/shard_map/ppermute | solution.py:101
  88.3 5.6 %collective-permute-done.14.sl_ref.sl_b = bf16[512,768]{1,0:T(8,128)(2,1)S(1)} collective-permute-done((bf16[512,768]{1,0:T(8,128)(2,1)}, bf16[512,768]{1,0:T(8,128)(2,1)S(1)}, u32[]{:S(2)}, u32[]{:S(2)}) %collective-permute-start.14) | collective-permute-done | bytes 786464 | tf_op jit(solution)/shard_map/ppermute | solution.py:104
  94.8 10.1 %ff_far.1 = (bf16[512,768]{1,0:T(8,128)(2,1)}, bf16[512,768]{1,0:T(8,128)(2,1)}, bf16[2,512,768]{2,1,0:T(8,128)(2,1)S(1)}, bf16[2,512,768]{2,1,0:T(8,128)(2,1)S(...) custom-call(s32[6]{0:T(128)S(1)} %stack.94.meta, ...), custom_call_target="tpu_custom_call" | custom-call | flops 1 | bytes 1 | tf_op jit(solution)/shard_map/ff_far/pallas_call | solution.py:743
  106.5 8.1 %ff_near.1 = (bf16[512,768]{1,0:T(8,128)(2,1)S(1)}, bf16[512,768]{1,0:T(8,128)(2,1)}, bf16[2,512,768]{2,1,0:T(8,128)(2,1)S(1)}, bf16[2,512,768]{2,1,0:T(8,128)(2...) custom-call(s32[6]{0:T(128)S(1)} %stack.94.meta, bf16[512,768]{1,0:T(8,128)(2,1)S(1)} %copy-done, ...), custom_call_target="tpu_custom_call" | custom-call | flops 1 | bytes 1 | tf_op jit(solution)/shard_map/ff_near/pallas_call | solution.py:743
  114.5 7.4 %ff_grad.1 = (bf16[4,96,768]{2,1,0:T(8,128)(2,1)}, bf16[4,96,768]{2,1,0:T(8,128)(2,1)}, bf16[4,96,768]{2,1,0:T(8,128)(2,1)}, bf16[4,96,768]{2,1,0:T(8,128)(2,1)}...) custom-call(s32[6]{0:T(128)S(1)} %stack.94.meta, ...), custom_call_target="tpu_custom_call" | custom-call | flops 1 | bytes 1 | tf_op jit(solution)/shard_map/ff_grad/pallas_call | solution.py:743
  125.4 7.1 %attn_bwd.1 = (bf16[2,512,1152]{2,1,0:T(8,128)(2,1)S(1)}, bf16[512,768]{1,0:T(8,128)(2,1)S(1)}, f32[512,768]{1,0:T(8,128)S(1)}, f32[8,768]{1,0:T(8,128)S(1)}, f32[2,768]{1,0:T(2,128)S(1)}) custom-call(s32[6]{0:T(128)S(1)} %stack.94.meta, bf16[512,768]{1,0:T(8,128)(2,1)S(1)} %get-tuple-element.170.sga_ref, ...), custom_call_target="tpu_custom_call" | custom-call | flops 1 | bytes 1 | tf_op jit(solution)/shard_map/attn_bwd/pallas_call | solution.py:743
  135.0 4.9 %attn_grad.1 = (bf16[2,2,48,1536]{3,2,1,0:T(8,128)(2,1)S(1)}, bf16[2,2,48,1536]{3,2,1,0:T(8,128)(2,1)S(1)}, bf16[2,2,48,1536]{3,2,1,0:T(8,128)(2,1)S(1)}, bf16[2...) custom-call(s32[6]{0:T(128)S(1)} %stack.94.meta, ...), custom_call_target="tpu_custom_call" | custom-call | flops 1 | bytes 1 | tf_op jit(solution)/shard_map/attn_grad/pallas_call | solution.py:743
  141.0 5.3 %input_grad.1 = (bf16[512,768]{1,0:T(8,128)(2,1)}, f32[8,768]{1,0:T(8,128)S(1)}) custom-call(s32[6]{0:T(128)S(1)} %stack.94.meta, bf16[2048,768]{1,0:T(8,128)(2,1)} %x_all.3, f32[512,768]{1,0:T(8,128)S(1)} %get-tuple-element.205.mg_ref, f32[6,768]{1,0:T(8,128)S(1)} %copy-done.5, bf16[2,512,1152]{2,1,0:T(8,128)(2,1)S(1)} %get-tuple-element.206.dqkv_ref, ...), custom_call_target="tpu_custom_call" | custom-call | flops 1 | bytes 1 | tf_op jit(solution)/shard_map/input_grad/pallas_call | solution.py:743
  146.3 3.3 %collective-permute-done.30.right = bf16[4,96,768]{2,1,0:T(8,128)(2,1)S(1)} collective-permute-done((bf16[4,96,768]{2,1,0:T(8,128)(2,1)S(1)}, bf16[4,96,768]{2,1,0:T(8,128)(2,1)S(1)}, u32[]{:S(2)}, u32[]{:S(2)}) %collective-permute-start.30) | collective-permute-done | bytes 589856 | tf_op jit(solution)/shard_map/ppermute | solution.py:101
  151.1 3.3 %add_first.1 = (bf16[2,4,48,1536]{3,2,1,0:T(8,128)(2,1)S(1)}, bf16[2,4,48,1536]{3,2,1,0:T(8,128)(2,1)}) custom-call(s32[6]{0:T(128)S(1)} %stack.94.meta, bf16[2,2,48,1536]{3,2,1,0:T(8,128)(2,1)S(1)} %get-tuple-element.197.refs_0_, bf16[2,2,48,1536]{3,2,1,0:T(8,128)(2,1)S(1)} %get-tuple-element.198.refs_1_, ...), custom_call_target="tpu_custom_call" | custom-call | flops 1 | bytes 1 | tf_op jit(solution)/shard_map/add_first/pallas_call | solution.py:743
  156.5 4.9 %collective-permute-start.35 = (bf16[96,768]{1,0:T(8,128)(2,1)S(1)}, bf16[96,768]{1,0:T(8,128)(2,1)S(1)}, u32[]{:S(2)}, u32[]{:S(2)}) collective-permute-start(bf16[96,768]{1,0:T(8,128)(2,1)S(1)} %get-tuple-element.222), channel_id=1, source_target_pairs={{0,8},{1,9},{2,10},{3,11},{4,12},{5,13},{6,14},{7,15},{8,16},{9,17... | collective-permute-start | bytes 442376 | tf_op jit(solution)/shard_map/ppermute | solution.py:107
  165.6 2.7 %collective-permute-start.37 = (bf16[96,768]{1,0:T(8,128)(2,1)}, bf16[96,768]{1,0:T(8,128)(2,1)}, u32[]{:S(2)}, u32[]{:S(2)}) collective-permute-start(bf16[96,768]{1,0:T(8,128)(2,1)} %get-tuple-element.224), channel_id=1, source_target_pairs={{0,24},{1,25},{2,26},{3,27},{4,28},{5,29},{6,30},{7,31},{8,0},{9,1... | collective-permute-start | bytes 442376 | tf_op jit(solution)/shard_map/ppermute | solution.py:107
  169.6 18.8 %all_to_all.10 = f32[32,1,384]{2,1,0:T(1,128)S(1)} all-to-all(f32[32,1,384]{2,1,0:T(1,128)} %vectors.1), channel_id=1, replica_groups=mesh['dp'=8,'mp'=4] {'dp','mp'}, dimensions={0} | all-to-all | bytes 98304 | tf_op jit(solution)/shard_map/all_to_all | solution.py:1043
  191.6 5.1 %collective-permute-start.41 = (bf16[96,768]{1,0:T(8,128)(2,1)S(1)}, bf16[96,768]{1,0:T(8,128)(2,1)S(1)}, u32[]{:S(2)}, u32[]{:S(2)}) collective-permute-start(bf16[96,768]{1,0:T(8,128)(2,1)S(1)} %get-tuple-element.233), channel_id=1, source_target_pairs={{0,8},{1,9},{2,10},{3,11},{4,12},{5,13},{6,14},{7,15},{8,16},{9,17... | collective-permute-start | bytes 442376 | tf_op jit(solution)/shard_map/ppermute | solution.py:107
  198.7 2.8 %collective-permute-start.43 = (bf16[96,768]{1,0:T(8,128)(2,1)S(1)}, bf16[96,768]{1,0:T(8,128)(2,1)S(1)}, u32[]{:S(2)}, u32[]{:S(2)}) collective-permute-start(bf16[96,768]{1,0:T(8,128)(2,1)S(1)} %get-tuple-element.235), channel_id=1, source_target_pairs={{0,24},{1,25},{2,26},{3,27},{4,28},{5,29},{6,30},{7,31},{8,0},{9,1... | collective-permute-start | bytes 442376 | tf_op jit(solution)/shard_map/ppermute | solution.py:107
  201.6 5.2 %collective-permute-done.42.refs_6_ = bf16[96,768]{1,0:T(8,128)(2,1)S(1)} collective-permute-done((bf16[96,768]{1,0:T(8,128)(2,1)S(1)}, bf16[96,768]{1,0:T(8,128)(2,1)S(1)}, u32[]{:S(2)}, u32[]{:S(2)}) %collective-permute-start.42) | collective-permute-done | bytes 147488 | tf_op jit(solution)/shard_map/ppermute | solution.py:107
  211.1 4.6 %collective-permute-start.47 = (bf16[48,1536]{1,0:T(8,128)(2,1)S(1)}, bf16[48,1536]{1,0:T(8,128)(2,1)S(1)}, u32[]{:S(2)}, u32[]{:S(2)}) collective-permute-start(bf16[48,1536]{1,0:T(8,128)(2,1)S(1)} %get-tuple-element.242), channel_id=1, source_target_pairs={{0,8},{1,9},{2,10},{3,11},{4,12},{5,13},{6,14},{7,15},{8,16},{9,17... | collective-permute-start | bytes 442376 | tf_op jit(solution)/shard_map/ppermute | solution.py:107
  215.7 3.4 %collective-permute-start.48 = (bf16[48,1536]{1,0:T(8,128)(2,1)S(1)}, bf16[48,1536]{1,0:T(8,128)(2,1)S(1)}, u32[]{:S(2)}, u32[]{:S(2)}) collective-permute-start(bf16[48,1536]{1,0:T(8,128)(2,1)S(1)} %get-tuple-element.243), channel_id=1, source_target_pairs={{0,16},{1,17},{2,18},{3,19},{4,20},{5,21},{6,22},{7,23},{8,24},{9,... | collective-permute-start | bytes 442376 | tf_op jit(solution)/shard_map/ppermute | solution.py:107
  219.1 2.4 ff_total.1
  223.7 5.0 %collective-permute-done.48.refs_2_ = bf16[48,1536]{1,0:T(8,128)(2,1)S(1)} collective-permute-done((bf16[48,1536]{1,0:T(8,128)(2,1)S(1)}, bf16[48,1536]{1,0:T(8,128)(2,1)S(1)}, u32[]{:S(2)}, u32[]{:S(2)}) %collective-permute-start.48) | collective-permute-done | bytes 147488 | tf_op jit(solution)/shard_map/ppermute | solution.py:107
  228.7 2.3 total.1
  231.5 4.9 %all-to-all-start.1 = ((f32[32,1,512]{2,1,0:T(1,128)}), f32[32,1,512]{2,1,0:T(1,128)S(1)}, u32[]{:S(2)}, u32[]{:S(2)}) async-start(f32[32,1,512]{2,1,0:T(1,128)} %get-tuple-element.249), calls=%async_computation.1 | async-start | bytes 131072 | tf_op jit(solution)/shard_map/all_to_all | solution.py:1118
  245.0 5.0 %adam.1 = (f32[3,96,192]{2,1,0:T(8,128)}, f32[3,96,192]{2,1,0:T(8,128)}, f32[3,96,192]{2,1,0:T(8,128)}, f32[192,96]{1,0:T(8,128)}, f32[192,96]{1,0:T(8,128)}, /*...) custom-call(s32[6]{0:T(128)} %copy-done.14, ...), custom_call_target="tpu_custom_call" | custom-call | flops 1 | bytes 1 | tf_op jit(solution)/shard_map/adam/pallas_call | solution.py:1138
  (205 shorter events, 66.3 us)
Async XLA Ops:
  9.4 12.8 %collective-permute-start.2 = (bf16[48,1536]{1,0:T(8,128)(2,1)S(1)}, bf16[48,1536]{1,0:T(8,128)(2,1)S(1)}, u32[]{:S(2)}, u32[]{:S(2)}) collective-permute-start(bf16[48,1536]{1,0:T(8,128)(2,1)S(1)} %bitcast.96), channel_id=1, source_target_pairs={{0,16},{1,17},{2,18},{3,19},{4,20},{5,21},{6,22},{7,23},{8,24},{9,... | collective-permute-start | bytes 442376 | tf_op jit(solution)/shard_map/ppermute | solution.py:107
  9.4 12.8 %collective-permute-start.1 = (bf16[48,1536]{1,0:T(8,128)(2,1)S(1)}, bf16[48,1536]{1,0:T(8,128)(2,1)S(1)}, u32[]{:S(2)}, u32[]{:S(2)}) collective-permute-start(bf16[48,1536]{1,0:T(8,128)(2,1)S(1)} %bitcast.97), channel_id=1, source_target_pairs={{0,8},{1,9},{2,10},{3,11},{4,12},{5,13},{6,14},{7,15},{8,16},{9,17... | collective-permute-start | bytes 442376 | tf_op jit(solution)/shard_map/ppermute | solution.py:107
  22.4 9.9 %collective-permute-start.4 = (bf16[4,48,1536]{2,1,0:T(8,128)(2,1)S(1)}, bf16[4,48,1536]{2,1,0:T(8,128)(2,1)S(1)}, u32[]{:S(2)}, u32[]{:S(2)}) collective-permute-start(bf16[4,48,1536]{2,1,0:T(8,128)(2,1)S(1)} %get-tuple-element.277), channel_id=1, source_target_pairs={{0,4},{1,3},{2,6},{3,1},{4,0},{5,7},{6,2},{7,5},{8,12},{9,11},{10,... | collective-permute-start | bytes 1769480 | tf_op jit(solution)/shard_map/ppermute | solution.py:112
  33.7 16.2 %collective-permute-start.8 = (bf16[2,4,48,1536]{3,2,1,0:T(8,128)(2,1)S(1)}, bf16[2,4,48,1536]{3,2,1,0:T(8,128)(2,1)S(1)}, u32[]{:S(2)}, u32[]{:S(2)}) collective-permute-start(bf16[2,4,48,1536]{3,2,1,0:T(8,128)(2,1)S(1)} %pad_maximum_fusion.refs_0_), channel_id=1, source_target_pairs={{0,2},{1,5},{2,0},{3,7},{4,6},{5,1},{6,4},{7,3},{8,10},{9,13},{10,... | collective-permute-start | bytes 3538952 | tf_op jit(solution)/shard_map/ppermute | solution.py:119
  35.9 9.8 %collective-permute-start.9 = (bf16[96,768]{1,0:T(8,128)(2,1)S(1)}, bf16[96,768]{1,0:T(8,128)(2,1)S(1)}, u32[]{:S(2)}, u32[]{:S(2)}) collective-permute-start(bf16[96,768]{1,0:T(8,128)(2,1)S(1)} %convert_element_type.18), channel_id=1, source_target_pairs={{0,16},{1,17},{2,18},{3,19},{4,20},{5,21},{6,22},{7,23},{8,24},{9,... | collective-permute-start | bytes 442376 | tf_op jit(solution)/shard_map/ppermute | solution.py:107
  36.8 23.1 %collective-permute-start.12 = (bf16[2,4,48,1536]{3,2,1,0:T(8,128)(2,1)S(1)}, bf16[2,4,48,1536]{3,2,1,0:T(8,128)(2,1)}, u32[]{:S(2)}, u32[]{:S(2)}) collective-permute-start(bf16[2,4,48,1536]{3,2,1,0:T(8,128)(2,1)S(1)} %pad_maximum_fusion.refs_0_), channel_id=1, source_target_pairs={{0,1},{1,0},{2,3},{3,2},{4,5},{5,4},{6,7},{7,6},{8,9},{9,8},{10,11... | collective-permute-start | bytes 3538952 | tf_op jit(solution)/shard_map/ppermute | solution.py:98
  49.9 10.0 %collective-permute-start.13 = (bf16[2,4,48,1536]{3,2,1,0:T(8,128)(2,1)S(1)}, bf16[2,4,48,1536]{3,2,1,0:T(8,128)(2,1)}, u32[]{:S(2)}, u32[]{:S(2)}) collective-permute-start(bf16[2,4,48,1536]{3,2,1,0:T(8,128)(2,1)S(1)} %collective-permute-done.8.refs_1_), channel_id=1, source_target_pairs={{0,1},{1,0},{2,3},{3,2},{4,5},{5,4},{6,7},{7,6},{8,9},{9,8},{10,11... | collective-permute-start | bytes 3538952 | tf_op jit(solution)/shard_map/ppermute | solution.py:98
  50.6 22.2 %collective-permute-start.19 = (bf16[96,768]{1,0:T(8,128)(2,1)}, bf16[96,768]{1,0:T(8,128)(2,1)S(1)}, u32[]{:S(2)}, u32[]{:S(2)}) collective-permute-start(bf16[96,768]{1,0:T(8,128)(2,1)} %bitcast_convert_fusion), channel_id=1, source_target_pairs={{0,24},{1,25},{2,26},{3,27},{4,28},{5,29},{6,30},{7,31},{8,0},{9,1... | collective-permute-start | bytes 442376 | tf_op jit(solution)/shard_map/ppermute | solution.py:107
  54.5 18.4 %collective-permute-start.18 = (bf16[96,768]{1,0:T(8,128)(2,1)}, bf16[96,768]{1,0:T(8,128)(2,1)}, u32[]{:S(2)}, u32[]{:S(2)}) collective-permute-start(bf16[96,768]{1,0:T(8,128)(2,1)} %bitcast_convert_fusion), channel_id=1, source_target_pairs={{0,16},{1,17},{2,18},{3,19},{4,20},{5,21},{6,22},{7,23},{8,24},{9,... | collective-permute-start | bytes 442376 | tf_op jit(solution)/shard_map/ppermute | solution.py:107
  59.3 17.7 %collective-permute-start.15 = (bf16[4,96,768]{2,1,0:T(8,128)(2,1)S(1)}, bf16[4,96,768]{2,1,0:T(8,128)(2,1)S(1)}, u32[]{:S(2)}, u32[]{:S(2)}) collective-permute-start(bf16[4,96,768]{2,1,0:T(8,128)(2,1)S(1)} %pad_maximum_fusion.2.refs_0_), channel_id=1, source_target_pairs={{0,4},{1,5},{2,6},{3,7},{4,0},{5,1},{6,2},{7,3},{8,12},{9,13},{10,... | collective-permute-start | bytes 1769480 | tf_op jit(solution)/shard_map/ppermute | solution.py:101
  74.0 14.3 %collective-permute-start.20 = (bf16[4,96,768]{2,1,0:T(8,128)(2,1)S(1)}, bf16[4,96,768]{2,1,0:T(8,128)(2,1)S(1)}, u32[]{:S(2)}, u32[]{:S(2)}) collective-permute-start(bf16[4,96,768]{2,1,0:T(8,128)(2,1)S(1)} %pad_maximum_fusion.3.refs_4_), channel_id=1, source_target_pairs={{0,4},{1,5},{2,6},{3,7},{4,0},{5,1},{6,2},{7,3},{8,12},{9,13},{10,... | collective-permute-start | bytes 1769480 | tf_op jit(solution)/shard_map/ppermute | solution.py:101
  75.5 18.3 %collective-permute-start.14 = (bf16[512,768]{1,0:T(8,128)(2,1)}, bf16[512,768]{1,0:T(8,128)(2,1)S(1)}, u32[]{:S(2)}, u32[]{:S(2)}) collective-permute-start(bf16[512,768]{1,0:T(8,128)(2,1)} %get-tuple-element.161.sl_ref.sl_a), channel_id=1, source_target_pairs={{0,2},{1,3},{2,0},{3,1},{4,6},{5,7},{6,4},{7,5},{8,10},{9,11},{10,... | collective-permute-start | bytes 2359304 | tf_op jit(solution)/shard_map/ppermute | solution.py:104
  77.1 11.2 %collective-permute-start.16 = (bf16[4,96,768]{2,1,0:T(8,128)(2,1)S(1)}, bf16[4,96,768]{2,1,0:T(8,128)(2,1)S(1)}, u32[]{:S(2)}, u32[]{:S(2)}) collective-permute-start(bf16[4,96,768]{2,1,0:T(8,128)(2,1)S(1)} %pad_maximum_fusion.2.refs_0_), channel_id=1, source_target_pairs={{0,1},{1,0},{2,3},{3,2},{4,5},{5,4},{6,7},{7,6},{8,9},{9,8},{10,11... | collective-permute-start | bytes 1769480 | tf_op jit(solution)/shard_map/ppermute | solution.py:98
  77.1 11.2 %collective-permute-start.17 = (bf16[4,96,768]{2,1,0:T(8,128)(2,1)S(1)}, bf16[4,96,768]{2,1,0:T(8,128)(2,1)S(1)}, u32[]{:S(2)}, u32[]{:S(2)}) collective-permute-start(bf16[4,96,768]{2,1,0:T(8,128)(2,1)S(1)} %collective-permute-done.15.refs_1_), channel_id=1, source_target_pairs={{0,1},{1,0},{2,3},{3,2},{4,5},{5,4},{6,7},{7,6},{8,9},{9,8},{10,11... | collective-permute-start | bytes 1769480 | tf_op jit(solution)/shard_map/ppermute | solution.py:98
  77.6 10.7 %collective-permute-start.21 = (bf16[4,96,768]{2,1,0:T(8,128)(2,1)S(1)}, bf16[4,96,768]{2,1,0:T(8,128)(2,1)S(1)}, u32[]{:S(2)}, u32[]{:S(2)}) collective-permute-start(bf16[4,96,768]{2,1,0:T(8,128)(2,1)S(1)} %pad_maximum_fusion.3.refs_4_), channel_id=1, source_target_pairs={{0,1},{1,0},{2,3},{3,2},{4,5},{5,4},{6,7},{7,6},{8,9},{9,8},{10,11... | collective-permute-start | bytes 1769480 | tf_op jit(solution)/shard_map/ppermute | solution.py:98
  104.9 17.7 %collective-permute-start.23 = (bf16[512,768]{1,0:T(8,128)(2,1)}, bf16[512,768]{1,0:T(8,128)(2,1)S(1)}, u32[]{:S(2)}, u32[]{:S(2)}) collective-permute-start(bf16[512,768]{1,0:T(8,128)(2,1)} %get-tuple-element.171), channel_id=1, source_target_pairs={{0,2},{1,3},{2,0},{3,1},{4,6},{5,7},{6,4},{7,5},{8,10},{9,11},{10,... | collective-permute-start | bytes 2359304 | tf_op jit(solution)/shard_map/ppermute | solution.py:104
  122.6 17.3 %collective-permute-start.28 = (bf16[512,768]{1,0:T(8,128)(2,1)S(1)}, bf16[512,768]{1,0:T(8,128)(2,1)S(1)}, u32[]{:S(2)}, u32[]{:S(2)}) collective-permute-start(bf16[512,768]{1,0:T(8,128)(2,1)S(1)} %copy-done.2), channel_id=1, source_target_pairs={{0,2},{1,3},{2,0},{3,1},{4,6},{5,7},{6,4},{7,5},{8,10},{9,11},{10,... | collective-permute-start | bytes 2359304 | tf_op jit(solution)/shard_map/ppermute | solution.py:104
  134.4 15.2 %collective-permute-start.30 = (bf16[4,96,768]{2,1,0:T(8,128)(2,1)S(1)}, bf16[4,96,768]{2,1,0:T(8,128)(2,1)S(1)}, u32[]{:S(2)}, u32[]{:S(2)}) collective-permute-start(bf16[4,96,768]{2,1,0:T(8,128)(2,1)S(1)} %bitcast.79), channel_id=1, source_target_pairs={{0,4},{1,5},{2,6},{3,7},{4,0},{5,1},{6,2},{7,3},{8,12},{9,13},{10,... | collective-permute-start | bytes 1769480 | tf_op jit(solution)/shard_map/ppermute | solution.py:101
  154.4 34.0 %collective-permute-start.34 = (bf16[2,4,48,1536]{3,2,1,0:T(8,128)(2,1)}, bf16[2,4,48,1536]{3,2,1,0:T(8,128)(2,1)S(1)}, u32[]{:S(2)}, u32[]{:S(2)}) collective-permute-start(bf16[2,4,48,1536]{3,2,1,0:T(8,128)(2,1)} %get-tuple-element.213), channel_id=1, source_target_pairs={{0,2},{1,5},{2,0},{3,7},{4,6},{5,1},{6,4},{7,3},{8,10},{9,13},{10,... | collective-permute-start | bytes 3538952 | tf_op jit(solution)/shard_map/ppermute | solution.py:119
  154.7 33.7 %collective-permute-start.38 = (bf16[4,96,768]{2,1,0:T(8,128)(2,1)}, bf16[4,96,768]{2,1,0:T(8,128)(2,1)}, u32[]{:S(2)}, u32[]{:S(2)}) collective-permute-start(bf16[4,96,768]{2,1,0:T(8,128)(2,1)} %bitcast.33), channel_id=1, source_target_pairs={{0,4},{1,5},{2,6},{3,7},{4,0},{5,1},{6,2},{7,3},{8,12},{9,13},{10,... | collective-permute-start | bytes 1769480 | tf_op jit(solution)/shard_map/ppermute | solution.py:101
  161.5 40.1 %collective-permute-start.40 = (bf16[512,768]{1,0:T(8,128)(2,1)}, bf16[512,768]{1,0:T(8,128)(2,1)}, u32[]{:S(2)}, u32[]{:S(2)}) collective-permute-start(bf16[512,768]{1,0:T(8,128)(2,1)} %get-tuple-element.238.pre_a), channel_id=1, source_target_pairs={{0,2},{1,3},{2,0},{3,1},{4,6},{5,7},{6,4},{7,5},{8,10},{9,11},{10,... | collective-permute-start | bytes 2359304 | tf_op jit(solution)/shard_map/ppermute | solution.py:104
  163.4 25.0 %collective-permute-start.36 = (bf16[96,768]{1,0:T(8,128)(2,1)}, bf16[96,768]{1,0:T(8,128)(2,1)}, u32[]{:S(2)}, u32[]{:S(2)}) collective-permute-start(bf16[96,768]{1,0:T(8,128)(2,1)} %get-tuple-element.223), channel_id=1, source_target_pairs={{0,16},{1,17},{2,18},{3,19},{4,20},{5,21},{6,22},{7,23},{8,24},{9,... | collective-permute-start | bytes 442376 | tf_op jit(solution)/shard_map/ppermute | solution.py:107
  165.6 22.8 %collective-permute-start.37 = (bf16[96,768]{1,0:T(8,128)(2,1)}, bf16[96,768]{1,0:T(8,128)(2,1)}, u32[]{:S(2)}, u32[]{:S(2)}) collective-permute-start(bf16[96,768]{1,0:T(8,128)(2,1)} %get-tuple-element.224), channel_id=1, source_target_pairs={{0,24},{1,25},{2,26},{3,27},{4,28},{5,29},{6,30},{7,31},{8,0},{9,1... | collective-permute-start | bytes 442376 | tf_op jit(solution)/shard_map/ppermute | solution.py:107
  189.3 17.5 %collective-permute-start.39 = (bf16[4,48,1536]{2,1,0:T(8,128)(2,1)S(1)}, bf16[4,48,1536]{2,1,0:T(8,128)(2,1)S(1)}, u32[]{:S(2)}, u32[]{:S(2)}) collective-permute-start(bf16[4,48,1536]{2,1,0:T(8,128)(2,1)S(1)} %bitcast.80), channel_id=1, source_target_pairs={{0,4},{1,3},{2,6},{3,1},{4,0},{5,7},{6,2},{7,5},{8,12},{9,11},{10,... | collective-permute-start | bytes 1769480 | tf_op jit(solution)/shard_map/ppermute | solution.py:112
  191.6 10.0 %collective-permute-start.41 = (bf16[96,768]{1,0:T(8,128)(2,1)S(1)}, bf16[96,768]{1,0:T(8,128)(2,1)S(1)}, u32[]{:S(2)}, u32[]{:S(2)}) collective-permute-start(bf16[96,768]{1,0:T(8,128)(2,1)S(1)} %get-tuple-element.233), channel_id=1, source_target_pairs={{0,8},{1,9},{2,10},{3,11},{4,12},{5,13},{6,14},{7,15},{8,16},{9,17... | collective-permute-start | bytes 442376 | tf_op jit(solution)/shard_map/ppermute | solution.py:107
  196.7 10.1 %collective-permute-start.42 = (bf16[96,768]{1,0:T(8,128)(2,1)S(1)}, bf16[96,768]{1,0:T(8,128)(2,1)S(1)}, u32[]{:S(2)}, u32[]{:S(2)}) collective-permute-start(bf16[96,768]{1,0:T(8,128)(2,1)S(1)} %get-tuple-element.234), channel_id=1, source_target_pairs={{0,16},{1,17},{2,18},{3,19},{4,20},{5,21},{6,22},{7,23},{8,24},{9,... | collective-permute-start | bytes 442376 | tf_op jit(solution)/shard_map/ppermute | solution.py:107
  209.8 11.6 %collective-permute-start.45 = (bf16[512,768]{1,0:T(8,128)(2,1)S(1)}, bf16[512,768]{1,0:T(8,128)(2,1)S(1)}, u32[]{:S(2)}, u32[]{:S(2)}) collective-permute-start(bf16[512,768]{1,0:T(8,128)(2,1)S(1)} %get-tuple-element.240.by_y), channel_id=1, source_target_pairs={{0,1},{1,0},{2,3},{3,2},{4,5},{5,4},{6,7},{7,6},{8,9},{9,8},{10,11... | collective-permute-start | bytes 2359304 | tf_op jit(solution)/shard_map/ppermute | solution.py:98
  210.3 26.1 %collective-permute-start.46 = (bf16[512,768]{1,0:T(8,128)(2,1)S(1)}, bf16[512,768]{1,0:T(8,128)(2,1)S(1)}, u32[]{:S(2)}, u32[]{:S(2)}) collective-permute-start(bf16[512,768]{1,0:T(8,128)(2,1)S(1)} %copy-done.1), channel_id=1, source_target_pairs={{0,2},{1,3},{2,0},{3,1},{4,6},{5,7},{6,4},{7,5},{8,10},{9,11},{10,... | collective-permute-start | bytes 2359304 | tf_op jit(solution)/shard_map/ppermute | solution.py:104
  211.1 12.6 %collective-permute-start.47 = (bf16[48,1536]{1,0:T(8,128)(2,1)S(1)}, bf16[48,1536]{1,0:T(8,128)(2,1)S(1)}, u32[]{:S(2)}, u32[]{:S(2)}) collective-permute-start(bf16[48,1536]{1,0:T(8,128)(2,1)S(1)} %get-tuple-element.242), channel_id=1, source_target_pairs={{0,8},{1,9},{2,10},{3,11},{4,12},{5,13},{6,14},{7,15},{8,16},{9,17... | collective-permute-start | bytes 442376 | tf_op jit(solution)/shard_map/ppermute | solution.py:107
  215.7 13.0 %collective-permute-start.48 = (bf16[48,1536]{1,0:T(8,128)(2,1)S(1)}, bf16[48,1536]{1,0:T(8,128)(2,1)S(1)}, u32[]{:S(2)}, u32[]{:S(2)}) collective-permute-start(bf16[48,1536]{1,0:T(8,128)(2,1)S(1)} %get-tuple-element.243), channel_id=1, source_target_pairs={{0,16},{1,17},{2,18},{3,19},{4,20},{5,21},{6,22},{7,23},{8,24},{9,... | collective-permute-start | bytes 442376 | tf_op jit(solution)/shard_map/ppermute | solution.py:107
  231.0 11.1 %collective-permute-start.50 = (bf16[512,768]{1,0:T(8,128)(2,1)S(1)}, bf16[512,768]{1,0:T(8,128)(2,1)S(1)}, u32[]{:S(2)}, u32[]{:S(2)}) collective-permute-start(bf16[512,768]{1,0:T(8,128)(2,1)S(1)} %copy-done.1), channel_id=1, source_target_pairs={{0,1},{1,0},{2,3},{3,2},{4,5},{5,4},{6,7},{7,6},{8,9},{9,8},{10,11... | collective-permute-start | bytes 2359304 | tf_op jit(solution)/shard_map/ppermute | solution.py:98
  231.5 12.8 %all-to-all-start.1 = ((f32[32,1,512]{2,1,0:T(1,128)}), f32[32,1,512]{2,1,0:T(1,128)S(1)}, u32[]{:S(2)}, u32[]{:S(2)}) async-start(f32[32,1,512]{2,1,0:T(1,128)} %get-tuple-element.249), calls=%async_computation.1 | async-start | bytes 131072 | tf_op jit(solution)/shard_map/all_to_all | solution.py:1118
  (56 other events, 712.9 us)

commit v4 on v3

--- a/solution.py
+++ b/solution.py
@@ -693,9 +693,19 @@
         owned(lambda m: line(8 * width + m * part, part)),
     )
     ins, outs = refs[: 4 * 4 + 3 * 3], refs[4 * 4 + 3 * 3 : -1]
+    attn = {}
+    if plan.direct:
+        mine, other = ins[3][...], ins[7][...]
+        low = jnp.where(meta[4] == 0, mine, other)
+        high = jnp.where(meta[4] == 0, other, mine)
+        for p in range(4):
+            at = slice(p * quarter, (p + 1) * quarter)
+            attn[p] = jnp.concatenate([low[:, at], high[:, at]], axis=0)
     for i, (rate, decay) in enumerate(rates):
         if i < 4:
             w_ref, m_ref, s_ref, g_ref = ins[4 * i : 4 * i + 4]
+            if plan.direct and i < 2:
+                g_ref = attn if i == 0 else {Ellipsis: attn[3].T}
         else:
             w_ref, m_ref, s_ref = ins[3 * i + 4 : 3 * i + 7]
             g_ref = {Ellipsis: small[i - 4]}
@@ -852,7 +862,7 @@
     e_spread = after(jnp.stack([e_unit] + e_z), attn_w[1])
     e_x = plan.along_x(e_spread)
     attn_w = attn_w + [plan.core(v) for v in attn_w]
-    attn_w[1] = after(attn_w[1], e_spread, r_z[0])
+    attn_w[1] = after(attn_w[1], e_spread)
 
     if not plan.direct:
         attn_w = [absolute_attn(plan, jnp.stack(attn_w[:2]), jnp.stack(attn_w[2:]), z, x, y, c)]
@@ -891,7 +901,7 @@
     )
 
     sl_far = plan.along_y(sl)
-    r_spread = jnp.stack([r_unit, r_z[0]] + [after(v, sl) for v in r_z[1:]])
+    r_spread = jnp.stack([r_unit] + [after(v, sl) for v in r_z])
     r_x = plan.along_x(r_spread)
     e_x = after(e_x, sl)
     ff_w = []
@@ -1026,8 +1036,8 @@
     attn_got[0] = after(attn_got[0], ig, e_got)
     attn_keep, attn_send = add_first(meta, attn_mine, attn_got)
     attn_got = plan.second(attn_send)
+    r_got = plan.along_x(after(r_send, attn_send))
     pre_far = plan.along_y(after(pre_near, attn_send))
-    r_got = plan.along_x(after(r_send, attn_send))
     e_parts = add_parts(meta, e_keep, after(e_got, attn_send))
     e_z = [e_parts[0]] + [plan.along_z(e_parts[k], k) for k in range(1, nz)]
     size = -(-(8 * width + hidden) // (LANES * plan.ndev)) * LANES
@@ -1043,29 +1053,14 @@
     got = lax.all_to_all(vectors, AXES, 0, 0, tiled=True)
     local = jnp.sum(got, axis=0)
 
-    attn_got = after(attn_got, local, *e_z, r_got)
+    attn_got = after(attn_got, local, r_got, *e_z)
     attn_keep, attn_send = add_parts(meta, attn_keep, attn_got)
-    r_parts = add_parts(meta, r_keep, after(r_got, attn_send))
+    attn_got = plan.first(attn_send)
+    r_got = after(r_got, attn_send)
+    r_parts = add_parts(meta, r_keep, r_got)
     r_z = [r_parts[0]] + [plan.along_z(r_parts[k], k) for k in range(1, nz)]
-    attn_got = plan.first(attn_send)
-
-    attn_parts = add_parts(meta, attn_keep, after(attn_got, pre_far, *r_z))
-
-    ff_in = [*e_z, *r_z]
-    grad_expand, grad_reduce, ff_square = call(
-        ff_total_kernel,
-        "ff_total",
-        (1,),
-        [(v, *whole(v.shape)) for v in ff_in],
-        [
-            (SDS((rows, part), f32), *whole((rows, part))),
-            (SDS((rows, part), f32), *whole((rows, part))),
-            (SDS((1, 1), f32), *whole((1, 1))),
-        ],
-        [],
-    )(meta, *ff_in)
-
-    pre_in = after(pre_near, attn_parts[0])
+
+    pre_in, pre_far = after(pre_near, attn_send), after(pre_far, attn_send)
     out, out_pair = call(
         out_kernel,
         "out_sum",
@@ -1080,10 +1075,7 @@
         [(SDS((count, width), bf16), *chunk(width))] * 2,
         [],
     )(meta, pre_in, fed_far, pre_far, fed_send, norm_params)
-    ig = after(ig, attn_parts[0])
-    ig_pair = plan.along_y(ig)
-    attn_z = [attn_parts[0]] + [plan.along_z(attn_parts[k], k) for k in range(1, nz)]
-    total_in = attn_z + [ff_square, local]
+
     def everywhere(block, by_y):
         blocks = [block, by_y, plan.core(block), plan.core(by_y)]
         return call(
@@ -1096,7 +1088,26 @@
         )(meta, *blocks)[0]
 
     outputs = everywhere(out, out_pair)
-    total_in[-1] = after(total_in[-1], outputs)
+    attn_parts = add_parts(meta, attn_keep, after(attn_got, outputs, *r_z))
+
+    ff_in = [*e_z, *r_z]
+    grad_expand, grad_reduce, ff_square = call(
+        ff_total_kernel,
+        "ff_total",
+        (1,),
+        [(v, *whole(v.shape)) for v in ff_in],
+        [
+            (SDS((rows, part), f32), *whole((rows, part))),
+            (SDS((rows, part), f32), *whole((rows, part))),
+            (SDS((1, 1), f32), *whole((1, 1))),
+        ],
+        [],
+    )(meta, *ff_in)
+
+    ig = after(ig, attn_parts[0])
+    ig_pair = plan.along_y(ig)
+    attn_z = [attn_parts[0]] + [plan.along_z(attn_parts[k], k) for k in range(1, nz)]
+    total_in = attn_z + [ff_square, local]
     keep, send, payload = call(
         total_kernel,
         "total",
@@ -1117,15 +1128,16 @@
     input_gradient = everywhere(ig, ig_pair)
     got = after(lax.all_to_all(payload, AXES, 0, 0, tiled=True), input_gradient)
 
-    low, high = jnp.where(core_zero, keep, by_core), jnp.where(core_zero, by_core, keep)
-    shard = jnp.concatenate([low, high], axis=0).reshape(rows, 4, quarter)
-    grad_triple = shard[:, :3].transpose(1, 0, 2)
-    grad_outward = shard[:, 3].T
+    if not plan.direct:
+        low, high = jnp.where(core_zero, keep, by_core), jnp.where(core_zero, by_core, keep)
+        shard = jnp.concatenate([low, high], axis=0).reshape(rows, 4, quarter)
+        keep = shard[:, :3].transpose(1, 0, 2)
+        by_core = shard[:, 3].T
 
     matrix, vector = (LR_MATRIX, DECAY), (LR_VECTOR, 0.0)
     groups = [
-        [triple_weight, triple_first, triple_second, grad_triple],
-        [outward_weight, outward_first, outward_second, grad_outward],
+        [triple_weight, triple_first, triple_second, keep],
+        [outward_weight, outward_first, outward_second, by_core],
         [expand_weight, expand_first, expand_second, grad_expand],
         [reduce_weight.T, reduce_first.T, reduce_second.T, grad_reduce],
         [norm_params, norm_first, norm_second],

time: 251 us -> 244 us (0.972)
  starting transfers between devices: 65.5 us -> 56.9 us
  waiting for transfers between devices: 64.1 us -> 72.1 us
  local copies, waits for them, and re-layouts: 10.1 us -> 6.08 us
    ppermute x18, starting transfers between devices: 39.7 us -> 28.2 us  [along_z(): lax.ppermute(value, AXES, self.perm(lambda z, x, y, c: ((z + step) % self...]
    all_to_all x1, waiting for transfers between devices: 0.01 us -> 5.13 us  [per_device(): got = after(lax.all_to_all(payload, AXES, 0, 0, tiled=True), input_gradient)]
    transpose x3 -> x0, local copies, waits for them, and re-layouts: 3.4 us -> none  [the longest x2 1.87 us: per_device(): grad_triple = shard[:, :3].transpose(1, 0, 2)]
  transfers between devices with their start and end apart: 54 -> 54, of which waited for: 17 -> 19; matrix products, arithmetic and copies ran while one was open for 5% -> 2% of each run, Pallas kernels for 25% -> 25%
where the time goes in v4:
time: 244 us; the launch traced here: 243 us
  Pallas kernels  83 us (34%)
  waiting for transfers between devices  72.1 us (30%)
  starting transfers between devices  56.9 us (23%)
  blocking collectives  18.6 us (8%)
  local copies, waits for them, and re-layouts  6.08 us (2%)
  other arithmetic  4.55 us (2%)
    pallas_call x9, Pallas kernels, local_call(): return kernel_call(meta, *map(place, ins))  60.3 us
    ppermute x18, waiting for transfers between devices, along_z(): lax.ppermute(value, AXES, self.perm(lambda z, x, y, c: ((z + step) % self...  37.6 us
    ppermute x18, starting transfers between devices, along_z(): lax.ppermute(value, AXES, self.perm(lambda z, x, y, c: ((z + step) % self...  28.2 us
    all_to_all x1, blocking collectives, per_device(): got = lax.all_to_all(vectors, AXES, 0, 0, tiled=True)  18.6 us
    ppermute x4, waiting for transfers between devices, along_x(): lax.ppermute(value, AXES, self.perm(lambda z, x, y, c: (z, 1 - x, y, c)))  14.4 us
    ppermute x6, starting transfers between devices, along_y(): lax.ppermute(value, AXES, self.perm(lambda z, x, y, c: (z, x, 1 - y, c)))  8.71 us
    ppermute x6, waiting for transfers between devices, along_y(): lax.ppermute(value, AXES, self.perm(lambda z, x, y, c: (z, x, 1 - y, c)))  8.62 us
    all_to_all x1, starting transfers between devices, per_device(): got = after(lax.all_to_all(payload, AXES, 0, 0, tiled=True), input_gradient)  6.37 us
  transfers between devices with their start and end apart: 54, of which 19 were waited for; matrix products, arithmetic and copies ran while one was open for 2% of the time, Pallas kernels for 25%

profile of v4, /device:TPU:0, one launch (start us, length us, event | category | flops | bytes accessed | tf_op | source)
XLA Modules:
  0.0 242.9 jit_solution(5154689375278987159)
XLA Ops:
  4.4 5.0 %collective-permute-start.3 = (bf16[48,1536]{1,0:T(8,128)(2,1)S(1)}, bf16[48,1536]{1,0:T(8,128)(2,1)S(1)}, u32[]{:S(2)}, u32[]{:S(2)}) collective-permute-start(bf16[48,1536]{1,0:T(8,128)(2,1)S(1)} %bitcast.89), channel_id=1, source_target_pairs={{0,24},{1,25},{2,26},{3,27},{4,28},{5,29},{6,30},{7,31},{8,0},{9,1... | collective-permute-start | bytes 442376 | tf_op jit(solution)/shard_map/ppermute | solution.py:107
  10.7 3.0 %collective-permute-done.3 = bf16[48,1536]{1,0:T(8,128)(2,1)S(1)} collective-permute-done((bf16[48,1536]{1,0:T(8,128)(2,1)S(1)}, bf16[48,1536]{1,0:T(8,128)(2,1)S(1)}, u32[]{:S(2)}, u32[]{:S(2)}) %collective-permute-start.3) | collective-permute-done | bytes 147488 | tf_op jit(solution)/shard_map/ppermute | solution.py:107
  13.7 8.5 %collective-permute-done.2 = bf16[48,1536]{1,0:T(8,128)(2,1)S(1)} collective-permute-done((bf16[48,1536]{1,0:T(8,128)(2,1)S(1)}, bf16[48,1536]{1,0:T(8,128)(2,1)S(1)}, u32[]{:S(2)}, u32[]{:S(2)}) %collective-permute-start.2) | collective-permute-done | bytes 147488 | tf_op jit(solution)/shard_map/ppermute | solution.py:107
  29.7 2.6 %collective-permute-done.4 = bf16[4,48,1536]{2,1,0:T(8,128)(2,1)S(1)} collective-permute-done((bf16[4,48,1536]{2,1,0:T(8,128)(2,1)S(1)}, bf16[4,48,1536]{2,1,0:T(8,128)(2,1)S(1)}, u32[]{:S(2)}, u32[]{:S(2)}) %collective-permute-start.4) | collective-permute-done | bytes 589856 | tf_op jit(solution)/shard_map/ppermute | solution.py:112
  38.7 3.4 %collective-permute-done.10 = bf16[96,768]{1,0:T(8,128)(2,1)S(1)} collective-permute-done((bf16[96,768]{1,0:T(8,128)(2,1)S(1)}, bf16[96,768]{1,0:T(8,128)(2,1)S(1)}, u32[]{:S(2)}, u32[]{:S(2)}) %collective-permute-start.10) | collective-permute-done | bytes 147488 | tf_op jit(solution)/shard_map/ppermute | solution.py:107
  42.0 5.1 %collective-permute-done.9 = bf16[96,768]{1,0:T(8,128)(2,1)S(1)} collective-permute-done((bf16[96,768]{1,0:T(8,128)(2,1)S(1)}, bf16[96,768]{1,0:T(8,128)(2,1)S(1)}, u32[]{:S(2)}, u32[]{:S(2)}) %collective-permute-start.9) | collective-permute-done | bytes 147488 | tf_op jit(solution)/shard_map/ppermute | solution.py:107
  47.2 3.5 %collective-permute-done.8.refs_1_ = bf16[2,4,48,1536]{3,2,1,0:T(8,128)(2,1)} collective-permute-done((bf16[2,4,48,1536]{3,2,1,0:T(8,128)(2,1)S(1)}, bf16[2,4,48,1536]{3,2,1,0:T(8,128)(2,1)}, u32[]{:S(2)}, u32[]{:S(2)}) %collective-permute-start.8) | collective-permute-done | bytes 1179680 | tf_op jit(solution)/shard_map/ppermute | solution.py:119
  57.4 13.0 %attn_fwd.1 = (bf16[512,768]{1,0:T(8,128)(2,1)}, f32[512,768]{1,0:T(8,128)S(1)}, bf16[512,768]{1,0:T(8,128)(2,1)S(1)}, bf16[2,512,1152]{2,1,0:T(8,128)(2,1)S(1)}...) custom-call(s32[6]{0:T(128)S(1)} %stack.94.meta, ...), custom_call_target="tpu_custom_call" | custom-call | flops 1 | bytes 1 | tf_op jit(solution)/shard_map/attn_fwd/pallas_call | solution.py:753
  73.2 12.0 %collective-permute-done.20.refs_5_ = bf16[4,96,768]{2,1,0:T(8,128)(2,1)S(1)} collective-permute-done((bf16[4,96,768]{2,1,0:T(8,128)(2,1)S(1)}, bf16[4,96,768]{2,1,0:T(8,128)(2,1)S(1)}, u32[]{:S(2)}, u32[]{:S(2)}) %collective-permute-start.20) | collective-permute-done | bytes 589856 | tf_op jit(solution)/shard_map/ppermute | solution.py:101
  85.2 4.6 %collective-permute-done.13.sl_ref.sl_b = bf16[512,768]{1,0:T(8,128)(2,1)S(1)} collective-permute-done((bf16[512,768]{1,0:T(8,128)(2,1)}, bf16[512,768]{1,0:T(8,128)(2,1)S(1)}, u32[]{:S(2)}, u32[]{:S(2)}) %collective-permute-start.13) | collective-permute-done | bytes 786464 | tf_op jit(solution)/shard_map/ppermute | solution.py:104
  90.7 10.1 %ff_far.1 = (bf16[512,768]{1,0:T(8,128)(2,1)}, bf16[512,768]{1,0:T(8,128)(2,1)}, bf16[2,512,768]{2,1,0:T(8,128)(2,1)S(1)}, bf16[2,512,768]{2,1,0:T(8,128)(2,1)S(...) custom-call(s32[6]{0:T(128)S(1)} %stack.94.meta, ...), custom_call_target="tpu_custom_call" | custom-call | flops 1 | bytes 1 | tf_op jit(solution)/shard_map/ff_far/pallas_call | solution.py:753
  102.4 8.1 %ff_near.1 = (bf16[512,768]{1,0:T(8,128)(2,1)S(1)}, bf16[512,768]{1,0:T(8,128)(2,1)}, bf16[2,512,768]{2,1,0:T(8,128)(2,1)S(1)}, bf16[2,512,768]{2,1,0:T(8,128)(2...) custom-call(s32[6]{0:T(128)S(1)} %stack.94.meta, bf16[512,768]{1,0:T(8,128)(2,1)S(1)} %copy-done, ...), custom_call_target="tpu_custom_call" | custom-call | flops 1 | bytes 1 | tf_op jit(solution)/shard_map/ff_near/pallas_call | solution.py:753
  110.5 7.4 %ff_grad.1 = (bf16[4,96,768]{2,1,0:T(8,128)(2,1)}, bf16[4,96,768]{2,1,0:T(8,128)(2,1)}, bf16[4,96,768]{2,1,0:T(8,128)(2,1)}, bf16[4,96,768]{2,1,0:T(8,128)(2,1)}...) custom-call(s32[6]{0:T(128)S(1)} %stack.94.meta, ...), custom_call_target="tpu_custom_call" | custom-call | flops 1 | bytes 1 | tf_op jit(solution)/shard_map/ff_grad/pallas_call | solution.py:753
  121.4 7.2 %attn_bwd.1 = (bf16[2,512,1152]{2,1,0:T(8,128)(2,1)S(1)}, bf16[512,768]{1,0:T(8,128)(2,1)S(1)}, f32[512,768]{1,0:T(8,128)S(1)}, f32[8,768]{1,0:T(8,128)S(1)}, f32[2,768]{1,0:T(2,128)S(1)}) custom-call(s32[6]{0:T(128)S(1)} %stack.94.meta, bf16[512,768]{1,0:T(8,128)(2,1)S(1)} %get-tuple-element.172.sga_ref, ...), custom_call_target="tpu_custom_call" | custom-call | flops 1 | bytes 1 | tf_op jit(solution)/shard_map/attn_bwd/pallas_call | solution.py:753
  131.9 5.0 %attn_grad.1 = (bf16[2,2,48,1536]{3,2,1,0:T(8,128)(2,1)S(1)}, bf16[2,2,48,1536]{3,2,1,0:T(8,128)(2,1)S(1)}, bf16[2,2,48,1536]{3,2,1,0:T(8,128)(2,1)S(1)}, bf16[2...) custom-call(s32[6]{0:T(128)S(1)} %stack.94.meta, ...), custom_call_target="tpu_custom_call" | custom-call | flops 1 | bytes 1 | tf_op jit(solution)/shard_map/attn_grad/pallas_call | solution.py:753
  137.9 5.3 %input_grad.1 = (bf16[512,768]{1,0:T(8,128)(2,1)}, f32[8,768]{1,0:T(8,128)S(1)}) custom-call(s32[6]{0:T(128)S(1)} %stack.94.meta, bf16[2048,768]{1,0:T(8,128)(2,1)} %x_all.3, f32[512,768]{1,0:T(8,128)S(1)} %get-tuple-element.207.mg_ref, f32[6,768]{1,0:T(8,128)S(1)} %copy-done.5, bf16[2,512,1152]{2,1,0:T(8,128)(2,1)S(1)} %get-tuple-element.208.dqkv_ref, ...), custom_call_target="tpu_custom_call" | custom-call | flops 1 | bytes 1 | tf_op jit(solution)/shard_map/input_grad/pallas_call | solution.py:753
  143.2 2.4 collective-permute-done.30.right
  147.0 3.3 %add_first.1 = (bf16[2,4,48,1536]{3,2,1,0:T(8,128)(2,1)S(1)}, bf16[2,4,48,1536]{3,2,1,0:T(8,128)(2,1)}) custom-call(s32[6]{0:T(128)S(1)} %stack.94.meta, bf16[2,2,48,1536]{3,2,1,0:T(8,128)(2,1)S(1)} %get-tuple-element.199.refs_0_, bf16[2,2,48,1536]{3,2,1,0:T(8,128)(2,1)S(1)} %get-tuple-element.200.refs_1_, ...), custom_call_target="tpu_custom_call" | custom-call | flops 1 | bytes 1 | tf_op jit(solution)/shard_map/add_first/pallas_call | solution.py:753
  155.6 2.5 %collective-permute-start.37 = (bf16[96,768]{1,0:T(8,128)(2,1)}, bf16[96,768]{1,0:T(8,128)(2,1)}, u32[]{:S(2)}, u32[]{:S(2)}) collective-permute-start(bf16[96,768]{1,0:T(8,128)(2,1)} %get-tuple-element.226), channel_id=1, source_target_pairs={{0,16},{1,17},{2,18},{3,19},{4,20},{5,21},{6,22},{7,23},{8,24},{9,... | collective-permute-start | bytes 442376 | tf_op jit(solution)/shard_map/ppermute | solution.py:107
  158.1 5.3 %collective-permute-done.36.refs_1_ = bf16[96,768]{1,0:T(8,128)(2,1)S(1)} collective-permute-done((bf16[96,768]{1,0:T(8,128)(2,1)S(1)}, bf16[96,768]{1,0:T(8,128)(2,1)S(1)}, u32[]{:S(2)}, u32[]{:S(2)}) %collective-permute-start.36) | collective-permute-done | bytes 147488 | tf_op jit(solution)/shard_map/ppermute | solution.py:107
  165.1 18.6 %all_to_all.10 = f32[32,1,384]{2,1,0:T(1,128)S(1)} all-to-all(f32[32,1,384]{2,1,0:T(1,128)} %vectors.1), channel_id=1, replica_groups=mesh['dp'=8,'mp'=4] {'dp','mp'}, dimensions={0} | all-to-all | bytes 98304 | tf_op jit(solution)/shard_map/all_to_all | solution.py:1053
  190.4 2.5 %collective-permute-start.44 = (bf16[96,768]{1,0:T(8,128)(2,1)S(1)}, bf16[96,768]{1,0:T(8,128)(2,1)S(1)}, u32[]{:S(2)}, u32[]{:S(2)}) collective-permute-start(bf16[96,768]{1,0:T(8,128)(2,1)S(1)} %get-tuple-element.240), channel_id=1, source_target_pairs={{0,16},{1,17},{2,18},{3,19},{4,20},{5,21},{6,22},{7,23},{8,24},{9,... | collective-permute-start | bytes 442376 | tf_op jit(solution)/shard_map/ppermute | solution.py:107
  194.6 2.2 place.2
  198.5 5.2 %collective-permute-done.44.refs_6_ = bf16[96,768]{1,0:T(8,128)(2,1)S(1)} collective-permute-done((bf16[96,768]{1,0:T(8,128)(2,1)S(1)}, bf16[96,768]{1,0:T(8,128)(2,1)S(1)}, u32[]{:S(2)}, u32[]{:S(2)}) %collective-permute-start.44) | collective-permute-done | bytes 147488 | tf_op jit(solution)/shard_map/ppermute | solution.py:107
  205.5 3.4 %collective-permute-start.47 = (bf16[48,1536]{1,0:T(8,128)(2,1)S(1)}, bf16[48,1536]{1,0:T(8,128)(2,1)S(1)}, u32[]{:S(2)}, u32[]{:S(2)}) collective-permute-start(bf16[48,1536]{1,0:T(8,128)(2,1)S(1)} %get-tuple-element.245), channel_id=1, source_target_pairs={{0,8},{1,9},{2,10},{3,11},{4,12},{5,13},{6,14},{7,15},{8,16},{9,17... | collective-permute-start | bytes 442376 | tf_op jit(solution)/shard_map/ppermute | solution.py:107
  211.3 2.4 ff_total.1
  213.7 5.2 %collective-permute-done.48.refs_2_ = bf16[48,1536]{1,0:T(8,128)(2,1)S(1)} collective-permute-done((bf16[48,1536]{1,0:T(8,128)(2,1)S(1)}, bf16[48,1536]{1,0:T(8,128)(2,1)S(1)}, u32[]{:S(2)}, u32[]{:S(2)}) %collective-permute-start.48) | collective-permute-done | bytes 147488 | tf_op jit(solution)/shard_map/ppermute | solution.py:107
  218.9 2.3 total.1
  223.3 6.4 %all-to-all-start.1 = ((f32[32,1,512]{2,1,0:T(1,128)}), f32[32,1,512]{2,1,0:T(1,128)S(1)}, u32[]{:S(2)}, u32[]{:S(2)}) async-start(f32[32,1,512]{2,1,0:T(1,128)} %get-tuple-element.251), calls=%async_computation.1 | async-start | bytes 131072 | tf_op jit(solution)/shard_map/all_to_all | solution.py:1129
  229.7 2.2 place.3
  231.9 5.1 %all-to-all-done.1.got = f32[32,1,512]{2,1,0:T(1,128)S(1)} async-done(((f32[32,1,512]{2,1,0:T(1,128)}), f32[32,1,512]{2,1,0:T(1,128)S(1)}, u32[]{:S(2)}, u32[]{:S(2)}) %all-to-all-start.1) | async-done | bytes 65568 | tf_op jit(solution)/shard_map/all_to_all | solution.py:1129
  237.6 5.1 %adam.1 = (f32[3,96,192]{2,1,0:T(8,128)}, f32[3,96,192]{2,1,0:T(8,128)}, f32[3,96,192]{2,1,0:T(8,128)}, f32[192,96]{1,0:T(8,128)}, f32[192,96]{1,0:T(8,128)}, /*...) custom-call(s32[6]{0:T(128)} %copy-done.14, ...), custom_call_target="tpu_custom_call" | custom-call | flops 1 | bytes 1 | tf_op jit(solution)/shard_map/adam/pallas_call | solution.py:1150
  (201 shorter events, 63.6 us)
Async XLA Ops:
  9.4 12.8 %collective-permute-start.2 = (bf16[48,1536]{1,0:T(8,128)(2,1)S(1)}, bf16[48,1536]{1,0:T(8,128)(2,1)S(1)}, u32[]{:S(2)}, u32[]{:S(2)}) collective-permute-start(bf16[48,1536]{1,0:T(8,128)(2,1)S(1)} %bitcast.90), channel_id=1, source_target_pairs={{0,16},{1,17},{2,18},{3,19},{4,20},{5,21},{6,22},{7,23},{8,24},{9,... | collective-permute-start | bytes 442376 | tf_op jit(solution)/shard_map/ppermute | solution.py:107
  9.4 12.8 %collective-permute-start.1 = (bf16[48,1536]{1,0:T(8,128)(2,1)S(1)}, bf16[48,1536]{1,0:T(8,128)(2,1)S(1)}, u32[]{:S(2)}, u32[]{:S(2)}) collective-permute-start(bf16[48,1536]{1,0:T(8,128)(2,1)S(1)} %bitcast.91), channel_id=1, source_target_pairs={{0,8},{1,9},{2,10},{3,11},{4,12},{5,13},{6,14},{7,15},{8,16},{9,17... | collective-permute-start | bytes 442376 | tf_op jit(solution)/shard_map/ppermute | solution.py:107
  22.4 9.9 %collective-permute-start.4 = (bf16[4,48,1536]{2,1,0:T(8,128)(2,1)S(1)}, bf16[4,48,1536]{2,1,0:T(8,128)(2,1)S(1)}, u32[]{:S(2)}, u32[]{:S(2)}) collective-permute-start(bf16[4,48,1536]{2,1,0:T(8,128)(2,1)S(1)} %get-tuple-element.279), channel_id=1, source_target_pairs={{0,4},{1,3},{2,6},{3,1},{4,0},{5,7},{6,2},{7,5},{8,12},{9,11},{10,... | collective-permute-start | bytes 1769480 | tf_op jit(solution)/shard_map/ppermute | solution.py:112
  34.3 16.4 %collective-permute-start.8 = (bf16[2,4,48,1536]{3,2,1,0:T(8,128)(2,1)S(1)}, bf16[2,4,48,1536]{3,2,1,0:T(8,128)(2,1)}, u32[]{:S(2)}, u32[]{:S(2)}) collective-permute-start(bf16[2,4,48,1536]{3,2,1,0:T(8,128)(2,1)S(1)} %pad_maximum_fusion.refs_0_), channel_id=1, source_target_pairs={{0,2},{1,5},{2,0},{3,7},{4,6},{5,1},{6,4},{7,3},{8,10},{9,13},{10,... | collective-permute-start | bytes 3538952 | tf_op jit(solution)/shard_map/ppermute | solution.py:119
  37.2 9.9 %collective-permute-start.9 = (bf16[96,768]{1,0:T(8,128)(2,1)S(1)}, bf16[96,768]{1,0:T(8,128)(2,1)S(1)}, u32[]{:S(2)}, u32[]{:S(2)}) collective-permute-start(bf16[96,768]{1,0:T(8,128)(2,1)S(1)} %convert_element_type.18), channel_id=1, source_target_pairs={{0,16},{1,17},{2,18},{3,19},{4,20},{5,21},{6,22},{7,23},{8,24},{9,... | collective-permute-start | bytes 442376 | tf_op jit(solution)/shard_map/ppermute | solution.py:107
  38.7 17.1 %collective-permute-start.11 = (bf16[2,4,48,1536]{3,2,1,0:T(8,128)(2,1)S(1)}, bf16[2,4,48,1536]{3,2,1,0:T(8,128)(2,1)}, u32[]{:S(2)}, u32[]{:S(2)}) collective-permute-start(bf16[2,4,48,1536]{3,2,1,0:T(8,128)(2,1)S(1)} %pad_maximum_fusion.refs_0_), channel_id=1, source_target_pairs={{0,1},{1,0},{2,3},{3,2},{4,5},{5,4},{6,7},{7,6},{8,9},{9,8},{10,11... | collective-permute-start | bytes 3538952 | tf_op jit(solution)/shard_map/ppermute | solution.py:98
  50.7 19.6 %collective-permute-start.19 = (bf16[96,768]{1,0:T(8,128)(2,1)S(1)}, bf16[96,768]{1,0:T(8,128)(2,1)S(1)}, u32[]{:S(2)}, u32[]{:S(2)}) collective-permute-start(bf16[96,768]{1,0:T(8,128)(2,1)S(1)} %bitcast_convert_fusion), channel_id=1, source_target_pairs={{0,24},{1,25},{2,26},{3,27},{4,28},{5,29},{6,30},{7,31},{8,0},{9,1... | collective-permute-start | bytes 442376 | tf_op jit(solution)/shard_map/ppermute | solution.py:107
  52.1 18.3 %collective-permute-start.18 = (bf16[96,768]{1,0:T(8,128)(2,1)S(1)}, bf16[96,768]{1,0:T(8,128)(2,1)S(1)}, u32[]{:S(2)}, u32[]{:S(2)}) collective-permute-start(bf16[96,768]{1,0:T(8,128)(2,1)S(1)} %bitcast_convert_fusion), channel_id=1, source_target_pairs={{0,16},{1,17},{2,18},{3,19},{4,20},{5,21},{6,22},{7,23},{8,24},{9,... | collective-permute-start | bytes 442376 | tf_op jit(solution)/shard_map/ppermute | solution.py:107
  53.6 16.8 %collective-permute-start.17 = (bf16[96,768]{1,0:T(8,128)(2,1)S(1)}, bf16[96,768]{1,0:T(8,128)(2,1)S(1)}, u32[]{:S(2)}, u32[]{:S(2)}) collective-permute-start(bf16[96,768]{1,0:T(8,128)(2,1)S(1)} %bitcast_convert_fusion), channel_id=1, source_target_pairs={{0,8},{1,9},{2,10},{3,11},{4,12},{5,13},{6,14},{7,15},{8,16},{9,17... | collective-permute-start | bytes 442376 | tf_op jit(solution)/shard_map/ppermute | solution.py:107
  55.8 16.8 %collective-permute-start.14 = (bf16[4,96,768]{2,1,0:T(8,128)(2,1)S(1)}, bf16[4,96,768]{2,1,0:T(8,128)(2,1)S(1)}, u32[]{:S(2)}, u32[]{:S(2)}) collective-permute-start(bf16[4,96,768]{2,1,0:T(8,128)(2,1)S(1)} %pad_maximum_fusion.2.refs_0_), channel_id=1, source_target_pairs={{0,4},{1,5},{2,6},{3,7},{4,0},{5,1},{6,2},{7,3},{8,12},{9,13},{10,... | collective-permute-start | bytes 1769480 | tf_op jit(solution)/shard_map/ppermute | solution.py:101
  70.5 14.7 %collective-permute-start.20 = (bf16[4,96,768]{2,1,0:T(8,128)(2,1)S(1)}, bf16[4,96,768]{2,1,0:T(8,128)(2,1)S(1)}, u32[]{:S(2)}, u32[]{:S(2)}) collective-permute-start(bf16[4,96,768]{2,1,0:T(8,128)(2,1)S(1)} %pad_maximum_fusion.3.refs_4_), channel_id=1, source_target_pairs={{0,4},{1,5},{2,6},{3,7},{4,0},{5,1},{6,2},{7,3},{8,12},{9,13},{10,... | collective-permute-start | bytes 1769480 | tf_op jit(solution)/shard_map/ppermute | solution.py:101
  71.1 18.8 %collective-permute-start.13 = (bf16[512,768]{1,0:T(8,128)(2,1)}, bf16[512,768]{1,0:T(8,128)(2,1)S(1)}, u32[]{:S(2)}, u32[]{:S(2)}) collective-permute-start(bf16[512,768]{1,0:T(8,128)(2,1)} %get-tuple-element.161.sl_ref.sl_a), channel_id=1, source_target_pairs={{0,2},{1,3},{2,0},{3,1},{4,6},{5,7},{6,4},{7,5},{8,10},{9,11},{10,... | collective-permute-start | bytes 2359304 | tf_op jit(solution)/shard_map/ppermute | solution.py:104
  72.6 12.6 %collective-permute-start.15 = (bf16[4,96,768]{2,1,0:T(8,128)(2,1)S(1)}, bf16[4,96,768]{2,1,0:T(8,128)(2,1)S(1)}, u32[]{:S(2)}, u32[]{:S(2)}) collective-permute-start(bf16[4,96,768]{2,1,0:T(8,128)(2,1)S(1)} %pad_maximum_fusion.2.refs_0_), channel_id=1, source_target_pairs={{0,1},{1,0},{2,3},{3,2},{4,5},{5,4},{6,7},{7,6},{8,9},{9,8},{10,11... | collective-permute-start | bytes 1769480 | tf_op jit(solution)/shard_map/ppermute | solution.py:98
  72.6 12.6 %collective-permute-start.16 = (bf16[4,96,768]{2,1,0:T(8,128)(2,1)S(1)}, bf16[4,96,768]{2,1,0:T(8,128)(2,1)S(1)}, u32[]{:S(2)}, u32[]{:S(2)}) collective-permute-start(bf16[4,96,768]{2,1,0:T(8,128)(2,1)S(1)} %collective-permute-done.14.refs_1_), channel_id=1, source_target_pairs={{0,1},{1,0},{2,3},{3,2},{4,5},{5,4},{6,7},{7,6},{8,9},{9,8},{10,11... | collective-permute-start | bytes 1769480 | tf_op jit(solution)/shard_map/ppermute | solution.py:98
  73.1 12.1 %collective-permute-start.21 = (bf16[4,96,768]{2,1,0:T(8,128)(2,1)S(1)}, bf16[4,96,768]{2,1,0:T(8,128)(2,1)S(1)}, u32[]{:S(2)}, u32[]{:S(2)}) collective-permute-start(bf16[4,96,768]{2,1,0:T(8,128)(2,1)S(1)} %pad_maximum_fusion.3.refs_4_), channel_id=1, source_target_pairs={{0,1},{1,0},{2,3},{3,2},{4,5},{5,4},{6,7},{7,6},{8,9},{9,8},{10,11... | collective-permute-start | bytes 1769480 | tf_op jit(solution)/shard_map/ppermute | solution.py:98
  100.8 18.0 %collective-permute-start.23 = (bf16[512,768]{1,0:T(8,128)(2,1)}, bf16[512,768]{1,0:T(8,128)(2,1)S(1)}, u32[]{:S(2)}, u32[]{:S(2)}) collective-permute-start(bf16[512,768]{1,0:T(8,128)(2,1)} %get-tuple-element.173), channel_id=1, source_target_pairs={{0,2},{1,3},{2,0},{3,1},{4,6},{5,7},{6,4},{7,5},{8,10},{9,11},{10,... | collective-permute-start | bytes 2359304 | tf_op jit(solution)/shard_map/ppermute | solution.py:104
  118.8 18.0 %collective-permute-start.28 = (bf16[512,768]{1,0:T(8,128)(2,1)S(1)}, bf16[512,768]{1,0:T(8,128)(2,1)S(1)}, u32[]{:S(2)}, u32[]{:S(2)}) collective-permute-start(bf16[512,768]{1,0:T(8,128)(2,1)S(1)} %copy-done.2), channel_id=1, source_target_pairs={{0,2},{1,3},{2,0},{3,1},{4,6},{5,7},{6,4},{7,5},{8,10},{9,11},{10,... | collective-permute-start | bytes 2359304 | tf_op jit(solution)/shard_map/ppermute | solution.py:104
  130.4 15.2 %collective-permute-start.30 = (bf16[4,96,768]{2,1,0:T(8,128)(2,1)S(1)}, bf16[4,96,768]{2,1,0:T(8,128)(2,1)S(1)}, u32[]{:S(2)}, u32[]{:S(2)}) collective-permute-start(bf16[4,96,768]{2,1,0:T(8,128)(2,1)S(1)} %bitcast.73), channel_id=1, source_target_pairs={{0,4},{1,5},{2,6},{3,7},{4,0},{5,1},{6,2},{7,3},{8,12},{9,13},{10,... | collective-permute-start | bytes 1769480 | tf_op jit(solution)/shard_map/ppermute | solution.py:101
  150.3 33.5 %collective-permute-start.34 = (bf16[2,4,48,1536]{3,2,1,0:T(8,128)(2,1)}, bf16[2,4,48,1536]{3,2,1,0:T(8,128)(2,1)S(1)}, u32[]{:S(2)}, u32[]{:S(2)}) collective-permute-start(bf16[2,4,48,1536]{3,2,1,0:T(8,128)(2,1)} %get-tuple-element.215), channel_id=1, source_target_pairs={{0,2},{1,5},{2,0},{3,7},{4,6},{5,1},{6,4},{7,3},{8,10},{9,13},{10,... | collective-permute-start | bytes 3538952 | tf_op jit(solution)/shard_map/ppermute | solution.py:119
  150.9 33.7 %collective-permute-start.39 = (bf16[512,768]{1,0:T(8,128)(2,1)}, bf16[512,768]{1,0:T(8,128)(2,1)}, u32[]{:S(2)}, u32[]{:S(2)}) collective-permute-start(bf16[512,768]{1,0:T(8,128)(2,1)} %get-tuple-element.231.pre_a), channel_id=1, source_target_pairs={{0,2},{1,3},{2,0},{3,1},{4,6},{5,7},{6,4},{7,5},{8,10},{9,11},{10,... | collective-permute-start | bytes 2359304 | tf_op jit(solution)/shard_map/ppermute | solution.py:104
  152.4 31.3 %collective-permute-start.35 = (bf16[4,96,768]{2,1,0:T(8,128)(2,1)}, bf16[4,96,768]{2,1,0:T(8,128)(2,1)}, u32[]{:S(2)}, u32[]{:S(2)}) collective-permute-start(bf16[4,96,768]{2,1,0:T(8,128)(2,1)} %bitcast.33), channel_id=1, source_target_pairs={{0,4},{1,5},{2,6},{3,7},{4,0},{5,1},{6,2},{7,3},{8,12},{9,13},{10,... | collective-permute-start | bytes 1769480 | tf_op jit(solution)/shard_map/ppermute | solution.py:101
  155.6 28.1 %collective-permute-start.37 = (bf16[96,768]{1,0:T(8,128)(2,1)}, bf16[96,768]{1,0:T(8,128)(2,1)}, u32[]{:S(2)}, u32[]{:S(2)}) collective-permute-start(bf16[96,768]{1,0:T(8,128)(2,1)} %get-tuple-element.226), channel_id=1, source_target_pairs={{0,16},{1,17},{2,18},{3,19},{4,20},{5,21},{6,22},{7,23},{8,24},{9,... | collective-permute-start | bytes 442376 | tf_op jit(solution)/shard_map/ppermute | solution.py:107
  163.4 20.3 %collective-permute-start.38 = (bf16[96,768]{1,0:T(8,128)(2,1)}, bf16[96,768]{1,0:T(8,128)(2,1)}, u32[]{:S(2)}, u32[]{:S(2)}) collective-permute-start(bf16[96,768]{1,0:T(8,128)(2,1)} %get-tuple-element.227), channel_id=1, source_target_pairs={{0,24},{1,25},{2,26},{3,27},{4,28},{5,29},{6,30},{7,31},{8,0},{9,1... | collective-permute-start | bytes 442376 | tf_op jit(solution)/shard_map/ppermute | solution.py:107
  187.6 16.2 %collective-permute-start.42 = (bf16[4,48,1536]{2,1,0:T(8,128)(2,1)S(1)}, bf16[4,48,1536]{2,1,0:T(8,128)(2,1)S(1)}, u32[]{:S(2)}, u32[]{:S(2)}) collective-permute-start(bf16[4,48,1536]{2,1,0:T(8,128)(2,1)S(1)} %bitcast.72), channel_id=1, source_target_pairs={{0,4},{1,3},{2,6},{3,1},{4,0},{5,7},{6,2},{7,5},{8,12},{9,11},{10,... | collective-permute-start | bytes 1769480 | tf_op jit(solution)/shard_map/ppermute | solution.py:112
  190.4 13.4 %collective-permute-start.44 = (bf16[96,768]{1,0:T(8,128)(2,1)S(1)}, bf16[96,768]{1,0:T(8,128)(2,1)S(1)}, u32[]{:S(2)}, u32[]{:S(2)}) collective-permute-start(bf16[96,768]{1,0:T(8,128)(2,1)S(1)} %get-tuple-element.240), channel_id=1, source_target_pairs={{0,16},{1,17},{2,18},{3,19},{4,20},{5,21},{6,22},{7,23},{8,24},{9,... | collective-permute-start | bytes 442376 | tf_op jit(solution)/shard_map/ppermute | solution.py:107
  192.9 10.9 %collective-permute-start.45 = (bf16[96,768]{1,0:T(8,128)(2,1)S(1)}, bf16[96,768]{1,0:T(8,128)(2,1)S(1)}, u32[]{:S(2)}, u32[]{:S(2)}) collective-permute-start(bf16[96,768]{1,0:T(8,128)(2,1)S(1)} %get-tuple-element.241), channel_id=1, source_target_pairs={{0,24},{1,25},{2,26},{3,27},{4,28},{5,29},{6,30},{7,31},{8,0},{9,1... | collective-permute-start | bytes 442376 | tf_op jit(solution)/shard_map/ppermute | solution.py:107
  204.5 18.2 %collective-permute-start.46 = (bf16[512,768]{1,0:T(8,128)(2,1)S(1)}, bf16[512,768]{1,0:T(8,128)(2,1)S(1)}, u32[]{:S(2)}, u32[]{:S(2)}) collective-permute-start(bf16[512,768]{1,0:T(8,128)(2,1)S(1)} %copy-done.1), channel_id=1, source_target_pairs={{0,2},{1,3},{2,0},{3,1},{4,6},{5,7},{6,4},{7,5},{8,10},{9,11},{10,... | collective-permute-start | bytes 2359304 | tf_op jit(solution)/shard_map/ppermute | solution.py:104
  209.0 9.9 %collective-permute-start.48 = (bf16[48,1536]{1,0:T(8,128)(2,1)S(1)}, bf16[48,1536]{1,0:T(8,128)(2,1)S(1)}, u32[]{:S(2)}, u32[]{:S(2)}) collective-permute-start(bf16[48,1536]{1,0:T(8,128)(2,1)S(1)} %get-tuple-element.246), channel_id=1, source_target_pairs={{0,16},{1,17},{2,18},{3,19},{4,20},{5,21},{6,22},{7,23},{8,24},{9,... | collective-permute-start | bytes 442376 | tf_op jit(solution)/shard_map/ppermute | solution.py:107
  209.4 9.5 %collective-permute-start.49 = (bf16[48,1536]{1,0:T(8,128)(2,1)S(1)}, bf16[48,1536]{1,0:T(8,128)(2,1)S(1)}, u32[]{:S(2)}, u32[]{:S(2)}) collective-permute-start(bf16[48,1536]{1,0:T(8,128)(2,1)S(1)} %get-tuple-element.247), channel_id=1, source_target_pairs={{0,24},{1,25},{2,26},{3,27},{4,28},{5,29},{6,30},{7,31},{8,0},{9,1... | collective-permute-start | bytes 442376 | tf_op jit(solution)/shard_map/ppermute | solution.py:107
  213.7 16.0 %collective-permute-start.50 = (bf16[512,768]{1,0:T(8,128)(2,1)S(1)}, bf16[512,768]{1,0:T(8,128)(2,1)S(1)}, u32[]{:S(2)}, u32[]{:S(2)}) collective-permute-start(bf16[512,768]{1,0:T(8,128)(2,1)S(1)} %copy-done.1), channel_id=1, source_target_pairs={{0,1},{1,0},{2,3},{3,2},{4,5},{5,4},{6,7},{7,6},{8,9},{9,8},{10,11... | collective-permute-start | bytes 2359304 | tf_op jit(solution)/shard_map/ppermute | solution.py:98
  222.7 14.3 %collective-permute-start.52 = (f32[48,768]{1,0:T(8,128)S(1)}, f32[48,768]{1,0:T(8,128)}, u32[]{:S(2)}, u32[]{:S(2)}) collective-permute-start(f32[48,768]{1,0:T(8,128)S(1)} %get-tuple-element.253), channel_id=1, source_target_pairs={{0,1},{1,0},{2,3},{3,2},{4,5},{5,4},{6,7},{7,6},{8,9},{9,8},{10,11... | collective-permute-start | bytes 442376 | tf_op jit(solution)/shard_map/ppermute | solution.py:98
  223.3 13.8 %all-to-all-start.1 = ((f32[32,1,512]{2,1,0:T(1,128)}), f32[32,1,512]{2,1,0:T(1,128)S(1)}, u32[]{:S(2)}, u32[]{:S(2)}) async-start(f32[32,1,512]{2,1,0:T(1,128)} %get-tuple-element.251), calls=%async_computation.1 | async-start | bytes 131072 | tf_op jit(solution)/shard_map/all_to_all | solution.py:1129
  (57 other events, 676.3 us)

commit v5 on v3

--- a/solution.py
+++ b/solution.py
@@ -174,23 +174,26 @@
     return slice(base + b * cols + p * LANES, base + b * cols + (p + 1) * LANES)
 
 
-def attn_fwd_kernel(plan, meta, x_all, segc_ref, segr_ref, np_ref, pb_ref, *refs):
+def attn_prep_kernel(meta, x_all, np_ref, x_ref, fl_ref, sem):
+    load = token_copy(x_all, meta[0], x_ref, sem.at[0])
+    load.start()
+    load.wait()
+
+    def body(i, at):
+        normal, _ = norm_stats(x_ref[at, :].astype(f32))
+        fl_ref[at, :] = (normal * np_ref[0:1, :] + np_ref[1:2, :]).astype(bf16)
+
+    chunks(x_ref.shape[0], body)
+
+
+def attn_fwd_kernel(plan, meta, x_ref, fl_ref, segc_ref, segr_ref, np_ref, pb_ref, *refs):
     srcs, refs = refs[:4], refs[4:]
-    sl_ref, mid_ref, fl_ref, qkv_ref, p_ref, ctx_ref, w, sl_buf, x_ref, sem, sem_x = refs
+    sl_ref, mid_ref, qkv_ref, p_ref, ctx_ref, w, sl_buf, sem, sem_x = refs
     cols = plan.cols
     count = x_ref.shape[0]
     copies = attn_weight_copies(plan, meta, srcs, w, sem, slice(None))
-    load = token_copy(x_all, meta[0], x_ref, sem_x.at[0])
-    load.start()
     for copy in copies:
         copy.start()
-    load.wait()
-
-    def first(i, at):
-        normal, _ = norm_stats(x_ref[at, :].astype(f32))
-        fl_ref[at, :] = (normal * np_ref[0:1, :] + np_ref[1:2, :]).astype(bf16)
-
-    chunks(count, first)
     for copy in copies:
         copy.wait()
     tiles = CHUNK // LANES
@@ -473,14 +476,11 @@
 
 
 def input_grad_kernel(
-    plan, meta, x_all, mg_ref, np_ref, dqkv_ref, w, ig_ref, vec_ref, x_ref, buf, sem
+    plan, meta, x_ref, mg_ref, np_ref, dqkv_ref, w, ig_ref, vec_ref, buf, sem
 ):
     cols = plan.cols
     count = x_ref.shape[0]
-    load = token_copy(x_all, meta[0], x_ref, sem.at[0])
-    load.start()
     vec_ref[...] = jnp.zeros_like(vec_ref)
-    load.wait()
 
     def body(i, at):
         normal, scaled = norm_stats(x_ref[at, :].astype(f32))
@@ -693,9 +693,19 @@
         owned(lambda m: line(8 * width + m * part, part)),
     )
     ins, outs = refs[: 4 * 4 + 3 * 3], refs[4 * 4 + 3 * 3 : -1]
+    attn = {}
+    if plan.direct:
+        mine, other = ins[3][...], ins[7][...]
+        low = jnp.where(meta[4] == 0, mine, other)
+        high = jnp.where(meta[4] == 0, other, mine)
+        for p in range(4):
+            at = slice(p * quarter, (p + 1) * quarter)
+            attn[p] = jnp.concatenate([low[:, at], high[:, at]], axis=0)
     for i, (rate, decay) in enumerate(rates):
         if i < 4:
             w_ref, m_ref, s_ref, g_ref = ins[4 * i : 4 * i + 4]
+            if plan.direct and i < 2:
+                g_ref = attn if i == 0 else {Ellipsis: attn[3].T}
         else:
             w_ref, m_ref, s_ref = ins[3 * i + 4 : 3 * i + 7]
             g_ref = {Ellipsis: small[i - 4]}
@@ -817,7 +827,7 @@
     low = jnp.where(core_zero, keep, got)
     high = jnp.where(core_zero, got, keep)
     unit = jnp.concatenate([low, high], axis=2).reshape(half, 4 * cols)
-    attn_z = [plan.along_z(unit, k) for k in range(1, nz)]
+    attn_z = [plan.along_z(unit, k) for k in range(nz - 1, 0, -1)][::-1]
 
     e_unit = after(expand_weight.astype(bf16), attn_z[0])
     e_z = [plan.along_z(e_unit, k) for k in range(1, nz)]
@@ -848,11 +858,23 @@
     spread, *_, meta, mark_col, mark_row, pair_full, hidden_rows = lax.optimization_barrier(
         (spread, e_z[0], meta, mark_col, mark_row, pair_full, hidden_rows)
     )
-    attn_w = [spread, after(plan.second(spread), *e_z)]
+    dma = pltpu.SemaphoreType.DMA
+    tokens_low, tokens_f32 = SDS((count, width), bf16), SDS((count, width), f32)
+    sem_x = dma((2 * steps,))
+    buf_low = pltpu.VMEM((count, width), bf16)
+    own_x, fl = local_call(
+        meta,
+        attn_prep_kernel,
+        "attn_prep",
+        [(inputs, False), (norm_params, True)],
+        [(tokens_low, True), (tokens_low, True)],
+        [sem_x],
+    )
+    attn_w = [spread, after(plan.second(spread), fl, *e_z)]
     e_spread = after(jnp.stack([e_unit] + e_z), attn_w[1])
     e_x = plan.along_x(e_spread)
     attn_w = attn_w + [plan.core(v) for v in attn_w]
-    attn_w[1] = after(attn_w[1], e_spread, r_z[0])
+    attn_w[1] = after(attn_w[1], e_spread)
 
     if not plan.direct:
         attn_w = [absolute_attn(plan, jnp.stack(attn_w[:2]), jnp.stack(attn_w[2:]), z, x, y, c)]
@@ -861,17 +883,14 @@
     whole = lambda shape: (shape, lambda i, m: (0,) * len(shape))
     chunk = lambda n: ((CHUNK, n), lambda i, m: (i, 0))
     pieces = 2 * 2 * 2 * nz if plan.direct else 1
-    dma = pltpu.SemaphoreType.DMA
-
-    tokens_low, tokens_f32 = SDS((count, width), bf16), SDS((count, width), f32)
-    sem_x = dma((2 * steps,))
-    buf_low = pltpu.VMEM((count, width), bf16)
-    sl, middle, fl, qkv, probs, ctx, attn_full = local_call(
+
+    sl, middle, qkv, probs, ctx, attn_full = local_call(
         meta,
         functools.partial(attn_fwd_kernel, plan),
         "attn_fwd",
         [
-            (inputs, False),
+            (own_x, True),
+            (fl, True),
             (mark_col, True),
             (mark_row, True),
             (norm_params, True),
@@ -881,17 +900,16 @@
         [
             (tokens_low, False),
             (tokens_f32, True),
-            (tokens_low, True),
             (SDS((2, count, 3 * cols), bf16), True),
             (SDS((count // LANES * 2, 2 * cols, LANES), bf16), True),
             (tokens_low, True),
             (SDS((2, width, 4 * cols), bf16), True),
         ],
-        [buf_low, buf_low, dma((pieces,)), sem_x],
+        [buf_low, dma((pieces,)), sem_x],
     )
 
     sl_far = plan.along_y(sl)
-    r_spread = jnp.stack([r_unit, r_z[0]] + [after(v, sl) for v in r_z[1:]])
+    r_spread = jnp.stack([r_unit] + [after(v, sl) for v in r_z])
     r_x = plan.along_x(r_spread)
     e_x = after(e_x, sl)
     ff_w = []
@@ -1014,19 +1032,18 @@
         functools.partial(input_grad_kernel, plan),
         "input_grad",
         [
-            (inputs, False),
+            (own_x, True),
             (mg, True),
             (norm_params, True),
             (dqkv_late, True),
             (attn_full, True),
         ],
         [(tokens_low, False), (SDS((8, width), f32), True)],
-        [buf_low, buf_low, sem_x],
+        [buf_low, sem_x],
     )
     attn_got[0] = after(attn_got[0], ig, e_got)
     attn_keep, attn_send = add_first(meta, attn_mine, attn_got)
     attn_got = plan.second(attn_send)
-    pre_far = plan.along_y(after(pre_near, attn_send))
     r_got = plan.along_x(after(r_send, attn_send))
     e_parts = add_parts(meta, e_keep, after(e_got, attn_send))
     e_z = [e_parts[0]] + [plan.along_z(e_parts[k], k) for k in range(1, nz)]
@@ -1043,13 +1060,15 @@
     got = lax.all_to_all(vectors, AXES, 0, 0, tiled=True)
     local = jnp.sum(got, axis=0)
 
-    attn_got = after(attn_got, local, *e_z, r_got)
+    attn_got = after(attn_got, local, r_got, *e_z)
     attn_keep, attn_send = add_parts(meta, attn_keep, attn_got)
-    r_parts = add_parts(meta, r_keep, after(r_got, attn_send))
+    attn_got = plan.first(attn_send)
+    pre_far = plan.along_y(after(pre_near, attn_send))
+    r_got = after(r_got, attn_send)
+    r_parts = add_parts(meta, r_keep, r_got)
     r_z = [r_parts[0]] + [plan.along_z(r_parts[k], k) for k in range(1, nz)]
-    attn_got = plan.first(attn_send)
-
-    attn_parts = add_parts(meta, attn_keep, after(attn_got, pre_far, *r_z))
+
+    attn_parts = add_parts(meta, attn_keep, after(attn_got, *r_z))
 
     ff_in = [*e_z, *r_z]
     grad_expand, grad_reduce, ff_square = call(
@@ -1065,7 +1084,10 @@
         [],
     )(meta, *ff_in)
 
-    pre_in = after(pre_near, attn_parts[0])
+    ig = after(ig, attn_parts[0])
+    ig_pair = plan.along_y(ig)
+    attn_z = [attn_parts[0]] + [plan.along_z(attn_parts[k], k) for k in range(1, nz)]
+    pre_in, pre_far = pre_near, after(pre_far, attn_z[1])
     out, out_pair = call(
         out_kernel,
         "out_sum",
@@ -1080,10 +1102,7 @@
         [(SDS((count, width), bf16), *chunk(width))] * 2,
         [],
     )(meta, pre_in, fed_far, pre_far, fed_send, norm_params)
-    ig = after(ig, attn_parts[0])
-    ig_pair = plan.along_y(ig)
-    attn_z = [attn_parts[0]] + [plan.along_z(attn_parts[k], k) for k in range(1, nz)]
-    total_in = attn_z + [ff_square, local]
+    total_in = attn_z + [ff_square, after(local, out)]
     def everywhere(block, by_y):
         blocks = [block, by_y, plan.core(block), plan.core(by_y)]
         return call(
@@ -1095,8 +1114,6 @@
             [dma((4,))],
         )(meta, *blocks)[0]
 
-    outputs = everywhere(out, out_pair)
-    total_in[-1] = after(total_in[-1], outputs)
     keep, send, payload = call(
         total_kernel,
         "total",
@@ -1114,18 +1131,20 @@
     )(meta, *total_in)
     by_core = plan.core(send)
     ig_pair = after(ig_pair, keep)
+    outputs = everywhere(out, out_pair)
     input_gradient = everywhere(ig, ig_pair)
-    got = after(lax.all_to_all(payload, AXES, 0, 0, tiled=True), input_gradient)
-
-    low, high = jnp.where(core_zero, keep, by_core), jnp.where(core_zero, by_core, keep)
-    shard = jnp.concatenate([low, high], axis=0).reshape(rows, 4, quarter)
-    grad_triple = shard[:, :3].transpose(1, 0, 2)
-    grad_outward = shard[:, 3].T
+    got = after(lax.all_to_all(payload, AXES, 0, 0, tiled=True), input_gradient, outputs)
+
+    if not plan.direct:
+        low, high = jnp.where(core_zero, keep, by_core), jnp.where(core_zero, by_core, keep)
+        shard = jnp.concatenate([low, high], axis=0).reshape(rows, 4, quarter)
+        keep = shard[:, :3].transpose(1, 0, 2)
+        by_core = shard[:, 3].T
 
     matrix, vector = (LR_MATRIX, DECAY), (LR_VECTOR, 0.0)
     groups = [
-        [triple_weight, triple_first, triple_second, grad_triple],
-        [outward_weight, outward_first, outward_second, grad_outward],
+        [triple_weight, triple_first, triple_second, keep],
+        [outward_weight, outward_first, outward_second, by_core],
         [expand_weight, expand_first, expand_second, grad_expand],
         [reduce_weight.T, reduce_first.T, reduce_second.T, grad_reduce],
         [norm_params, norm_first, norm_second],

time: 251 us -> 239 us (0.952)
  starting transfers between devices: 65.5 us -> 53.3 us
  local copies, waits for them, and re-layouts: 10.1 us -> 5.15 us
  Pallas kernels: 83 us -> 86.8 us
  waiting for transfers between devices: 64.1 us -> 67.8 us
  other arithmetic: 7.03 us -> 4.49 us
    ppermute x18, starting transfers between devices: 39.7 us -> 27.3 us  [along_z(): lax.ppermute(value, AXES, self.perm(lambda z, x, y, c: ((z + step) % self...]
    ppermute x6, waiting for transfers between devices: 8.42 us -> 15.8 us  [along_y(): lax.ppermute(value, AXES, self.perm(lambda z, x, y, c: (z, x, 1 - y, c)))]
    ppermute x18, waiting for transfers between devices: 35.3 us -> 30.2 us  [along_z(): lax.ppermute(value, AXES, self.perm(lambda z, x, y, c: ((z + step) % self...]
    transpose x3 -> x0, local copies, waits for them, and re-layouts: 3.4 us -> none  [the longest x2 1.87 us: per_device(): grad_triple = shard[:, :3].transpose(1, 0, 2)]
    pallas_call x2, Pallas kernels: 4.48 us -> 7.2 us  [everywhere(): call(place_kernel, 'place', (1,), [(b, *whole((count, width))) for b in b...]
    pallas_call x9 -> x10, Pallas kernels: 60.3 us -> 61.9 us  [local_call(): return kernel_call(meta, *map(place, ins))]
  transfers between devices with their start and end apart: 54 -> 54, of which waited for: 17 -> 19; matrix products, arithmetic and copies ran while one was open for 5% -> 2% of each run, Pallas kernels for 25% -> 28%
where the time goes in v5:
time: 239 us
  Pallas kernels  86.8 us (36%)
  waiting for transfers between devices  67.8 us (28%)
  starting transfers between devices  53.3 us (22%)
  blocking collectives  19.4 us (8%)
  local copies, waits for them, and re-layouts  5.15 us (2%)
  other arithmetic  4.49 us (2%)
    pallas_call x10, Pallas kernels, local_call(): return kernel_call(meta, *map(place, ins))  61.9 us
    ppermute x18, waiting for transfers between devices, along_z(): lax.ppermute(value, AXES, self.perm(lambda z, x, y, c: ((z + step) % self...  30.2 us
    ppermute x18, starting transfers between devices, along_z(): lax.ppermute(value, AXES, self.perm(lambda z, x, y, c: ((z + step) % self...  27.3 us
    all_to_all x1, blocking collectives, per_device(): got = lax.all_to_all(vectors, AXES, 0, 0, tiled=True)  19.4 us
    ppermute x6, waiting for transfers between devices, along_y(): lax.ppermute(value, AXES, self.perm(lambda z, x, y, c: (z, x, 1 - y, c)))  15.8 us
    ppermute x4, waiting for transfers between devices, along_x(): lax.ppermute(value, AXES, self.perm(lambda z, x, y, c: (z, 1 - x, y, c)))  15.1 us
    ppermute x6, starting transfers between devices, along_y(): lax.ppermute(value, AXES, self.perm(lambda z, x, y, c: (z, x, 1 - y, c)))  8.35 us
    pallas_call x2, Pallas kernels, everywhere(): call(place_kernel, 'place', (1,), [(b, *whole((count, width))) for b in b...  7.2 us
  transfers between devices with their start and end apart: 54, of which 19 were waited for; matrix products, arithmetic and copies ran while one was open for 2% of the time, Pallas kernels for 28%

profile of v5, /device:TPU:0, one launch (start us, length us, event | category | flops | bytes accessed | tf_op | source)
XLA Modules:
  0.0 238.5 jit_solution(13826119661941064568)
XLA Ops:
  4.4 5.0 %collective-permute-start.3 = (bf16[48,1536]{1,0:T(8,128)(2,1)S(1)}, bf16[48,1536]{1,0:T(8,128)(2,1)S(1)}, u32[]{:S(2)}, u32[]{:S(2)}) collective-permute-start(bf16[48,1536]{1,0:T(8,128)(2,1)S(1)} %bitcast.89), channel_id=1, source_target_pairs={{0,24},{1,25},{2,26},{3,27},{4,28},{5,29},{6,30},{7,31},{8,0},{9,1... | collective-permute-start | bytes 442376 | tf_op jit(solution)/shard_map/ppermute | solution.py:107
  10.7 3.0 %collective-permute-done.3 = bf16[48,1536]{1,0:T(8,128)(2,1)S(1)} collective-permute-done((bf16[48,1536]{1,0:T(8,128)(2,1)S(1)}, bf16[48,1536]{1,0:T(8,128)(2,1)S(1)}, u32[]{:S(2)}, u32[]{:S(2)}) %collective-permute-start.3) | collective-permute-done | bytes 147488 | tf_op jit(solution)/shard_map/ppermute | solution.py:107
  13.7 8.5 %collective-permute-done.2 = bf16[48,1536]{1,0:T(8,128)(2,1)S(1)} collective-permute-done((bf16[48,1536]{1,0:T(8,128)(2,1)S(1)}, bf16[48,1536]{1,0:T(8,128)(2,1)S(1)}, u32[]{:S(2)}, u32[]{:S(2)}) %collective-permute-start.2) | collective-permute-done | bytes 147488 | tf_op jit(solution)/shard_map/ppermute | solution.py:107
  29.7 2.6 %collective-permute-done.4 = bf16[4,48,1536]{2,1,0:T(8,128)(2,1)S(1)} collective-permute-done((bf16[4,48,1536]{2,1,0:T(8,128)(2,1)S(1)}, bf16[4,48,1536]{2,1,0:T(8,128)(2,1)S(1)}, u32[]{:S(2)}, u32[]{:S(2)}) %collective-permute-start.4) | collective-permute-done | bytes 589856 | tf_op jit(solution)/shard_map/ppermute | solution.py:112
  37.7 2.3 attn_prep.1
  41.1 5.1 %collective-permute-done.9 = bf16[96,768]{1,0:T(8,128)(2,1)S(1)} collective-permute-done((bf16[96,768]{1,0:T(8,128)(2,1)S(1)}, bf16[96,768]{1,0:T(8,128)(2,1)S(1)}, u32[]{:S(2)}, u32[]{:S(2)}) %collective-permute-start.9) | collective-permute-done | bytes 147488 | tf_op jit(solution)/shard_map/ppermute | solution.py:107
  46.2 3.7 %collective-permute-done.8.refs_1_ = bf16[2,4,48,1536]{3,2,1,0:T(8,128)(2,1)} collective-permute-done((bf16[2,4,48,1536]{3,2,1,0:T(8,128)(2,1)}, bf16[2,4,48,1536]{3,2,1,0:T(8,128)(2,1)}, u32[]{:S(2)}, u32[]{:S(2)}) %collective-permute-start.8) | collective-permute-done | bytes 1179680 | tf_op jit(solution)/shard_map/ppermute | solution.py:119
  56.6 12.1 %attn_fwd.1 = (bf16[512,768]{1,0:T(8,128)(2,1)}, f32[512,768]{1,0:T(8,128)S(1)}, bf16[2,512,1152]{2,1,0:T(8,128)(2,1)S(1)}, bf16[8,768,128]{2,1,0:T(8,128)(2,1)S...) custom-call(s32[6]{0:T(128)S(1)} %stack.94.meta, bf16[512,768]{1,0:T(8,128)(2,1)S(1)} %get-tuple-element.155.x_ref, ...), custom_call_target="tpu_custom_call" | custom-call | flops 1 | bytes 1 | tf_op jit(solution)/shard_map/attn_fwd/pallas_call | solution.py:753
  71.6 12.0 %collective-permute-done.20.refs_5_ = bf16[4,96,768]{2,1,0:T(8,128)(2,1)S(1)} collective-permute-done((bf16[4,96,768]{2,1,0:T(8,128)(2,1)S(1)}, bf16[4,96,768]{2,1,0:T(8,128)(2,1)S(1)}, u32[]{:S(2)}, u32[]{:S(2)}) %collective-permute-start.20) | collective-permute-done | bytes 589856 | tf_op jit(solution)/shard_map/ppermute | solution.py:101
  83.6 4.6 %collective-permute-done.13.sl_ref.sl_b = bf16[512,768]{1,0:T(8,128)(2,1)S(1)} collective-permute-done((bf16[512,768]{1,0:T(8,128)(2,1)}, bf16[512,768]{1,0:T(8,128)(2,1)S(1)}, u32[]{:S(2)}, u32[]{:S(2)}) %collective-permute-start.13) | collective-permute-done | bytes 786464 | tf_op jit(solution)/shard_map/ppermute | solution.py:104
  89.1 10.4 %ff_far.1 = (bf16[512,768]{1,0:T(8,128)(2,1)}, bf16[512,768]{1,0:T(8,128)(2,1)}, bf16[2,512,768]{2,1,0:T(8,128)(2,1)S(1)}, bf16[2,512,768]{2,1,0:T(8,128)(2,1)S(...) custom-call(s32[6]{0:T(128)S(1)} %stack.94.meta, ...), custom_call_target="tpu_custom_call" | custom-call | flops 1 | bytes 1 | tf_op jit(solution)/shard_map/ff_far/pallas_call | solution.py:753
  101.1 8.4 %ff_near.1 = (bf16[512,768]{1,0:T(8,128)(2,1)S(1)}, bf16[512,768]{1,0:T(8,128)(2,1)}, bf16[2,512,768]{2,1,0:T(8,128)(2,1)S(1)}, bf16[2,512,768]{2,1,0:T(8,128)(2...) custom-call(s32[6]{0:T(128)S(1)} %stack.94.meta, bf16[512,768]{1,0:T(8,128)(2,1)S(1)} %copy-done, ...), custom_call_target="tpu_custom_call" | custom-call | flops 1 | bytes 1 | tf_op jit(solution)/shard_map/ff_near/pallas_call | solution.py:753
  109.5 7.4 %ff_grad.1 = (bf16[4,96,768]{2,1,0:T(8,128)(2,1)}, bf16[4,96,768]{2,1,0:T(8,128)(2,1)}, bf16[4,96,768]{2,1,0:T(8,128)(2,1)}, bf16[4,96,768]{2,1,0:T(8,128)(2,1)}...) custom-call(s32[6]{0:T(128)S(1)} %stack.94.meta, ...), custom_call_target="tpu_custom_call" | custom-call | flops 1 | bytes 1 | tf_op jit(solution)/shard_map/ff_grad/pallas_call | solution.py:753
  120.0 7.3 %attn_bwd.1 = (bf16[2,512,1152]{2,1,0:T(8,128)(2,1)S(1)}, bf16[512,768]{1,0:T(8,128)(2,1)S(1)}, f32[512,768]{1,0:T(8,128)S(1)}, f32[8,768]{1,0:T(8,128)S(1)}, f32[2,768]{1,0:T(2,128)S(1)}) custom-call(s32[6]{0:T(128)S(1)} %stack.94.meta, bf16[512,768]{1,0:T(8,128)(2,1)S(1)} %get-tuple-element.185.sga_ref, ...), custom_call_target="tpu_custom_call" | custom-call | flops 1 | bytes 1 | tf_op jit(solution)/shard_map/attn_bwd/pallas_call | solution.py:753
  130.7 5.0 %attn_grad.1 = (bf16[2,2,48,1536]{3,2,1,0:T(8,128)(2,1)S(1)}, bf16[2,2,48,1536]{3,2,1,0:T(8,128)(2,1)S(1)}, bf16[2,2,48,1536]{3,2,1,0:T(8,128)(2,1)S(1)}, bf16[2...) custom-call(s32[6]{0:T(128)S(1)} %stack.94.meta, ...), custom_call_target="tpu_custom_call" | custom-call | flops 1 | bytes 1 | tf_op jit(solution)/shard_map/attn_grad/pallas_call | solution.py:753
  136.8 4.5 %input_grad.1 = (bf16[512,768]{1,0:T(8,128)(2,1)}, f32[8,768]{1,0:T(8,128)S(1)}) custom-call(s32[6]{0:T(128)S(1)} %stack.94.meta, bf16[512,768]{1,0:T(8,128)(2,1)S(1)} %get-tuple-element.155.x_ref, f32[512,768]{1,0:T(8,128)S(1)} %get-tuple-element.209.mg_ref, f32[6,768]{1,0:T(8,128)S(1)} %copy-done.1, bf16[2,512,1152]{2,1,0:T(8,128)(2,1)S(1)} %get-tuple-element.210.dqkv_ref, ...), custom_call_target="tpu_custom_call" | custom-call | flops 1 | bytes 1 | tf_op jit(solution)/shard_map/input_grad/pallas_call | solution.py:753
  141.3 3.1 %collective-permute-done.30.right = bf16[4,96,768]{2,1,0:T(8,128)(2,1)S(1)} collective-permute-done((bf16[4,96,768]{2,1,0:T(8,128)(2,1)S(1)}, bf16[4,96,768]{2,1,0:T(8,128)(2,1)S(1)}, u32[]{:S(2)}, u32[]{:S(2)}) %collective-permute-start.30) | collective-permute-done | bytes 589856 | tf_op jit(solution)/shard_map/ppermute | solution.py:101
  145.8 3.3 %add_first.1 = (bf16[2,4,48,1536]{3,2,1,0:T(8,128)(2,1)S(1)}, bf16[2,4,48,1536]{3,2,1,0:T(8,128)(2,1)}) custom-call(s32[6]{0:T(128)S(1)} %stack.94.meta, bf16[2,2,48,1536]{3,2,1,0:T(8,128)(2,1)S(1)} %get-tuple-element.203.refs_0_, bf16[2,2,48,1536]{3,2,1,0:T(8,128)(2,1)S(1)} %get-tuple-element.204.refs_1_, ...), custom_call_target="tpu_custom_call" | custom-call | flops 1 | bytes 1 | tf_op jit(solution)/shard_map/add_first/pallas_call | solution.py:753
  153.0 2.5 %collective-permute-start.37 = (bf16[96,768]{1,0:T(8,128)(2,1)}, bf16[96,768]{1,0:T(8,128)(2,1)S(1)}, u32[]{:S(2)}, u32[]{:S(2)}) collective-permute-start(bf16[96,768]{1,0:T(8,128)(2,1)} %get-tuple-element.228), channel_id=1, source_target_pairs={{0,16},{1,17},{2,18},{3,19},{4,20},{5,21},{6,22},{7,23},{8,24},{9,... | collective-permute-start | bytes 442376 | tf_op jit(solution)/shard_map/ppermute | solution.py:107
  157.5 19.4 %all_to_all.10 = f32[32,1,384]{2,1,0:T(1,128)S(1)} all-to-all(f32[32,1,384]{2,1,0:T(1,128)} %vectors.1), channel_id=1, replica_groups=mesh['dp'=8,'mp'=4] {'dp','mp'}, dimensions={0} | all-to-all | bytes 98304 | tf_op jit(solution)/shard_map/all_to_all | solution.py:1060
  181.8 2.4 %collective-permute-start.42 = (bf16[96,768]{1,0:T(8,128)(2,1)S(1)}, bf16[96,768]{1,0:T(8,128)(2,1)S(1)}, u32[]{:S(2)}, u32[]{:S(2)}) collective-permute-start(bf16[96,768]{1,0:T(8,128)(2,1)S(1)} %get-tuple-element.238), channel_id=1, source_target_pairs={{0,16},{1,17},{2,18},{3,19},{4,20},{5,21},{6,22},{7,23},{8,24},{9,... | collective-permute-start | bytes 442376 | tf_op jit(solution)/shard_map/ppermute | solution.py:107
  186.6 3.3 %collective-permute-done.41.refs_5_ = bf16[96,768]{1,0:T(8,128)(2,1)S(1)} collective-permute-done((bf16[96,768]{1,0:T(8,128)(2,1)S(1)}, bf16[96,768]{1,0:T(8,128)(2,1)S(1)}, u32[]{:S(2)}, u32[]{:S(2)}) %collective-permute-start.41) | collective-permute-done | bytes 147488 | tf_op jit(solution)/shard_map/ppermute | solution.py:107
  189.9 5.2 %collective-permute-done.42.refs_6_ = bf16[96,768]{1,0:T(8,128)(2,1)S(1)} collective-permute-done((bf16[96,768]{1,0:T(8,128)(2,1)S(1)}, bf16[96,768]{1,0:T(8,128)(2,1)S(1)}, u32[]{:S(2)}, u32[]{:S(2)}) %collective-permute-start.42) | collective-permute-done | bytes 147488 | tf_op jit(solution)/shard_map/ppermute | solution.py:107
  196.4 2.8 %collective-permute-start.44 = (bf16[48,1536]{1,0:T(8,128)(2,1)S(1)}, bf16[48,1536]{1,0:T(8,128)(2,1)S(1)}, u32[]{:S(2)}, u32[]{:S(2)}) collective-permute-start(bf16[48,1536]{1,0:T(8,128)(2,1)S(1)} %get-tuple-element.241), channel_id=1, source_target_pairs={{0,8},{1,9},{2,10},{3,11},{4,12},{5,13},{6,14},{7,15},{8,16},{9,17... | collective-permute-start | bytes 442376 | tf_op jit(solution)/shard_map/ppermute | solution.py:107
  201.6 2.3 ff_total.1
  207.3 2.7 %collective-permute-done.48.refs_2_ = bf16[48,1536]{1,0:T(8,128)(2,1)S(1)} collective-permute-done((bf16[48,1536]{1,0:T(8,128)(2,1)S(1)}, bf16[48,1536]{1,0:T(8,128)(2,1)S(1)}, u32[]{:S(2)}, u32[]{:S(2)}) %collective-permute-start.48) | collective-permute-done | bytes 147488 | tf_op jit(solution)/shard_map/ppermute | solution.py:107
  210.0 2.3 total.1
  213.0 8.1 %collective-permute-done.47.by_y = bf16[512,768]{1,0:T(8,128)(2,1)S(1)} collective-permute-done((bf16[512,768]{1,0:T(8,128)(2,1)S(1)}, bf16[512,768]{1,0:T(8,128)(2,1)S(1)}, u32[]{:S(2)}, u32[]{:S(2)}) %collective-permute-start.47) | collective-permute-done | bytes 786464 | tf_op jit(solution)/shard_map/ppermute | solution.py:104
  221.6 3.5 %all-to-all-start.1 = ((f32[32,1,512]{2,1,0:T(1,128)}), f32[32,1,512]{2,1,0:T(1,128)S(1)}, u32[]{:S(2)}, u32[]{:S(2)}) async-start(f32[32,1,512]{2,1,0:T(1,128)} %get-tuple-element.253), calls=%async_computation.1 | async-start | bytes 131072 | tf_op jit(solution)/shard_map/all_to_all | solution.py:1136
  225.2 3.8 %place.2 = bf16[2048,768]{1,0:T(8,128)(2,1)} custom-call(s32[6]{0:T(128)S(1)} %stack.94.meta, bf16[512,768]{1,0:T(8,128)(2,1)S(1)} %get-tuple-element.243.own, bf16[512,768]{1,0:T(8,128)(2,1)} %get-tuple-element.244.by_y, bf16[512,768]{1,0:T(8,128)(2,1)} %collective-permute-done.45.by_c, bf16[512,768]{1,0:T(8,128)(2,1)} %collective-permute-done.46.by_yc), custom_call_target="tpu_custom_call" | custom-call | flops 1 | bytes 1 | tf_op jit(solution)/shard_map/place/pallas_call | solution.py:1108
  229.1 3.4 %place.3 = bf16[2048,768]{1,0:T(8,128)(2,1)} custom-call(s32[6]{0:T(128)S(1)} %stack.94.meta, bf16[512,768]{1,0:T(8,128)(2,1)S(1)} %copy-done.2, bf16[512,768]{1,0:T(8,128)(2,1)S(1)} %collective-permute-done.47.by_y, bf16[512,768]{1,0:T(8,128)(2,1)S(1)} %collective-permute-done.50.by_c, bf16[512,768]{1,0:T(8,128)(2,1)} %collective-permute-done.51.by_yc), custom_call_target="tpu_custom_call" | custom-call | flops 1 | bytes 1 | tf_op jit(solution)/shard_map/place/pallas_call | solution.py:1108
  233.3 5.1 %adam.1 = (f32[3,96,192]{2,1,0:T(8,128)}, f32[3,96,192]{2,1,0:T(8,128)}, f32[3,96,192]{2,1,0:T(8,128)}, f32[192,96]{1,0:T(8,128)}, f32[192,96]{1,0:T(8,128)}, /*...) custom-call(s32[6]{0:T(128)} %copy-done.14, ...), custom_call_target="tpu_custom_call" | custom-call | flops 1 | bytes 1 | tf_op jit(solution)/shard_map/adam/pallas_call | solution.py:1157
  (200 shorter events, 61.6 us)
Async XLA Ops:
  9.4 12.8 %collective-permute-start.2 = (bf16[48,1536]{1,0:T(8,128)(2,1)S(1)}, bf16[48,1536]{1,0:T(8,128)(2,1)S(1)}, u32[]{:S(2)}, u32[]{:S(2)}) collective-permute-start(bf16[48,1536]{1,0:T(8,128)(2,1)S(1)} %bitcast.90), channel_id=1, source_target_pairs={{0,16},{1,17},{2,18},{3,19},{4,20},{5,21},{6,22},{7,23},{8,24},{9,... | collective-permute-start | bytes 442376 | tf_op jit(solution)/shard_map/ppermute | solution.py:107
  9.4 12.8 %collective-permute-start.1 = (bf16[48,1536]{1,0:T(8,128)(2,1)S(1)}, bf16[48,1536]{1,0:T(8,128)(2,1)S(1)}, u32[]{:S(2)}, u32[]{:S(2)}) collective-permute-start(bf16[48,1536]{1,0:T(8,128)(2,1)S(1)} %bitcast.91), channel_id=1, source_target_pairs={{0,8},{1,9},{2,10},{3,11},{4,12},{5,13},{6,14},{7,15},{8,16},{9,17... | collective-permute-start | bytes 442376 | tf_op jit(solution)/shard_map/ppermute | solution.py:107
  33.4 16.5 %collective-permute-start.8 = (bf16[2,4,48,1536]{3,2,1,0:T(8,128)(2,1)}, bf16[2,4,48,1536]{3,2,1,0:T(8,128)(2,1)}, u32[]{:S(2)}, u32[]{:S(2)}) collective-permute-start(bf16[2,4,48,1536]{3,2,1,0:T(8,128)(2,1)} %pad_maximum_fusion.refs_0_), channel_id=1, source_target_pairs={{0,2},{1,5},{2,0},{3,7},{4,6},{5,1},{6,4},{7,3},{8,10},{9,13},{10,... | collective-permute-start | bytes 3538952 | tf_op jit(solution)/shard_map/ppermute | solution.py:119
  37.7 17.3 %collective-permute-start.11 = (bf16[2,4,48,1536]{3,2,1,0:T(8,128)(2,1)}, bf16[2,4,48,1536]{3,2,1,0:T(8,128)(2,1)}, u32[]{:S(2)}, u32[]{:S(2)}) collective-permute-start(bf16[2,4,48,1536]{3,2,1,0:T(8,128)(2,1)} %pad_maximum_fusion.refs_0_), channel_id=1, source_target_pairs={{0,1},{1,0},{2,3},{3,2},{4,5},{5,4},{6,7},{7,6},{8,9},{9,8},{10,11... | collective-permute-start | bytes 3538952 | tf_op jit(solution)/shard_map/ppermute | solution.py:98
  50.0 18.8 %collective-permute-start.19 = (bf16[96,768]{1,0:T(8,128)(2,1)S(1)}, bf16[96,768]{1,0:T(8,128)(2,1)S(1)}, u32[]{:S(2)}, u32[]{:S(2)}) collective-permute-start(bf16[96,768]{1,0:T(8,128)(2,1)S(1)} %bitcast_convert_fusion), channel_id=1, source_target_pairs={{0,24},{1,25},{2,26},{3,27},{4,28},{5,29},{6,30},{7,31},{8,0},{9,1... | collective-permute-start | bytes 442376 | tf_op jit(solution)/shard_map/ppermute | solution.py:107
  51.4 17.4 %collective-permute-start.18 = (bf16[96,768]{1,0:T(8,128)(2,1)S(1)}, bf16[96,768]{1,0:T(8,128)(2,1)S(1)}, u32[]{:S(2)}, u32[]{:S(2)}) collective-permute-start(bf16[96,768]{1,0:T(8,128)(2,1)S(1)} %bitcast_convert_fusion), channel_id=1, source_target_pairs={{0,16},{1,17},{2,18},{3,19},{4,20},{5,21},{6,22},{7,23},{8,24},{9,... | collective-permute-start | bytes 442376 | tf_op jit(solution)/shard_map/ppermute | solution.py:107
  52.9 15.9 %collective-permute-start.17 = (bf16[96,768]{1,0:T(8,128)(2,1)S(1)}, bf16[96,768]{1,0:T(8,128)(2,1)S(1)}, u32[]{:S(2)}, u32[]{:S(2)}) collective-permute-start(bf16[96,768]{1,0:T(8,128)(2,1)S(1)} %bitcast_convert_fusion), channel_id=1, source_target_pairs={{0,8},{1,9},{2,10},{3,11},{4,12},{5,13},{6,14},{7,15},{8,16},{9,17... | collective-permute-start | bytes 442376 | tf_op jit(solution)/shard_map/ppermute | solution.py:107
  55.1 15.9 %collective-permute-start.14 = (bf16[4,96,768]{2,1,0:T(8,128)(2,1)S(1)}, bf16[4,96,768]{2,1,0:T(8,128)(2,1)S(1)}, u32[]{:S(2)}, u32[]{:S(2)}) collective-permute-start(bf16[4,96,768]{2,1,0:T(8,128)(2,1)S(1)} %pad_maximum_fusion.2.refs_0_), channel_id=1, source_target_pairs={{0,4},{1,5},{2,6},{3,7},{4,0},{5,1},{6,2},{7,3},{8,12},{9,13},{10,... | collective-permute-start | bytes 1769480 | tf_op jit(solution)/shard_map/ppermute | solution.py:101
  68.9 14.7 %collective-permute-start.20 = (bf16[4,96,768]{2,1,0:T(8,128)(2,1)S(1)}, bf16[4,96,768]{2,1,0:T(8,128)(2,1)S(1)}, u32[]{:S(2)}, u32[]{:S(2)}) collective-permute-start(bf16[4,96,768]{2,1,0:T(8,128)(2,1)S(1)} %pad_maximum_fusion.3.refs_4_), channel_id=1, source_target_pairs={{0,4},{1,5},{2,6},{3,7},{4,0},{5,1},{6,2},{7,3},{8,12},{9,13},{10,... | collective-permute-start | bytes 1769480 | tf_op jit(solution)/shard_map/ppermute | solution.py:101
  69.5 18.8 %collective-permute-start.13 = (bf16[512,768]{1,0:T(8,128)(2,1)}, bf16[512,768]{1,0:T(8,128)(2,1)S(1)}, u32[]{:S(2)}, u32[]{:S(2)}) collective-permute-start(bf16[512,768]{1,0:T(8,128)(2,1)} %get-tuple-element.164.sl_ref.sl_a), channel_id=1, source_target_pairs={{0,2},{1,3},{2,0},{3,1},{4,6},{5,7},{6,4},{7,5},{8,10},{9,11},{10,... | collective-permute-start | bytes 2359304 | tf_op jit(solution)/shard_map/ppermute | solution.py:104
  71.0 12.6 %collective-permute-start.15 = (bf16[4,96,768]{2,1,0:T(8,128)(2,1)S(1)}, bf16[4,96,768]{2,1,0:T(8,128)(2,1)S(1)}, u32[]{:S(2)}, u32[]{:S(2)}) collective-permute-start(bf16[4,96,768]{2,1,0:T(8,128)(2,1)S(1)} %pad_maximum_fusion.2.refs_0_), channel_id=1, source_target_pairs={{0,1},{1,0},{2,3},{3,2},{4,5},{5,4},{6,7},{7,6},{8,9},{9,8},{10,11... | collective-permute-start | bytes 1769480 | tf_op jit(solution)/shard_map/ppermute | solution.py:98
  71.0 12.6 %collective-permute-start.16 = (bf16[4,96,768]{2,1,0:T(8,128)(2,1)S(1)}, bf16[4,96,768]{2,1,0:T(8,128)(2,1)S(1)}, u32[]{:S(2)}, u32[]{:S(2)}) collective-permute-start(bf16[4,96,768]{2,1,0:T(8,128)(2,1)S(1)} %collective-permute-done.14.refs_1_), channel_id=1, source_target_pairs={{0,1},{1,0},{2,3},{3,2},{4,5},{5,4},{6,7},{7,6},{8,9},{9,8},{10,11... | collective-permute-start | bytes 1769480 | tf_op jit(solution)/shard_map/ppermute | solution.py:98
  71.5 12.1 %collective-permute-start.21 = (bf16[4,96,768]{2,1,0:T(8,128)(2,1)S(1)}, bf16[4,96,768]{2,1,0:T(8,128)(2,1)S(1)}, u32[]{:S(2)}, u32[]{:S(2)}) collective-permute-start(bf16[4,96,768]{2,1,0:T(8,128)(2,1)S(1)} %pad_maximum_fusion.3.refs_4_), channel_id=1, source_target_pairs={{0,1},{1,0},{2,3},{3,2},{4,5},{5,4},{6,7},{7,6},{8,9},{9,8},{10,11... | collective-permute-start | bytes 1769480 | tf_op jit(solution)/shard_map/ppermute | solution.py:98
  99.5 17.9 %collective-permute-start.23 = (bf16[512,768]{1,0:T(8,128)(2,1)}, bf16[512,768]{1,0:T(8,128)(2,1)S(1)}, u32[]{:S(2)}, u32[]{:S(2)}) collective-permute-start(bf16[512,768]{1,0:T(8,128)(2,1)} %get-tuple-element.175), channel_id=1, source_target_pairs={{0,2},{1,3},{2,0},{3,1},{4,6},{5,7},{6,4},{7,5},{8,10},{9,11},{10,... | collective-permute-start | bytes 2359304 | tf_op jit(solution)/shard_map/ppermute | solution.py:104
  117.4 18.3 %collective-permute-start.24 = (bf16[512,768]{1,0:T(8,128)(2,1)S(1)}, bf16[512,768]{1,0:T(8,128)(2,1)S(1)}, u32[]{:S(2)}, u32[]{:S(2)}) collective-permute-start(bf16[512,768]{1,0:T(8,128)(2,1)S(1)} %copy-done.3), channel_id=1, source_target_pairs={{0,2},{1,3},{2,0},{3,1},{4,6},{5,7},{6,4},{7,5},{8,10},{9,11},{10,... | collective-permute-start | bytes 2359304 | tf_op jit(solution)/shard_map/ppermute | solution.py:104
  129.2 15.2 %collective-permute-start.30 = (bf16[4,96,768]{2,1,0:T(8,128)(2,1)S(1)}, bf16[4,96,768]{2,1,0:T(8,128)(2,1)S(1)}, u32[]{:S(2)}, u32[]{:S(2)}) collective-permute-start(bf16[4,96,768]{2,1,0:T(8,128)(2,1)S(1)} %bitcast.72), channel_id=1, source_target_pairs={{0,4},{1,5},{2,6},{3,7},{4,0},{5,1},{6,2},{7,3},{8,12},{9,13},{10,... | collective-permute-start | bytes 1769480 | tf_op jit(solution)/shard_map/ppermute | solution.py:101
  149.1 27.9 %collective-permute-start.34 = (bf16[2,4,48,1536]{3,2,1,0:T(8,128)(2,1)}, bf16[2,4,48,1536]{3,2,1,0:T(8,128)(2,1)S(1)}, u32[]{:S(2)}, u32[]{:S(2)}) collective-permute-start(bf16[2,4,48,1536]{3,2,1,0:T(8,128)(2,1)} %get-tuple-element.217), channel_id=1, source_target_pairs={{0,2},{1,5},{2,0},{3,7},{4,6},{5,1},{6,4},{7,3},{8,10},{9,13},{10,... | collective-permute-start | bytes 3538952 | tf_op jit(solution)/shard_map/ppermute | solution.py:119
  149.6 27.4 %collective-permute-start.35 = (bf16[4,96,768]{2,1,0:T(8,128)(2,1)}, bf16[4,96,768]{2,1,0:T(8,128)(2,1)}, u32[]{:S(2)}, u32[]{:S(2)}) collective-permute-start(bf16[4,96,768]{2,1,0:T(8,128)(2,1)} %bitcast.33), channel_id=1, source_target_pairs={{0,4},{1,5},{2,6},{3,7},{4,0},{5,1},{6,2},{7,3},{8,12},{9,13},{10,... | collective-permute-start | bytes 1769480 | tf_op jit(solution)/shard_map/ppermute | solution.py:101
  152.5 24.6 %collective-permute-start.36 = (bf16[96,768]{1,0:T(8,128)(2,1)}, bf16[96,768]{1,0:T(8,128)(2,1)S(1)}, u32[]{:S(2)}, u32[]{:S(2)}) collective-permute-start(bf16[96,768]{1,0:T(8,128)(2,1)} %get-tuple-element.227), channel_id=1, source_target_pairs={{0,8},{1,9},{2,10},{3,11},{4,12},{5,13},{6,14},{7,15},{8,16},{9,17... | collective-permute-start | bytes 442376 | tf_op jit(solution)/shard_map/ppermute | solution.py:107
  153.0 24.0 %collective-permute-start.37 = (bf16[96,768]{1,0:T(8,128)(2,1)}, bf16[96,768]{1,0:T(8,128)(2,1)S(1)}, u32[]{:S(2)}, u32[]{:S(2)}) collective-permute-start(bf16[96,768]{1,0:T(8,128)(2,1)} %get-tuple-element.228), channel_id=1, source_target_pairs={{0,16},{1,17},{2,18},{3,19},{4,20},{5,21},{6,22},{7,23},{8,24},{9,... | collective-permute-start | bytes 442376 | tf_op jit(solution)/shard_map/ppermute | solution.py:107
  155.5 21.6 %collective-permute-start.38 = (bf16[96,768]{1,0:T(8,128)(2,1)}, bf16[96,768]{1,0:T(8,128)(2,1)}, u32[]{:S(2)}, u32[]{:S(2)}) collective-permute-start(bf16[96,768]{1,0:T(8,128)(2,1)} %get-tuple-element.229), channel_id=1, source_target_pairs={{0,24},{1,25},{2,26},{3,27},{4,28},{5,29},{6,30},{7,31},{8,0},{9,1... | collective-permute-start | bytes 442376 | tf_op jit(solution)/shard_map/ppermute | solution.py:107
  177.9 17.2 %collective-permute-start.40 = (bf16[4,48,1536]{2,1,0:T(8,128)(2,1)S(1)}, bf16[4,48,1536]{2,1,0:T(8,128)(2,1)S(1)}, u32[]{:S(2)}, u32[]{:S(2)}) collective-permute-start(bf16[4,48,1536]{2,1,0:T(8,128)(2,1)S(1)} %bitcast.73), channel_id=1, source_target_pairs={{0,4},{1,3},{2,6},{3,1},{4,0},{5,7},{6,2},{7,5},{8,12},{9,11},{10,... | collective-permute-start | bytes 1769480 | tf_op jit(solution)/shard_map/ppermute | solution.py:112
  181.8 13.3 %collective-permute-start.42 = (bf16[96,768]{1,0:T(8,128)(2,1)S(1)}, bf16[96,768]{1,0:T(8,128)(2,1)S(1)}, u32[]{:S(2)}, u32[]{:S(2)}) collective-permute-start(bf16[96,768]{1,0:T(8,128)(2,1)S(1)} %get-tuple-element.238), channel_id=1, source_target_pairs={{0,16},{1,17},{2,18},{3,19},{4,20},{5,21},{6,22},{7,23},{8,24},{9,... | collective-permute-start | bytes 442376 | tf_op jit(solution)/shard_map/ppermute | solution.py:107
  184.2 10.9 %collective-permute-start.43 = (bf16[96,768]{1,0:T(8,128)(2,1)S(1)}, bf16[96,768]{1,0:T(8,128)(2,1)S(1)}, u32[]{:S(2)}, u32[]{:S(2)}) collective-permute-start(bf16[96,768]{1,0:T(8,128)(2,1)S(1)} %get-tuple-element.239), channel_id=1, source_target_pairs={{0,24},{1,25},{2,26},{3,27},{4,28},{5,29},{6,30},{7,31},{8,0},{9,1... | collective-permute-start | bytes 442376 | tf_op jit(solution)/shard_map/ppermute | solution.py:107
  185.1 20.5 %collective-permute-start.39 = (bf16[512,768]{1,0:T(8,128)(2,1)S(1)}, bf16[512,768]{1,0:T(8,128)(2,1)S(1)}, u32[]{:S(2)}, u32[]{:S(2)}) collective-permute-start(bf16[512,768]{1,0:T(8,128)(2,1)S(1)} %copy-done.5), channel_id=1, source_target_pairs={{0,2},{1,3},{2,0},{3,1},{4,6},{5,7},{6,4},{7,5},{8,10},{9,11},{10,... | collective-permute-start | bytes 2359304 | tf_op jit(solution)/shard_map/ppermute | solution.py:104
  195.8 25.3 %collective-permute-start.47 = (bf16[512,768]{1,0:T(8,128)(2,1)S(1)}, bf16[512,768]{1,0:T(8,128)(2,1)S(1)}, u32[]{:S(2)}, u32[]{:S(2)}) collective-permute-start(bf16[512,768]{1,0:T(8,128)(2,1)S(1)} %copy-done.2), channel_id=1, source_target_pairs={{0,2},{1,3},{2,0},{3,1},{4,6},{5,7},{6,4},{7,5},{8,10},{9,11},{10,... | collective-permute-start | bytes 2359304 | tf_op jit(solution)/shard_map/ppermute | solution.py:104
  199.3 10.8 %collective-permute-start.48 = (bf16[48,1536]{1,0:T(8,128)(2,1)S(1)}, bf16[48,1536]{1,0:T(8,128)(2,1)S(1)}, u32[]{:S(2)}, u32[]{:S(2)}) collective-permute-start(bf16[48,1536]{1,0:T(8,128)(2,1)S(1)} %get-tuple-element.247), channel_id=1, source_target_pairs={{0,16},{1,17},{2,18},{3,19},{4,20},{5,21},{6,22},{7,23},{8,24},{9,... | collective-permute-start | bytes 442376 | tf_op jit(solution)/shard_map/ppermute | solution.py:107
  205.1 24.0 %collective-permute-start.50 = (bf16[512,768]{1,0:T(8,128)(2,1)S(1)}, bf16[512,768]{1,0:T(8,128)(2,1)S(1)}, u32[]{:S(2)}, u32[]{:S(2)}) collective-permute-start(bf16[512,768]{1,0:T(8,128)(2,1)S(1)} %copy-done.2), channel_id=1, source_target_pairs={{0,1},{1,0},{2,3},{3,2},{4,5},{5,4},{6,7},{7,6},{8,9},{9,8},{10,11... | collective-permute-start | bytes 2359304 | tf_op jit(solution)/shard_map/ppermute | solution.py:98
  207.3 17.9 %collective-permute-start.45 = (bf16[512,768]{1,0:T(8,128)(2,1)S(1)}, bf16[512,768]{1,0:T(8,128)(2,1)}, u32[]{:S(2)}, u32[]{:S(2)}) collective-permute-start(bf16[512,768]{1,0:T(8,128)(2,1)S(1)} %get-tuple-element.243.own), channel_id=1, source_target_pairs={{0,1},{1,0},{2,3},{3,2},{4,5},{5,4},{6,7},{7,6},{8,9},{9,8},{10,11... | collective-permute-start | bytes 2359304 | tf_op jit(solution)/shard_map/ppermute | solution.py:98
  210.0 15.1 %collective-permute-start.46 = (bf16[512,768]{1,0:T(8,128)(2,1)}, bf16[512,768]{1,0:T(8,128)(2,1)}, u32[]{:S(2)}, u32[]{:S(2)}) collective-permute-start(bf16[512,768]{1,0:T(8,128)(2,1)} %get-tuple-element.244.by_y), channel_id=1, source_target_pairs={{0,1},{1,0},{2,3},{3,2},{4,5},{5,4},{6,7},{7,6},{8,9},{9,8},{10,11... | collective-permute-start | bytes 2359304 | tf_op jit(solution)/shard_map/ppermute | solution.py:98
  221.1 11.5 %collective-permute-start.52 = (f32[48,768]{1,0:T(8,128)S(1)}, f32[48,768]{1,0:T(8,128)S(1)}, u32[]{:S(2)}, u32[]{:S(2)}) collective-permute-start(f32[48,768]{1,0:T(8,128)S(1)} %get-tuple-element.255), channel_id=1, source_target_pairs={{0,1},{1,0},{2,3},{3,2},{4,5},{5,4},{6,7},{7,6},{8,9},{9,8},{10,11... | collective-permute-start | bytes 442376 | tf_op jit(solution)/shard_map/ppermute | solution.py:98
  221.6 11.0 %all-to-all-start.1 = ((f32[32,1,512]{2,1,0:T(1,128)}), f32[32,1,512]{2,1,0:T(1,128)S(1)}, u32[]{:S(2)}, u32[]{:S(2)}) async-start(f32[32,1,512]{2,1,0:T(1,128)} %get-tuple-element.253), calls=%async_computation.1 | async-start | bytes 131072 | tf_op jit(solution)/shard_map/all_to_all | solution.py:1136
  (56 other events, 683.2 us)

commit v6 on v5

--- a/solution.py
+++ b/solution.py
@@ -666,7 +666,23 @@
     per = got.shape[2] // LANES - 1
     total = jnp.sum(got[:, 0, per * LANES :], axis=0, keepdims=True)[:, 0:1]
     norm = jnp.sqrt(total)
-    refs[-1][...] = norm
+    results = 3 * len(rates) + 1
+    inputs = 4 * 4 + 3 * 3
+    sources, finals = refs[:inputs], refs[inputs : inputs + results]
+    ins, bufs = refs[inputs + results : -2 - results], refs[-2 - results : -2]
+    sem_in, sem_out = refs[-2:]
+    loads = [
+        pltpu.make_async_copy(source, buf, sem_in.at[i])
+        for i, (source, buf) in enumerate(zip(sources, ins))
+    ]
+    stores = [
+        pltpu.make_async_copy(buf, final, sem_out.at[i])
+        for i, (buf, final) in enumerate(zip(bufs, finals))
+    ]
+    for load in loads:
+        load.start()
+    bufs[-1][...] = norm
+    stores[-1].start()
     factor = jnp.minimum(1.0, CLIP / norm)
     correction = 1.0 - BETA**STEP
     width, quarter, part = plan.width, plan.width // 4, plan.part
@@ -692,8 +708,10 @@
         ),
         owned(lambda m: line(8 * width + m * part, part)),
     )
-    ins, outs = refs[: 4 * 4 + 3 * 3], refs[4 * 4 + 3 * 3 : -1]
+    outs = bufs[:-1]
     attn = {}
+    for i in (3, 7):
+        loads[i].wait()
     if plan.direct:
         mine, other = ins[3][...], ins[7][...]
         low = jnp.where(meta[4] == 0, mine, other)
@@ -703,12 +721,17 @@
             attn[p] = jnp.concatenate([low[:, at], high[:, at]], axis=0)
     for i, (rate, decay) in enumerate(rates):
         if i < 4:
+            first_in = 4 * i
             w_ref, m_ref, s_ref, g_ref = ins[4 * i : 4 * i + 4]
             if plan.direct and i < 2:
                 g_ref = attn if i == 0 else {Ellipsis: attn[3].T}
         else:
+            first_in = 3 * i + 4
             w_ref, m_ref, s_ref = ins[3 * i + 4 : 3 * i + 7]
             g_ref = {Ellipsis: small[i - 4]}
+        for j in range(first_in, first_in + (4 if i < 4 else 3)):
+            if j not in (3, 7):
+                loads[j].wait()
         m_out, s_out, w_out = outs[3 * i : 3 * i + 3]
         planes = range(w_ref.shape[0]) if len(w_ref.shape) == 3 else (Ellipsis,)
         for p in planes:
@@ -723,6 +746,10 @@
             m_out[p] = first.reshape(shape)
             s_out[p] = second.reshape(shape)
             w_out[p] = (weight - rate * (direction + decay * weight)).reshape(shape)
+        for store in stores[3 * i : 3 * i + 3]:
+            store.start()
+    for store in stores:
+        store.wait()
 
 
 def after(value, *others):
@@ -1154,15 +1181,16 @@
     flat = [got] + [v for group in groups for v in group]
     new_shapes = [SDS(group[0].shape, f32) for group in groups for _ in range(3)]
     new_shapes.append(SDS((1, 1), f32))
-    new = call(
+    new = local_call(
+        meta,
         functools.partial(adam_kernel, plan, (matrix,) * 4 + (vector,) * 3),
         "adam",
-        (1,),
-        [(v, *whole(v.shape)) for v in flat],
-        [(s, *whole(s.shape)) for s in new_shapes],
-        [],
-        vmem=60,
-    )(meta, *flat)
+        [(flat[0], True)] + [(v, False) for v in flat[1:]],
+        [(v, False) for v in new_shapes],
+        [pltpu.VMEM(v.shape, f32) for v in (*flat[1:], *new_shapes)]
+        + [dma((len(flat) - 1,)), dma((len(new_shapes),))],
+        vmem=32,
+    )
     new = list(new)
     gradient_norm = new.pop().reshape(())
     new[9:12] = [v.T for v in new[9:12]]

time: 239 us -> 238 us (level)
    pallas_call x1 -> x0, Pallas kernels: 5.07 us -> none  [per_device(): call(functools.partial(adam_kernel, plan, (matrix,) * 4 + (vector,) * 3),...]
    pallas_call x10 -> x11, Pallas kernels: 61.9 us -> 66.1 us  [local_call(): return kernel_call(meta, *map(place, ins))]
where the time goes in v6:
time: 238 us
  Pallas kernels  85.9 us (36%)
  waiting for transfers between devices  67.9 us (29%)
  starting transfers between devices  53.2 us (22%)
  blocking collectives  19.4 us (8%)
  local copies, waits for them, and re-layouts  5.13 us (2%)
  other arithmetic  4.49 us (2%)
    pallas_call x11, Pallas kernels, local_call(): return kernel_call(meta, *map(place, ins))  66.1 us
    ppermute x18, waiting for transfers between devices, along_z(): lax.ppermute(value, AXES, self.perm(lambda z, x, y, c: ((z + step) % self...  30.2 us
    ppermute x18, starting transfers between devices, along_z(): lax.ppermute(value, AXES, self.perm(lambda z, x, y, c: ((z + step) % self...  27.3 us
    all_to_all x1, blocking collectives, per_device(): got = lax.all_to_all(vectors, AXES, 0, 0, tiled=True)  19.4 us
    ppermute x6, waiting for transfers between devices, along_y(): lax.ppermute(value, AXES, self.perm(lambda z, x, y, c: (z, x, 1 - y, c)))  15.9 us
    ppermute x4, waiting for transfers between devices, along_x(): lax.ppermute(value, AXES, self.perm(lambda z, x, y, c: (z, 1 - x, y, c)))  15.1 us
    ppermute x6, starting transfers between devices, along_y(): lax.ppermute(value, AXES, self.perm(lambda z, x, y, c: (z, x, 1 - y, c)))  8.3 us
    pallas_call x2, Pallas kernels, everywhere(): call(place_kernel, 'place', (1,), [(b, *whole((count, width))) for b in b...  7.2 us
  transfers between devices with their start and end apart: 54, of which 19 were waited for; matrix products, arithmetic and copies ran while one was open for 2% of the time, Pallas kernels for 28%

profile of v6, /device:TPU:0, one launch (start us, length us, event | category | flops | bytes accessed | tf_op | source)
XLA Modules:
  0.0 237.6 jit_solution(7643070411043018761)
XLA Ops:
  4.4 5.0 %collective-permute-start.3 = (bf16[48,1536]{1,0:T(8,128)(2,1)S(1)}, bf16[48,1536]{1,0:T(8,128)(2,1)S(1)}, u32[]{:S(2)}, u32[]{:S(2)}) collective-permute-start(bf16[48,1536]{1,0:T(8,128)(2,1)S(1)} %bitcast.89), channel_id=1, source_target_pairs={{0,24},{1,25},{2,26},{3,27},{4,28},{5,29},{6,30},{7,31},{8,0},{9,1... | collective-permute-start | bytes 442376 | tf_op jit(solution)/shard_map/ppermute | solution.py:107
  10.7 3.0 %collective-permute-done.3 = bf16[48,1536]{1,0:T(8,128)(2,1)S(1)} collective-permute-done((bf16[48,1536]{1,0:T(8,128)(2,1)S(1)}, bf16[48,1536]{1,0:T(8,128)(2,1)S(1)}, u32[]{:S(2)}, u32[]{:S(2)}) %collective-permute-start.3) | collective-permute-done | bytes 147488 | tf_op jit(solution)/shard_map/ppermute | solution.py:107
  13.7 8.5 %collective-permute-done.2 = bf16[48,1536]{1,0:T(8,128)(2,1)S(1)} collective-permute-done((bf16[48,1536]{1,0:T(8,128)(2,1)S(1)}, bf16[48,1536]{1,0:T(8,128)(2,1)S(1)}, u32[]{:S(2)}, u32[]{:S(2)}) %collective-permute-start.2) | collective-permute-done | bytes 147488 | tf_op jit(solution)/shard_map/ppermute | solution.py:107
  29.7 2.6 %collective-permute-done.4 = bf16[4,48,1536]{2,1,0:T(8,128)(2,1)S(1)} collective-permute-done((bf16[4,48,1536]{2,1,0:T(8,128)(2,1)S(1)}, bf16[4,48,1536]{2,1,0:T(8,128)(2,1)S(1)}, u32[]{:S(2)}, u32[]{:S(2)}) %collective-permute-start.4) | collective-permute-done | bytes 589856 | tf_op jit(solution)/shard_map/ppermute | solution.py:112
  37.7 2.3 attn_prep.1
  41.1 5.1 %collective-permute-done.9 = bf16[96,768]{1,0:T(8,128)(2,1)S(1)} collective-permute-done((bf16[96,768]{1,0:T(8,128)(2,1)S(1)}, bf16[96,768]{1,0:T(8,128)(2,1)S(1)}, u32[]{:S(2)}, u32[]{:S(2)}) %collective-permute-start.9) | collective-permute-done | bytes 147488 | tf_op jit(solution)/shard_map/ppermute | solution.py:107
  46.2 3.7 %collective-permute-done.8.refs_1_ = bf16[2,4,48,1536]{3,2,1,0:T(8,128)(2,1)} collective-permute-done((bf16[2,4,48,1536]{3,2,1,0:T(8,128)(2,1)}, bf16[2,4,48,1536]{3,2,1,0:T(8,128)(2,1)}, u32[]{:S(2)}, u32[]{:S(2)}) %collective-permute-start.8) | collective-permute-done | bytes 1179680 | tf_op jit(solution)/shard_map/ppermute | solution.py:119
  56.6 12.1 %attn_fwd.1 = (bf16[512,768]{1,0:T(8,128)(2,1)}, f32[512,768]{1,0:T(8,128)S(1)}, bf16[2,512,1152]{2,1,0:T(8,128)(2,1)S(1)}, bf16[8,768,128]{2,1,0:T(8,128)(2,1)S...) custom-call(s32[6]{0:T(128)S(1)} %stack.94.meta, bf16[512,768]{1,0:T(8,128)(2,1)S(1)} %get-tuple-element.155.x_ref, ...), custom_call_target="tpu_custom_call" | custom-call | flops 1 | bytes 1 | tf_op jit(solution)/shard_map/attn_fwd/pallas_call | solution.py:780
  71.6 12.0 %collective-permute-done.20.refs_5_ = bf16[4,96,768]{2,1,0:T(8,128)(2,1)S(1)} collective-permute-done((bf16[4,96,768]{2,1,0:T(8,128)(2,1)S(1)}, bf16[4,96,768]{2,1,0:T(8,128)(2,1)S(1)}, u32[]{:S(2)}, u32[]{:S(2)}) %collective-permute-start.20) | collective-permute-done | bytes 589856 | tf_op jit(solution)/shard_map/ppermute | solution.py:101
  83.6 4.6 %collective-permute-done.13.sl_ref.sl_b = bf16[512,768]{1,0:T(8,128)(2,1)S(1)} collective-permute-done((bf16[512,768]{1,0:T(8,128)(2,1)}, bf16[512,768]{1,0:T(8,128)(2,1)S(1)}, u32[]{:S(2)}, u32[]{:S(2)}) %collective-permute-start.13) | collective-permute-done | bytes 786464 | tf_op jit(solution)/shard_map/ppermute | solution.py:104
  89.1 10.4 %ff_far.1 = (bf16[512,768]{1,0:T(8,128)(2,1)}, bf16[512,768]{1,0:T(8,128)(2,1)}, bf16[2,512,768]{2,1,0:T(8,128)(2,1)S(1)}, bf16[2,512,768]{2,1,0:T(8,128)(2,1)S(...) custom-call(s32[6]{0:T(128)S(1)} %stack.94.meta, ...), custom_call_target="tpu_custom_call" | custom-call | flops 1 | bytes 1 | tf_op jit(solution)/shard_map/ff_far/pallas_call | solution.py:780
  101.1 8.4 %ff_near.1 = (bf16[512,768]{1,0:T(8,128)(2,1)S(1)}, bf16[512,768]{1,0:T(8,128)(2,1)}, bf16[2,512,768]{2,1,0:T(8,128)(2,1)S(1)}, bf16[2,512,768]{2,1,0:T(8,128)(2...) custom-call(s32[6]{0:T(128)S(1)} %stack.94.meta, bf16[512,768]{1,0:T(8,128)(2,1)S(1)} %copy-done, ...), custom_call_target="tpu_custom_call" | custom-call | flops 1 | bytes 1 | tf_op jit(solution)/shard_map/ff_near/pallas_call | solution.py:780
  109.5 7.4 %ff_grad.1 = (bf16[4,96,768]{2,1,0:T(8,128)(2,1)}, bf16[4,96,768]{2,1,0:T(8,128)(2,1)}, bf16[4,96,768]{2,1,0:T(8,128)(2,1)}, bf16[4,96,768]{2,1,0:T(8,128)(2,1)}...) custom-call(s32[6]{0:T(128)S(1)} %stack.94.meta, ...), custom_call_target="tpu_custom_call" | custom-call | flops 1 | bytes 1 | tf_op jit(solution)/shard_map/ff_grad/pallas_call | solution.py:780
  120.0 7.3 %attn_bwd.1 = (bf16[2,512,1152]{2,1,0:T(8,128)(2,1)S(1)}, bf16[512,768]{1,0:T(8,128)(2,1)S(1)}, f32[512,768]{1,0:T(8,128)S(1)}, f32[8,768]{1,0:T(8,128)S(1)}, f32[2,768]{1,0:T(2,128)S(1)}) custom-call(s32[6]{0:T(128)S(1)} %stack.94.meta, bf16[512,768]{1,0:T(8,128)(2,1)S(1)} %get-tuple-element.185.sga_ref, ...), custom_call_target="tpu_custom_call" | custom-call | flops 1 | bytes 1 | tf_op jit(solution)/shard_map/attn_bwd/pallas_call | solution.py:780
  130.6 5.0 %attn_grad.1 = (bf16[2,2,48,1536]{3,2,1,0:T(8,128)(2,1)S(1)}, bf16[2,2,48,1536]{3,2,1,0:T(8,128)(2,1)S(1)}, bf16[2,2,48,1536]{3,2,1,0:T(8,128)(2,1)S(1)}, bf16[2...) custom-call(s32[6]{0:T(128)S(1)} %stack.94.meta, ...), custom_call_target="tpu_custom_call" | custom-call | flops 1 | bytes 1 | tf_op jit(solution)/shard_map/attn_grad/pallas_call | solution.py:780
  136.7 4.5 %input_grad.1 = (bf16[512,768]{1,0:T(8,128)(2,1)}, f32[8,768]{1,0:T(8,128)S(1)}) custom-call(s32[6]{0:T(128)S(1)} %stack.94.meta, bf16[512,768]{1,0:T(8,128)(2,1)S(1)} %get-tuple-element.155.x_ref, f32[512,768]{1,0:T(8,128)S(1)} %get-tuple-element.209.mg_ref, f32[6,768]{1,0:T(8,128)S(1)} %copy-done.1, bf16[2,512,1152]{2,1,0:T(8,128)(2,1)S(1)} %get-tuple-element.210.dqkv_ref, ...), custom_call_target="tpu_custom_call" | custom-call | flops 1 | bytes 1 | tf_op jit(solution)/shard_map/input_grad/pallas_call | solution.py:780
  141.3 3.1 %collective-permute-done.30.right = bf16[4,96,768]{2,1,0:T(8,128)(2,1)S(1)} collective-permute-done((bf16[4,96,768]{2,1,0:T(8,128)(2,1)S(1)}, bf16[4,96,768]{2,1,0:T(8,128)(2,1)S(1)}, u32[]{:S(2)}, u32[]{:S(2)}) %collective-permute-start.30) | collective-permute-done | bytes 589856 | tf_op jit(solution)/shard_map/ppermute | solution.py:101
  145.8 3.3 %add_first.1 = (bf16[2,4,48,1536]{3,2,1,0:T(8,128)(2,1)S(1)}, bf16[2,4,48,1536]{3,2,1,0:T(8,128)(2,1)}) custom-call(s32[6]{0:T(128)S(1)} %stack.94.meta, bf16[2,2,48,1536]{3,2,1,0:T(8,128)(2,1)S(1)} %get-tuple-element.203.refs_0_, bf16[2,2,48,1536]{3,2,1,0:T(8,128)(2,1)S(1)} %get-tuple-element.204.refs_1_, ...), custom_call_target="tpu_custom_call" | custom-call | flops 1 | bytes 1 | tf_op jit(solution)/shard_map/add_first/pallas_call | solution.py:780
  153.0 2.5 %collective-permute-start.37 = (bf16[96,768]{1,0:T(8,128)(2,1)}, bf16[96,768]{1,0:T(8,128)(2,1)S(1)}, u32[]{:S(2)}, u32[]{:S(2)}) collective-permute-start(bf16[96,768]{1,0:T(8,128)(2,1)} %get-tuple-element.228), channel_id=1, source_target_pairs={{0,16},{1,17},{2,18},{3,19},{4,20},{5,21},{6,22},{7,23},{8,24},{9,... | collective-permute-start | bytes 442376 | tf_op jit(solution)/shard_map/ppermute | solution.py:107
  157.5 19.4 %all_to_all.10 = f32[32,1,384]{2,1,0:T(1,128)S(1)} all-to-all(f32[32,1,384]{2,1,0:T(1,128)} %vectors.1), channel_id=1, replica_groups=mesh['dp'=8,'mp'=4] {'dp','mp'}, dimensions={0} | all-to-all | bytes 98304 | tf_op jit(solution)/shard_map/all_to_all | solution.py:1087
  181.7 2.5 %collective-permute-start.42 = (bf16[96,768]{1,0:T(8,128)(2,1)S(1)}, bf16[96,768]{1,0:T(8,128)(2,1)S(1)}, u32[]{:S(2)}, u32[]{:S(2)}) collective-permute-start(bf16[96,768]{1,0:T(8,128)(2,1)S(1)} %get-tuple-element.238), channel_id=1, source_target_pairs={{0,16},{1,17},{2,18},{3,19},{4,20},{5,21},{6,22},{7,23},{8,24},{9,... | collective-permute-start | bytes 442376 | tf_op jit(solution)/shard_map/ppermute | solution.py:107
  186.6 3.3 %collective-permute-done.41.refs_5_ = bf16[96,768]{1,0:T(8,128)(2,1)S(1)} collective-permute-done((bf16[96,768]{1,0:T(8,128)(2,1)S(1)}, bf16[96,768]{1,0:T(8,128)(2,1)S(1)}, u32[]{:S(2)}, u32[]{:S(2)}) %collective-permute-start.41) | collective-permute-done | bytes 147488 | tf_op jit(solution)/shard_map/ppermute | solution.py:107
  189.9 5.2 %collective-permute-done.42.refs_6_ = bf16[96,768]{1,0:T(8,128)(2,1)S(1)} collective-permute-done((bf16[96,768]{1,0:T(8,128)(2,1)S(1)}, bf16[96,768]{1,0:T(8,128)(2,1)S(1)}, u32[]{:S(2)}, u32[]{:S(2)}) %collective-permute-start.42) | collective-permute-done | bytes 147488 | tf_op jit(solution)/shard_map/ppermute | solution.py:107
  196.4 2.8 %collective-permute-start.44 = (bf16[48,1536]{1,0:T(8,128)(2,1)S(1)}, bf16[48,1536]{1,0:T(8,128)(2,1)S(1)}, u32[]{:S(2)}, u32[]{:S(2)}) collective-permute-start(bf16[48,1536]{1,0:T(8,128)(2,1)S(1)} %get-tuple-element.241), channel_id=1, source_target_pairs={{0,8},{1,9},{2,10},{3,11},{4,12},{5,13},{6,14},{7,15},{8,16},{9,17... | collective-permute-start | bytes 442376 | tf_op jit(solution)/shard_map/ppermute | solution.py:107
  201.6 2.3 ff_total.1
  207.3 2.7 %collective-permute-done.48.refs_2_ = bf16[48,1536]{1,0:T(8,128)(2,1)S(1)} collective-permute-done((bf16[48,1536]{1,0:T(8,128)(2,1)S(1)}, bf16[48,1536]{1,0:T(8,128)(2,1)S(1)}, u32[]{:S(2)}, u32[]{:S(2)}) %collective-permute-start.48) | collective-permute-done | bytes 147488 | tf_op jit(solution)/shard_map/ppermute | solution.py:107
  210.0 2.3 total.1
  213.0 8.1 %collective-permute-done.47.by_y = bf16[512,768]{1,0:T(8,128)(2,1)S(1)} collective-permute-done((bf16[512,768]{1,0:T(8,128)(2,1)S(1)}, bf16[512,768]{1,0:T(8,128)(2,1)S(1)}, u32[]{:S(2)}, u32[]{:S(2)}) %collective-permute-start.47) | collective-permute-done | bytes 786464 | tf_op jit(solution)/shard_map/ppermute | solution.py:104
  221.6 3.5 %all-to-all-start.1 = ((f32[32,1,512]{2,1,0:T(1,128)}), f32[32,1,512]{2,1,0:T(1,128)S(1)}, u32[]{:S(2)}, u32[]{:S(2)}) async-start(f32[32,1,512]{2,1,0:T(1,128)} %get-tuple-element.253), calls=%async_computation.1 | async-start | bytes 131072 | tf_op jit(solution)/shard_map/all_to_all | solution.py:1163
  225.2 3.8 %place.2 = bf16[2048,768]{1,0:T(8,128)(2,1)} custom-call(s32[6]{0:T(128)S(1)} %stack.94.meta, bf16[512,768]{1,0:T(8,128)(2,1)S(1)} %get-tuple-element.243.own, bf16[512,768]{1,0:T(8,128)(2,1)} %get-tuple-element.244.by_y, bf16[512,768]{1,0:T(8,128)(2,1)} %collective-permute-done.45.by_c, bf16[512,768]{1,0:T(8,128)(2,1)} %collective-permute-done.46.by_yc), custom_call_target="tpu_custom_call" | custom-call | flops 1 | bytes 1 | tf_op jit(solution)/shard_map/place/pallas_call | solution.py:1135
  229.0 3.4 %place.3 = bf16[2048,768]{1,0:T(8,128)(2,1)} custom-call(s32[6]{0:T(128)S(1)} %stack.94.meta, bf16[512,768]{1,0:T(8,128)(2,1)S(1)} %copy-done.2, bf16[512,768]{1,0:T(8,128)(2,1)S(1)} %collective-permute-done.47.by_y, bf16[512,768]{1,0:T(8,128)(2,1)S(1)} %collective-permute-done.50.by_c, bf16[512,768]{1,0:T(8,128)(2,1)} %collective-permute-done.51.by_yc), custom_call_target="tpu_custom_call" | custom-call | flops 1 | bytes 1 | tf_op jit(solution)/shard_map/place/pallas_call | solution.py:1135
  233.2 4.2 %adam.1 = (f32[3,96,192]{2,1,0:T(8,128)}, f32[3,96,192]{2,1,0:T(8,128)}, f32[3,96,192]{2,1,0:T(8,128)}, f32[192,96]{1,0:T(8,128)}, f32[192,96]{1,0:T(8,128)}, /*...) custom-call(s32[6]{0:T(128)S(1)} %stack.94.meta, ...), custom_call_target="tpu_custom_call" | custom-call | flops 1 | bytes 1 | tf_op jit(solution)/shard_map/adam/pallas_call | solution.py:780
  (196 shorter events, 61.5 us)
Async XLA Ops:
  9.4 12.8 %collective-permute-start.2 = (bf16[48,1536]{1,0:T(8,128)(2,1)S(1)}, bf16[48,1536]{1,0:T(8,128)(2,1)S(1)}, u32[]{:S(2)}, u32[]{:S(2)}) collective-permute-start(bf16[48,1536]{1,0:T(8,128)(2,1)S(1)} %bitcast.90), channel_id=1, source_target_pairs={{0,16},{1,17},{2,18},{3,19},{4,20},{5,21},{6,22},{7,23},{8,24},{9,... | collective-permute-start | bytes 442376 | tf_op jit(solution)/shard_map/ppermute | solution.py:107
  9.4 12.8 %collective-permute-start.1 = (bf16[48,1536]{1,0:T(8,128)(2,1)S(1)}, bf16[48,1536]{1,0:T(8,128)(2,1)S(1)}, u32[]{:S(2)}, u32[]{:S(2)}) collective-permute-start(bf16[48,1536]{1,0:T(8,128)(2,1)S(1)} %bitcast.91), channel_id=1, source_target_pairs={{0,8},{1,9},{2,10},{3,11},{4,12},{5,13},{6,14},{7,15},{8,16},{9,17... | collective-permute-start | bytes 442376 | tf_op jit(solution)/shard_map/ppermute | solution.py:107
  33.4 16.5 %collective-permute-start.8 = (bf16[2,4,48,1536]{3,2,1,0:T(8,128)(2,1)}, bf16[2,4,48,1536]{3,2,1,0:T(8,128)(2,1)}, u32[]{:S(2)}, u32[]{:S(2)}) collective-permute-start(bf16[2,4,48,1536]{3,2,1,0:T(8,128)(2,1)} %pad_maximum_fusion.refs_0_), channel_id=1, source_target_pairs={{0,2},{1,5},{2,0},{3,7},{4,6},{5,1},{6,4},{7,3},{8,10},{9,13},{10,... | collective-permute-start | bytes 3538952 | tf_op jit(solution)/shard_map/ppermute | solution.py:119
  37.7 17.3 %collective-permute-start.11 = (bf16[2,4,48,1536]{3,2,1,0:T(8,128)(2,1)}, bf16[2,4,48,1536]{3,2,1,0:T(8,128)(2,1)}, u32[]{:S(2)}, u32[]{:S(2)}) collective-permute-start(bf16[2,4,48,1536]{3,2,1,0:T(8,128)(2,1)} %pad_maximum_fusion.refs_0_), channel_id=1, source_target_pairs={{0,1},{1,0},{2,3},{3,2},{4,5},{5,4},{6,7},{7,6},{8,9},{9,8},{10,11... | collective-permute-start | bytes 3538952 | tf_op jit(solution)/shard_map/ppermute | solution.py:98
  50.0 18.8 %collective-permute-start.19 = (bf16[96,768]{1,0:T(8,128)(2,1)S(1)}, bf16[96,768]{1,0:T(8,128)(2,1)S(1)}, u32[]{:S(2)}, u32[]{:S(2)}) collective-permute-start(bf16[96,768]{1,0:T(8,128)(2,1)S(1)} %bitcast_convert_fusion), channel_id=1, source_target_pairs={{0,24},{1,25},{2,26},{3,27},{4,28},{5,29},{6,30},{7,31},{8,0},{9,1... | collective-permute-start | bytes 442376 | tf_op jit(solution)/shard_map/ppermute | solution.py:107
  51.4 17.4 %collective-permute-start.18 = (bf16[96,768]{1,0:T(8,128)(2,1)S(1)}, bf16[96,768]{1,0:T(8,128)(2,1)S(1)}, u32[]{:S(2)}, u32[]{:S(2)}) collective-permute-start(bf16[96,768]{1,0:T(8,128)(2,1)S(1)} %bitcast_convert_fusion), channel_id=1, source_target_pairs={{0,16},{1,17},{2,18},{3,19},{4,20},{5,21},{6,22},{7,23},{8,24},{9,... | collective-permute-start | bytes 442376 | tf_op jit(solution)/shard_map/ppermute | solution.py:107
  52.9 15.9 %collective-permute-start.17 = (bf16[96,768]{1,0:T(8,128)(2,1)S(1)}, bf16[96,768]{1,0:T(8,128)(2,1)S(1)}, u32[]{:S(2)}, u32[]{:S(2)}) collective-permute-start(bf16[96,768]{1,0:T(8,128)(2,1)S(1)} %bitcast_convert_fusion), channel_id=1, source_target_pairs={{0,8},{1,9},{2,10},{3,11},{4,12},{5,13},{6,14},{7,15},{8,16},{9,17... | collective-permute-start | bytes 442376 | tf_op jit(solution)/shard_map/ppermute | solution.py:107
  55.1 15.9 %collective-permute-start.14 = (bf16[4,96,768]{2,1,0:T(8,128)(2,1)S(1)}, bf16[4,96,768]{2,1,0:T(8,128)(2,1)S(1)}, u32[]{:S(2)}, u32[]{:S(2)}) collective-permute-start(bf16[4,96,768]{2,1,0:T(8,128)(2,1)S(1)} %pad_maximum_fusion.2.refs_0_), channel_id=1, source_target_pairs={{0,4},{1,5},{2,6},{3,7},{4,0},{5,1},{6,2},{7,3},{8,12},{9,13},{10,... | collective-permute-start | bytes 1769480 | tf_op jit(solution)/shard_map/ppermute | solution.py:101
  68.9 14.7 %collective-permute-start.20 = (bf16[4,96,768]{2,1,0:T(8,128)(2,1)S(1)}, bf16[4,96,768]{2,1,0:T(8,128)(2,1)S(1)}, u32[]{:S(2)}, u32[]{:S(2)}) collective-permute-start(bf16[4,96,768]{2,1,0:T(8,128)(2,1)S(1)} %pad_maximum_fusion.3.refs_4_), channel_id=1, source_target_pairs={{0,4},{1,5},{2,6},{3,7},{4,0},{5,1},{6,2},{7,3},{8,12},{9,13},{10,... | collective-permute-start | bytes 1769480 | tf_op jit(solution)/shard_map/ppermute | solution.py:101
  69.5 18.8 %collective-permute-start.13 = (bf16[512,768]{1,0:T(8,128)(2,1)}, bf16[512,768]{1,0:T(8,128)(2,1)S(1)}, u32[]{:S(2)}, u32[]{:S(2)}) collective-permute-start(bf16[512,768]{1,0:T(8,128)(2,1)} %get-tuple-element.164.sl_ref.sl_a), channel_id=1, source_target_pairs={{0,2},{1,3},{2,0},{3,1},{4,6},{5,7},{6,4},{7,5},{8,10},{9,11},{10,... | collective-permute-start | bytes 2359304 | tf_op jit(solution)/shard_map/ppermute | solution.py:104
  71.0 12.6 %collective-permute-start.15 = (bf16[4,96,768]{2,1,0:T(8,128)(2,1)S(1)}, bf16[4,96,768]{2,1,0:T(8,128)(2,1)S(1)}, u32[]{:S(2)}, u32[]{:S(2)}) collective-permute-start(bf16[4,96,768]{2,1,0:T(8,128)(2,1)S(1)} %pad_maximum_fusion.2.refs_0_), channel_id=1, source_target_pairs={{0,1},{1,0},{2,3},{3,2},{4,5},{5,4},{6,7},{7,6},{8,9},{9,8},{10,11... | collective-permute-start | bytes 1769480 | tf_op jit(solution)/shard_map/ppermute | solution.py:98
  71.0 12.6 %collective-permute-start.16 = (bf16[4,96,768]{2,1,0:T(8,128)(2,1)S(1)}, bf16[4,96,768]{2,1,0:T(8,128)(2,1)S(1)}, u32[]{:S(2)}, u32[]{:S(2)}) collective-permute-start(bf16[4,96,768]{2,1,0:T(8,128)(2,1)S(1)} %collective-permute-done.14.refs_1_), channel_id=1, source_target_pairs={{0,1},{1,0},{2,3},{3,2},{4,5},{5,4},{6,7},{7,6},{8,9},{9,8},{10,11... | collective-permute-start | bytes 1769480 | tf_op jit(solution)/shard_map/ppermute | solution.py:98
  71.5 12.1 %collective-permute-start.21 = (bf16[4,96,768]{2,1,0:T(8,128)(2,1)S(1)}, bf16[4,96,768]{2,1,0:T(8,128)(2,1)S(1)}, u32[]{:S(2)}, u32[]{:S(2)}) collective-permute-start(bf16[4,96,768]{2,1,0:T(8,128)(2,1)S(1)} %pad_maximum_fusion.3.refs_4_), channel_id=1, source_target_pairs={{0,1},{1,0},{2,3},{3,2},{4,5},{5,4},{6,7},{7,6},{8,9},{9,8},{10,11... | collective-permute-start | bytes 1769480 | tf_op jit(solution)/shard_map/ppermute | solution.py:98
  99.5 17.9 %collective-permute-start.23 = (bf16[512,768]{1,0:T(8,128)(2,1)}, bf16[512,768]{1,0:T(8,128)(2,1)S(1)}, u32[]{:S(2)}, u32[]{:S(2)}) collective-permute-start(bf16[512,768]{1,0:T(8,128)(2,1)} %get-tuple-element.175), channel_id=1, source_target_pairs={{0,2},{1,3},{2,0},{3,1},{4,6},{5,7},{6,4},{7,5},{8,10},{9,11},{10,... | collective-permute-start | bytes 2359304 | tf_op jit(solution)/shard_map/ppermute | solution.py:104
  117.4 18.2 %collective-permute-start.24 = (bf16[512,768]{1,0:T(8,128)(2,1)S(1)}, bf16[512,768]{1,0:T(8,128)(2,1)S(1)}, u32[]{:S(2)}, u32[]{:S(2)}) collective-permute-start(bf16[512,768]{1,0:T(8,128)(2,1)S(1)} %copy-done.3), channel_id=1, source_target_pairs={{0,2},{1,3},{2,0},{3,1},{4,6},{5,7},{6,4},{7,5},{8,10},{9,11},{10,... | collective-permute-start | bytes 2359304 | tf_op jit(solution)/shard_map/ppermute | solution.py:104
  129.2 15.2 %collective-permute-start.30 = (bf16[4,96,768]{2,1,0:T(8,128)(2,1)S(1)}, bf16[4,96,768]{2,1,0:T(8,128)(2,1)S(1)}, u32[]{:S(2)}, u32[]{:S(2)}) collective-permute-start(bf16[4,96,768]{2,1,0:T(8,128)(2,1)S(1)} %bitcast.72), channel_id=1, source_target_pairs={{0,4},{1,5},{2,6},{3,7},{4,0},{5,1},{6,2},{7,3},{8,12},{9,13},{10,... | collective-permute-start | bytes 1769480 | tf_op jit(solution)/shard_map/ppermute | solution.py:101
  149.1 27.9 %collective-permute-start.34 = (bf16[2,4,48,1536]{3,2,1,0:T(8,128)(2,1)}, bf16[2,4,48,1536]{3,2,1,0:T(8,128)(2,1)S(1)}, u32[]{:S(2)}, u32[]{:S(2)}) collective-permute-start(bf16[2,4,48,1536]{3,2,1,0:T(8,128)(2,1)} %get-tuple-element.217), channel_id=1, source_target_pairs={{0,2},{1,5},{2,0},{3,7},{4,6},{5,1},{6,4},{7,3},{8,10},{9,13},{10,... | collective-permute-start | bytes 3538952 | tf_op jit(solution)/shard_map/ppermute | solution.py:119
  149.6 27.4 %collective-permute-start.35 = (bf16[4,96,768]{2,1,0:T(8,128)(2,1)}, bf16[4,96,768]{2,1,0:T(8,128)(2,1)}, u32[]{:S(2)}, u32[]{:S(2)}) collective-permute-start(bf16[4,96,768]{2,1,0:T(8,128)(2,1)} %bitcast.33), channel_id=1, source_target_pairs={{0,4},{1,5},{2,6},{3,7},{4,0},{5,1},{6,2},{7,3},{8,12},{9,13},{10,... | collective-permute-start | bytes 1769480 | tf_op jit(solution)/shard_map/ppermute | solution.py:101
  152.4 24.6 %collective-permute-start.36 = (bf16[96,768]{1,0:T(8,128)(2,1)}, bf16[96,768]{1,0:T(8,128)(2,1)S(1)}, u32[]{:S(2)}, u32[]{:S(2)}) collective-permute-start(bf16[96,768]{1,0:T(8,128)(2,1)} %get-tuple-element.227), channel_id=1, source_target_pairs={{0,8},{1,9},{2,10},{3,11},{4,12},{5,13},{6,14},{7,15},{8,16},{9,17... | collective-permute-start | bytes 442376 | tf_op jit(solution)/shard_map/ppermute | solution.py:107
  153.0 24.0 %collective-permute-start.37 = (bf16[96,768]{1,0:T(8,128)(2,1)}, bf16[96,768]{1,0:T(8,128)(2,1)S(1)}, u32[]{:S(2)}, u32[]{:S(2)}) collective-permute-start(bf16[96,768]{1,0:T(8,128)(2,1)} %get-tuple-element.228), channel_id=1, source_target_pairs={{0,16},{1,17},{2,18},{3,19},{4,20},{5,21},{6,22},{7,23},{8,24},{9,... | collective-permute-start | bytes 442376 | tf_op jit(solution)/shard_map/ppermute | solution.py:107
  155.5 21.6 %collective-permute-start.38 = (bf16[96,768]{1,0:T(8,128)(2,1)}, bf16[96,768]{1,0:T(8,128)(2,1)}, u32[]{:S(2)}, u32[]{:S(2)}) collective-permute-start(bf16[96,768]{1,0:T(8,128)(2,1)} %get-tuple-element.229), channel_id=1, source_target_pairs={{0,24},{1,25},{2,26},{3,27},{4,28},{5,29},{6,30},{7,31},{8,0},{9,1... | collective-permute-start | bytes 442376 | tf_op jit(solution)/shard_map/ppermute | solution.py:107
  177.9 17.2 %collective-permute-start.40 = (bf16[4,48,1536]{2,1,0:T(8,128)(2,1)S(1)}, bf16[4,48,1536]{2,1,0:T(8,128)(2,1)S(1)}, u32[]{:S(2)}, u32[]{:S(2)}) collective-permute-start(bf16[4,48,1536]{2,1,0:T(8,128)(2,1)S(1)} %bitcast.73), channel_id=1, source_target_pairs={{0,4},{1,3},{2,6},{3,1},{4,0},{5,7},{6,2},{7,5},{8,12},{9,11},{10,... | collective-permute-start | bytes 1769480 | tf_op jit(solution)/shard_map/ppermute | solution.py:112
  181.7 13.4 %collective-permute-start.42 = (bf16[96,768]{1,0:T(8,128)(2,1)S(1)}, bf16[96,768]{1,0:T(8,128)(2,1)S(1)}, u32[]{:S(2)}, u32[]{:S(2)}) collective-permute-start(bf16[96,768]{1,0:T(8,128)(2,1)S(1)} %get-tuple-element.238), channel_id=1, source_target_pairs={{0,16},{1,17},{2,18},{3,19},{4,20},{5,21},{6,22},{7,23},{8,24},{9,... | collective-permute-start | bytes 442376 | tf_op jit(solution)/shard_map/ppermute | solution.py:107
  184.2 10.9 %collective-permute-start.43 = (bf16[96,768]{1,0:T(8,128)(2,1)S(1)}, bf16[96,768]{1,0:T(8,128)(2,1)S(1)}, u32[]{:S(2)}, u32[]{:S(2)}) collective-permute-start(bf16[96,768]{1,0:T(8,128)(2,1)S(1)} %get-tuple-element.239), channel_id=1, source_target_pairs={{0,24},{1,25},{2,26},{3,27},{4,28},{5,29},{6,30},{7,31},{8,0},{9,1... | collective-permute-start | bytes 442376 | tf_op jit(solution)/shard_map/ppermute | solution.py:107
  185.1 20.4 %collective-permute-start.39 = (bf16[512,768]{1,0:T(8,128)(2,1)S(1)}, bf16[512,768]{1,0:T(8,128)(2,1)S(1)}, u32[]{:S(2)}, u32[]{:S(2)}) collective-permute-start(bf16[512,768]{1,0:T(8,128)(2,1)S(1)} %copy-done.5), channel_id=1, source_target_pairs={{0,2},{1,3},{2,0},{3,1},{4,6},{5,7},{6,4},{7,5},{8,10},{9,11},{10,... | collective-permute-start | bytes 2359304 | tf_op jit(solution)/shard_map/ppermute | solution.py:104
  195.8 25.3 %collective-permute-start.47 = (bf16[512,768]{1,0:T(8,128)(2,1)S(1)}, bf16[512,768]{1,0:T(8,128)(2,1)S(1)}, u32[]{:S(2)}, u32[]{:S(2)}) collective-permute-start(bf16[512,768]{1,0:T(8,128)(2,1)S(1)} %copy-done.2), channel_id=1, source_target_pairs={{0,2},{1,3},{2,0},{3,1},{4,6},{5,7},{6,4},{7,5},{8,10},{9,11},{10,... | collective-permute-start | bytes 2359304 | tf_op jit(solution)/shard_map/ppermute | solution.py:104
  199.2 10.8 %collective-permute-start.48 = (bf16[48,1536]{1,0:T(8,128)(2,1)S(1)}, bf16[48,1536]{1,0:T(8,128)(2,1)S(1)}, u32[]{:S(2)}, u32[]{:S(2)}) collective-permute-start(bf16[48,1536]{1,0:T(8,128)(2,1)S(1)} %get-tuple-element.247), channel_id=1, source_target_pairs={{0,16},{1,17},{2,18},{3,19},{4,20},{5,21},{6,22},{7,23},{8,24},{9,... | collective-permute-start | bytes 442376 | tf_op jit(solution)/shard_map/ppermute | solution.py:107
  205.1 23.9 %collective-permute-start.50 = (bf16[512,768]{1,0:T(8,128)(2,1)S(1)}, bf16[512,768]{1,0:T(8,128)(2,1)S(1)}, u32[]{:S(2)}, u32[]{:S(2)}) collective-permute-start(bf16[512,768]{1,0:T(8,128)(2,1)S(1)} %copy-done.2), channel_id=1, source_target_pairs={{0,1},{1,0},{2,3},{3,2},{4,5},{5,4},{6,7},{7,6},{8,9},{9,8},{10,11... | collective-permute-start | bytes 2359304 | tf_op jit(solution)/shard_map/ppermute | solution.py:98
  207.3 17.9 %collective-permute-start.45 = (bf16[512,768]{1,0:T(8,128)(2,1)S(1)}, bf16[512,768]{1,0:T(8,128)(2,1)}, u32[]{:S(2)}, u32[]{:S(2)}) collective-permute-start(bf16[512,768]{1,0:T(8,128)(2,1)S(1)} %get-tuple-element.243.own), channel_id=1, source_target_pairs={{0,1},{1,0},{2,3},{3,2},{4,5},{5,4},{6,7},{7,6},{8,9},{9,8},{10,11... | collective-permute-start | bytes 2359304 | tf_op jit(solution)/shard_map/ppermute | solution.py:98
  210.0 15.1 %collective-permute-start.46 = (bf16[512,768]{1,0:T(8,128)(2,1)}, bf16[512,768]{1,0:T(8,128)(2,1)}, u32[]{:S(2)}, u32[]{:S(2)}) collective-permute-start(bf16[512,768]{1,0:T(8,128)(2,1)} %get-tuple-element.244.by_y), channel_id=1, source_target_pairs={{0,1},{1,0},{2,3},{3,2},{4,5},{5,4},{6,7},{7,6},{8,9},{9,8},{10,11... | collective-permute-start | bytes 2359304 | tf_op jit(solution)/shard_map/ppermute | solution.py:98
  221.1 11.4 %collective-permute-start.52 = (f32[48,768]{1,0:T(8,128)S(1)}, f32[48,768]{1,0:T(8,128)S(1)}, u32[]{:S(2)}, u32[]{:S(2)}) collective-permute-start(f32[48,768]{1,0:T(8,128)S(1)} %get-tuple-element.255), channel_id=1, source_target_pairs={{0,1},{1,0},{2,3},{3,2},{4,5},{5,4},{6,7},{7,6},{8,9},{9,8},{10,11... | collective-permute-start | bytes 442376 | tf_op jit(solution)/shard_map/ppermute | solution.py:98
  221.6 10.9 %all-to-all-start.1 = ((f32[32,1,512]{2,1,0:T(1,128)}), f32[32,1,512]{2,1,0:T(1,128)S(1)}, u32[]{:S(2)}, u32[]{:S(2)}) async-start(f32[32,1,512]{2,1,0:T(1,128)} %get-tuple-element.253), calls=%async_computation.1 | async-start | bytes 131072 | tf_op jit(solution)/shard_map/all_to_all | solution.py:1163
  (54 other events, 478.5 us)

commit v7 on v6

--- a/solution.py
+++ b/solution.py
@@ -167,7 +167,7 @@
         body(i, pl.ds(pl.multiple_of(i * CHUNK, CHUNK), CHUNK))
         return carry
 
-    lax.fori_loop(0, count // CHUNK, step, 0)
+    lax.fori_loop(0, count // CHUNK, step, 0, unroll=True)
 
 
 def lanes_of(base, b, cols, p):

time: 238 us -> 241 us (1.013); the launches traced: 238 us -> 237 us
  no operation moved by 1% of the time
where the time goes in v7:
time: 241 us; the launch traced here: 237 us
  Pallas kernels  85 us (35%)
  waiting for transfers between devices  68.3 us (28%)
  starting transfers between devices  53.5 us (22%)
  blocking collectives  19.4 us (8%)
  local copies, waits for them, and re-layouts  5.13 us (2%)
  other arithmetic  4.49 us (2%)
    pallas_call x11, Pallas kernels, local_call(): return kernel_call(meta, *map(place, ins))  65.2 us
    ppermute x18, waiting for transfers between devices, along_z(): lax.ppermute(value, AXES, self.perm(lambda z, x, y, c: ((z + step) % self...  30.3 us
    ppermute x18, starting transfers between devices, along_z(): lax.ppermute(value, AXES, self.perm(lambda z, x, y, c: ((z + step) % self...  27.7 us
    all_to_all x1, blocking collectives, per_device(): got = lax.all_to_all(vectors, AXES, 0, 0, tiled=True)  19.4 us
    ppermute x6, waiting for transfers between devices, along_y(): lax.ppermute(value, AXES, self.perm(lambda z, x, y, c: (z, x, 1 - y, c)))  15.8 us
    ppermute x4, waiting for transfers between devices, along_x(): lax.ppermute(value, AXES, self.perm(lambda z, x, y, c: (z, 1 - x, y, c)))  15.5 us
    ppermute x6, starting transfers between devices, along_y(): lax.ppermute(value, AXES, self.perm(lambda z, x, y, c: (z, x, 1 - y, c)))  8.3 us
    pallas_call x2, Pallas kernels, everywhere(): call(place_kernel, 'place', (1,), [(b, *whole((count, width))) for b in b...  7.2 us
  transfers between devices with their start and end apart: 54, of which 19 were waited for; matrix products, arithmetic and copies ran while one was open for 2% of the time, Pallas kernels for 28%

profile of v7, /device:TPU:0, one launch (start us, length us, event | category | flops | bytes accessed | tf_op | source)
XLA Modules:
  0.0 237.5 jit_solution(619714058306683333)
XLA Ops:
  4.4 5.0 %collective-permute-start.3 = (bf16[48,1536]{1,0:T(8,128)(2,1)S(1)}, bf16[48,1536]{1,0:T(8,128)(2,1)S(1)}, u32[]{:S(2)}, u32[]{:S(2)}) collective-permute-start(bf16[48,1536]{1,0:T(8,128)(2,1)S(1)} %bitcast.89), channel_id=1, source_target_pairs={{0,24},{1,25},{2,26},{3,27},{4,28},{5,29},{6,30},{7,31},{8,0},{9,1... | collective-permute-start | bytes 442376 | tf_op jit(solution)/shard_map/ppermute | solution.py:107
  10.7 3.0 %collective-permute-done.3 = bf16[48,1536]{1,0:T(8,128)(2,1)S(1)} collective-permute-done((bf16[48,1536]{1,0:T(8,128)(2,1)S(1)}, bf16[48,1536]{1,0:T(8,128)(2,1)S(1)}, u32[]{:S(2)}, u32[]{:S(2)}) %collective-permute-start.3) | collective-permute-done | bytes 147488 | tf_op jit(solution)/shard_map/ppermute | solution.py:107
  13.7 8.5 %collective-permute-done.2 = bf16[48,1536]{1,0:T(8,128)(2,1)S(1)} collective-permute-done((bf16[48,1536]{1,0:T(8,128)(2,1)S(1)}, bf16[48,1536]{1,0:T(8,128)(2,1)S(1)}, u32[]{:S(2)}, u32[]{:S(2)}) %collective-permute-start.2) | collective-permute-done | bytes 147488 | tf_op jit(solution)/shard_map/ppermute | solution.py:107
  29.7 2.6 %collective-permute-done.4 = bf16[4,48,1536]{2,1,0:T(8,128)(2,1)S(1)} collective-permute-done((bf16[4,48,1536]{2,1,0:T(8,128)(2,1)S(1)}, bf16[4,48,1536]{2,1,0:T(8,128)(2,1)S(1)}, u32[]{:S(2)}, u32[]{:S(2)}) %collective-permute-start.4) | collective-permute-done | bytes 589856 | tf_op jit(solution)/shard_map/ppermute | solution.py:112
  37.7 2.3 attn_prep.1
  41.1 5.1 %collective-permute-done.9 = bf16[96,768]{1,0:T(8,128)(2,1)S(1)} collective-permute-done((bf16[96,768]{1,0:T(8,128)(2,1)S(1)}, bf16[96,768]{1,0:T(8,128)(2,1)S(1)}, u32[]{:S(2)}, u32[]{:S(2)}) %collective-permute-start.9) | collective-permute-done | bytes 147488 | tf_op jit(solution)/shard_map/ppermute | solution.py:107
  46.2 3.7 %collective-permute-done.8.refs_1_ = bf16[2,4,48,1536]{3,2,1,0:T(8,128)(2,1)} collective-permute-done((bf16[2,4,48,1536]{3,2,1,0:T(8,128)(2,1)}, bf16[2,4,48,1536]{3,2,1,0:T(8,128)(2,1)}, u32[]{:S(2)}, u32[]{:S(2)}) %collective-permute-start.8) | collective-permute-done | bytes 1179680 | tf_op jit(solution)/shard_map/ppermute | solution.py:119
  56.8 11.5 %attn_fwd.1 = (bf16[512,768]{1,0:T(8,128)(2,1)}, f32[512,768]{1,0:T(8,128)S(1)}, bf16[2,512,1152]{2,1,0:T(8,128)(2,1)S(1)}, bf16[8,768,128]{2,1,0:T(8,128)(2,1)S...) custom-call(s32[6]{0:T(128)S(1)} %stack.94.meta, bf16[512,768]{1,0:T(8,128)(2,1)S(1)} %get-tuple-element.155.x_ref, ...), custom_call_target="tpu_custom_call" | custom-call | flops 1 | bytes 1 | tf_op jit(solution)/shard_map/attn_fwd/pallas_call | solution.py:780
  71.1 12.0 %collective-permute-done.20.refs_5_ = bf16[4,96,768]{2,1,0:T(8,128)(2,1)S(1)} collective-permute-done((bf16[4,96,768]{2,1,0:T(8,128)(2,1)S(1)}, bf16[4,96,768]{2,1,0:T(8,128)(2,1)S(1)}, u32[]{:S(2)}, u32[]{:S(2)}) %collective-permute-start.20) | collective-permute-done | bytes 589856 | tf_op jit(solution)/shard_map/ppermute | solution.py:101
  83.1 4.6 %collective-permute-done.13.sl_ref.sl_b = bf16[512,768]{1,0:T(8,128)(2,1)S(1)} collective-permute-done((bf16[512,768]{1,0:T(8,128)(2,1)}, bf16[512,768]{1,0:T(8,128)(2,1)S(1)}, u32[]{:S(2)}, u32[]{:S(2)}) %collective-permute-start.13) | collective-permute-done | bytes 786464 | tf_op jit(solution)/shard_map/ppermute | solution.py:104
  88.6 10.5 %ff_far.1 = (bf16[512,768]{1,0:T(8,128)(2,1)}, bf16[512,768]{1,0:T(8,128)(2,1)}, bf16[2,512,768]{2,1,0:T(8,128)(2,1)S(1)}, bf16[2,512,768]{2,1,0:T(8,128)(2,1)S(...) custom-call(s32[6]{0:T(128)S(1)} %stack.94.meta, ...), custom_call_target="tpu_custom_call" | custom-call | flops 1 | bytes 1 | tf_op jit(solution)/shard_map/ff_far/pallas_call | solution.py:780
  100.7 8.3 %ff_near.1 = (bf16[512,768]{1,0:T(8,128)(2,1)S(1)}, bf16[512,768]{1,0:T(8,128)(2,1)}, bf16[2,512,768]{2,1,0:T(8,128)(2,1)S(1)}, bf16[2,512,768]{2,1,0:T(8,128)(2...) custom-call(s32[6]{0:T(128)S(1)} %stack.94.meta, bf16[512,768]{1,0:T(8,128)(2,1)S(1)} %copy-done, ...), custom_call_target="tpu_custom_call" | custom-call | flops 1 | bytes 1 | tf_op jit(solution)/shard_map/ff_near/pallas_call | solution.py:780
  109.1 7.4 %ff_grad.1 = (bf16[4,96,768]{2,1,0:T(8,128)(2,1)}, bf16[4,96,768]{2,1,0:T(8,128)(2,1)}, bf16[4,96,768]{2,1,0:T(8,128)(2,1)}, bf16[4,96,768]{2,1,0:T(8,128)(2,1)}...) custom-call(s32[6]{0:T(128)S(1)} %stack.94.meta, ...), custom_call_target="tpu_custom_call" | custom-call | flops 1 | bytes 1 | tf_op jit(solution)/shard_map/ff_grad/pallas_call | solution.py:780
  119.7 7.4 %attn_bwd.1 = (bf16[2,512,1152]{2,1,0:T(8,128)(2,1)S(1)}, bf16[512,768]{1,0:T(8,128)(2,1)S(1)}, f32[512,768]{1,0:T(8,128)S(1)}, f32[8,768]{1,0:T(8,128)S(1)}, f32[2,768]{1,0:T(2,128)S(1)}) custom-call(s32[6]{0:T(128)S(1)} %stack.94.meta, bf16[512,768]{1,0:T(8,128)(2,1)S(1)} %get-tuple-element.185.sga_ref, ...), custom_call_target="tpu_custom_call" | custom-call | flops 1 | bytes 1 | tf_op jit(solution)/shard_map/attn_bwd/pallas_call | solution.py:780
  130.4 5.0 %attn_grad.1 = (bf16[2,2,48,1536]{3,2,1,0:T(8,128)(2,1)S(1)}, bf16[2,2,48,1536]{3,2,1,0:T(8,128)(2,1)S(1)}, bf16[2,2,48,1536]{3,2,1,0:T(8,128)(2,1)S(1)}, bf16[2...) custom-call(s32[6]{0:T(128)S(1)} %stack.94.meta, ...), custom_call_target="tpu_custom_call" | custom-call | flops 1 | bytes 1 | tf_op jit(solution)/shard_map/attn_grad/pallas_call | solution.py:780
  136.5 4.2 %input_grad.1 = (bf16[512,768]{1,0:T(8,128)(2,1)}, f32[8,768]{1,0:T(8,128)S(1)}) custom-call(s32[6]{0:T(128)S(1)} %stack.94.meta, bf16[512,768]{1,0:T(8,128)(2,1)S(1)} %get-tuple-element.155.x_ref, f32[512,768]{1,0:T(8,128)S(1)} %get-tuple-element.209.mg_ref, f32[6,768]{1,0:T(8,128)S(1)} %copy-done.1, bf16[2,512,1152]{2,1,0:T(8,128)(2,1)S(1)} %get-tuple-element.210.dqkv_ref, ...), custom_call_target="tpu_custom_call" | custom-call | flops 1 | bytes 1 | tf_op jit(solution)/shard_map/input_grad/pallas_call | solution.py:780
  140.7 3.5 %collective-permute-done.30.right = bf16[4,96,768]{2,1,0:T(8,128)(2,1)S(1)} collective-permute-done((bf16[4,96,768]{2,1,0:T(8,128)(2,1)S(1)}, bf16[4,96,768]{2,1,0:T(8,128)(2,1)S(1)}, u32[]{:S(2)}, u32[]{:S(2)}) %collective-permute-start.30) | collective-permute-done | bytes 589856 | tf_op jit(solution)/shard_map/ppermute | solution.py:101
  145.6 3.3 %add_first.1 = (bf16[2,4,48,1536]{3,2,1,0:T(8,128)(2,1)S(1)}, bf16[2,4,48,1536]{3,2,1,0:T(8,128)(2,1)}) custom-call(s32[6]{0:T(128)S(1)} %stack.94.meta, bf16[2,2,48,1536]{3,2,1,0:T(8,128)(2,1)S(1)} %get-tuple-element.203.refs_0_, bf16[2,2,48,1536]{3,2,1,0:T(8,128)(2,1)S(1)} %get-tuple-element.204.refs_1_, ...), custom_call_target="tpu_custom_call" | custom-call | flops 1 | bytes 1 | tf_op jit(solution)/shard_map/add_first/pallas_call | solution.py:780
  152.8 2.4 %collective-permute-start.37 = (bf16[96,768]{1,0:T(8,128)(2,1)}, bf16[96,768]{1,0:T(8,128)(2,1)S(1)}, u32[]{:S(2)}, u32[]{:S(2)}) collective-permute-start(bf16[96,768]{1,0:T(8,128)(2,1)} %get-tuple-element.228), channel_id=1, source_target_pairs={{0,16},{1,17},{2,18},{3,19},{4,20},{5,21},{6,22},{7,23},{8,24},{9,... | collective-permute-start | bytes 442376 | tf_op jit(solution)/shard_map/ppermute | solution.py:107
  157.3 19.4 %all_to_all.10 = f32[32,1,384]{2,1,0:T(1,128)S(1)} all-to-all(f32[32,1,384]{2,1,0:T(1,128)} %vectors.1), channel_id=1, replica_groups=mesh['dp'=8,'mp'=4] {'dp','mp'}, dimensions={0} | all-to-all | bytes 98304 | tf_op jit(solution)/shard_map/all_to_all | solution.py:1087
  181.6 2.4 %collective-permute-start.42 = (bf16[96,768]{1,0:T(8,128)(2,1)S(1)}, bf16[96,768]{1,0:T(8,128)(2,1)S(1)}, u32[]{:S(2)}, u32[]{:S(2)}) collective-permute-start(bf16[96,768]{1,0:T(8,128)(2,1)S(1)} %get-tuple-element.238), channel_id=1, source_target_pairs={{0,16},{1,17},{2,18},{3,19},{4,20},{5,21},{6,22},{7,23},{8,24},{9,... | collective-permute-start | bytes 442376 | tf_op jit(solution)/shard_map/ppermute | solution.py:107
  186.4 3.2 %collective-permute-done.41.refs_5_ = bf16[96,768]{1,0:T(8,128)(2,1)S(1)} collective-permute-done((bf16[96,768]{1,0:T(8,128)(2,1)S(1)}, bf16[96,768]{1,0:T(8,128)(2,1)S(1)}, u32[]{:S(2)}, u32[]{:S(2)}) %collective-permute-start.41) | collective-permute-done | bytes 147488 | tf_op jit(solution)/shard_map/ppermute | solution.py:107
  189.6 5.2 %collective-permute-done.42.refs_6_ = bf16[96,768]{1,0:T(8,128)(2,1)S(1)} collective-permute-done((bf16[96,768]{1,0:T(8,128)(2,1)S(1)}, bf16[96,768]{1,0:T(8,128)(2,1)S(1)}, u32[]{:S(2)}, u32[]{:S(2)}) %collective-permute-start.42) | collective-permute-done | bytes 147488 | tf_op jit(solution)/shard_map/ppermute | solution.py:107
  196.2 2.9 %collective-permute-start.44 = (bf16[48,1536]{1,0:T(8,128)(2,1)S(1)}, bf16[48,1536]{1,0:T(8,128)(2,1)S(1)}, u32[]{:S(2)}, u32[]{:S(2)}) collective-permute-start(bf16[48,1536]{1,0:T(8,128)(2,1)S(1)} %get-tuple-element.241), channel_id=1, source_target_pairs={{0,8},{1,9},{2,10},{3,11},{4,12},{5,13},{6,14},{7,15},{8,16},{9,17... | collective-permute-start | bytes 442376 | tf_op jit(solution)/shard_map/ppermute | solution.py:107
  201.4 2.3 ff_total.1
  207.3 2.7 %collective-permute-done.48.refs_2_ = bf16[48,1536]{1,0:T(8,128)(2,1)S(1)} collective-permute-done((bf16[48,1536]{1,0:T(8,128)(2,1)S(1)}, bf16[48,1536]{1,0:T(8,128)(2,1)S(1)}, u32[]{:S(2)}, u32[]{:S(2)}) %collective-permute-start.48) | collective-permute-done | bytes 147488 | tf_op jit(solution)/shard_map/ppermute | solution.py:107
  210.1 2.3 total.1
  213.0 8.2 %collective-permute-done.47.by_y = bf16[512,768]{1,0:T(8,128)(2,1)S(1)} collective-permute-done((bf16[512,768]{1,0:T(8,128)(2,1)S(1)}, bf16[512,768]{1,0:T(8,128)(2,1)S(1)}, u32[]{:S(2)}, u32[]{:S(2)}) %collective-permute-start.47) | collective-permute-done | bytes 786464 | tf_op jit(solution)/shard_map/ppermute | solution.py:104
  221.7 3.3 %all-to-all-start.1 = ((f32[32,1,512]{2,1,0:T(1,128)}), f32[32,1,512]{2,1,0:T(1,128)S(1)}, u32[]{:S(2)}, u32[]{:S(2)}) async-start(f32[32,1,512]{2,1,0:T(1,128)} %get-tuple-element.253), calls=%async_computation.1 | async-start | bytes 131072 | tf_op jit(solution)/shard_map/all_to_all | solution.py:1163
  225.0 3.8 %place.2 = bf16[2048,768]{1,0:T(8,128)(2,1)} custom-call(s32[6]{0:T(128)S(1)} %stack.94.meta, bf16[512,768]{1,0:T(8,128)(2,1)S(1)} %get-tuple-element.243.own, bf16[512,768]{1,0:T(8,128)(2,1)} %get-tuple-element.244.by_y, bf16[512,768]{1,0:T(8,128)(2,1)} %collective-permute-done.45.by_c, bf16[512,768]{1,0:T(8,128)(2,1)} %collective-permute-done.46.by_yc), custom_call_target="tpu_custom_call" | custom-call | flops 1 | bytes 1 | tf_op jit(solution)/shard_map/place/pallas_call | solution.py:1135
  228.9 3.4 %place.3 = bf16[2048,768]{1,0:T(8,128)(2,1)} custom-call(s32[6]{0:T(128)S(1)} %stack.94.meta, bf16[512,768]{1,0:T(8,128)(2,1)S(1)} %copy-done.2, bf16[512,768]{1,0:T(8,128)(2,1)S(1)} %collective-permute-done.47.by_y, bf16[512,768]{1,0:T(8,128)(2,1)S(1)} %collective-permute-done.50.by_c, bf16[512,768]{1,0:T(8,128)(2,1)} %collective-permute-done.51.by_yc), custom_call_target="tpu_custom_call" | custom-call | flops 1 | bytes 1 | tf_op jit(solution)/shard_map/place/pallas_call | solution.py:1135
  233.1 4.2 %adam.1 = (f32[3,96,192]{2,1,0:T(8,128)}, f32[3,96,192]{2,1,0:T(8,128)}, f32[3,96,192]{2,1,0:T(8,128)}, f32[192,96]{1,0:T(8,128)}, f32[192,96]{1,0:T(8,128)}, /*...) custom-call(s32[6]{0:T(128)S(1)} %stack.94.meta, ...), custom_call_target="tpu_custom_call" | custom-call | flops 1 | bytes 1 | tf_op jit(solution)/shard_map/adam/pallas_call | solution.py:780
  (196 shorter events, 62.2 us)
Async XLA Ops:
  9.4 12.8 %collective-permute-start.2 = (bf16[48,1536]{1,0:T(8,128)(2,1)S(1)}, bf16[48,1536]{1,0:T(8,128)(2,1)S(1)}, u32[]{:S(2)}, u32[]{:S(2)}) collective-permute-start(bf16[48,1536]{1,0:T(8,128)(2,1)S(1)} %bitcast.90), channel_id=1, source_target_pairs={{0,16},{1,17},{2,18},{3,19},{4,20},{5,21},{6,22},{7,23},{8,24},{9,... | collective-permute-start | bytes 442376 | tf_op jit(solution)/shard_map/ppermute | solution.py:107
  9.4 12.8 %collective-permute-start.1 = (bf16[48,1536]{1,0:T(8,128)(2,1)S(1)}, bf16[48,1536]{1,0:T(8,128)(2,1)S(1)}, u32[]{:S(2)}, u32[]{:S(2)}) collective-permute-start(bf16[48,1536]{1,0:T(8,128)(2,1)S(1)} %bitcast.91), channel_id=1, source_target_pairs={{0,8},{1,9},{2,10},{3,11},{4,12},{5,13},{6,14},{7,15},{8,16},{9,17... | collective-permute-start | bytes 442376 | tf_op jit(solution)/shard_map/ppermute | solution.py:107
  33.4 16.5 %collective-permute-start.8 = (bf16[2,4,48,1536]{3,2,1,0:T(8,128)(2,1)}, bf16[2,4,48,1536]{3,2,1,0:T(8,128)(2,1)}, u32[]{:S(2)}, u32[]{:S(2)}) collective-permute-start(bf16[2,4,48,1536]{3,2,1,0:T(8,128)(2,1)} %pad_maximum_fusion.refs_0_), channel_id=1, source_target_pairs={{0,2},{1,5},{2,0},{3,7},{4,6},{5,1},{6,4},{7,3},{8,10},{9,13},{10,... | collective-permute-start | bytes 3538952 | tf_op jit(solution)/shard_map/ppermute | solution.py:119
  37.7 17.5 %collective-permute-start.11 = (bf16[2,4,48,1536]{3,2,1,0:T(8,128)(2,1)}, bf16[2,4,48,1536]{3,2,1,0:T(8,128)(2,1)}, u32[]{:S(2)}, u32[]{:S(2)}) collective-permute-start(bf16[2,4,48,1536]{3,2,1,0:T(8,128)(2,1)} %pad_maximum_fusion.refs_0_), channel_id=1, source_target_pairs={{0,1},{1,0},{2,3},{3,2},{4,5},{5,4},{6,7},{7,6},{8,9},{9,8},{10,11... | collective-permute-start | bytes 3538952 | tf_op jit(solution)/shard_map/ppermute | solution.py:98
  50.0 18.3 %collective-permute-start.19 = (bf16[96,768]{1,0:T(8,128)(2,1)S(1)}, bf16[96,768]{1,0:T(8,128)(2,1)S(1)}, u32[]{:S(2)}, u32[]{:S(2)}) collective-permute-start(bf16[96,768]{1,0:T(8,128)(2,1)S(1)} %bitcast_convert_fusion), channel_id=1, source_target_pairs={{0,24},{1,25},{2,26},{3,27},{4,28},{5,29},{6,30},{7,31},{8,0},{9,1... | collective-permute-start | bytes 442376 | tf_op jit(solution)/shard_map/ppermute | solution.py:107
  51.4 16.9 %collective-permute-start.18 = (bf16[96,768]{1,0:T(8,128)(2,1)S(1)}, bf16[96,768]{1,0:T(8,128)(2,1)S(1)}, u32[]{:S(2)}, u32[]{:S(2)}) collective-permute-start(bf16[96,768]{1,0:T(8,128)(2,1)S(1)} %bitcast_convert_fusion), channel_id=1, source_target_pairs={{0,16},{1,17},{2,18},{3,19},{4,20},{5,21},{6,22},{7,23},{8,24},{9,... | collective-permute-start | bytes 442376 | tf_op jit(solution)/shard_map/ppermute | solution.py:107
  52.9 15.4 %collective-permute-start.17 = (bf16[96,768]{1,0:T(8,128)(2,1)S(1)}, bf16[96,768]{1,0:T(8,128)(2,1)S(1)}, u32[]{:S(2)}, u32[]{:S(2)}) collective-permute-start(bf16[96,768]{1,0:T(8,128)(2,1)S(1)} %bitcast_convert_fusion), channel_id=1, source_target_pairs={{0,8},{1,9},{2,10},{3,11},{4,12},{5,13},{6,14},{7,15},{8,16},{9,17... | collective-permute-start | bytes 442376 | tf_op jit(solution)/shard_map/ppermute | solution.py:107
  55.2 15.3 %collective-permute-start.14 = (bf16[4,96,768]{2,1,0:T(8,128)(2,1)S(1)}, bf16[4,96,768]{2,1,0:T(8,128)(2,1)S(1)}, u32[]{:S(2)}, u32[]{:S(2)}) collective-permute-start(bf16[4,96,768]{2,1,0:T(8,128)(2,1)S(1)} %pad_maximum_fusion.2.refs_0_), channel_id=1, source_target_pairs={{0,4},{1,5},{2,6},{3,7},{4,0},{5,1},{6,2},{7,3},{8,12},{9,13},{10,... | collective-permute-start | bytes 1769480 | tf_op jit(solution)/shard_map/ppermute | solution.py:101
  68.4 14.7 %collective-permute-start.20 = (bf16[4,96,768]{2,1,0:T(8,128)(2,1)S(1)}, bf16[4,96,768]{2,1,0:T(8,128)(2,1)S(1)}, u32[]{:S(2)}, u32[]{:S(2)}) collective-permute-start(bf16[4,96,768]{2,1,0:T(8,128)(2,1)S(1)} %pad_maximum_fusion.3.refs_4_), channel_id=1, source_target_pairs={{0,4},{1,5},{2,6},{3,7},{4,0},{5,1},{6,2},{7,3},{8,12},{9,13},{10,... | collective-permute-start | bytes 1769480 | tf_op jit(solution)/shard_map/ppermute | solution.py:101
  69.0 18.8 %collective-permute-start.13 = (bf16[512,768]{1,0:T(8,128)(2,1)}, bf16[512,768]{1,0:T(8,128)(2,1)S(1)}, u32[]{:S(2)}, u32[]{:S(2)}) collective-permute-start(bf16[512,768]{1,0:T(8,128)(2,1)} %get-tuple-element.164.sl_ref.sl_a), channel_id=1, source_target_pairs={{0,2},{1,3},{2,0},{3,1},{4,6},{5,7},{6,4},{7,5},{8,10},{9,11},{10,... | collective-permute-start | bytes 2359304 | tf_op jit(solution)/shard_map/ppermute | solution.py:104
  70.5 12.6 %collective-permute-start.15 = (bf16[4,96,768]{2,1,0:T(8,128)(2,1)S(1)}, bf16[4,96,768]{2,1,0:T(8,128)(2,1)S(1)}, u32[]{:S(2)}, u32[]{:S(2)}) collective-permute-start(bf16[4,96,768]{2,1,0:T(8,128)(2,1)S(1)} %pad_maximum_fusion.2.refs_0_), channel_id=1, source_target_pairs={{0,1},{1,0},{2,3},{3,2},{4,5},{5,4},{6,7},{7,6},{8,9},{9,8},{10,11... | collective-permute-start | bytes 1769480 | tf_op jit(solution)/shard_map/ppermute | solution.py:98
  70.5 12.6 %collective-permute-start.16 = (bf16[4,96,768]{2,1,0:T(8,128)(2,1)S(1)}, bf16[4,96,768]{2,1,0:T(8,128)(2,1)S(1)}, u32[]{:S(2)}, u32[]{:S(2)}) collective-permute-start(bf16[4,96,768]{2,1,0:T(8,128)(2,1)S(1)} %collective-permute-done.14.refs_1_), channel_id=1, source_target_pairs={{0,1},{1,0},{2,3},{3,2},{4,5},{5,4},{6,7},{7,6},{8,9},{9,8},{10,11... | collective-permute-start | bytes 1769480 | tf_op jit(solution)/shard_map/ppermute | solution.py:98
  71.0 12.1 %collective-permute-start.21 = (bf16[4,96,768]{2,1,0:T(8,128)(2,1)S(1)}, bf16[4,96,768]{2,1,0:T(8,128)(2,1)S(1)}, u32[]{:S(2)}, u32[]{:S(2)}) collective-permute-start(bf16[4,96,768]{2,1,0:T(8,128)(2,1)S(1)} %pad_maximum_fusion.3.refs_4_), channel_id=1, source_target_pairs={{0,1},{1,0},{2,3},{3,2},{4,5},{5,4},{6,7},{7,6},{8,9},{9,8},{10,11... | collective-permute-start | bytes 1769480 | tf_op jit(solution)/shard_map/ppermute | solution.py:98
  99.2 17.9 %collective-permute-start.23 = (bf16[512,768]{1,0:T(8,128)(2,1)}, bf16[512,768]{1,0:T(8,128)(2,1)S(1)}, u32[]{:S(2)}, u32[]{:S(2)}) collective-permute-start(bf16[512,768]{1,0:T(8,128)(2,1)} %get-tuple-element.175), channel_id=1, source_target_pairs={{0,2},{1,3},{2,0},{3,1},{4,6},{5,7},{6,4},{7,5},{8,10},{9,11},{10,... | collective-permute-start | bytes 2359304 | tf_op jit(solution)/shard_map/ppermute | solution.py:104
  117.1 18.3 %collective-permute-start.24 = (bf16[512,768]{1,0:T(8,128)(2,1)S(1)}, bf16[512,768]{1,0:T(8,128)(2,1)S(1)}, u32[]{:S(2)}, u32[]{:S(2)}) collective-permute-start(bf16[512,768]{1,0:T(8,128)(2,1)S(1)} %copy-done.3), channel_id=1, source_target_pairs={{0,2},{1,3},{2,0},{3,1},{4,6},{5,7},{6,4},{7,5},{8,10},{9,11},{10,... | collective-permute-start | bytes 2359304 | tf_op jit(solution)/shard_map/ppermute | solution.py:104
  128.9 15.2 %collective-permute-start.30 = (bf16[4,96,768]{2,1,0:T(8,128)(2,1)S(1)}, bf16[4,96,768]{2,1,0:T(8,128)(2,1)S(1)}, u32[]{:S(2)}, u32[]{:S(2)}) collective-permute-start(bf16[4,96,768]{2,1,0:T(8,128)(2,1)S(1)} %bitcast.72), channel_id=1, source_target_pairs={{0,4},{1,5},{2,6},{3,7},{4,0},{5,1},{6,2},{7,3},{8,12},{9,13},{10,... | collective-permute-start | bytes 1769480 | tf_op jit(solution)/shard_map/ppermute | solution.py:101
  148.9 27.9 %collective-permute-start.34 = (bf16[2,4,48,1536]{3,2,1,0:T(8,128)(2,1)}, bf16[2,4,48,1536]{3,2,1,0:T(8,128)(2,1)S(1)}, u32[]{:S(2)}, u32[]{:S(2)}) collective-permute-start(bf16[2,4,48,1536]{3,2,1,0:T(8,128)(2,1)} %get-tuple-element.217), channel_id=1, source_target_pairs={{0,2},{1,5},{2,0},{3,7},{4,6},{5,1},{6,4},{7,3},{8,10},{9,13},{10,... | collective-permute-start | bytes 3538952 | tf_op jit(solution)/shard_map/ppermute | solution.py:119
  149.4 27.4 %collective-permute-start.35 = (bf16[4,96,768]{2,1,0:T(8,128)(2,1)}, bf16[4,96,768]{2,1,0:T(8,128)(2,1)}, u32[]{:S(2)}, u32[]{:S(2)}) collective-permute-start(bf16[4,96,768]{2,1,0:T(8,128)(2,1)} %bitcast.33), channel_id=1, source_target_pairs={{0,4},{1,5},{2,6},{3,7},{4,0},{5,1},{6,2},{7,3},{8,12},{9,13},{10,... | collective-permute-start | bytes 1769480 | tf_op jit(solution)/shard_map/ppermute | solution.py:101
  152.2 24.5 %collective-permute-start.36 = (bf16[96,768]{1,0:T(8,128)(2,1)}, bf16[96,768]{1,0:T(8,128)(2,1)S(1)}, u32[]{:S(2)}, u32[]{:S(2)}) collective-permute-start(bf16[96,768]{1,0:T(8,128)(2,1)} %get-tuple-element.227), channel_id=1, source_target_pairs={{0,8},{1,9},{2,10},{3,11},{4,12},{5,13},{6,14},{7,15},{8,16},{9,17... | collective-permute-start | bytes 442376 | tf_op jit(solution)/shard_map/ppermute | solution.py:107
  152.8 24.0 %collective-permute-start.37 = (bf16[96,768]{1,0:T(8,128)(2,1)}, bf16[96,768]{1,0:T(8,128)(2,1)S(1)}, u32[]{:S(2)}, u32[]{:S(2)}) collective-permute-start(bf16[96,768]{1,0:T(8,128)(2,1)} %get-tuple-element.228), channel_id=1, source_target_pairs={{0,16},{1,17},{2,18},{3,19},{4,20},{5,21},{6,22},{7,23},{8,24},{9,... | collective-permute-start | bytes 442376 | tf_op jit(solution)/shard_map/ppermute | solution.py:107
  155.2 21.6 %collective-permute-start.38 = (bf16[96,768]{1,0:T(8,128)(2,1)}, bf16[96,768]{1,0:T(8,128)(2,1)}, u32[]{:S(2)}, u32[]{:S(2)}) collective-permute-start(bf16[96,768]{1,0:T(8,128)(2,1)} %get-tuple-element.229), channel_id=1, source_target_pairs={{0,24},{1,25},{2,26},{3,27},{4,28},{5,29},{6,30},{7,31},{8,0},{9,1... | collective-permute-start | bytes 442376 | tf_op jit(solution)/shard_map/ppermute | solution.py:107
  177.7 17.2 %collective-permute-start.40 = (bf16[4,48,1536]{2,1,0:T(8,128)(2,1)S(1)}, bf16[4,48,1536]{2,1,0:T(8,128)(2,1)S(1)}, u32[]{:S(2)}, u32[]{:S(2)}) collective-permute-start(bf16[4,48,1536]{2,1,0:T(8,128)(2,1)S(1)} %bitcast.73), channel_id=1, source_target_pairs={{0,4},{1,3},{2,6},{3,1},{4,0},{5,7},{6,2},{7,5},{8,12},{9,11},{10,... | collective-permute-start | bytes 1769480 | tf_op jit(solution)/shard_map/ppermute | solution.py:112
  181.6 13.3 %collective-permute-start.42 = (bf16[96,768]{1,0:T(8,128)(2,1)S(1)}, bf16[96,768]{1,0:T(8,128)(2,1)S(1)}, u32[]{:S(2)}, u32[]{:S(2)}) collective-permute-start(bf16[96,768]{1,0:T(8,128)(2,1)S(1)} %get-tuple-element.238), channel_id=1, source_target_pairs={{0,16},{1,17},{2,18},{3,19},{4,20},{5,21},{6,22},{7,23},{8,24},{9,... | collective-permute-start | bytes 442376 | tf_op jit(solution)/shard_map/ppermute | solution.py:107
  184.0 10.9 %collective-permute-start.43 = (bf16[96,768]{1,0:T(8,128)(2,1)S(1)}, bf16[96,768]{1,0:T(8,128)(2,1)S(1)}, u32[]{:S(2)}, u32[]{:S(2)}) collective-permute-start(bf16[96,768]{1,0:T(8,128)(2,1)S(1)} %get-tuple-element.239), channel_id=1, source_target_pairs={{0,24},{1,25},{2,26},{3,27},{4,28},{5,29},{6,30},{7,31},{8,0},{9,1... | collective-permute-start | bytes 442376 | tf_op jit(solution)/shard_map/ppermute | solution.py:107
  185.0 20.4 %collective-permute-start.39 = (bf16[512,768]{1,0:T(8,128)(2,1)S(1)}, bf16[512,768]{1,0:T(8,128)(2,1)S(1)}, u32[]{:S(2)}, u32[]{:S(2)}) collective-permute-start(bf16[512,768]{1,0:T(8,128)(2,1)S(1)} %copy-done.5), channel_id=1, source_target_pairs={{0,2},{1,3},{2,0},{3,1},{4,6},{5,7},{6,4},{7,5},{8,10},{9,11},{10,... | collective-permute-start | bytes 2359304 | tf_op jit(solution)/shard_map/ppermute | solution.py:104
  195.5 25.6 %collective-permute-start.47 = (bf16[512,768]{1,0:T(8,128)(2,1)S(1)}, bf16[512,768]{1,0:T(8,128)(2,1)S(1)}, u32[]{:S(2)}, u32[]{:S(2)}) collective-permute-start(bf16[512,768]{1,0:T(8,128)(2,1)S(1)} %copy-done.2), channel_id=1, source_target_pairs={{0,2},{1,3},{2,0},{3,1},{4,6},{5,7},{6,4},{7,5},{8,10},{9,11},{10,... | collective-permute-start | bytes 2359304 | tf_op jit(solution)/shard_map/ppermute | solution.py:104
  199.1 11.0 %collective-permute-start.48 = (bf16[48,1536]{1,0:T(8,128)(2,1)S(1)}, bf16[48,1536]{1,0:T(8,128)(2,1)S(1)}, u32[]{:S(2)}, u32[]{:S(2)}) collective-permute-start(bf16[48,1536]{1,0:T(8,128)(2,1)S(1)} %get-tuple-element.247), channel_id=1, source_target_pairs={{0,16},{1,17},{2,18},{3,19},{4,20},{5,21},{6,22},{7,23},{8,24},{9,... | collective-permute-start | bytes 442376 | tf_op jit(solution)/shard_map/ppermute | solution.py:107
  205.1 23.8 %collective-permute-start.50 = (bf16[512,768]{1,0:T(8,128)(2,1)S(1)}, bf16[512,768]{1,0:T(8,128)(2,1)S(1)}, u32[]{:S(2)}, u32[]{:S(2)}) collective-permute-start(bf16[512,768]{1,0:T(8,128)(2,1)S(1)} %copy-done.2), channel_id=1, source_target_pairs={{0,1},{1,0},{2,3},{3,2},{4,5},{5,4},{6,7},{7,6},{8,9},{9,8},{10,11... | collective-permute-start | bytes 2359304 | tf_op jit(solution)/shard_map/ppermute | solution.py:98
  207.1 17.9 %collective-permute-start.45 = (bf16[512,768]{1,0:T(8,128)(2,1)S(1)}, bf16[512,768]{1,0:T(8,128)(2,1)}, u32[]{:S(2)}, u32[]{:S(2)}) collective-permute-start(bf16[512,768]{1,0:T(8,128)(2,1)S(1)} %get-tuple-element.243.own), channel_id=1, source_target_pairs={{0,1},{1,0},{2,3},{3,2},{4,5},{5,4},{6,7},{7,6},{8,9},{9,8},{10,11... | collective-permute-start | bytes 2359304 | tf_op jit(solution)/shard_map/ppermute | solution.py:98
  210.1 14.9 %collective-permute-start.46 = (bf16[512,768]{1,0:T(8,128)(2,1)}, bf16[512,768]{1,0:T(8,128)(2,1)}, u32[]{:S(2)}, u32[]{:S(2)}) collective-permute-start(bf16[512,768]{1,0:T(8,128)(2,1)} %get-tuple-element.244.by_y), channel_id=1, source_target_pairs={{0,1},{1,0},{2,3},{3,2},{4,5},{5,4},{6,7},{7,6},{8,9},{9,8},{10,11... | collective-permute-start | bytes 2359304 | tf_op jit(solution)/shard_map/ppermute | solution.py:98
  221.2 11.2 %collective-permute-start.52 = (f32[48,768]{1,0:T(8,128)S(1)}, f32[48,768]{1,0:T(8,128)S(1)}, u32[]{:S(2)}, u32[]{:S(2)}) collective-permute-start(f32[48,768]{1,0:T(8,128)S(1)} %get-tuple-element.255), channel_id=1, source_target_pairs={{0,1},{1,0},{2,3},{3,2},{4,5},{5,4},{6,7},{7,6},{8,9},{9,8},{10,11... | collective-permute-start | bytes 442376 | tf_op jit(solution)/shard_map/ppermute | solution.py:98
  221.7 10.7 %all-to-all-start.1 = ((f32[32,1,512]{2,1,0:T(1,128)}), f32[32,1,512]{2,1,0:T(1,128)S(1)}, u32[]{:S(2)}, u32[]{:S(2)}) async-start(f32[32,1,512]{2,1,0:T(1,128)} %get-tuple-element.253), calls=%async_computation.1 | async-start | bytes 131072 | tf_op jit(solution)/shard_map/all_to_all | solution.py:1163
  (54 other events, 479.1 us)
